TPU v7x, 128 devices: a whole 4x4x4 slice. The times are simulated.
128 devices in a mesh: batch: 16 (over y, z), proto: 8 (over x, core).
Axes of the slice: x: 4, y: 4, z: 4, core: 2. Of those that a mesh axis runs over, the one named last changes fastest.
Arguments:
- features: bfloat16 [16384, 2048], P(('batch', 'proto')), may hold values from -24 to 24
- w_first: bfloat16 [2048, 2048], replicated, may hold values from -0.125 to 0.125
- bn_gain: float32 [2048], replicated, may hold values from 0.1 to 1.9
- bn_bias: float32 [2048], replicated, may hold values from -3 to 3
- w_second: bfloat16 [2048, 256], replicated, may hold values from -0.125 to 0.125
- prototypes: bfloat16 [16384, 256], P('proto'), may hold values from -16 to 16
- pair: int32 [16384], P('batch'), may hold values from 0 to 16383, as said below
Outputs:
- grad_first: float32 [2048, 2048], P(('batch', 'proto'))
- grad_second: float32 [2048, 256], P(('batch', 'proto'))
- grad_gain: float32 [2048], replicated
- grad_bias: float32 [2048], replicated
- grad_proto: float32 [16384, 256], P('proto', 'batch')
- loss: float32 [], replicated
Inputs may be any that keep to these rules, and one draw needn't show every extreme that they name: pair is an involution without fixed points: pair[pair[i]] = i and pair[i] != i, and rows i and pair[i] lie in the same aligned block of 1024 rows.
All inputs are finite; a program needn't handle non-finite values.
Results may differ from a plain program's by a relative error of at most 0.015.
Values may be sent and summed in bfloat16 or wider, within the bound.
No kernel may reach another device: no remote copies, remote signals or barrier semaphores. Data moves between devices by JAX's collectives and lax.ppermute only.
A program may use at most 128 MiB of HBM per device.

v0:
```python
import jax
import jax.numpy as jnp
from jax import lax
from jax.sharding import PartitionSpec as P

ITERS = 3


transport_entropy_weight = 0.05
sharpness_divisor = 0.1


def unit_rows(values):
    rescaling_multiplier = lax.rsqrt(jnp.sum(values * values, axis=1, keepdims=True) + 1e-06)
    return (values * rescaling_multiplier, rescaling_multiplier)


def cluster_balancing_pass(transport_exponential_matrix, sample_normalizer):
    incomplete_cluster_totals = jnp.dot(
        sample_normalizer, transport_exponential_matrix, precision=lax.Precision.HIGHEST
    )
    return 1.0 / lax.psum(incomplete_cluster_totals, "batch")


def local(features, w_first, bn_gain, bn_bias, w_second, prototypes, pair):
    n_batch = lax.axis_size("batch")
    n_proto = lax.axis_size("proto")
    own_rows = features.shape[0]
    total_rows = own_rows * n_batch * n_proto
    block_rows = own_rows * n_proto
    pre = jnp.dot(features, w_first, preferred_element_type=jnp.float32)
    sum_act, sum_square = lax.psum(
        (jnp.sum(pre, axis=0), jnp.sum(pre * pre, axis=0)), ("batch", "proto")
    )
    mean_act = sum_act / total_rows
    inv_std = lax.rsqrt(sum_square / total_rows - mean_act * mean_act + 1e-05)
    normed = (pre - mean_act) * inv_std
    shifted = normed * bn_gain + bn_bias
    hidden = jax.nn.gelu(shifted).astype(jnp.bfloat16)
    embed = jnp.dot(hidden, w_second, preferred_element_type=jnp.float32)
    unit_embed, embed_scale = unit_rows(embed)
    embed_bf = unit_embed.astype(jnp.bfloat16)
    unit_proto, proto_scale = unit_rows(prototypes.astype(jnp.float32))
    proto_bf = unit_proto.astype(jnp.bfloat16)
    block_embed = lax.all_gather(embed_bf, "proto", axis=0, tiled=True)
    centroid_similarity_matrix = lax.dot_general(
        block_embed, proto_bf, (((1,), (1,)), ((), ())), preferred_element_type=jnp.float32
    )
    transport_exponential_matrix = jnp.exp(centroid_similarity_matrix / transport_entropy_weight)
    centroid_affinities = centroid_similarity_matrix / sharpness_divisor
    exponentiated_entries = jnp.exp(centroid_affinities)
    soft_part = jnp.sum(exponentiated_entries, axis=1)
    sample_normalizer = jnp.ones((block_rows,), jnp.float32)
    per_cluster_multiplier = jnp.ones((transport_exponential_matrix.shape[1],), jnp.float32)
    for step in range(ITERS):
        per_cluster_multiplier = cluster_balancing_pass(
            transport_exponential_matrix, sample_normalizer
        )
        sample_normalizer = 1.0 / lax.psum(
            jnp.dot(
                transport_exponential_matrix,
                per_cluster_multiplier,
                precision=lax.Precision.HIGHEST,
            ),
            "proto",
        )
    normalizing_partition = lax.psum(soft_part, "proto")
    cluster_allocation = (
        transport_exponential_matrix * sample_normalizer[:, None] * per_cluster_multiplier[None, :]
    )
    first_row = lax.axis_index("batch") * block_rows
    goal_allocations = jnp.take(cluster_allocation, pair - first_row, axis=0)
    logp = centroid_affinities - jnp.log(normalizing_partition)[:, None]
    loss_part = -jnp.sum(goal_allocations * logp)
    similarity_derivative = (
        (exponentiated_entries / normalizing_partition[:, None] - goal_allocations)
        / sharpness_divisor
    ).astype(jnp.bfloat16)
    d_unit = lax.psum_scatter(
        jnp.dot(similarity_derivative, proto_bf, preferred_element_type=jnp.float32),
        "proto",
        scatter_dimension=0,
        tiled=True,
    )
    proto_acc = lax.dot_general(
        similarity_derivative,
        block_embed,
        (((0,), (0,)), ((), ())),
        preferred_element_type=jnp.float32,
    )
    proto_term = (
        proto_acc - unit_proto * jnp.sum(unit_proto * proto_acc, axis=1, keepdims=True)
    ) * proto_scale
    grad_proto = lax.psum_scatter(
        proto_term.astype(jnp.bfloat16), "batch", scatter_dimension=1, tiled=True
    ).astype(jnp.float32)
    d_embed = (
        (d_unit - unit_embed * jnp.sum(unit_embed * d_unit, axis=1, keepdims=True)) * embed_scale
    ).astype(jnp.bfloat16)
    second_term = lax.dot_general(
        hidden, d_embed, (((0,), (0,)), ((), ())), preferred_element_type=jnp.float32
    )
    d_hidden = lax.dot_general(
        d_embed, w_second, (((1,), (1,)), ((), ())), preferred_element_type=jnp.float32
    )
    d_shift = jax.vjp(jax.nn.gelu, shifted)[1](d_hidden)[0]
    grad_gain, grad_bias, loss_sum = lax.psum(
        (jnp.sum(d_shift * normed, axis=0), jnp.sum(d_shift, axis=0), loss_part), ("batch", "proto")
    )
    d_pre = (
        bn_gain * inv_std * (d_shift - grad_bias / total_rows - normed * grad_gain / total_rows)
    ).astype(jnp.bfloat16)
    grad_first = lax.psum_scatter(
        lax.dot_general(
            features, d_pre, (((0,), (0,)), ((), ())), preferred_element_type=jnp.float32
        ),
        ("batch", "proto"),
        scatter_dimension=0,
        tiled=True,
    )
    grad_second = lax.psum_scatter(second_term, ("batch", "proto"), scatter_dimension=0, tiled=True)
    loss = loss_sum / total_rows
    return (grad_first, grad_second, grad_gain, grad_bias, grad_proto, loss)


def solution(mesh):
    return jax.shard_map(
        local,
        mesh=mesh,
        in_specs=(P(("batch", "proto"), None), P(), P(), P(), P(), P("proto", None), P("batch")),
        out_specs=(
            P(("batch", "proto"), None),
            P(("batch", "proto"), None),
            P(),
            P(),
            P("proto", "batch"),
            P(),
        ),
        check_vma=False,
    )
```

profile of v0, /device:TPU:1, one launch (start us, length us, event | category | flops | bytes accessed | tf_op | source)
XLA Modules:
  0.0 1758.7 jit_solution(4030735092820657672)
XLA Ops:
  7.2 0.0 reduce-scatter.7.cloned.1.call-start
  7.2 0.8 compare_and_fusion
  8.0 0.7 fusion.31
  8.7 1.5 copy.15
  10.2 0.2 fusion.13
  10.5 4.9 fusion.42
  15.3 68.9 %all-reduce.1 = (f32[2048]{0:T(1024)S(1)}, f32[2048]{0:T(1024)S(1)}) all-reduce(f32[2048]{0:T(1024)S(1)} %get-tuple-element.21, f32[2048]{0:T(1024)S(1)} %get-tuple-element.20), channel_id=1, replica_groups=mesh['batch'=16,'proto'=8] {'batch','proto'}, use_global_device_ids=true, to_apply=%region_1.0 | all-reduce | flops 4096 | bytes 32768 | tf_op jit(solution)/shard_map/psum | solution.py:32
  84.3 0.5 multiply_convert_fusion.2
  84.8 0.4 multiply_reduce_fusion.4
  85.2 0.1 multiply_convert_fusion.5
  85.3 0.3 copy-done.2
  85.6 13.8 all_gather.3
  99.5 1.7 exponential_reduce_fusion
  101.2 3.2 copy-done.1
  104.4 4.7 fusion.8
  109.1 31.2 %psum.87 = f32[2048]{0:T(1024)S(1)} all-reduce(f32[2048]{0:T(1024)S(1)} %bitcast.37), channel_id=1, replica_groups=mesh['batch'=16,'proto'=8] {'batch'}, use_global_device_ids=true, to_apply=%region_8.0 | all-reduce | flops 2048 | bytes 16384 | tf_op jit(solution)/shard_map/psum | solution.py:22
  140.4 10.2 fusion.7
  150.6 19.2 %psum.88 = f32[1024]{0:T(1024)S(1)} all-reduce(f32[1024]{0:T(1024)S(1)} %bitcast.39), channel_id=1, replica_groups=mesh['batch'=16,'proto'=8] {'proto'}, use_global_device_ids=true, to_apply=%region_9.0 | all-reduce | flops 1024 | bytes 8192 | tf_op jit(solution)/shard_map/psum | solution.py:59
  169.8 7.1 fusion.6
  176.8 29.3 %psum.89 = f32[2048]{0:T(1024)S(1)} all-reduce(f32[2048]{0:T(1024)S(1)} %bitcast.34), channel_id=1, replica_groups=mesh['batch'=16,'proto'=8] {'batch'}, use_global_device_ids=true, to_apply=%region_10.0 | all-reduce | flops 2048 | bytes 16384 | tf_op jit(solution)/shard_map/psum | solution.py:22
  206.2 10.2 fusion.5
  216.4 19.1 %psum.90 = f32[1024]{0:T(1024)S(1)} all-reduce(f32[1024]{0:T(1024)S(1)} %bitcast.41), channel_id=1, replica_groups=mesh['batch'=16,'proto'=8] {'proto'}, use_global_device_ids=true, to_apply=%region_11.0 | all-reduce | flops 1024 | bytes 8192 | tf_op jit(solution)/shard_map/psum | solution.py:59
  235.4 7.1 fusion.4
  242.5 31.3 %psum.91 = f32[2048]{0:T(1024)S(1)} all-reduce(f32[2048]{0:T(1024)S(1)} %bitcast.36), channel_id=1, replica_groups=mesh['batch'=16,'proto'=8] {'batch'}, use_global_device_ids=true, to_apply=%region_12.0 | all-reduce | flops 2048 | bytes 16384 | tf_op jit(solution)/shard_map/psum | solution.py:22
  273.8 10.2 fusion.3
  284.0 19.5 %all-reduce.2 = (f32[1024]{0:T(1024)S(1)}, f32[1024]{0:T(1024)S(1)}) all-reduce(f32[1024]{0:T(1024)S(1)} %bitcast.38, f32[1024]{0:T(1024)S(1)} %get-tuple-element.38), channel_id=1, replica_groups=mesh['batch'=16,'proto'=8] {'proto'}, use_global_device_ids=true, to_apply=%region_13.0 | all-reduce | flops 2048 | bytes 16384 | tf_op jit(solution)/shard_map/psum | solution.py:59
  303.5 6.3 multiply_multiply_fusion
  309.8 12.5 gather_fusion
  322.3 10.6 multiply_reduce_fusion
  332.9 1.9 copy-done.3
  334.8 2.3 fusion.20
  337.2 0.0 reduce-scatter.11.cloned.1.call-start
  337.2 3.6 fusion.9
  340.9 1.4 fusion.12
  342.3 0.3 reduce-scatter.9.cloned.1.call-start
  342.6 17.6 %reduce-scatter.7.cloned.1.call-done = f32[128,256]{1,0:T(8,128)} async-done(((f32[1024,256]{1,0:T(8,128)}), f32[128,256]{1,0:T(8,128)}) %reduce-scatter.7.cloned.1.call-update) | async-done | bytes 131088 | tf_op jit(solution)/shard_map/reduce_scatter | solution.py:79
  360.2 1.1 multiply_reduce_fusion.3
  361.3 1.0 multiply_convert_fusion.4
  362.3 2.8 fusion.44
  365.1 0.0 reduce-scatter.13.cloned.1.call-start
  365.8 2.1 fusion.41
  368.0 68.3 %all-reduce = (f32[2048]{0:T(1024)S(1)}, f32[2048]{0:T(1024)S(1)}, f32[]{:T(128)}) all-reduce(f32[2048]{0:T(1024)S(1)} %get-tuple-element.19, f32[2048]{0:T(1024)S(1)} %get-tuple-element.18, f32[]{:T(128)S(6)} %neg.3), channel_id=1, replica_groups=mesh['batch'=16,'proto'=8] {'batch','proto'}, use_global_device_ids=true, to_apply=%region_19.20 | all-reduce | flops 4097 | bytes 32776 | tf_op jit(solution)/shard_map/psum | solution.py:107
  436.3 9.3 convolution_bitcast_fusion
  445.7 17.6 %copy.17 = f32[2048,2048]{1,0:T(8,128)} copy(f32[2048,2048]{0,1:T(8,128)} %convolution_bitcast_fusion) | data formatting | bytes 33554432
  464.0 0.0 reduce-scatter.11.cloned.1.call-done
  464.0 1.5 convert_element_type.35
  465.5 616.6 %reduce-scatter.9.cloned.1.call-done = f32[16,256]{1,0:T(8,128)} async-done(((f32[2048,256]{1,0:T(8,128)}), f32[16,256]{1,0:T(8,128)}) %reduce-scatter.9.cloned.1.call-update) | async-done | bytes 16400 | tf_op jit(solution)/shard_map/reduce_scatter | solution.py:121
  1082.1 668.5 %reduce-scatter.13.cloned.1.call-done = f32[16,2048]{1,0:T(8,128)} async-done(((f32[2048,2048]{1,0:T(8,128)}), f32[16,2048]{1,0:T(8,128)}) %reduce-scatter.13.cloned.1.call-update) | async-done | bytes 131088
  (32 shorter events, 0.2 us)
Async XLA Ops:
  7.2 77.6 %copy-start = (bf16[2048,256]{1,0:T(8,128)(2,1)S(1)}, bf16[2048,256]{1,0:T(8,128)(2,1)}, u32[]{:S(2)}) copy-start(bf16[2048,256]{1,0:T(8,128)(2,1)} %param.11) | copy-start | bytes 3145732
  7.2 353.0 %reduce-scatter.7.cloned.1.call-start = ((), (), s32[]{:S(2)}) async-start(), calls=%async_computation.4 | async-start | bytes 1179648 | tf_op jit(solution)/shard_map/reduce_scatter | solution.py:79
  10.2 74.1 %copy-start.7 = (f32[2048]{0:T(1024)S(1)}, f32[2048]{0:T(1024)}, u32[]{:S(2)}) copy-start(f32[2048]{0:T(1024)} %param.9) | copy-start | bytes 24580
  10.2 74.1 %copy-start.8 = (f32[2048]{0:T(1024)S(1)}, f32[2048]{0:T(1024)}, u32[]{:S(2)}) copy-start(f32[2048]{0:T(1024)} %param.10) | copy-start | bytes 24580
  84.8 0.8 copy-start.2
  99.5 9.7 copy-start.5
  101.2 3.2 copy-start.1
  332.9 1.9 copy-start.3
  337.2 126.8 %reduce-scatter.11.cloned.1.call-start = ((), (), s32[]{:S(2)}) async-start(), calls=%async_computation.6 | async-start | bytes 1114112 | tf_op jit(solution)/shard_map/reduce_scatter | solution.py:94
  342.2 94.1 %copy-start.4 = (bf16[128,2048]{1,0:T(8,128)(2,1)S(1)}, bf16[128,2048]{1,0:T(8,128)(2,1)}, u32[]{:S(2)}) copy-start(bf16[128,2048]{1,0:T(8,128)(2,1)} %param.7) | copy-start | bytes 1572868
  342.3 739.8 %reduce-scatter.9.cloned.1.call-start = ((), (), s32[]{:S(2)}) async-start(), calls=%async_computation.5 | async-start | bytes 2113536 | tf_op jit(solution)/shard_map/reduce_scatter | solution.py:121
  365.1 1385.5 %reduce-scatter.13.cloned.1.call-start = ((), (), s32[]{:S(2)}) async-start(), calls=%async_computation.7 | async-start | bytes 16908288
  436.3 9.4 copy-start.6
  436.3 9.4 copy-start.9
Sparse Core Ops, SparseCore 0:
  337.3 22.8 reduce-scatter.6
  363.4 73.9 reduce-scatter.10
  440.4 641.6 reduce-scatter.8
  1084.9 665.6 reduce-scatter.12
where the time goes:
time: 1770 us; the launch traced here: 1760 us
  waiting for transfers between devices  1300 us (73%)
  blocking collectives  301 us (17%)
  matrix products  76.6 us (4%)
  local copies, waits for them, and re-layouts  37.1 us (2%)
  other arithmetic  24.2 us (1%)
    unnamed x5, waiting for transfers between devices  669 us
    reduce_scatter x1, waiting for transfers between devices, local(): lax.psum_scatter(second_term, ('batch', 'proto'), scatter_dimension=0, ti...  617 us
    psum x3, blocking collectives, cluster_balancing_pass(): return 1.0 / lax.psum(incomplete_cluster_totals, 'batch')  91.9 us
    psum x1, blocking collectives, local(): lax.psum((jnp.sum(pre, axis=0), jnp.sum(pre * pre, axis=0)), ('batch', 'p...  68.9 us
    psum x1, blocking collectives, local(): lax.psum((jnp.sum(d_shift * normed, axis=0), jnp.sum(d_shift, axis=0), lo...  68.3 us
    psum x3, blocking collectives, local(): lax.psum(jnp.dot(transport_exponential_matrix, per_cluster_multiplier, pr...  57.7 us
  transfers between devices with their start and end apart: 4, of which 3 were waited for; matrix products, arithmetic and copies ran while one was open for 2% of the time, Pallas kernels for 0%

commit v1 on v0

v1 whole, which is shorter than its diff:
```python
import jax
import jax.numpy as jnp
from jax import lax
from jax.experimental import pallas as pl
from jax.experimental.pallas import tpu as pltpu
from jax.sharding import PartitionSpec as P

ITERS = 3
BF = jnp.bfloat16
F32 = jnp.float32


def spread(x, axis):
    n = lax.axis_size(axis)
    return lax.all_to_all(jnp.broadcast_to(x[None], (n,) + x.shape), axis, 0, 0, tiled=True)


def deal(x, axis):
    return lax.all_to_all(x, axis, 0, 0, tiled=True)


def split3(v):
    hi = v.astype(BF)
    rest = v - hi.astype(F32)
    mid = rest.astype(BF)
    low = (rest - mid.astype(F32)).astype(BF)
    shape = (8, v.shape[1])
    row = lax.broadcasted_iota(jnp.int32, shape, 0)
    parts = jnp.where(row == 0, hi.astype(F32), jnp.where(row == 1, mid.astype(F32), low.astype(F32)))
    return jnp.where(row < 3, parts, 0.0).astype(BF)


def score_kernel(embed_ref, proto_t_ref, kern_ref, col_ref, soft_ref, acc_ref):
    step = pl.program_id(0)

    @pl.when(step == 0)
    def _():
        acc_ref[...] = jnp.zeros_like(acc_ref)

    scores = jnp.dot(embed_ref[...], proto_t_ref[...], preferred_element_type=F32)
    tempered = jnp.exp(scores * 10.0)
    kern = tempered * tempered
    kern_ref[...] = kern.astype(BF)
    acc_ref[0:1, :] += jnp.sum(kern, axis=0, keepdims=True)
    soft = jnp.sum(tempered, axis=1, keepdims=True)
    rows = soft.shape[0]
    eye = lax.broadcasted_iota(jnp.int32, (rows, rows), 0) == lax.broadcasted_iota(jnp.int32, (rows, rows), 1)
    soft_row = jnp.sum(jnp.where(eye, soft, 0.0), axis=0, keepdims=True)
    soft_ref[...] = jnp.broadcast_to(soft_row, soft_ref.shape)

    @pl.when(step == pl.num_programs(0) - 1)
    def _():
        col_ref[...] = jnp.broadcast_to(acc_ref[0:1, :], col_ref.shape)


def row_kernel(recv_ref, kern_ref, out_ref, split_ref):
    @pl.when(pl.program_id(0) == 0)
    def _():
        split_ref[...] = split3(1.0 / jnp.sum(recv_ref[...], axis=0, keepdims=True))

    sums = lax.dot_general(split_ref[...], kern_ref[...], (((1,), (1,)), ((), ())), preferred_element_type=F32)
    out_ref[...] = jnp.broadcast_to(jnp.sum(sums, axis=0, keepdims=True), out_ref.shape)


def col_kernel(recv_ref, kern_ref, out_ref, acc_ref):
    step = pl.program_id(0)

    @pl.when(step == 0)
    def _():
        acc_ref[...] = jnp.zeros_like(acc_ref)

    scale = split3(1.0 / jnp.sum(recv_ref[...], axis=0, keepdims=True))
    acc_ref[...] += jnp.dot(scale, kern_ref[...], preferred_element_type=F32)

    @pl.when(step == pl.num_programs(0) - 1)
    def _():
        out_ref[...] = jnp.broadcast_to(jnp.sum(acc_ref[...], axis=0, keepdims=True), out_ref.shape)


def final_kernel(
    embed_ref, mate_ref, pair_ref, proto_t_ref, proto_ref, raw_t_ref, recv_col_ref, recv_row_ref, recv_soft_ref,
    d_unit_ref, term_ref, loss_ref, acc_ref, loss_acc_ref,
):
    step = pl.program_id(0)
    rows = embed_ref.shape[0]

    @pl.when(step == 0)
    def _():
        acc_ref[...] = jnp.zeros_like(acc_ref)
        loss_acc_ref[...] = jnp.zeros_like(loss_acc_ref)

    row_scale = 1.0 / jnp.sum(recv_row_ref[...], axis=0, keepdims=True)
    soft_row = jnp.sum(recv_soft_ref[...], axis=0, keepdims=True)
    col_scale = 1.0 / jnp.sum(recv_col_ref[...], axis=0, keepdims=True)
    total = row_scale.shape[1]
    lane = lax.broadcasted_iota(jnp.int32, (rows, total), 1)
    here = lax.broadcasted_iota(jnp.int32, (rows, total), 0) + step * rows
    mate_scale = jnp.sum(jnp.where(lane == pair_ref[...], row_scale, 0.0), axis=1, keepdims=True)
    soft = jnp.sum(jnp.where(lane == here, soft_row, 0.0), axis=1, keepdims=True)
    scores = jnp.dot(embed_ref[...], proto_t_ref[...], preferred_element_type=F32) * 10.0
    mates = jnp.dot(mate_ref[...], proto_t_ref[...], preferred_element_type=F32)
    target = jnp.exp(mates * 20.0) * mate_scale * col_scale
    loss_acc_ref[0:1, :] += jnp.sum(target * (scores - jnp.log(soft)), axis=0, keepdims=True)
    grad = ((jnp.exp(scores) * (1.0 / soft) - target) * 10.0).astype(BF)
    d_unit_ref[...] = jnp.dot(grad, proto_ref[...], preferred_element_type=F32).astype(d_unit_ref.dtype)
    acc_ref[...] += lax.dot_general(
        embed_ref[...], grad, (((0,), (0,)), ((), ())), preferred_element_type=F32
    )

    @pl.when(step == pl.num_programs(0) - 1)
    def _():
        raw = raw_t_ref[...].astype(F32)
        scale = lax.rsqrt(jnp.sum(raw * raw, axis=0, keepdims=True) + 1e-06)
        unit = raw * scale
        acc = acc_ref[...]
        term = (acc - unit * jnp.sum(unit * acc, axis=0, keepdims=True)) * scale
        term_ref[...] = term.astype(BF)
        loss_ref[...] = jnp.broadcast_to(jnp.sum(loss_acc_ref[0:1, :], axis=1, keepdims=True), loss_ref.shape)


def whole(shape):
    return pl.BlockSpec(shape, lambda i: (0,) * len(shape))


def tiled_rows(rows, width):
    return pl.BlockSpec((rows, width), lambda i: (i, 0))


def sinkhorn_and_loss(block_embed, mates, pair_col, proto_t, proto_bf, raw_t):
    n_batch = lax.axis_size("batch")
    n_proto = lax.axis_size("proto")
    rows, width = block_embed.shape
    cols = proto_t.shape[1]
    tile = 256
    steps = rows // tile
    kern, col_part, soft_part = pl.pallas_call(
        score_kernel,
        grid=(steps,),
        in_specs=[tiled_rows(tile, width), whole((width, cols))],
        out_specs=[tiled_rows(tile, cols), whole((n_batch, cols)), pl.BlockSpec((n_proto, tile), lambda i: (0, i))],
        out_shape=[
            jax.ShapeDtypeStruct((rows, cols), BF),
            jax.ShapeDtypeStruct((n_batch, cols), F32),
            jax.ShapeDtypeStruct((n_proto, rows), F32),
        ],
        scratch_shapes=[pltpu.VMEM((8, cols), F32)],
        name="score_kernel",
    )(block_embed, proto_t)
    row_pass = pl.pallas_call(
        row_kernel,
        grid=(steps,),
        in_specs=[whole((n_batch, cols)), tiled_rows(tile, cols)],
        out_specs=pl.BlockSpec((n_proto, tile), lambda i: (0, i)),
        out_shape=jax.ShapeDtypeStruct((n_proto, rows), F32),
        scratch_shapes=[pltpu.VMEM((8, cols), BF)],
        name="row_kernel",
    )
    col_pass = pl.pallas_call(
        col_kernel,
        grid=(steps,),
        in_specs=[pl.BlockSpec((n_proto, tile), lambda i: (0, i)), tiled_rows(tile, cols)],
        out_specs=whole((n_batch, cols)),
        out_shape=jax.ShapeDtypeStruct((n_batch, cols), F32),
        scratch_shapes=[pltpu.VMEM((8, cols), F32)],
        name="col_kernel",
    )
    recv_soft = deal(soft_part, "proto")
    for step in range(ITERS):
        recv_col = deal(col_part, "batch")
        recv_row = deal(row_pass(recv_col, kern), "proto")
        if step + 1 < ITERS:
            col_part = col_pass(recv_row, kern)
    return pl.pallas_call(
        final_kernel,
        grid=(steps,),
        in_specs=[
            tiled_rows(tile, width),
            tiled_rows(tile, width),
            tiled_rows(tile, 1),
            whole((width, cols)),
            whole((cols, width)),
            whole((width, cols)),
            whole((n_batch, cols)),
            whole((n_proto, rows)),
            whole((n_proto, rows)),
        ],
        out_specs=[tiled_rows(tile, width), whole((width, cols)), whole((8, 128))],
        out_shape=[
            jax.ShapeDtypeStruct((rows, width), BF),
            jax.ShapeDtypeStruct((width, cols), BF),
            jax.ShapeDtypeStruct((8, 128), F32),
        ],
        scratch_shapes=[pltpu.VMEM((width, cols), F32), pltpu.VMEM((8, cols), F32)],
        name="final_kernel",
    )(block_embed, mates, pair_col, proto_t, proto_bf, raw_t, recv_col, recv_row, recv_soft)


def unit_rows(values):
    scale = lax.rsqrt(jnp.sum(values * values, axis=1, keepdims=True) + 1e-06)
    return (values * scale, scale)


def local(features, w_first, bn_gain, bn_bias, w_second, prototypes, pair):
    n_batch = lax.axis_size("batch")
    n_proto = lax.axis_size("proto")
    own_rows, d_in = features.shape
    d_hid, width = w_second.shape
    total_rows = own_rows * n_batch * n_proto
    block_rows = own_rows * n_proto
    part = lax.axis_index("proto")
    slab = d_hid // n_proto

    raw_t = prototypes.T
    raw_t32 = raw_t.astype(F32)
    proto_t = (raw_t32 * lax.rsqrt(jnp.sum(raw_t32 * raw_t32, axis=0, keepdims=True) + 1e-06)).astype(BF)
    proto_bf = unit_rows(prototypes.astype(F32))[0].astype(BF)

    pre = jnp.dot(features, w_first, preferred_element_type=F32)
    stats = jnp.stack([jnp.sum(pre, axis=0), jnp.sum(pre * pre, axis=0)])
    stats = jnp.sum(spread(stats, "batch"), axis=0)
    stats = jnp.sum(spread(stats, "proto"), axis=0)
    mean_act = stats[0] / total_rows
    inv_std = lax.rsqrt(stats[1] / total_rows - mean_act * mean_act + 1e-05)
    hidden = jax.nn.gelu((pre - mean_act) * inv_std * bn_gain + bn_bias).astype(BF)
    embed = jnp.dot(hidden, w_second, preferred_element_type=F32)
    unit_embed, embed_scale = unit_rows(embed)
    block_embed = spread(unit_embed.astype(BF), "proto").reshape(block_rows, width)

    first_row = lax.axis_index("batch") * block_rows
    mate_row = pair - first_row
    mates = jnp.take(block_embed, mate_row, axis=0)
    d_unit_part, term_t, loss_tile = sinkhorn_and_loss(
        block_embed, mates, mate_row[:, None], proto_t, proto_bf, raw_t
    )

    block_features = spread(features, "proto").reshape(block_rows, d_in)
    w_slab = lax.dynamic_slice(w_first, (0, part * slab), (d_in, slab))
    w2_slab = lax.dynamic_slice(w_second, (part * slab, 0), (slab, width))

    def cut(v):
        return lax.dynamic_slice(v, (part * slab,), (slab,))

    mean_s, inv_s, gain_s, bias_s = cut(mean_act), cut(inv_std), cut(bn_gain), cut(bn_bias)
    normed = (jnp.dot(block_features, w_slab, preferred_element_type=F32) - mean_s) * inv_s
    shifted = normed * gain_s + bias_s
    hidden_s, gelu_back = jax.vjp(jax.nn.gelu, shifted)
    hidden_s = hidden_s.astype(BF)

    term_got = deal(term_t.reshape(n_batch, width // n_batch, -1), "batch")
    grad_proto = jnp.sum(term_got.astype(F32), axis=0).T

    d_unit = jnp.sum(deal(d_unit_part.reshape(n_proto, own_rows, width), "proto").astype(F32), axis=0)
    d_embed = (
        (d_unit - unit_embed * jnp.sum(unit_embed * d_unit, axis=1, keepdims=True)) * embed_scale
    ).astype(BF)
    d_embed = spread(d_embed, "proto").reshape(block_rows, width)

    d_hidden = lax.dot_general(d_embed, w2_slab, (((1,), (1,)), ((), ())), preferred_element_type=F32)
    d_shift = gelu_back(d_hidden)[0]
    sums = jnp.stack(
        [jnp.sum(d_shift * normed, axis=0), jnp.sum(d_shift, axis=0), jnp.broadcast_to(loss_tile[0, :1], (slab,))]
    )
    sums = jnp.sum(spread(sums, "batch"), axis=0)
    gain_sum, bias_sum = sums[0], sums[1]
    d_pre = (gain_s * inv_s * (d_shift - bias_sum / total_rows - normed * gain_sum / total_rows)).astype(BF)
    first_part = lax.dot_general(
        block_features, d_pre, (((0,), (0,)), ((), ())), preferred_element_type=F32
    ).astype(BF)
    got = deal(first_part.reshape(n_batch * n_proto, -1, slab), ("batch", "proto"))
    got = jnp.sum(got.reshape(n_batch, n_proto, -1, slab).astype(F32), axis=0)
    grad_first = jnp.transpose(got, (1, 0, 2)).reshape(-1, d_hid)

    second_part = lax.dot_general(hidden_s, d_embed, (((0,), (0,)), ((), ())), preferred_element_type=F32)
    second = jnp.sum(deal(second_part.reshape(n_batch, -1, width), "batch"), axis=0)
    grad_second = lax.ppermute(
        second,
        ("batch", "proto"),
        [(b * n_proto + p, p * n_batch + b) for b in range(n_batch) for p in range(n_proto)],
    )
    everywhere = spread(sums, "proto")
    grad_gain = everywhere[:, 0].reshape(-1)
    grad_bias = everywhere[:, 1].reshape(-1)
    loss = -jnp.sum(everywhere[:, 2, 0]) / total_rows
    return (grad_first, grad_second, grad_gain, grad_bias, grad_proto, loss)


def solution(mesh):
    return jax.shard_map(
        local,
        mesh=mesh,
        in_specs=(P(("batch", "proto"), None), P(), P(), P(), P(), P("proto", None), P("batch")),
        out_specs=(
            P(("batch", "proto"), None),
            P(("batch", "proto"), None),
            P(),
            P(),
            P("proto", "batch"),
            P(),
        ),
        check_vma=False,
    )
```

time: 1770 us -> 344 us (0.19)
  waiting for transfers between devices: 1300 us -> 125 us
  blocking collectives: 301 us -> 32.9 us
  starting transfers between devices: 0.42 us -> 82 us
  matrix products: 76.6 us -> 19.8 us
  Pallas kernels: 0 us -> 40.1 us
    unnamed x5 -> x0, waiting for transfers between devices: 669 us -> none
    reduce_scatter x3 -> x0, waiting for transfers between devices: 634 us -> none  [the longest x1 617 us: local(): lax.psum_scatter(second_term, ('batch', 'proto'), scatter_dimension=0, ti...]
    psum x8 -> x0, blocking collectives: 287 us -> none  [the longest x3 91.9 us: cluster_balancing_pass(): return 1.0 / lax.psum(incomplete_cluster_totals, 'batch')]
    all_to_all x0 -> x15, waiting for transfers between devices: none -> 120 us  [the longest x6 75.6 us: spread(): lax.all_to_all(jnp.broadcast_to(x[None], (n,) + x.shape), axis, 0, 0, til...]
    all_to_all x0 -> x15, starting transfers between devices: none -> 76.6 us  [the longest x9 40.9 us: deal(): return lax.all_to_all(x, axis, 0, 0, tiled=True)]
    dot_general x14 -> x6, matrix products: 76.6 us -> 19.8 us  [the longest x1 5.95 us: local(): pre = jnp.dot(features, w_first, preferred_element_type=F32)]
    pallas_call x0 -> x7, Pallas kernels: none -> 40.1 us  [the longest x3 13.7 us: sinkhorn_and_loss(): recv_row = deal(row_pass(recv_col, kern), 'proto')]
    all_to_all x0 -> x3, blocking collectives: none -> 32.9 us  [the longest x2 23.3 us: deal(): return lax.all_to_all(x, axis, 0, 0, tiled=True)]
  transfers between devices with their start and end apart: 4 -> 16, of which waited for: 3 -> 15; matrix products, arithmetic and copies ran while one was open for 2% -> 9% of each run, Pallas kernels for 0% -> 1%
where the time goes in v1:
time: 344 us; the launch traced here: 342 us
  waiting for transfers between devices  125 us (36%)
  starting transfers between devices  82 us (24%)
  Pallas kernels  40.1 us (12%)
  local copies, waits for them, and re-layouts  33.3 us (10%)
  blocking collectives  32.9 us (10%)
  matrix products  19.8 us (6%)
  other arithmetic  6.58 us (2%)
    all_to_all x6, waiting for transfers between devices, spread(): lax.all_to_all(jnp.broadcast_to(x[None], (n,) + x.shape), axis, 0, 0, til...  75.6 us
    all_to_all x9, waiting for transfers between devices, deal(): return lax.all_to_all(x, axis, 0, 0, tiled=True)  44.7 us
    all_to_all x9, starting transfers between devices, deal(): return lax.all_to_all(x, axis, 0, 0, tiled=True)  40.9 us
    all_to_all x6, starting transfers between devices, spread(): lax.all_to_all(jnp.broadcast_to(x[None], (n,) + x.shape), axis, 0, 0, til...  35.6 us
    all_to_all x2, blocking collectives, deal(): return lax.all_to_all(x, axis, 0, 0, tiled=True)  23.3 us
    pallas_call x3, Pallas kernels, sinkhorn_and_loss(): recv_row = deal(row_pass(recv_col, kern), 'proto')  13.7 us
    pallas_call x1, Pallas kernels, sinkhorn_and_loss(): pl.pallas_call(final_kernel, grid=(steps,), in_specs=[tiled_rows(tile, wi...  12.4 us
    all_to_all x1, blocking collectives, spread(): lax.all_to_all(jnp.broadcast_to(x[None], (n,) + x.shape), axis, 0, 0, til...  9.63 us
  transfers between devices with their start and end apart: 16, of which 15 were waited for; matrix products, arithmetic and copies ran while one was open for 9% of the time, Pallas kernels for 1%

profile of v1, /device:TPU:1, one launch (start us, length us, event | category | flops | bytes accessed | tf_op | source)
XLA Modules:
  0.0 342.3 jit_solution(7122407865196152284)
XLA Ops:
  0.7 6.0 %fusion.55 = (f32[2048]{0:T(1024)S(1)}, f32[2048]{0:T(1024)S(1)}, f32[128,2048]{1,0:T(8,128)}) fusion(bf16[128,2048]{1,0:T(8,128)(2,1)} %param.7, bf16[2048,2048]{1,0:T(8,128)(2,1)} %param.8), kind=kOutput, calls=%fused_computation.96 | convolution fusion | flops 1074524160 | bytes 9977856 | tf_op jit(solution)/shard_map/dot_general | solution.py:218
  7.5 8.6 %all-to-all-start = ((f32[16,2,2048]{2,1,0:T(2,128)}), f32[16,2,2048]{2,1,0:T(2,128)S(1)}, u32[]{:S(2)}, u32[]{:S(2)}) async-start(f32[16,2,2048]{2,1,0:T(2,128)} %broadcast_in_dim.28), calls=%async_computation | async-start | bytes 524288 | tf_op jit(solution)/shard_map/all_to_all | solution.py:15
  17.0 6.5 %all-to-all-done = f32[16,2,2048]{2,1,0:T(2,128)S(1)} async-done(((f32[16,2,2048]{2,1,0:T(2,128)}), f32[16,2,2048]{2,1,0:T(2,128)S(1)}, u32[]{:S(2)}, u32[]{:S(2)}) %all-to-all-start) | async-done | bytes 262176 | tf_op jit(solution)/shard_map/all_to_all | solution.py:15
  24.3 6.3 %all-to-all-start.1 = ((f32[8,2,2048]{2,1,0:T(2,128)}), f32[8,2,2048]{2,1,0:T(2,128)S(1)}, u32[]{:S(2)}, u32[]{:S(2)}) async-start(f32[8,2,2048]{2,1,0:T(2,128)} %broadcast_in_dim.29), calls=%async_computation.1 | async-start | bytes 262144 | tf_op jit(solution)/shard_map/all_to_all | solution.py:15
  30.6 5.2 %all-to-all-done.1 = f32[8,2,2048]{2,1,0:T(2,128)S(1)} async-done(((f32[8,2,2048]{2,1,0:T(2,128)}), f32[8,2,2048]{2,1,0:T(2,128)S(1)}, u32[]{:S(2)}, u32[]{:S(2)}) %all-to-all-start.1) | async-done | bytes 131104 | tf_op jit(solution)/shard_map/all_to_all | solution.py:15
  36.0 1.9 multiply_reduce_fusion.2
  38.8 4.3 %all-to-all-start.2 = ((bf16[8,128,256]{2,1,0:T(8,128)(2,1)}), bf16[8,128,256]{2,1,0:T(8,128)(2,1)S(1)}, u32[]{:S(2)}, u32[]{:S(2)}) async-start(bf16[8,128,256]{2,1,0:T(8,128)(2,1)} %broadcast_in_dim.30), calls=%async_computation.2 | async-start | bytes 1048576 | tf_op jit(solution)/shard_map/all_to_all | solution.py:15
  44.3 8.1 %all-to-all-done.2 = bf16[8,128,256]{2,1,0:T(8,128)(2,1)S(1)} async-done(((bf16[8,128,256]{2,1,0:T(8,128)(2,1)}), bf16[8,128,256]{2,1,0:T(8,128)(2,1)S(1)}, u32[]{:S(2)}, u32[]{:S(2)}) %all-to-all-start.2) | async-done | bytes 524320 | tf_op jit(solution)/shard_map/all_to_all | solution.py:15
  53.2 5.8 %score_kernel.1 = (bf16[1024,2048]{1,0:T(8,128)(2,1)}, f32[16,2048]{1,0:T(8,128)}, f32[8,1024]{1,0:T(8,128)}) custom-call(bf16[1024,256]{1,0:T(8,128)(2,1)} %bitcast.91, bf16[256,2048]{1,0:T(8,128)(2,1)} %fusion.2.proto_t_ref), custom_call_target="tpu_custom_call" | custom-call | tf_op jit(solution)/shard_map/score_kernel/pallas_call | solution.py:136
  60.1 9.8 %all_to_all.132 = f32[16,1,2048]{2,1,0:T(1,128)S(1)} all-to-all(f32[16,1,2048]{2,1,0:T(1,128)S(1)} %copy.76), channel_id=1, replica_groups=mesh['batch'=16,'proto'=8] {'batch'}, dimensions={0} | all-to-all | bytes 262144 | tf_op jit(solution)/shard_map/all_to_all | solution.py:19
  70.7 4.6 %row_kernel.3 = f32[8,1024]{1,0:T(8,128)} custom-call(f32[16,2048]{1,0:T(8,128)} %bitcast.102, bf16[1024,2048]{1,0:T(8,128)(2,1)} %get-tuple-element.13.kern_ref), custom_call_target="tpu_custom_call" | custom-call | tf_op jit(solution)/shard_map/row_kernel/pallas_call | solution.py:170
  76.6 5.6 %all-to-all-start.4 = ((f32[8,1,1024]{2,1,0:T(1,128)}), f32[8,1,1024]{2,1,0:T(1,128)S(1)}, u32[]{:S(2)}, u32[]{:S(2)}) async-start(f32[8,1,1024]{2,1,0:T(1,128)} %copy.77), calls=%async_computation.4 | async-start | bytes 65536 | tf_op jit(solution)/shard_map/all_to_all | solution.py:19
  82.6 4.4 %all-to-all-done.4 = f32[8,1,1024]{2,1,0:T(1,128)S(1)} async-done(((f32[8,1,1024]{2,1,0:T(1,128)}), f32[8,1,1024]{2,1,0:T(1,128)S(1)}, u32[]{:S(2)}, u32[]{:S(2)}) %all-to-all-start.4) | async-done | bytes 32800 | tf_op jit(solution)/shard_map/all_to_all | solution.py:19
  87.6 4.2 %col_kernel.2 = f32[16,2048]{1,0:T(8,128)} custom-call(f32[8,1024]{1,0:T(8,128)} %bitcast.111, bf16[1024,2048]{1,0:T(8,128)(2,1)} %get-tuple-element.13.kern_ref), custom_call_target="tpu_custom_call" | custom-call | tf_op jit(solution)/shard_map/col_kernel/pallas_call | solution.py:172
  93.5 3.5 %all-to-all-start.5 = ((f32[16,1,2048]{2,1,0:T(1,128)}), f32[16,1,2048]{2,1,0:T(1,128)S(1)}, u32[]{:S(2)}, u32[]{:S(2)}) async-start(f32[16,1,2048]{2,1,0:T(1,128)} %copy.78), calls=%async_computation.5 | async-start | bytes 262144 | tf_op jit(solution)/shard_map/all_to_all | solution.py:19
  97.0 6.8 %all-to-all-done.5 = f32[16,1,2048]{2,1,0:T(1,128)S(1)} async-done(((f32[16,1,2048]{2,1,0:T(1,128)}), f32[16,1,2048]{2,1,0:T(1,128)S(1)}, u32[]{:S(2)}, u32[]{:S(2)}) %all-to-all-start.5) | async-done | bytes 131104 | tf_op jit(solution)/shard_map/all_to_all | solution.py:19
  104.5 4.6 %row_kernel.4 = f32[8,1024]{1,0:T(8,128)} custom-call(f32[16,2048]{1,0:T(8,128)} %bitcast.104, bf16[1024,2048]{1,0:T(8,128)(2,1)} %get-tuple-element.13.kern_ref), custom_call_target="tpu_custom_call" | custom-call | tf_op jit(solution)/shard_map/row_kernel/pallas_call | solution.py:170
  110.5 5.1 %all-to-all-start.6 = ((f32[8,1,1024]{2,1,0:T(1,128)}), f32[8,1,1024]{2,1,0:T(1,128)S(1)}, u32[]{:S(2)}, u32[]{:S(2)}) async-start(f32[8,1,1024]{2,1,0:T(1,128)} %copy.79), calls=%async_computation.6 | async-start | bytes 65536 | tf_op jit(solution)/shard_map/all_to_all | solution.py:19
  117.0 3.4 all-to-all-done.6
  121.0 4.1 %col_kernel.3 = f32[16,2048]{1,0:T(8,128)} custom-call(f32[8,1024]{1,0:T(8,128)} %bitcast.113, bf16[1024,2048]{1,0:T(8,128)(2,1)} %get-tuple-element.13.kern_ref), custom_call_target="tpu_custom_call" | custom-call | tf_op jit(solution)/shard_map/col_kernel/pallas_call | solution.py:172
  126.8 3.5 %all-to-all-start.7 = ((f32[16,1,2048]{2,1,0:T(1,128)}), f32[16,1,2048]{2,1,0:T(1,128)S(1)}, u32[]{:S(2)}, u32[]{:S(2)}) async-start(f32[16,1,2048]{2,1,0:T(1,128)} %copy.80), calls=%async_computation.7 | async-start | bytes 262144 | tf_op jit(solution)/shard_map/all_to_all | solution.py:19
  131.0 6.1 %all-to-all-done.7 = f32[16,1,2048]{2,1,0:T(1,128)S(1)} async-done(((f32[16,1,2048]{2,1,0:T(1,128)}), f32[16,1,2048]{2,1,0:T(1,128)S(1)}, u32[]{:S(2)}, u32[]{:S(2)}) %all-to-all-start.7) | async-done | bytes 131104 | tf_op jit(solution)/shard_map/all_to_all | solution.py:19
  137.1 5.1 %all-to-all-start.9 = ((f32[8,1,1024]{2,1,0:T(1,128)}), f32[8,1,1024]{2,1,0:T(1,128)S(1)}, u32[]{:S(2)}, u32[]{:S(2)}) async-start(f32[8,1,1024]{2,1,0:T(1,128)} %copy.82), calls=%async_computation.9 | async-start | bytes 65536 | tf_op jit(solution)/shard_map/all_to_all | solution.py:19
  143.3 3.9 %gather_fusion = bf16[1024,256]{1,0:T(8,128)(2,1)S(1)} fusion(bf16[1024,256]{1,0:T(8,128)(2,1)S(1)} %bitcast.93, s32[1024]{0:T(1024)S(1)} %fusion.47), kind=kCustom, calls=%fused_computation | custom fusion | bytes 1052672 | tf_op jit(solution)/shard_map/jit(_take)/gather | solution.py:231
  147.9 4.6 %row_kernel.5 = f32[8,1024]{1,0:T(8,128)} custom-call(f32[16,2048]{1,0:T(8,128)} %bitcast.99, bf16[1024,2048]{1,0:T(8,128)(2,1)} %get-tuple-element.13.kern_ref), custom_call_target="tpu_custom_call" | custom-call | tf_op jit(solution)/shard_map/row_kernel/pallas_call | solution.py:170
  153.9 4.8 %all-to-all-start.8 = ((f32[8,1,1024]{2,1,0:T(1,128)}), f32[8,1,1024]{2,1,0:T(1,128)S(1)}, u32[]{:S(2)}, u32[]{:S(2)}) async-start(f32[8,1,1024]{2,1,0:T(1,128)} %copy.81), calls=%async_computation.8 | async-start | bytes 65536 | tf_op jit(solution)/shard_map/all_to_all | solution.py:19
  160.4 3.1 all-to-all-done.8
  164.1 12.4 %final_kernel.1 = (bf16[1024,256]{1,0:T(8,128)(2,1)}, bf16[256,2048]{1,0:T(8,128)(2,1)}, f32[8,128]{1,0:T(8,128)}) custom-call(bf16[1024,256]{1,0:T(8,128)(2,1)} %bitcast.92, bf16[1024,256]{1,0:T(8,128)(2,1)} %broadcast_select_fusion.mate_ref, s32[1024,1]{1,0:T(8,128)} %copy.83.pair_ref, bf16[256,2048]{1,0:T(8,128)(2,1)} %fusion.2.proto_t_ref, ...), custom_call_target="tpu_custom_call" | custom-call | tf_op jit(solution)/shard_map/final_kernel/pallas_call | solution.py:173
  176.5 13.5 %all_to_all.133 = bf16[8,128,256]{2,1,0:T(8,128)(2,1)S(1)} all-to-all(bf16[8,128,256]{2,1,0:T(8,128)(2,1)} %bitcast.107), channel_id=1, replica_groups=mesh['batch'=16,'proto'=8] {'proto'}, dimensions={0} | all-to-all | bytes 1048576 | tf_op jit(solution)/shard_map/all_to_all | solution.py:19
  189.9 2.5 broadcast_in_dim.36
  192.5 5.5 %all-to-all-start.12 = ((bf16[8,128,2048]{2,1,0:T(8,128)(2,1)}), bf16[8,128,2048]{2,1,0:T(8,128)(2,1)}, u32[]{:S(2)}, u32[]{:S(2)}) async-start(bf16[8,128,2048]{2,1,0:T(8,128)(2,1)} %broadcast_in_dim.36), calls=%async_computation.12 | async-start | bytes 8388608 | tf_op jit(solution)/shard_map/all_to_all | solution.py:15
  200.4 46.4 %all-to-all-done.12 = bf16[8,128,2048]{2,1,0:T(8,128)(2,1)} async-done(((bf16[8,128,2048]{2,1,0:T(8,128)(2,1)}), bf16[8,128,2048]{2,1,0:T(8,128)(2,1)}, u32[]{:S(2)}, u32[]{:S(2)}) %all-to-all-start.12) | async-done | bytes 4194336 | tf_op jit(solution)/shard_map/all_to_all | solution.py:15
  247.6 4.4 %all-to-all-start.11 = ((bf16[8,128,256]{2,1,0:T(8,128)(2,1)}), bf16[8,128,256]{2,1,0:T(8,128)(2,1)S(1)}, u32[]{:S(2)}, u32[]{:S(2)}) async-start(bf16[8,128,256]{2,1,0:T(8,128)(2,1)} %broadcast_in_dim.35), calls=%async_computation.11 | async-start | bytes 1048576 | tf_op jit(solution)/shard_map/all_to_all | solution.py:15
  252.0 4.8 %fusion.27 = (bf16[256,1024]{0,1:T(8,128)(2,1)}, f32[256,1024]{0,1:T(8,128)S(1)}) fusion(f32[256]{0:T(256)S(1)} %dynamic_slice.26, f32[256]{0:T(256)S(1)} %get-tuple-element.23, f32[256]{0:T(256)S(1)} %bitcast.127, f32[256]{0:T(256)S(1)} %bitcast.128, bf16[1024,2048]{1,0:T(8,128)(2,1)} %bitcast.17, bf16[2048,2048]{1,0:T(8,128)(2,1)} %param.8, s32[]{:T(128)S(6)} %select_n.17), kind=kOutput, calls=%fused_computation.40 | convolution fusion | flops 1077149696 | bytes 6819844 | tf_op jit(solution)/shard_map/dot_general | solution.py:244
  256.8 4.6 %all-to-all-done.11 = bf16[8,128,256]{2,1,0:T(8,128)(2,1)S(1)} async-done(((bf16[8,128,256]{2,1,0:T(8,128)(2,1)}), bf16[8,128,256]{2,1,0:T(8,128)(2,1)S(1)}, u32[]{:S(2)}, u32[]{:S(2)}) %all-to-all-start.11) | async-done | bytes 524320 | tf_op jit(solution)/shard_map/all_to_all | solution.py:15
  261.3 2.0 fusion.29
  263.5 9.6 %all_to_all.134 = f32[16,3,256]{2,1,0:T(4,128)S(1)} all-to-all(f32[16,3,256]{2,1,0:T(4,128)S(1)} %broadcast_in_dim.37), channel_id=1, replica_groups=mesh['batch'=16,'proto'=8] {'batch'}, dimensions={0} | all-to-all | bytes 98304 | tf_op jit(solution)/shard_map/all_to_all | solution.py:15
  273.1 3.7 %all-to-all-start.17 = ((bf16[16,16,2048]{2,1,0:T(8,128)(2,1)}), bf16[16,16,2048]{2,1,0:T(8,128)(2,1)S(1)}, u32[]{:S(2)}, u32[]{:S(2)}) async-start(bf16[16,16,2048]{2,1,0:T(8,128)(2,1)} %bitcast.101), calls=%async_computation.17 | async-start | bytes 2097152 | tf_op jit(solution)/shard_map/all_to_all | solution.py:19
  279.0 12.3 %all-to-all-done.17 = bf16[16,16,2048]{2,1,0:T(8,128)(2,1)S(1)} async-done(((bf16[16,16,2048]{2,1,0:T(8,128)(2,1)}), bf16[16,16,2048]{2,1,0:T(8,128)(2,1)S(1)}, u32[]{:S(2)}, u32[]{:S(2)}) %all-to-all-start.17) | async-done | bytes 1048608 | tf_op jit(solution)/shard_map/all_to_all | solution.py:19
  292.0 6.7 %all-to-all-start.16 = ((f32[8,3,256]{2,1,0:T(4,128)}), f32[8,3,256]{2,1,0:T(4,128)S(1)}, u32[]{:S(2)}, u32[]{:S(2)}) async-start(f32[8,3,256]{2,1,0:T(4,128)} %broadcast_in_dim.38), calls=%async_computation.16 | async-start | bytes 65536 | tf_op jit(solution)/shard_map/all_to_all | solution.py:15
  298.6 4.7 %all-to-all-done.16 = f32[8,3,256]{2,1,0:T(4,128)S(1)} async-done(((f32[8,3,256]{2,1,0:T(4,128)}), f32[8,3,256]{2,1,0:T(4,128)S(1)}, u32[]{:S(2)}, u32[]{:S(2)}) %all-to-all-start.16) | async-done | bytes 24608 | tf_op jit(solution)/shard_map/all_to_all | solution.py:15
  303.4 3.5 %all-to-all-start.15 = ((f32[16,16,256]{2,1,0:T(8,128)}), f32[16,16,256]{2,1,0:T(8,128)S(1)}, u32[]{:S(2)}, u32[]{:S(2)}) async-start(f32[16,16,256]{2,1,0:T(8,128)} %fusion.58), calls=%async_computation.15 | async-start | bytes 524288 | tf_op jit(solution)/shard_map/all_to_all | solution.py:19
  306.9 4.1 %fusion = bf16[2048,256]{0,1:T(8,128)(2,1)S(1)} fusion(bf16[1024,2048]{1,0:T(8,128)(2,1)} %bitcast.17, f32[256,1024]{0,1:T(8,128)} %copy-done.12, f32[1024,256]{1,0:T(8,128)} %get-tuple-element.35, f32[256]{0:T(256)S(1)} %bitcast.130, f32[256]{0:T(256)S(1)} %bitcast.129, f32[256]{0:T(256)S(1)} %get-tuple-element.22), kind=kOutput, calls=%fused_computation.6 | convolution fusion | flops 1075838976 | bytes 7343104 | tf_op jit(solution)/shard_map/dot_general | solution.py:266
  312.4 2.0 all-to-all-done.15
  314.4 6.1 %all-to-all-start.14 = ((bf16[128,16,256]{2,1,0:T(8,128)(2,1)}), bf16[128,16,256]{2,1,0:T(8,128)(2,1)S(1)}, u32[]{:S(2)}, u32[]{:S(2)}) async-start(bf16[128,16,256]{2,1,0:T(8,128)(2,1)} %bitcast.26), calls=%async_computation.14 | async-start | bytes 2097152 | tf_op jit(solution)/shard_map/all_to_all | solution.py:19
  321.9 5.4 %collective-permute-start = (f32[16,256]{1,0:T(8,128)S(1)}, f32[16,256]{1,0:T(8,128)S(1)}, u32[]{:S(2)}, u32[]{:S(2)}) collective-permute-start(f32[16,256]{1,0:T(8,128)S(1)} %reduce_sum.157), channel_id=1, source_target_pairs={{0,0},{1,16},{2,32},{3,48},{4,64},{5,80},{6,96},{7,112},{8,1},{9,1... | collective-permute-start | bytes 49160 | tf_op jit(solution)/shard_map/ppermute | solution.py:275
  328.6 4.6 %collective-permute-done = f32[16,256]{1,0:T(8,128)S(1)} collective-permute-done((f32[16,256]{1,0:T(8,128)S(1)}, f32[16,256]{1,0:T(8,128)S(1)}, u32[]{:S(2)}, u32[]{:S(2)}) %collective-permute-start) | collective-permute-done | bytes 16416 | tf_op jit(solution)/shard_map/ppermute | solution.py:275
  333.2 6.5 %all-to-all-done.14 = bf16[128,16,256]{2,1,0:T(8,128)(2,1)S(1)} async-done(((bf16[128,16,256]{2,1,0:T(8,128)(2,1)}), bf16[128,16,256]{2,1,0:T(8,128)(2,1)S(1)}, u32[]{:S(2)}, u32[]{:S(2)}) %all-to-all-start.14) | async-done | bytes 1048608 | tf_op jit(solution)/shard_map/all_to_all | solution.py:19
  (85 shorter events, 34.4 us)
Async XLA Ops:
  0.6 35.3 %copy-start = (bf16[2048,256]{1,0:T(8,128)(2,1)S(1)}, bf16[2048,256]{1,0:T(8,128)(2,1)}, u32[]{:S(2)}) copy-start(bf16[2048,256]{1,0:T(8,128)(2,1)} %param.11) | copy-start | bytes 3145732
  0.6 15.4 %copy-start.4 = (bf16[2048,256]{1,0:T(8,128)(2,1)S(1)}, bf16[2048,256]{1,0:T(8,128)(2,1)}, u32[]{:S(2)}) copy-start(bf16[2048,256]{1,0:T(8,128)(2,1)} %param.12) | copy-start | bytes 3145732
  6.6 29.3 %copy-start.10 = (f32[2048]{0:T(1024)S(1)}, f32[2048]{0:T(1024)}, u32[]{:S(2)}) copy-start(f32[2048]{0:T(1024)} %param.10) | copy-start | bytes 24580
  6.6 29.3 %copy-start.11 = (f32[2048]{0:T(1024)S(1)}, f32[2048]{0:T(1024)}, u32[]{:S(2)}) copy-start(f32[2048]{0:T(1024)} %param.9) | copy-start | bytes 24580
  7.5 16.0 %all-to-all-start = ((f32[16,2,2048]{2,1,0:T(2,128)}), f32[16,2,2048]{2,1,0:T(2,128)S(1)}, u32[]{:S(2)}, u32[]{:S(2)}) async-start(f32[16,2,2048]{2,1,0:T(2,128)} %broadcast_in_dim.28), calls=%async_computation | async-start | bytes 524288 | tf_op jit(solution)/shard_map/all_to_all | solution.py:15
  16.7 27.6 %copy-start.3 = (bf16[2048,256]{0,1:T(8,128)(2,1)}, bf16[2048,256]{0,1:T(8,128)(2,1)S(1)}, u32[]{:S(2)}) copy-start(bf16[2048,256]{0,1:T(8,128)(2,1)S(1)} %copy.75) | copy-start | bytes 3145732
  24.3 11.6 %all-to-all-start.1 = ((f32[8,2,2048]{2,1,0:T(2,128)}), f32[8,2,2048]{2,1,0:T(2,128)S(1)}, u32[]{:S(2)}, u32[]{:S(2)}) async-start(f32[8,2,2048]{2,1,0:T(2,128)} %broadcast_in_dim.29), calls=%async_computation.1 | async-start | bytes 262144 | tf_op jit(solution)/shard_map/all_to_all | solution.py:15
  38.8 13.6 %all-to-all-start.2 = ((bf16[8,128,256]{2,1,0:T(8,128)(2,1)}), bf16[8,128,256]{2,1,0:T(8,128)(2,1)S(1)}, u32[]{:S(2)}, u32[]{:S(2)}) async-start(bf16[8,128,256]{2,1,0:T(8,128)(2,1)} %broadcast_in_dim.30), calls=%async_computation.2 | async-start | bytes 1048576 | tf_op jit(solution)/shard_map/all_to_all | solution.py:15
  52.5 0.8 copy-start.1
  52.5 29.8 %copy-start.5 = (bf16[2048,256]{1,0:T(8,128)(2,1)S(1)}, bf16[2048,256]{1,0:T(8,128)(2,1)}, u32[]{:S(2)}) copy-start(bf16[2048,256]{1,0:T(8,128)(2,1)} %param.12) | copy-start | bytes 3145732
  76.6 10.4 %all-to-all-start.4 = ((f32[8,1,1024]{2,1,0:T(1,128)}), f32[8,1,1024]{2,1,0:T(1,128)S(1)}, u32[]{:S(2)}, u32[]{:S(2)}) async-start(f32[8,1,1024]{2,1,0:T(1,128)} %copy.77), calls=%async_computation.4 | async-start | bytes 65536 | tf_op jit(solution)/shard_map/all_to_all | solution.py:19
  87.6 28.0 %copy-start.6 = (bf16[2048,256]{1,0:T(8,128)(2,1)S(1)}, bf16[2048,256]{1,0:T(8,128)(2,1)}, u32[]{:S(2)}) copy-start(bf16[2048,256]{1,0:T(8,128)(2,1)} %param.12) | copy-start | bytes 3145732
  93.5 10.3 %all-to-all-start.5 = ((f32[16,1,2048]{2,1,0:T(1,128)}), f32[16,1,2048]{2,1,0:T(1,128)S(1)}, u32[]{:S(2)}, u32[]{:S(2)}) async-start(f32[16,1,2048]{2,1,0:T(1,128)} %copy.78), calls=%async_computation.5 | async-start | bytes 262144 | tf_op jit(solution)/shard_map/all_to_all | solution.py:19
  109.1 21.2 %copy-start.9 = (s32[1024]{0:T(1024)S(1)}, s32[1024]{0:T(1024)}, u32[]{:S(2)}) copy-start(s32[1024]{0:T(1024)} %param.13) | copy-start | bytes 12292
  109.1 21.2 %copy-start.8 = (f32[8,1024]{1,0:T(8,128)S(1)}, f32[8,1024]{1,0:T(8,128)}, u32[]{:S(2)}) copy-start(f32[8,1024]{1,0:T(8,128)} %get-tuple-element.14) | copy-start | bytes 98308
  109.1 34.2 %copy-start.2 = (bf16[8,128,256]{2,1,0:T(8,128)(2,1)S(1)}, bf16[8,128,256]{2,1,0:T(8,128)(2,1)}, u32[]{:S(2)}) copy-start(bf16[8,128,256]{2,1,0:T(8,128)(2,1)} %copy-done.1) | copy-start | bytes 1572868
  110.5 9.8 %all-to-all-start.6 = ((f32[8,1,1024]{2,1,0:T(1,128)}), f32[8,1,1024]{2,1,0:T(1,128)S(1)}, u32[]{:S(2)}, u32[]{:S(2)}) async-start(f32[8,1,1024]{2,1,0:T(1,128)} %copy.79), calls=%async_computation.6 | async-start | bytes 65536 | tf_op jit(solution)/shard_map/all_to_all | solution.py:19
  126.8 10.3 %all-to-all-start.7 = ((f32[16,1,2048]{2,1,0:T(1,128)}), f32[16,1,2048]{2,1,0:T(1,128)S(1)}, u32[]{:S(2)}, u32[]{:S(2)}) async-start(f32[16,1,2048]{2,1,0:T(1,128)} %copy.80), calls=%async_computation.7 | async-start | bytes 262144 | tf_op jit(solution)/shard_map/all_to_all | solution.py:19
  137.1 16.8 %all-to-all-start.9 = ((f32[8,1,1024]{2,1,0:T(1,128)}), f32[8,1,1024]{2,1,0:T(1,128)S(1)}, u32[]{:S(2)}, u32[]{:S(2)}) async-start(f32[8,1,1024]{2,1,0:T(1,128)} %copy.82), calls=%async_computation.9 | async-start | bytes 65536 | tf_op jit(solution)/shard_map/all_to_all | solution.py:19
  152.5 37.4 %copy-start.7 = (bf16[128,2048]{1,0:T(8,128)(2,1)S(1)}, bf16[128,2048]{1,0:T(8,128)(2,1)}, u32[]{:S(2)}) copy-start(bf16[128,2048]{1,0:T(8,128)(2,1)} %param.7) | copy-start | bytes 1572868
  153.9 9.5 %all-to-all-start.8 = ((f32[8,1,1024]{2,1,0:T(1,128)}), f32[8,1,1024]{2,1,0:T(1,128)S(1)}, u32[]{:S(2)}, u32[]{:S(2)}) async-start(f32[8,1,1024]{2,1,0:T(1,128)} %copy.81), calls=%async_computation.8 | async-start | bytes 65536 | tf_op jit(solution)/shard_map/all_to_all | solution.py:19
  192.5 54.3 %all-to-all-start.12 = ((bf16[8,128,2048]{2,1,0:T(8,128)(2,1)}), bf16[8,128,2048]{2,1,0:T(8,128)(2,1)}, u32[]{:S(2)}, u32[]{:S(2)}) async-start(bf16[8,128,2048]{2,1,0:T(8,128)(2,1)} %broadcast_in_dim.36), calls=%async_computation.12 | async-start | bytes 8388608 | tf_op jit(solution)/shard_map/all_to_all | solution.py:15
  247.6 13.7 %all-to-all-start.11 = ((bf16[8,128,256]{2,1,0:T(8,128)(2,1)}), bf16[8,128,256]{2,1,0:T(8,128)(2,1)S(1)}, u32[]{:S(2)}, u32[]{:S(2)}) async-start(bf16[8,128,256]{2,1,0:T(8,128)(2,1)} %broadcast_in_dim.35), calls=%async_computation.11 | async-start | bytes 1048576 | tf_op jit(solution)/shard_map/all_to_all | solution.py:15
  256.8 16.3 %copy-start.12 = (f32[256,1024]{0,1:T(8,128)}, f32[256,1024]{0,1:T(8,128)S(1)}, u32[]{:S(2)}) copy-start(f32[256,1024]{0,1:T(8,128)S(1)} %get-tuple-element.37) | copy-start | bytes 3145732
  273.1 18.3 %all-to-all-start.17 = ((bf16[16,16,2048]{2,1,0:T(8,128)(2,1)}), bf16[16,16,2048]{2,1,0:T(8,128)(2,1)S(1)}, u32[]{:S(2)}, u32[]{:S(2)}) async-start(bf16[16,16,2048]{2,1,0:T(8,128)(2,1)} %bitcast.101), calls=%async_computation.17 | async-start | bytes 2097152 | tf_op jit(solution)/shard_map/all_to_all | solution.py:19
  292.0 11.4 %all-to-all-start.16 = ((f32[8,3,256]{2,1,0:T(4,128)}), f32[8,3,256]{2,1,0:T(4,128)S(1)}, u32[]{:S(2)}, u32[]{:S(2)}) async-start(f32[8,3,256]{2,1,0:T(4,128)} %broadcast_in_dim.38), calls=%async_computation.16 | async-start | bytes 65536 | tf_op jit(solution)/shard_map/all_to_all | solution.py:15
  303.4 11.0 %all-to-all-start.15 = ((f32[16,16,256]{2,1,0:T(8,128)}), f32[16,16,256]{2,1,0:T(8,128)S(1)}, u32[]{:S(2)}, u32[]{:S(2)}) async-start(f32[16,16,256]{2,1,0:T(8,128)} %fusion.58), calls=%async_computation.15 | async-start | bytes 524288 | tf_op jit(solution)/shard_map/all_to_all | solution.py:19
  314.4 25.3 %all-to-all-start.14 = ((bf16[128,16,256]{2,1,0:T(8,128)(2,1)}), bf16[128,16,256]{2,1,0:T(8,128)(2,1)S(1)}, u32[]{:S(2)}, u32[]{:S(2)}) async-start(bf16[128,16,256]{2,1,0:T(8,128)(2,1)} %bitcast.26), calls=%async_computation.14 | async-start | bytes 2097152 | tf_op jit(solution)/shard_map/all_to_all | solution.py:19
  321.9 11.3 %collective-permute-start = (f32[16,256]{1,0:T(8,128)S(1)}, f32[16,256]{1,0:T(8,128)S(1)}, u32[]{:S(2)}, u32[]{:S(2)}) collective-permute-start(f32[16,256]{1,0:T(8,128)S(1)} %reduce_sum.157), channel_id=1, source_target_pairs={{0,0},{1,16},{2,32},{3,48},{4,64},{5,80},{6,96},{7,112},{8,1},{9,1... | collective-permute-start | bytes 49160 | tf_op jit(solution)/shard_map/ppermute | solution.py:275

commit v2 on v0

v2 whole, which is shorter than its diff:
```python
import jax
import jax.numpy as jnp
from jax import lax
from jax.experimental import pallas as pl
from jax.experimental.pallas import tpu as pltpu
from jax.sharding import PartitionSpec as P

ITERS = 3
BF = jnp.bfloat16
F32 = jnp.float32
LANES = 128
TILE = 256
LOG2_E = 1.4426950408889634


def deal(x, axis):
    return lax.all_to_all(x, axis, 0, 0, tiled=True)


def tdot(a, b, a_dim, b_dim):
    return lax.dot_general(a, b, (((a_dim,), (b_dim,)), ((), ())), preferred_element_type=F32)


def fold_rows(v):
    return jnp.sum(v.reshape(v.shape[0] // 8, 8, LANES), axis=0)


def as_column(row):
    return jnp.broadcast_to(row, (LANES, LANES)).T


def lane(j):
    return slice(j * LANES, (j + 1) * LANES)


def whole(shape):
    return pl.BlockSpec(shape, lambda i, *_: (0,) * len(shape))


def rows_of(rows, width):
    return pl.BlockSpec((rows, width), lambda i, *_: (i, 0))


def cols_of(rows, width):
    return pl.BlockSpec((rows, width), lambda i, *_: (0, i))


def pre_kernel(features_ref, w_ref, pre_ref, msg_ref, stat_ref):
    step = pl.program_id(0)
    last = pl.num_programs(0) - 1
    pre = jnp.dot(features_ref[...], w_ref[...], preferred_element_type=F32)
    pre_ref[...] = pre
    chunks = TILE // LANES
    half = stat_ref.shape[0] // 2
    for h in range(chunks):
        part = pre[:, lane(h)]
        stat_ref[pl.ds(step * chunks + h, 1), :] = jnp.sum(part, axis=0, keepdims=True)
        stat_ref[pl.ds(half + step * chunks + h, 1), :] = jnp.sum(part * part, axis=0, keepdims=True)

    @pl.when(step == last)
    def _():
        msg_ref[...] = jnp.broadcast_to(stat_ref[...][None], msg_ref.shape)


def relay_kernel(recv_ref, msg_ref):
    msg_ref[...] = jnp.broadcast_to(jnp.sum(recv_ref[...], axis=0, keepdims=True), msg_ref.shape)


def embed_kernel(
    total_rows, pre_ref, recv_ref, gain_ref, bias_ref, w2_ref, unit_ref, scale_ref, mean_ref, inv_ref, msg_ref, hid_ref
):
    stats = jnp.sum(recv_ref[...], axis=0)
    half = stats.shape[0] // 2
    mean = stats[:half] / total_rows
    inv = lax.rsqrt(stats[half:] / total_rows - mean * mean + 1e-05)
    mean_ref[...] = mean
    inv_ref[...] = inv
    for j in range(half):
        normed = (pre_ref[:, lane(j)] - mean[j : j + 1]) * inv[j : j + 1]
        hid_ref[:, lane(j)] = jax.nn.gelu(normed * gain_ref[j : j + 1, :] + bias_ref[j : j + 1, :]).astype(BF)
    embed = jnp.dot(hid_ref[...], w2_ref[...], preferred_element_type=F32)
    scale = lax.rsqrt(jnp.sum(embed * embed, axis=1, keepdims=True) + 1e-06)
    unit = embed * scale
    unit_ref[...] = unit
    scale_ref[...] = jnp.broadcast_to(scale, scale_ref.shape)
    msg_ref[...] = jnp.broadcast_to(unit.astype(BF)[None], msg_ref.shape)


def proto_kernel(raw_ref, raw_t_ref, proto_ref, proto_t_ref):
    raw = raw_ref[...].astype(F32)
    proto_ref[...] = (raw * lax.rsqrt(jnp.sum(raw * raw, axis=1, keepdims=True) + 1e-06)).astype(BF)
    raw_t = raw_t_ref[...].astype(F32)
    proto_t_ref[...] = (raw_t * lax.rsqrt(jnp.sum(raw_t * raw_t, axis=0, keepdims=True) + 1e-06)).astype(BF)


def mate_kernel(pair_ref, embed_ref, mate_ref):
    rows = pair_ref.shape[0]
    total = embed_ref.shape[0]
    hot = lax.broadcasted_iota(jnp.int32, (rows, total), 1) == pair_ref[...]
    mate_ref[...] = jnp.dot(
        jnp.where(hot, 1.0, 0.0).astype(BF), embed_ref[...], preferred_element_type=F32
    ).astype(BF)


def score_kernel(embed_ref, proto_t_ref, kern_ref, msg_ref, soft_ref, acc_ref):
    step = pl.program_id(0)
    rows = embed_ref.shape[0]
    cols = proto_t_ref.shape[1]

    @pl.when(step == 0)
    def _():
        acc_ref[...] = jnp.zeros_like(acc_ref)

    soft = [None] * (rows // LANES)
    for j in range(cols // TILE):
        span = slice(j * TILE, (j + 1) * TILE)
        scores = jnp.dot(embed_ref[...], proto_t_ref[:, span], preferred_element_type=F32)
        tempered = jnp.exp2(scores * (10.0 * LOG2_E))
        kern = tempered * tempered
        kern_ref[:, span] = kern.astype(BF)
        for h in range(TILE // LANES):
            at = (j * (TILE // LANES) + h) * 8
            acc_ref[at : at + 8, :] += fold_rows(kern[:, lane(h)])
        for b in range(rows // LANES):
            part = tempered[b * LANES : (b + 1) * LANES]
            part = part[:, :LANES] + part[:, LANES:]
            soft[b] = part if soft[b] is None else soft[b] + part
    for b in range(rows // LANES):
        soft_ref[pl.ds(step * (rows // LANES) + b, 1), :] = jnp.sum(soft[b].T, axis=0, keepdims=True)

    @pl.when(step == pl.num_programs(0) - 1)
    def _():
        total = jnp.sum(acc_ref[...].reshape(cols // LANES, 8, LANES), axis=1)
        msg_ref[...] = jnp.broadcast_to(total[None], msg_ref.shape)


def row_kernel(recv_ref, kern_ref, *rest):
    soft_ref = rest[0] if len(rest) == 3 else None
    msg_ref, scale_ref = rest[-2:]
    step = pl.program_id(0)
    rows = kern_ref.shape[0]
    copies = msg_ref.shape[0]

    @pl.when(step == 0)
    def _():
        scale_ref[...] = 1.0 / jnp.sum(recv_ref[...], axis=0)
        if soft_ref is not None:
            half = soft_ref.shape[0]
            msg_ref[:, half:, :] = jnp.broadcast_to(soft_ref[...][None], (copies, half, LANES))

    for b in range(rows // LANES):
        acc = None
        for j in range(scale_ref.shape[0]):
            part = kern_ref[b * LANES : (b + 1) * LANES, lane(j)].astype(F32) * scale_ref[j : j + 1, :]
            acc = part if acc is None else acc + part
        row = jnp.sum(acc.T, axis=0, keepdims=True)
        msg_ref[:, pl.ds(step * (rows // LANES) + b, 1), :] = jnp.broadcast_to(row[None], (copies, 1, LANES))


def col_kernel(recv_ref, kern_ref, msg_ref, acc_ref, scale_ref):
    step = pl.program_id(0)
    rows, cols = kern_ref.shape

    @pl.when(step == 0)
    def _():
        acc_ref[...] = jnp.zeros_like(acc_ref)
        scale_ref[...] = 1.0 / jnp.sum(recv_ref[:, : scale_ref.shape[0], :], axis=0)

    for b in range(rows // LANES):
        scale = as_column(scale_ref[pl.ds(step * (rows // LANES) + b, 1), :])
        for j in range(cols // LANES):
            part = kern_ref[b * LANES : (b + 1) * LANES, lane(j)].astype(F32) * scale
            acc_ref[j * 8 : (j + 1) * 8, :] += fold_rows(part)

    @pl.when(step == pl.num_programs(0) - 1)
    def _():
        total = jnp.sum(acc_ref[...].reshape(cols // LANES, 8, LANES), axis=1)
        msg_ref[...] = jnp.broadcast_to(total[None], msg_ref.shape)


def final_kernel(
    embed_ref, mate_ref, pair_ref, proto_t_ref, proto_ref, raw_t_ref, recv_col_ref, recv_row_ref, recv_soft_ref,
    d_unit_ref, term_ref, loss_ref, acc_ref, loss_acc_ref, col_ref, row_ref, soft_ref,
):
    step = pl.program_id(0)
    rows = embed_ref.shape[0]
    cols = proto_t_ref.shape[1]
    bands = row_ref.shape[0]
    chunks = TILE // LANES

    @pl.when(step == 0)
    def _():
        acc_ref[...] = jnp.zeros_like(acc_ref)
        loss_acc_ref[...] = jnp.zeros_like(loss_acc_ref)
        col_ref[...] = 10.0 / jnp.sum(recv_col_ref[...], axis=0)
        row_ref[...] = 1.0 / jnp.sum(recv_row_ref[:, :bands, :], axis=0)
        soft_ref[...] = jnp.sum(recv_soft_ref[:, bands:, :], axis=0)
        loss_acc_ref[8:16, :] = jnp.log(soft_ref[...])

    pair = pair_ref[...]
    spot = lax.broadcasted_iota(jnp.int32, (rows, LANES), 1)
    found = jnp.zeros((rows, LANES), F32)
    for q in range(bands):
        found += jnp.where(spot + q * LANES == pair, row_ref[q : q + 1, :], 0.0)
    mate_scale = jnp.sum(found, axis=1, keepdims=True)
    base = step * (rows // LANES)
    soft = jnp.concatenate([as_column(soft_ref[pl.ds(base + b, 1), :]) for b in range(rows // LANES)], axis=0)
    inv_soft = 10.0 / soft
    d_unit = None
    loss_acc = jnp.zeros((8, LANES), F32)
    for j in range(cols // TILE):
        span = slice(j * TILE, (j + 1) * TILE)
        scores = jnp.dot(embed_ref[...], proto_t_ref[:, span], preferred_element_type=F32)
        mates = jnp.dot(mate_ref[...], proto_t_ref[:, span], preferred_element_type=F32)
        grads = []
        for h in range(chunks):
            at = j * chunks + h
            target = jnp.exp2(mates[:, lane(h)] * (20.0 * LOG2_E)) * mate_scale * col_ref[at : at + 1, :]
            score = scores[:, lane(h)]
            loss_acc += fold_rows(target * score)
            grads.append((jnp.exp2(score * (10.0 * LOG2_E)) * inv_soft - target).astype(BF))
        grad = jnp.concatenate(grads, axis=1)
        part = jnp.dot(grad, proto_ref[span, :], preferred_element_type=F32)
        d_unit = part if d_unit is None else d_unit + part
        acc_ref[:, span] += tdot(embed_ref[...], grad, 0, 0)
    d_unit_ref[...] = d_unit.astype(BF)
    loss_acc_ref[0:8, :] += loss_acc

    @pl.when(step == pl.num_programs(0) - 1)
    def _():
        for j in range(cols // TILE):
            span = slice(j * TILE, (j + 1) * TILE)
            raw = raw_t_ref[:, span].astype(F32)
            scale = lax.rsqrt(jnp.sum(raw * raw, axis=0, keepdims=True) + 1e-06)
            unit = raw * scale
            acc = acc_ref[:, span]
            term_ref[:, span] = ((acc - unit * jnp.sum(unit * acc, axis=0, keepdims=True)) * scale).astype(BF)
        loss_ref[...] = loss_acc_ref[...]


def d_embed_kernel(recv_ref, unit_ref, scale_ref, msg_ref):
    d_unit = jnp.sum(recv_ref[...].astype(F32), axis=0)
    unit = unit_ref[...]
    d_embed = (d_unit - unit * jnp.sum(unit * d_unit, axis=1, keepdims=True)) * scale_ref[:, :1]
    msg_ref[...] = jnp.broadcast_to(d_embed.astype(BF)[None], msg_ref.shape)


def gather_parts(refs):
    return jnp.concatenate([ref[...] for ref in refs], axis=0)


def slab_kernel(order_ref, mean_ref, inv_ref, gain_ref, bias_ref, w_ref, *rest):
    parts = rest[:-4]
    normed_ref, slope_ref, hid_ref, acc_ref = rest[-4:]
    step = pl.program_id(0)

    @pl.when(step == 0)
    def _():
        acc_ref[...] = jnp.zeros_like(acc_ref)

    acc_ref[...] += jnp.dot(gather_parts(parts), w_ref[...], preferred_element_type=F32)

    @pl.when(step == pl.num_programs(0) - 1)
    def _():
        chunks = acc_ref.shape[1] // LANES
        ones = jnp.ones((LANES, LANES), F32)
        for h in range(chunks):
            at = pl.ds(order_ref[0] * chunks + h, 1)
            mean, inv, gain, bias = mean_ref[at, :], inv_ref[at, :], gain_ref[at, :], bias_ref[at, :]
            for b in range(acc_ref.shape[0] // LANES):
                band = slice(b * LANES, (b + 1) * LANES)
                normed = (acc_ref[band, lane(h)] - mean) * inv
                hidden, back = jax.vjp(jax.nn.gelu, normed * gain + bias)
                normed_ref[band, lane(h)] = normed
                slope_ref[band, lane(h)] = back(ones)[0]
                hid_ref[band, lane(h)] = hidden.astype(BF)


def shift_kernel(order_ref, d_embed_ref, w2_ref, normed_ref, slope_ref, hid_ref, loss_ref, shift_ref, msg_ref, sum_ref, second_ref):
    step = pl.program_id(0)

    @pl.when(step == 0)
    def _():
        sum_ref[...] = jnp.zeros_like(sum_ref)
        second_ref[...] = jnp.zeros_like(second_ref)

    d_embed = d_embed_ref[0]
    d_shift = tdot(d_embed, w2_ref[...], 1, 1) * slope_ref[...]
    shift_ref[...] = d_shift
    sum_ref[0:1, :] += jnp.sum(d_shift * normed_ref[...], axis=0, keepdims=True)
    sum_ref[1:2, :] += jnp.sum(d_shift, axis=0, keepdims=True)
    second_ref[...] += tdot(hid_ref[...], d_embed, 0, 0)

    @pl.when(step == pl.num_programs(0) - 1)
    def _():
        hits = jnp.sum(loss_ref[0:8, :], axis=0, keepdims=True)
        logs = jnp.sum(loss_ref[8:16, :], axis=0, keepdims=True)
        sum_ref[2:3, :] = jnp.concatenate([hits, logs], axis=1)
        n, height, slab = msg_ref.shape
        msg_ref[:, :8, :] = jnp.broadcast_to(sum_ref[...][None], (n, 8, slab))
        msg_ref[:, 8:, :] = second_ref[...].reshape(n, height - 8, slab)


def first_kernel(
    total_rows, order_ref, recv_ref, shift_ref, normed_ref, inv_ref, gain_ref, *rest
):
    parts = rest[:-4]
    out_ref, sums_ref, second_ref, d_pre_ref = rest[-4:]
    step = pl.program_id(0)

    @pl.when(step == 0)
    def _():
        got = jnp.sum(recv_ref[...], axis=0)
        sums_ref[...] = jnp.broadcast_to(got[:8][None], sums_ref.shape)
        second_ref[...] = got[8:]
        chunks = d_pre_ref.shape[1] // LANES
        for h in range(chunks):
            at = pl.ds(order_ref[0] * chunks + h, 1)
            factor = gain_ref[at, :] * inv_ref[at, :]
            gain_mean = got[0:1, lane(h)] / total_rows
            bias_mean = got[1:2, lane(h)] / total_rows
            for b in range(d_pre_ref.shape[0] // LANES):
                band = slice(b * LANES, (b + 1) * LANES)
                d_pre = factor * (shift_ref[band, lane(h)] - bias_mean - normed_ref[band, lane(h)] * gain_mean)
                d_pre_ref[band, lane(h)] = d_pre.astype(BF)

    grad = tdot(gather_parts(parts), d_pre_ref[...], 0, 0)
    out_ref[...] = grad.astype(BF).reshape(out_ref.shape)


def tail_kernel(recv_ref, out_ref):
    out_ref[...] = jnp.sum(recv_ref[:, 0].astype(F32), axis=0)


def shape(dims, kind=F32):
    return jax.ShapeDtypeStruct(dims, kind)


def local(features, w_first, bn_gain, bn_bias, w_second, prototypes, pair):
    n_batch = lax.axis_size("batch")
    n_proto = lax.axis_size("proto")
    own, d_in = features.shape
    d_hid, width = w_second.shape
    cols = prototypes.shape[0]
    total_rows = own * n_batch * n_proto
    rows = own * n_proto
    part = lax.axis_index("proto")
    slab = d_hid // n_proto
    col_bands = cols // LANES
    row_bands = rows // LANES
    hid_bands = d_hid // LANES
    steps = rows // TILE
    gain = bn_gain.reshape(hid_bands, LANES)
    bias = bn_bias.reshape(hid_bands, LANES)

    def hop(x, moves):
        return lax.ppermute(x, "proto", moves)

    ring = n_proto // 2
    right = [(i * 2 + c, (i + 1) % ring * 2 + c) for i in range(ring) for c in range(2)]
    left = [(t, s) for s, t in right]
    swap = [(i, i ^ 1) for i in range(n_proto)]
    from_left = hop(features, right)
    from_right = hop(features, left)
    far_top = hop(from_left[: own // 2], right)
    far_low = hop(from_right[own // 2 :], left)
    mine = [features, from_right, from_left, far_top, far_low]
    parts = mine + [hop(piece, swap) for piece in mine]
    order = jnp.stack(
        [part] + [((part // 2 + d) % ring) * 2 + (part % 2) ^ o for o in range(2) for d in (0, 1, 3, 2)]
    ).astype(jnp.int32)

    raw_t = prototypes.T
    proto_bf, proto_t = pl.pallas_call(
        proto_kernel,
        grid=(cols // 512,),
        in_specs=[rows_of(512, width), cols_of(width, 512)],
        out_specs=[rows_of(512, width), cols_of(width, 512)],
        out_shape=[shape((cols, width), BF), shape((width, cols), BF)],
        name="proto_kernel",
    )(prototypes, raw_t)

    pre, msg = pl.pallas_call(
        pre_kernel,
        grid=(d_hid // TILE,),
        in_specs=[whole((own, d_in)), cols_of(d_in, TILE)],
        out_specs=[cols_of(own, TILE), whole((n_batch, 2 * hid_bands, LANES))],
        out_shape=[shape((own, d_hid)), shape((n_batch, 2 * hid_bands, LANES))],
        scratch_shapes=[pltpu.VMEM((2 * hid_bands, LANES), F32)],
        name="pre_kernel",
    )(features, w_first)
    msg = pl.pallas_call(
        relay_kernel, out_shape=shape((n_proto, 2 * hid_bands, LANES)), name="relay_kernel"
    )(deal(msg, "batch"))
    unit_embed, embed_scale, mean, inv, msg = pl.pallas_call(
        lambda *refs: embed_kernel(total_rows, *refs),
        out_shape=[
            shape((own, width)),
            shape((own, LANES)),
            shape((hid_bands, LANES)),
            shape((hid_bands, LANES)),
            shape((n_proto, own, width), BF),
        ],
        scratch_shapes=[pltpu.VMEM((own, d_hid), BF)],
        name="embed_kernel",
    )(pre, deal(msg, "proto"), gain, bias, w_second)
    block_embed = deal(msg, "proto").reshape(rows, width)

    kern, col_msg, soft = pl.pallas_call(
        score_kernel,
        grid=(steps,),
        in_specs=[rows_of(TILE, width), whole((width, cols))],
        out_specs=[rows_of(TILE, cols), whole((n_batch, col_bands, LANES)), whole((row_bands, LANES))],
        out_shape=[shape((rows, cols), BF), shape((n_batch, col_bands, LANES)), shape((row_bands, LANES))],
        scratch_shapes=[pltpu.VMEM((col_bands * 8, LANES), F32)],
        name="score_kernel",
    )(block_embed, proto_t)

    def row_pass(recv, extra):
        height = row_bands * (2 if extra else 1)
        return pl.pallas_call(
            row_kernel,
            grid=(steps,),
            in_specs=[whole((n_batch, col_bands, LANES)), rows_of(TILE, cols)]
            + [whole((row_bands, LANES)) for _ in extra],
            out_specs=whole((n_proto, height, LANES)),
            out_shape=shape((n_proto, height, LANES)),
            scratch_shapes=[pltpu.VMEM((col_bands, LANES), F32)],
            name="row_kernel",
        )(recv, kern, *extra)

    def col_pass(recv):
        return pl.pallas_call(
            col_kernel,
            grid=(steps,),
            in_specs=[whole(recv.shape), rows_of(TILE, cols)],
            out_specs=whole((n_batch, col_bands, LANES)),
            out_shape=shape((n_batch, col_bands, LANES)),
            scratch_shapes=[pltpu.VMEM((col_bands * 8, LANES), F32), pltpu.VMEM((row_bands, LANES), F32)],
            name="col_kernel",
        )(recv, kern)

    first_row = lax.axis_index("batch") * rows
    mate_row = (pair - first_row)[:, None]
    mates = pl.pallas_call(
        mate_kernel,
        grid=(steps,),
        in_specs=[rows_of(TILE, 1), whole((rows, width))],
        out_specs=rows_of(TILE, width),
        out_shape=shape((rows, width), BF),
        name="mate_kernel",
    )(mate_row, block_embed)

    recv_soft = None
    for step in range(ITERS):
        recv_col = deal(col_msg, "batch")
        recv_row = deal(row_pass(recv_col, () if step else (soft,)), "proto")
        recv_soft = recv_row if recv_soft is None else recv_soft
        if step + 1 < ITERS:
            col_msg = col_pass(recv_row)

    d_unit, term, loss_tile = pl.pallas_call(
        final_kernel,
        grid=(steps,),
        in_specs=[
            rows_of(TILE, width),
            rows_of(TILE, width),
            rows_of(TILE, 1),
            whole((width, cols)),
            whole((cols, width)),
            whole((width, cols)),
            whole(recv_col.shape),
            whole(recv_row.shape),
            whole(recv_soft.shape),
        ],
        out_specs=[rows_of(TILE, width), whole((width, cols)), whole((16, LANES))],
        out_shape=[shape((rows, width), BF), shape((width, cols), BF), shape((16, LANES))],
        scratch_shapes=[
            pltpu.VMEM((width, cols), F32),
            pltpu.VMEM((16, LANES), F32),
            pltpu.VMEM((col_bands, LANES), F32),
            pltpu.VMEM((row_bands, LANES), F32),
            pltpu.VMEM((row_bands, LANES), F32),
        ],
        name="final_kernel",
    )(block_embed, mates, mate_row, proto_t, proto_bf, raw_t, recv_col, recv_row, recv_soft)

    d_embed = pl.pallas_call(
        d_embed_kernel, out_shape=shape((n_proto, own, width), BF), name="d_embed_kernel"
    )(deal(d_unit.reshape(n_proto, own, width), "proto"), unit_embed, embed_scale)
    d_embed = deal(d_embed, "proto")
    term_got = deal(term.reshape(n_batch, width // n_batch, cols), "batch")
    grad_proto = jnp.sum(term_got.astype(F32), axis=0).T

    stat_spec = whole((hid_bands, LANES))
    part_specs = [pl.BlockSpec((piece.shape[0], TILE), lambda i, *_: (0, i)) for piece in parts]
    normed, slope, hid = pl.pallas_call(
        slab_kernel,
        grid_spec=pltpu.PrefetchScalarGridSpec(
            num_scalar_prefetch=1,
            grid=(d_in // TILE,),
            in_specs=[stat_spec] * 4 + [pl.BlockSpec((TILE, slab), lambda i, s: (i, s[0]))] + part_specs,
            out_specs=[whole((rows, slab))] * 3,
            scratch_shapes=[pltpu.VMEM((rows, slab), F32)],
        ),
        out_shape=[shape((rows, slab)), shape((rows, slab)), shape((rows, slab), BF)],
        name="slab_kernel",
    )(order, mean, inv, gain, bias, w_first, *parts)

    shift, msg = pl.pallas_call(
        shift_kernel,
        grid_spec=pltpu.PrefetchScalarGridSpec(
            num_scalar_prefetch=1,
            grid=(n_proto,),
            in_specs=[
                pl.BlockSpec((1, own, width), lambda i, s: (s[i + 1], 0, 0)),
                pl.BlockSpec((slab, width), lambda i, s: (s[0], 0)),
                rows_of(own, slab),
                rows_of(own, slab),
                rows_of(own, slab),
                whole((16, LANES)),
            ],
            out_specs=[rows_of(own, slab), whole((n_batch, 8 + slab // n_batch, width))],
            scratch_shapes=[pltpu.VMEM((8, slab), F32), pltpu.VMEM((slab, width), F32)],
        ),
        out_shape=[shape((rows, slab)), shape((n_batch, 8 + slab // n_batch, width))],
        name="shift_kernel",
    )(order, d_embed, w_second, normed, slope, hid, loss_tile)
    recv = deal(msg, "batch")

    share = d_in // (n_batch * n_proto)
    first, sums, second = pl.pallas_call(
        lambda *refs: first_kernel(total_rows, *refs),
        grid_spec=pltpu.PrefetchScalarGridSpec(
            num_scalar_prefetch=1,
            grid=(d_in // TILE,),
            in_specs=[whole(recv.shape), whole((rows, slab)), whole((rows, slab)), stat_spec, stat_spec] + part_specs,
            out_specs=[
                pl.BlockSpec((TILE // share, share, slab), lambda i, s: (i, 0, 0)),
                whole((n_proto, 8, slab)),
                whole((slab // n_batch, width)),
            ],
            scratch_shapes=[pltpu.VMEM((rows, slab), BF)],
        ),
        out_shape=[
            shape((n_batch * n_proto, share, slab), BF),
            shape((n_proto, 8, slab)),
            shape((slab // n_batch, width)),
        ],
        name="first_kernel",
    )(order, recv, shift, normed, inv, gain, *parts)

    first = deal(first, ("batch", "proto")).reshape(n_batch, n_proto, share, slab)
    grad_first = pl.pallas_call(
        tail_kernel,
        grid=(n_proto,),
        in_specs=[pl.BlockSpec((n_batch, 1, share, slab), lambda i: (0, i, 0, 0))],
        out_specs=cols_of(share, slab),
        out_shape=shape((share, d_hid)),
        name="tail_kernel",
    )(first)
    grad_second = lax.ppermute(
        second,
        ("batch", "proto"),
        [(b * n_proto + p, p * n_batch + b) for b in range(n_batch) for p in range(n_proto)],
    )
    sums = deal(sums, "proto")
    grad_gain = sums[:, 0].reshape(-1)
    grad_bias = sums[:, 1].reshape(-1)
    hits = jnp.sum(sums[:, 2, :LANES])
    logs = jnp.sum(sums[0, 2, LANES:])
    loss = (logs - hits) / total_rows
    return (grad_first, grad_second, grad_gain, grad_bias, grad_proto, loss)


def solution(mesh):
    return jax.shard_map(
        local,
        mesh=mesh,
        in_specs=(P(("batch", "proto"), None), P(), P(), P(), P(), P("proto", None), P("batch")),
        out_specs=(
            P(("batch", "proto"), None),
            P(("batch", "proto"), None),
            P(),
            P(),
            P("proto", "batch"),
            P(),
        ),
        check_vma=False,
    )
```

time: 1770 us -> 283 us (0.16)
  waiting for transfers between devices: 1300 us -> 30.7 us
  blocking collectives: 301 us -> 97.2 us
  Pallas kernels: 0 us -> 94.6 us
  matrix products: 76.6 us -> 0 us
  starting transfers between devices: 0.42 us -> 42.1 us
  local copies, waits for them, and re-layouts: 37.1 us -> 10.7 us
  other arithmetic: 24.2 us -> 2.01 us
    unnamed x5 -> x0, waiting for transfers between devices: 669 us -> none
    reduce_scatter x3 -> x0, waiting for transfers between devices: 634 us -> none  [the longest x1 617 us: local(): lax.psum_scatter(second_term, ('batch', 'proto'), scatter_dimension=0, ti...]
    psum x8 -> x0, blocking collectives: 287 us -> none  [the longest x3 91.9 us: cluster_balancing_pass(): return 1.0 / lax.psum(incomplete_cluster_totals, 'batch')]
    all_to_all x0 -> x8, blocking collectives: none -> 97.2 us  [deal(): return lax.all_to_all(x, axis, 0, 0, tiled=True)]
    pallas_call x0 -> x17, Pallas kernels: none -> 94.6 us  [the longest x1 14.3 us: local(): pl.pallas_call(final_kernel, grid=(steps,), in_specs=[rows_of(TILE, width...]
    dot_general x14 -> x0, matrix products: 76.6 us -> none  [the longest x3 30.5 us: local(): jnp.dot(transport_exponential_matrix, per_cluster_multiplier, precision=l...]
    all_to_all x0 -> x7, starting transfers between devices: none -> 30.9 us  [deal(): return lax.all_to_all(x, axis, 0, 0, tiled=True)]
    all_to_all x0 -> x7, waiting for transfers between devices: none -> 29.5 us  [deal(): return lax.all_to_all(x, axis, 0, 0, tiled=True)]
  transfers between devices with their start and end apart: 4 -> 17, of which waited for: 3 -> 8; matrix products, arithmetic and copies ran while one was open for 2% -> 3% of each run, Pallas kernels for 0% -> 17%
where the time goes in v2:
time: 283 us; the launch traced here: 280 us
  blocking collectives  97.2 us (34%)
  Pallas kernels  94.6 us (33%)
  starting transfers between devices  42.1 us (15%)
  waiting for transfers between devices  30.7 us (11%)
  local copies, waits for them, and re-layouts  10.7 us (4%)
  between operations  3.21 us (1%)
    all_to_all x8, blocking collectives, deal(): return lax.all_to_all(x, axis, 0, 0, tiled=True)  97.2 us
    all_to_all x7, starting transfers between devices, deal(): return lax.all_to_all(x, axis, 0, 0, tiled=True)  30.9 us
    all_to_all x7, waiting for transfers between devices, deal(): return lax.all_to_all(x, axis, 0, 0, tiled=True)  29.5 us
    pallas_call x1, Pallas kernels, local(): pl.pallas_call(final_kernel, grid=(steps,), in_specs=[rows_of(TILE, width...  14.3 us
    pallas_call x3, Pallas kernels, row_pass(): pl.pallas_call(row_kernel, grid=(steps,), in_specs=[whole((n_batch, col_b...  12.3 us
    pallas_call x1, Pallas kernels, local(): pl.pallas_call(slab_kernel, grid_spec=pltpu.PrefetchScalarGridSpec(num_sc...  9.25 us
    pallas_call x1, Pallas kernels, local(): pl.pallas_call(lambda *refs: first_kernel(total_rows, *refs), grid_spec=p...  8.84 us
    pallas_call x2, Pallas kernels, col_pass(): pl.pallas_call(col_kernel, grid=(steps,), in_specs=[whole(recv.shape), ro...  8.21 us
  transfers between devices with their start and end apart: 17, of which 8 were waited for; matrix products, arithmetic and copies ran while one was open for 3% of the time, Pallas kernels for 17%

profile of v2, /device:TPU:1, one launch (start us, length us, event | category | flops | bytes accessed | tf_op | source)
XLA Modules:
  0.0 280.5 jit_solution(7934172533980940188)
XLA Ops:
  0.6 8.2 %pre_kernel.1 = (f32[128,2048]{1,0:T(8,128)}, f32[16,32,128]{2,1,0:T(8,128)}) custom-call(bf16[128,2048]{1,0:T(8,128)(2,1)} %refs_6_.1, bf16[2048,2048]{1,0:T(8,128)(2,1)} %w_ref.3), custom_call_target="tpu_custom_call" | custom-call | tf_op jit(solution)/shard_map/pre_kernel/pallas_call | solution.py:383
  8.8 16.3 %all_to_all.75.recv_ref = f32[16,32,128]{2,1,0:T(8,128)} all-to-all(f32[16,32,128]{2,1,0:T(8,128)} %get-tuple-element.30), channel_id=1, replica_groups=mesh['batch'=16,'proto'=8] {'batch'}, dimensions={0} | all-to-all | bytes 524288 | tf_op jit(solution)/shard_map/all_to_all | solution.py:17
  25.1 1.6 relay_kernel.1
  26.7 11.6 %all_to_all.76.refs_1_ = f32[8,32,128]{2,1,0:T(8,128)} all-to-all(f32[8,32,128]{2,1,0:T(8,128)} %relay_kernel.1), channel_id=1, replica_groups=mesh['batch'=16,'proto'=8] {'proto'}, dimensions={0} | all-to-all | bytes 262144 | tf_op jit(solution)/shard_map/all_to_all | solution.py:17
  38.4 3.4 %embed_kernel.1 = (f32[128,256]{1,0:T(8,128)}, f32[128,128]{1,0:T(8,128)}, f32[16,128]{1,0:T(8,128)}, f32[16,128]{1,0:T(8,128)}, bf16[8,128,256]{2,1,0:T(8,128)(2,1)}) custom-call(f32[128,2048]{1,0:T(8,128)} %get-tuple-element.29.refs_0_, f32[8,32,128]{2,1,0:T(8,128)} %all_to_all.76.refs_1_, f32[16,128]{1,0:T(8,128)} %bitcast.28, f32[16,128]{1,0:T(8,128)} %bitcast.31, ...), custom_call_target="tpu_custom_call" | custom-call | tf_op jit(solution)/shard_map/embed_kernel/pallas_call | solution.py:395
  41.7 4.3 %all-to-all-start.2 = ((bf16[8,128,256]{2,1,0:T(8,128)(2,1)}), bf16[8,128,256]{2,1,0:T(8,128)(2,1)S(1)}, u32[]{:S(2)}, u32[]{:S(2)}) async-start(bf16[8,128,256]{2,1,0:T(8,128)(2,1)} %get-tuple-element.31), calls=%async_computation.2 | async-start | bytes 1048576 | tf_op jit(solution)/shard_map/all_to_all | solution.py:17
  46.0 1.4 copy.15
  47.4 4.1 %proto_kernel.1 = (bf16[2048,256]{1,0:T(8,128)(2,1)}, bf16[256,2048]{1,0:T(8,128)(2,1)}) custom-call(bf16[2048,256]{1,0:T(8,128)(2,1)} %raw_ref.1, bf16[256,2048]{1,0:T(8,128)(2,1)} %bitcast.20), custom_call_target="tpu_custom_call" | custom-call | tf_op jit(solution)/shard_map/proto_kernel/pallas_call | solution.py:374
  51.5 3.9 %all-to-all-done.2 = bf16[8,128,256]{2,1,0:T(8,128)(2,1)S(1)} async-done(((bf16[8,128,256]{2,1,0:T(8,128)(2,1)}), bf16[8,128,256]{2,1,0:T(8,128)(2,1)S(1)}, u32[]{:S(2)}, u32[]{:S(2)}) %all-to-all-start.2) | async-done | bytes 524320 | tf_op jit(solution)/shard_map/all_to_all | solution.py:17
  55.4 0.8 copy-done
  56.2 5.6 %score_kernel.1 = (bf16[1024,2048]{1,0:T(8,128)(2,1)}, f32[16,16,128]{2,1,0:T(8,128)}, f32[8,128]{1,0:T(8,128)}) custom-call(bf16[1024,256]{1,0:T(8,128)(2,1)} %bitcast.22, bf16[256,2048]{1,0:T(8,128)(2,1)} %get-tuple-element.32.proto_t_ref), custom_call_target="tpu_custom_call" | custom-call | tf_op jit(solution)/shard_map/score_kernel/pallas_call | solution.py:409
  61.8 11.0 %all_to_all.77.recv_ref = f32[16,16,128]{2,1,0:T(8,128)} all-to-all(f32[16,16,128]{2,1,0:T(8,128)} %get-tuple-element.34), channel_id=1, replica_groups=mesh['batch'=16,'proto'=8] {'batch'}, dimensions={0} | all-to-all | bytes 262144 | tf_op jit(solution)/shard_map/all_to_all | solution.py:17
  72.8 4.1 %row_kernel.3 = f32[8,16,128]{2,1,0:T(8,128)} custom-call(f32[16,16,128]{2,1,0:T(8,128)} %all_to_all.77.recv_ref, bf16[1024,2048]{1,0:T(8,128)(2,1)} %get-tuple-element.35.kern_ref, f32[8,128]{1,0:T(8,128)} %get-tuple-element.36.rest_0_), custom_call_target="tpu_custom_call" | custom-call | tf_op jit(solution)/shard_map/row_kernel/pallas_call | solution.py:421
  77.0 10.7 %all_to_all.78.recv_ref.recv_soft_ref = f32[8,16,128]{2,1,0:T(8,128)} all-to-all(f32[8,16,128]{2,1,0:T(8,128)} %row_kernel.3), channel_id=1, replica_groups=mesh['batch'=16,'proto'=8] {'proto'}, dimensions={0} | all-to-all | bytes 131072 | tf_op jit(solution)/shard_map/all_to_all | solution.py:17
  87.7 4.1 %col_kernel.2 = f32[16,16,128]{2,1,0:T(8,128)} custom-call(f32[8,16,128]{2,1,0:T(8,128)} %all_to_all.78.recv_ref.recv_soft_ref, bf16[1024,2048]{1,0:T(8,128)(2,1)} %get-tuple-element.35.kern_ref), custom_call_target="tpu_custom_call" | custom-call | tf_op jit(solution)/shard_map/col_kernel/pallas_call | solution.py:433
  91.8 10.9 %all_to_all.79.recv_ref = f32[16,16,128]{2,1,0:T(8,128)} all-to-all(f32[16,16,128]{2,1,0:T(8,128)} %col_kernel.2), channel_id=1, replica_groups=mesh['batch'=16,'proto'=8] {'batch'}, dimensions={0} | all-to-all | bytes 262144 | tf_op jit(solution)/shard_map/all_to_all | solution.py:17
  102.7 4.1 %row_kernel.4 = f32[8,8,128]{2,1,0:T(8,128)} custom-call(f32[16,16,128]{2,1,0:T(8,128)} %all_to_all.79.recv_ref, bf16[1024,2048]{1,0:T(8,128)(2,1)} %get-tuple-element.35.kern_ref), custom_call_target="tpu_custom_call" | custom-call | tf_op jit(solution)/shard_map/row_kernel/pallas_call | solution.py:421
  106.8 10.5 %all_to_all.80.recv_ref = f32[8,8,128]{2,1,0:T(8,128)} all-to-all(f32[8,8,128]{2,1,0:T(8,128)} %row_kernel.4), channel_id=1, replica_groups=mesh['batch'=16,'proto'=8] {'proto'}, dimensions={0} | all-to-all | bytes 65536 | tf_op jit(solution)/shard_map/all_to_all | solution.py:17
  117.3 4.1 %col_kernel.3 = f32[16,16,128]{2,1,0:T(8,128)} custom-call(f32[8,8,128]{2,1,0:T(8,128)} %all_to_all.80.recv_ref, bf16[1024,2048]{1,0:T(8,128)(2,1)} %get-tuple-element.35.kern_ref), custom_call_target="tpu_custom_call" | custom-call | tf_op jit(solution)/shard_map/col_kernel/pallas_call | solution.py:433
  121.5 3.5 %all-to-all-start.7 = ((f32[16,16,128]{2,1,0:T(8,128)}), f32[16,16,128]{2,1,0:T(8,128)S(1)}, u32[]{:S(2)}, u32[]{:S(2)}) async-start(f32[16,16,128]{2,1,0:T(8,128)} %col_kernel.3), calls=%async_computation.7 | async-start | bytes 262144 | tf_op jit(solution)/shard_map/all_to_all | solution.py:17
  125.0 1.0 collective-permute-start
  126.5 5.3 %all-to-all-done.7.recv_ref.recv_col_ref = f32[16,16,128]{2,1,0:T(8,128)S(1)} async-done(((f32[16,16,128]{2,1,0:T(8,128)}), f32[16,16,128]{2,1,0:T(8,128)S(1)}, u32[]{:S(2)}, u32[]{:S(2)}) %all-to-all-start.7) | async-done | bytes 131104 | tf_op jit(solution)/shard_map/all_to_all | solution.py:17
  132.4 4.1 %row_kernel.5 = f32[8,8,128]{2,1,0:T(8,128)} custom-call(f32[16,16,128]{2,1,0:T(8,128)} %copy-done.10, bf16[1024,2048]{1,0:T(8,128)(2,1)} %get-tuple-element.35.kern_ref), custom_call_target="tpu_custom_call" | custom-call | tf_op jit(solution)/shard_map/row_kernel/pallas_call | solution.py:421
  136.5 5.1 %all-to-all-start.8 = ((f32[8,8,128]{2,1,0:T(8,128)}), f32[8,8,128]{2,1,0:T(8,128)S(1)}, u32[]{:S(2)}, u32[]{:S(2)}) async-start(f32[8,8,128]{2,1,0:T(8,128)} %row_kernel.5), calls=%async_computation.8 | async-start | bytes 65536 | tf_op jit(solution)/shard_map/all_to_all | solution.py:17
  141.6 1.0 copy.14.pair_ref
  142.7 4.1 %mate_kernel.1.mate_ref = bf16[1024,256]{1,0:T(8,128)(2,1)} custom-call(s32[1024,1]{1,0:T(8,128)} %copy.14.pair_ref, bf16[1024,256]{1,0:T(8,128)(2,1)} %bitcast.23), custom_call_target="tpu_custom_call" | custom-call | tf_op jit(solution)/shard_map/mate_kernel/pallas_call | solution.py:445
  147.4 14.3 %final_kernel.1 = (bf16[1024,256]{1,0:T(8,128)(2,1)}, bf16[256,2048]{1,0:T(8,128)(2,1)}, f32[16,128]{1,0:T(8,128)}) custom-call(bf16[1024,256]{1,0:T(8,128)(2,1)} %bitcast.24, bf16[1024,256]{1,0:T(8,128)(2,1)} %mate_kernel.1.mate_ref, s32[1024,1]{1,0:T(8,128)} %copy.14.pair_ref, bf16[256,2048]{1,0:T(8,128)(2,1)} %get-tuple-element.32.proto_t_ref, ...), custom_call_target="tpu_custom_call" | custom-call | tf_op jit(solution)/shard_map/final_kernel/pallas_call | solution.py:462
  161.7 4.8 %all-to-all-start.9 = ((bf16[8,128,256]{2,1,0:T(8,128)(2,1)}), bf16[8,128,256]{2,1,0:T(8,128)(2,1)S(1)}, u32[]{:S(2)}, u32[]{:S(2)}) async-start(bf16[8,128,256]{2,1,0:T(8,128)(2,1)} %bitcast.26), calls=%async_computation.9 | async-start | bytes 1048576 | tf_op jit(solution)/shard_map/all_to_all | solution.py:17
  167.4 1.7 collective-permute-start.2
  170.4 1.3 collective-permute-start.3
  171.7 4.3 %all-to-all-done.9.recv_ref = bf16[8,128,256]{2,1,0:T(8,128)(2,1)S(1)} async-done(((bf16[8,128,256]{2,1,0:T(8,128)(2,1)}), bf16[8,128,256]{2,1,0:T(8,128)(2,1)S(1)}, u32[]{:S(2)}, u32[]{:S(2)}) %all-to-all-start.9) | async-done | bytes 524320 | tf_op jit(solution)/shard_map/all_to_all | solution.py:17
  176.0 0.8 copy-done.7
  176.8 2.1 d_embed_kernel.1
  178.9 5.1 %all-to-all-start.10 = ((bf16[8,128,256]{2,1,0:T(8,128)(2,1)}), bf16[8,128,256]{2,1,0:T(8,128)(2,1)S(1)}, u32[]{:S(2)}, u32[]{:S(2)}) async-start(bf16[8,128,256]{2,1,0:T(8,128)(2,1)} %d_embed_kernel.1), calls=%async_computation.10 | async-start | bytes 1048576 | tf_op jit(solution)/shard_map/all_to_all | solution.py:17
  186.3 9.3 %slab_kernel.1 = (f32[1024,256]{1,0:T(8,128)}, f32[1024,256]{1,0:T(8,128)}, bf16[1024,256]{1,0:T(8,128)(2,1)}) custom-call(s32[9]{0:T(128)} %stack.39.order_ref.refs_0_, f32[16,128]{1,0:T(8,128)} %get-tuple-element.40.mean_ref, f32[16,128]{1,0:T(8,128)} %get-tuple-element.41.inv_ref.refs_4_, f32[16,128]{1,0:T(8,128)} %bitcast.29, f32[16,128]{1,0:T(8,128)} %bitcast.32, ...), custom_call_target="tpu_custom_call" | custom-call | tf_op jit(solution)/shard_map/slab_kernel/pallas_call | solution.py:497
  195.6 0.8 copy-done.6
  196.4 7.5 %shift_kernel.1 = (f32[1024,256]{1,0:T(8,128)}, f32[16,24,256]{2,1,0:T(8,128)}) custom-call(s32[9]{0:T(128)} %stack.39.order_ref.refs_0_, bf16[8,128,256]{2,1,0:T(8,128)(2,1)} %copy-done.6, bf16[2048,256]{1,0:T(8,128)(2,1)} %w2_ref.1, f32[1024,256]{1,0:T(8,128)} %get-tuple-element.42.normed_ref.refs_3_, f32[1024,256]{1,0:T(8,128)} %get-tuple-element.43.slope_ref, ...), custom_call_target="tpu_custom_call" | custom-call | tf_op jit(solution)/shard_map/shift_kernel/pallas_call | solution.py:510
  203.9 13.4 %all_to_all.81.refs_1_ = f32[16,24,256]{2,1,0:T(8,128)} all-to-all(f32[16,24,256]{2,1,0:T(8,128)} %get-tuple-element.46), channel_id=1, replica_groups=mesh['batch'=16,'proto'=8] {'batch'}, dimensions={0} | all-to-all | bytes 786432 | tf_op jit(solution)/shard_map/all_to_all | solution.py:17
  217.3 3.8 %all-to-all-start.14 = ((bf16[16,16,2048]{2,1,0:T(8,128)(2,1)}), bf16[16,16,2048]{2,1,0:T(8,128)(2,1)S(1)}, u32[]{:S(2)}, u32[]{:S(2)}) async-start(bf16[16,16,2048]{2,1,0:T(8,128)(2,1)} %bitcast.18), calls=%async_computation.14 | async-start | bytes 2097152 | tf_op jit(solution)/shard_map/all_to_all | solution.py:17
  221.2 8.8 %first_kernel.1 = (bf16[128,16,256]{2,1,0:T(8,128)(2,1)}, f32[8,8,256]{2,1,0:T(8,128)}, f32[16,256]{1,0:T(8,128)}) custom-call(s32[9]{0:T(128)} %stack.39.order_ref.refs_0_, f32[16,24,256]{2,1,0:T(8,128)} %all_to_all.81.refs_1_, f32[1024,256]{1,0:T(8,128)} %get-tuple-element.47.refs_2_, f32[1024,256]{1,0:T(8,128)} %get-tuple-element.42.normed_ref.refs_3_, ...), custom_call_target="tpu_custom_call" | custom-call | tf_op jit(solution)/shard_map/first_kernel/pallas_call | solution.py:532
  230.0 6.5 %all-to-all-done.14 = bf16[16,16,2048]{2,1,0:T(8,128)(2,1)S(1)} async-done(((bf16[16,16,2048]{2,1,0:T(8,128)(2,1)}), bf16[16,16,2048]{2,1,0:T(8,128)(2,1)S(1)}, u32[]{:S(2)}, u32[]{:S(2)}) %all-to-all-start.14) | async-done | bytes 1048608 | tf_op jit(solution)/shard_map/all_to_all | solution.py:17
  236.5 12.7 %all_to_all.82 = f32[8,8,256]{2,1,0:T(8,128)S(1)} all-to-all(f32[8,8,256]{2,1,0:T(8,128)} %get-tuple-element.50), channel_id=1, replica_groups=mesh['batch'=16,'proto'=8] {'proto'}, dimensions={0} | all-to-all | bytes 131072 | tf_op jit(solution)/shard_map/all_to_all | solution.py:17
  249.2 4.2 %all-to-all-start.12 = ((bf16[128,16,256]{2,1,0:T(8,128)(2,1)}), bf16[128,16,256]{2,1,0:T(8,128)(2,1)S(1)}, u32[]{:S(2)}, u32[]{:S(2)}) async-start(bf16[128,16,256]{2,1,0:T(8,128)(2,1)} %get-tuple-element.48), calls=%async_computation.12 | async-start | bytes 2097152 | tf_op jit(solution)/shard_map/all_to_all | solution.py:17
  253.4 5.6 %collective-permute-start.9 = (f32[16,256]{1,0:T(8,128)}, f32[16,256]{1,0:T(8,128)S(1)}, u32[]{:S(2)}, u32[]{:S(2)}) collective-permute-start(f32[16,256]{1,0:T(8,128)} %get-tuple-element.49), channel_id=1, source_target_pairs={{0,0},{1,16},{2,32},{3,48},{4,64},{5,80},{6,96},{7,112},{8,1},{9,1... | collective-permute-start | bytes 49160 | tf_op jit(solution)/shard_map/ppermute | solution.py:562
  259.0 0.8 convert_reduce_fusion
  263.3 9.5 %all-to-all-done.12 = bf16[128,16,256]{2,1,0:T(8,128)(2,1)S(1)} async-done(((bf16[128,16,256]{2,1,0:T(8,128)(2,1)}), bf16[128,16,256]{2,1,0:T(8,128)(2,1)S(1)}, u32[]{:S(2)}, u32[]{:S(2)}) %all-to-all-start.12) | async-done | bytes 1048608 | tf_op jit(solution)/shard_map/all_to_all | solution.py:17
  272.8 1.0 copy-done.3
  273.7 5.0 %tail_kernel.1 = f32[16,2048]{1,0:T(8,128)} custom-call(bf16[16,8,16,256]{3,2,1,0:T(8,128)(2,1)} %bitcast.25), custom_call_target="tpu_custom_call" | custom-call | tf_op jit(solution)/shard_map/tail_kernel/pallas_call | solution.py:554
  (50 shorter events, 8.9 us)
Async XLA Ops:
  8.8 37.2 %copy-start.2 = (bf16[2048,256]{1,0:T(8,128)(2,1)S(1)}, bf16[2048,256]{1,0:T(8,128)(2,1)}, u32[]{:S(2)}) copy-start(bf16[2048,256]{1,0:T(8,128)(2,1)} %raw_ref.1) | copy-start | bytes 3145732
  41.7 13.6 %all-to-all-start.2 = ((bf16[8,128,256]{2,1,0:T(8,128)(2,1)}), bf16[8,128,256]{2,1,0:T(8,128)(2,1)S(1)}, u32[]{:S(2)}, u32[]{:S(2)}) async-start(bf16[8,128,256]{2,1,0:T(8,128)(2,1)} %get-tuple-element.31), calls=%async_computation.2 | async-start | bytes 1048576 | tf_op jit(solution)/shard_map/all_to_all | solution.py:17
  55.4 0.8 copy-start
  102.7 22.3 %copy-start.1 = (bf16[128,2048]{1,0:T(8,128)(2,1)S(1)}, bf16[128,2048]{1,0:T(8,128)(2,1)}, u32[]{:S(2)}) copy-start(bf16[128,2048]{1,0:T(8,128)(2,1)} %refs_6_.1) | copy-start | bytes 1572868
  117.3 24.3 %copy-start.13 = (s32[1024]{0:T(1024)S(1)}, s32[1024]{0:T(1024)}, u32[]{:S(2)}) copy-start(s32[1024]{0:T(1024)} %param.13) | copy-start | bytes 12292
  121.5 10.3 %all-to-all-start.7 = ((f32[16,16,128]{2,1,0:T(8,128)}), f32[16,16,128]{2,1,0:T(8,128)S(1)}, u32[]{:S(2)}, u32[]{:S(2)}) async-start(f32[16,16,128]{2,1,0:T(8,128)} %col_kernel.3), calls=%async_computation.7 | async-start | bytes 262144 | tf_op jit(solution)/shard_map/all_to_all | solution.py:17
  125.0 44.1 %collective-permute-start = (bf16[128,2048]{1,0:T(8,128)(2,1)S(1)}, bf16[128,2048]{1,0:T(8,128)(2,1)S(1)}, u32[]{:S(2)}, u32[]{:S(2)}) collective-permute-start(bf16[128,2048]{1,0:T(8,128)(2,1)S(1)} %copy-done.1), channel_id=1, source_target_pairs={{2,0},{3,1},{4,2},{5,3},{6,4},{7,5},{0,6},{1,7},{10,8},{11,9},{12,... | collective-permute-start | bytes 1572872 | tf_op jit(solution)/shard_map/ppermute | solution.py:357
  125.9 40.7 %collective-permute-start.1 = (bf16[128,2048]{1,0:T(8,128)(2,1)S(1)}, bf16[128,2048]{1,0:T(8,128)(2,1)S(1)}, u32[]{:S(2)}, u32[]{:S(2)}) collective-permute-start(bf16[128,2048]{1,0:T(8,128)(2,1)S(1)} %copy-done.1), channel_id=1, source_target_pairs={{0,2},{1,3},{2,4},{3,5},{4,6},{5,7},{6,0},{7,1},{8,10},{9,11},{10,... | collective-permute-start | bytes 1572872 | tf_op jit(solution)/shard_map/ppermute | solution.py:357
  131.8 0.7 copy-start.10
  136.5 10.3 %all-to-all-start.8 = ((f32[8,8,128]{2,1,0:T(8,128)}), f32[8,8,128]{2,1,0:T(8,128)S(1)}, u32[]{:S(2)}, u32[]{:S(2)}) async-start(f32[8,8,128]{2,1,0:T(8,128)} %row_kernel.5), calls=%async_computation.8 | async-start | bytes 65536 | tf_op jit(solution)/shard_map/all_to_all | solution.py:17
  146.8 0.6 copy-start.12
  161.7 14.2 %all-to-all-start.9 = ((bf16[8,128,256]{2,1,0:T(8,128)(2,1)}), bf16[8,128,256]{2,1,0:T(8,128)(2,1)S(1)}, u32[]{:S(2)}, u32[]{:S(2)}) async-start(bf16[8,128,256]{2,1,0:T(8,128)(2,1)} %bitcast.26), calls=%async_computation.9 | async-start | bytes 1048576 | tf_op jit(solution)/shard_map/all_to_all | solution.py:17
  166.6 18.7 %collective-permute-start.4 = (bf16[128,2048]{1,0:T(8,128)(2,1)S(1)}, bf16[128,2048]{1,0:T(8,128)(2,1)S(1)}, u32[]{:S(2)}, u32[]{:S(2)}) collective-permute-start(bf16[128,2048]{1,0:T(8,128)(2,1)S(1)} %copy-done.1), channel_id=1, source_target_pairs={{0,1},{1,0},{2,3},{3,2},{4,5},{5,4},{6,7},{7,6},{8,9},{9,8},{10,11... | collective-permute-start | bytes 1572872 | tf_op jit(solution)/shard_map/ppermute | solution.py:357
  166.6 19.6 %copy-start.5 = (bf16[128,2048]{1,0:T(8,128)(2,1)}, bf16[128,2048]{1,0:T(8,128)(2,1)S(1)}, u32[]{:S(2)}) copy-start(bf16[128,2048]{1,0:T(8,128)(2,1)S(1)} %collective-permute-done.1.rest_2_.refs_8_) | copy-start | bytes 1572868
  167.4 16.7 %collective-permute-start.2 = (bf16[64,2048]{1,0:T(8,128)(2,1)}, bf16[64,2048]{1,0:T(8,128)(2,1)S(1)}, u32[]{:S(2)}, u32[]{:S(2)}) collective-permute-start(bf16[64,2048]{1,0:T(8,128)(2,1)} %slice.24), channel_id=1, source_target_pairs={{0,2},{1,3},{2,4},{3,5},{4,6},{5,7},{6,0},{7,1},{8,10},{9,11},{10,... | collective-permute-start | bytes 786440 | tf_op jit(solution)/shard_map/ppermute | solution.py:357
  169.1 17.1 %copy-start.4 = (bf16[128,2048]{1,0:T(8,128)(2,1)}, bf16[128,2048]{1,0:T(8,128)(2,1)S(1)}, u32[]{:S(2)}) copy-start(bf16[128,2048]{1,0:T(8,128)(2,1)S(1)} %collective-permute-done.rest_1_.refs_7_) | copy-start | bytes 1572868
  169.1 16.2 %collective-permute-start.5 = (bf16[128,2048]{1,0:T(8,128)(2,1)S(1)}, bf16[128,2048]{1,0:T(8,128)(2,1)S(1)}, u32[]{:S(2)}, u32[]{:S(2)}) collective-permute-start(bf16[128,2048]{1,0:T(8,128)(2,1)S(1)} %collective-permute-done.rest_1_.refs_7_), channel_id=1, source_target_pairs={{0,1},{1,0},{2,3},{3,2},{4,5},{5,4},{6,7},{7,6},{8,9},{9,8},{10,11... | collective-permute-start | bytes 1572872 | tf_op jit(solution)/shard_map/ppermute | solution.py:357
  169.5 15.8 %collective-permute-start.6 = (bf16[128,2048]{1,0:T(8,128)(2,1)S(1)}, bf16[128,2048]{1,0:T(8,128)(2,1)}, u32[]{:S(2)}, u32[]{:S(2)}) collective-permute-start(bf16[128,2048]{1,0:T(8,128)(2,1)S(1)} %collective-permute-done.1.rest_2_.refs_8_), channel_id=1, source_target_pairs={{0,1},{1,0},{2,3},{3,2},{4,5},{5,4},{6,7},{7,6},{8,9},{9,8},{10,11... | collective-permute-start | bytes 1572872 | tf_op jit(solution)/shard_map/ppermute | solution.py:357
  170.4 13.9 %collective-permute-start.3 = (bf16[64,2048]{1,0:T(8,128)(2,1)}, bf16[64,2048]{1,0:T(8,128)(2,1)}, u32[]{:S(2)}, u32[]{:S(2)}) collective-permute-start(bf16[64,2048]{1,0:T(8,128)(2,1)} %slice.25), channel_id=1, source_target_pairs={{2,0},{3,1},{4,2},{5,3},{6,4},{7,5},{0,6},{1,7},{10,8},{11,9},{12,... | collective-permute-start | bytes 786440 | tf_op jit(solution)/shard_map/ppermute | solution.py:357
  176.0 0.8 copy-start.7
  178.9 16.6 %all-to-all-start.10 = ((bf16[8,128,256]{2,1,0:T(8,128)(2,1)}), bf16[8,128,256]{2,1,0:T(8,128)(2,1)S(1)}, u32[]{:S(2)}, u32[]{:S(2)}) async-start(bf16[8,128,256]{2,1,0:T(8,128)(2,1)} %d_embed_kernel.1), calls=%async_computation.10 | async-start | bytes 1048576 | tf_op jit(solution)/shard_map/all_to_all | solution.py:17
  184.0 2.1 copy-start.11
  184.1 1.7 collective-permute-start.7
  184.3 1.9 collective-permute-start.8
  185.3 0.9 copy-start.8
  185.3 1.0 copy-start.9
  195.6 0.8 copy-start.6
  217.3 19.2 %all-to-all-start.14 = ((bf16[16,16,2048]{2,1,0:T(8,128)(2,1)}), bf16[16,16,2048]{2,1,0:T(8,128)(2,1)S(1)}, u32[]{:S(2)}, u32[]{:S(2)}) async-start(bf16[16,16,2048]{2,1,0:T(8,128)(2,1)} %bitcast.18), calls=%async_computation.14 | async-start | bytes 2097152 | tf_op jit(solution)/shard_map/all_to_all | solution.py:17
  249.2 23.6 %all-to-all-start.12 = ((bf16[128,16,256]{2,1,0:T(8,128)(2,1)}), bf16[128,16,256]{2,1,0:T(8,128)(2,1)S(1)}, u32[]{:S(2)}, u32[]{:S(2)}) async-start(bf16[128,16,256]{2,1,0:T(8,128)(2,1)} %get-tuple-element.48), calls=%async_computation.12 | async-start | bytes 2097152 | tf_op jit(solution)/shard_map/all_to_all | solution.py:17
  253.4 6.7 %collective-permute-start.9 = (f32[16,256]{1,0:T(8,128)}, f32[16,256]{1,0:T(8,128)S(1)}, u32[]{:S(2)}, u32[]{:S(2)}) collective-permute-start(f32[16,256]{1,0:T(8,128)} %get-tuple-element.49), channel_id=1, source_target_pairs={{0,0},{1,16},{2,32},{3,48},{4,64},{5,80},{6,96},{7,112},{8,1},{9,1... | collective-permute-start | bytes 49160 | tf_op jit(solution)/shard_map/ppermute | solution.py:562
  272.8 1.0 copy-start.3

commit v3 on v2

v3 whole, which is shorter than its diff:
```python
import jax
import jax.numpy as jnp
from jax import lax
from jax.experimental import pallas as pl
from jax.experimental.pallas import tpu as pltpu
from jax.sharding import PartitionSpec as P


ITERS = 3
BF = jnp.bfloat16
F32 = jnp.float32
LANES = 128
TILE = 256
LOG2_E = 1.4426950408889634
PARAMS = pltpu.CompilerParams(vmem_limit_bytes=24 * 1024 * 1024)


def deal(x, axis):
    return lax.all_to_all(x, axis, 0, 0, tiled=True)


def tdot(a, b, a_dim, b_dim):
    return lax.dot_general(a, b, (((a_dim,), (b_dim,)), ((), ())), preferred_element_type=F32)


def fold_rows(v):
    return jnp.sum(v.reshape(v.shape[0] // 8, 8, LANES), axis=0)


def as_column(row):
    return jnp.broadcast_to(row, (LANES, LANES)).T


def lane(j):
    return slice(j * LANES, (j + 1) * LANES)


def whole(shape):
    return pl.BlockSpec(shape, lambda i, *_: (0,) * len(shape))


def rows_of(rows, width):
    return pl.BlockSpec((rows, width), lambda i, *_: (i, 0))


def cols_of(rows, width):
    return pl.BlockSpec((rows, width), lambda i, *_: (0, i))


def pre_kernel(features_ref, w_hbm, pre_ref, msg_ref, stat_ref, w_buf, sems):
    pieces = w_buf.shape[0]
    copies = [
        pltpu.make_async_copy(w_hbm.at[:, k * TILE : (k + 1) * TILE], w_buf.at[k], sems.at[k]) for k in range(pieces)
    ]
    for copy in copies:
        copy.start()
    chunks = TILE // LANES
    half = stat_ref.shape[0] // 2
    for k in range(pieces):
        copies[k].wait()
        pre = jnp.dot(features_ref[...], w_buf[k], preferred_element_type=F32)
        pre_ref[:, k * TILE : (k + 1) * TILE] = pre
        for h in range(chunks):
            at = k * chunks + h
            part = pre[:, lane(h)]
            stat_ref[at : at + 1, :] = jnp.sum(part, axis=0, keepdims=True)
            stat_ref[half + at : half + at + 1, :] = jnp.sum(part * part, axis=0, keepdims=True)
    msg_ref[...] = jnp.broadcast_to(stat_ref[...][None], msg_ref.shape)


def relay_kernel(recv_ref, msg_ref):
    msg_ref[...] = jnp.broadcast_to(jnp.sum(recv_ref[...], axis=0, keepdims=True), msg_ref.shape)


def embed_kernel(
    total_rows, pre_hbm, recv_ref, gain_ref, bias_ref, w2_hbm, unit_ref, scale_ref, mean_ref, inv_ref, msg_ref, hid_ref,
    pre_ref, w2_ref, sems,
):
    pre_copy = pltpu.make_async_copy(pre_hbm, pre_ref, sems.at[0])
    w2_copy = pltpu.make_async_copy(w2_hbm, w2_ref, sems.at[1])
    pre_copy.start()
    w2_copy.start()
    stats = jnp.sum(recv_ref[...], axis=0)
    half = stats.shape[0] // 2
    mean = stats[:half] / total_rows
    inv = lax.rsqrt(stats[half:] / total_rows - mean * mean + 1e-05)
    mean_ref[...] = mean
    inv_ref[...] = inv
    pre_copy.wait()
    for j in range(half):
        normed = (pre_ref[:, lane(j)] - mean[j : j + 1]) * inv[j : j + 1]
        hid_ref[:, lane(j)] = jax.nn.gelu(normed * gain_ref[j : j + 1, :] + bias_ref[j : j + 1, :]).astype(BF)
    w2_copy.wait()
    embed = jnp.dot(hid_ref[...], w2_ref[...], preferred_element_type=F32)
    scale = lax.rsqrt(jnp.sum(embed * embed, axis=1, keepdims=True) + 1e-06)
    unit = embed * scale
    unit_ref[...] = unit
    scale_ref[...] = jnp.broadcast_to(scale, scale_ref.shape)
    msg_ref[...] = jnp.broadcast_to(unit.astype(BF)[None], msg_ref.shape)


def proto_kernel(raw_ref, raw_t_ref, proto_ref, proto_t_ref):
    raw = raw_ref[...].astype(F32)
    proto_ref[...] = (raw * lax.rsqrt(jnp.sum(raw * raw, axis=1, keepdims=True) + 1e-06)).astype(BF)
    raw_t = raw_t_ref[...].astype(F32)
    proto_t_ref[...] = (raw_t * lax.rsqrt(jnp.sum(raw_t * raw_t, axis=0, keepdims=True) + 1e-06)).astype(BF)


def score_kernel(embed_ref, proto_t_hbm, kern_ref, msg_ref, soft_ref, acc_ref, proto_t_ref, sems):
    step = pl.program_id(0)
    rows = embed_ref.shape[0]
    cols = proto_t_ref.shape[1]

    def copy(j):
        span = slice(j * TILE, (j + 1) * TILE)
        return pltpu.make_async_copy(proto_t_hbm.at[:, span], proto_t_ref.at[:, span], sems.at[j])

    @pl.when(step == 0)
    def _():
        for j in range(cols // TILE):
            copy(j).start()
        acc_ref[...] = jnp.zeros_like(acc_ref)
        for j in range(cols // TILE):
            copy(j).wait()

    soft = [None] * (rows // LANES)
    for j in range(cols // TILE):
        span = slice(j * TILE, (j + 1) * TILE)
        scores = jnp.dot(embed_ref[...], proto_t_ref[:, span], preferred_element_type=F32)
        tempered = jnp.exp2(scores * (10.0 * LOG2_E))
        kern = tempered * tempered
        kern_ref[:, span] = kern.astype(BF)
        for h in range(TILE // LANES):
            at = (j * (TILE // LANES) + h) * 8
            acc_ref[at : at + 8, :] += fold_rows(kern[:, lane(h)])
        for b in range(rows // LANES):
            part = tempered[b * LANES : (b + 1) * LANES]
            part = part[:, :LANES] + part[:, LANES:]
            soft[b] = part if soft[b] is None else soft[b] + part
    for b in range(rows // LANES):
        soft_ref[pl.ds(step * (rows // LANES) + b, 1), :] = jnp.sum(soft[b].T, axis=0, keepdims=True)

    @pl.when(step == pl.num_programs(0) - 1)
    def _():
        total = jnp.sum(acc_ref[...].reshape(cols // LANES, 8, LANES), axis=1)
        msg_ref[...] = jnp.broadcast_to(total[None], msg_ref.shape)


def row_kernel(recv_ref, kern_ref, *rest):
    soft_ref = rest[0] if len(rest) == 3 else None
    msg_ref, scale_ref = rest[-2:]
    step = pl.program_id(0)
    rows = kern_ref.shape[0]
    copies = msg_ref.shape[0]

    @pl.when(step == 0)
    def _():
        scale_ref[...] = 1.0 / jnp.sum(recv_ref[...], axis=0)
        if soft_ref is not None:
            half = soft_ref.shape[0]
            msg_ref[:, half:, :] = jnp.broadcast_to(soft_ref[...][None], (copies, half, LANES))

    for b in range(rows // LANES):
        acc = None
        for j in range(scale_ref.shape[0]):
            part = kern_ref[b * LANES : (b + 1) * LANES, lane(j)].astype(F32) * scale_ref[j : j + 1, :]
            acc = part if acc is None else acc + part
        row = jnp.sum(acc.T, axis=0, keepdims=True)
        msg_ref[:, pl.ds(step * (rows // LANES) + b, 1), :] = jnp.broadcast_to(row[None], (copies, 1, LANES))


def col_kernel(recv_ref, kern_ref, msg_ref, acc_ref, scale_ref):
    step = pl.program_id(0)
    rows, cols = kern_ref.shape

    @pl.when(step == 0)
    def _():
        acc_ref[...] = jnp.zeros_like(acc_ref)
        scale_ref[...] = 1.0 / jnp.sum(recv_ref[:, : scale_ref.shape[0], :], axis=0)

    for b in range(rows // LANES):
        scale = as_column(scale_ref[pl.ds(step * (rows // LANES) + b, 1), :])
        for j in range(cols // LANES):
            part = kern_ref[b * LANES : (b + 1) * LANES, lane(j)].astype(F32) * scale
            acc_ref[j * 8 : (j + 1) * 8, :] += fold_rows(part)

    @pl.when(step == pl.num_programs(0) - 1)
    def _():
        total = jnp.sum(acc_ref[...].reshape(cols // LANES, 8, LANES), axis=1)
        msg_ref[...] = jnp.broadcast_to(total[None], msg_ref.shape)


def final_kernel(
    embed_ref, pair_ref, proto_t_ref, proto_ref, raw_t_ref, recv_col_ref, recv_row_ref, recv_soft_ref,
    d_unit_ref, term_ref, loss_ref, grad_ref, mate_ref, loss_acc_ref, col_ref, row_ref, soft_ref,
):
    step = pl.program_id(0)
    rows = d_unit_ref.shape[0]
    cols = proto_t_ref.shape[1]
    bands = row_ref.shape[0]
    chunks = TILE // LANES

    @pl.when(step == 0)
    def _():
        loss_acc_ref[...] = jnp.zeros_like(loss_acc_ref)
        col_ref[...] = 10.0 / jnp.sum(recv_col_ref[...], axis=0)
        row_ref[...] = 1.0 / jnp.sum(recv_row_ref[:, :bands, :], axis=0)
        soft_ref[...] = jnp.sum(recv_soft_ref[:, bands:, :], axis=0)
        loss_acc_ref[8:16, :] = jnp.log(soft_ref[...])

    base = step * (rows // LANES)
    here = pl.ds(pl.multiple_of(step * rows, rows), rows)
    spot = lax.broadcasted_iota(jnp.int32, (LANES, LANES), 1)
    scales = []
    for b in range(rows // LANES):
        pair = as_column(pair_ref[pl.ds(base + b, 1), :]).astype(jnp.int32)
        found = jnp.zeros((LANES, LANES), F32)
        for q in range(bands):
            hot = spot + q * LANES == pair
            found += jnp.where(hot, row_ref[q : q + 1, :], 0.0)
            mate_ref[b * LANES : (b + 1) * LANES, lane(q)] = jnp.where(hot, 1.0, 0.0).astype(BF)
        scales.append(jnp.broadcast_to(jnp.sum(found, axis=1, keepdims=True), (LANES, LANES)))
    mate_scale = jnp.concatenate(scales, axis=0)
    mate = jnp.dot(mate_ref[...], embed_ref[...], preferred_element_type=F32).astype(BF)
    soft = jnp.concatenate([as_column(soft_ref[pl.ds(base + b, 1), :]) for b in range(rows // LANES)], axis=0)
    inv_soft = 10.0 / soft
    loss_acc = jnp.zeros((8, LANES), F32)
    for j in range(cols // TILE):
        span = slice(j * TILE, (j + 1) * TILE)
        scores = jnp.dot(embed_ref[here, :], proto_t_ref[:, span], preferred_element_type=F32)
        mates = jnp.dot(mate, proto_t_ref[:, span], preferred_element_type=F32)
        for h in range(chunks):
            at = j * chunks + h
            target = jnp.exp2(mates[:, lane(h)] * (20.0 * LOG2_E)) * mate_scale * col_ref[at : at + 1, :]
            score = scores[:, lane(h)]
            loss_acc += fold_rows(target * score)
            grad_ref[here, lane(at)] = (jnp.exp2(score * (10.0 * LOG2_E)) * inv_soft - target).astype(BF)
    d_unit_ref[...] = jnp.dot(grad_ref[here, :], proto_ref[...], preferred_element_type=F32).astype(BF)
    loss_acc_ref[0:8, :] += loss_acc

    @pl.when(step == pl.num_programs(0) - 1)
    def _():
        embed_t = embed_ref[...].T
        for j in range(cols // TILE):
            span = slice(j * TILE, (j + 1) * TILE)
            raw = raw_t_ref[:, span].astype(F32)
            scale = lax.rsqrt(jnp.sum(raw * raw, axis=0, keepdims=True) + 1e-06)
            unit = raw * scale
            acc = jnp.dot(embed_t, grad_ref[:, span], preferred_element_type=F32)
            term_ref[:, span] = ((acc - unit * jnp.sum(unit * acc, axis=0, keepdims=True)) * scale).astype(BF)
        loss_ref[...] = loss_acc_ref[...]


def d_embed_kernel(recv_ref, unit_ref, scale_ref, msg_ref):
    d_unit = jnp.sum(recv_ref[...].astype(F32), axis=0)
    unit = unit_ref[...]
    d_embed = (d_unit - unit * jnp.sum(unit * d_unit, axis=1, keepdims=True)) * scale_ref[:, :1]
    msg_ref[...] = jnp.broadcast_to(d_embed.astype(BF)[None], msg_ref.shape)


def start_parts(parts, buf_ref, sems):
    copies = []
    at = 0
    for k, part in enumerate(parts):
        height = part.shape[0]
        copies.append(pltpu.make_async_copy(part, buf_ref.at[at : at + height], sems.at[k]))
        at += height
    for copy in copies:
        copy.start()
    return copies


def slab_kernel(order_ref, mean_ref, inv_ref, gain_ref, bias_ref, w_hbm, *rest):
    parts = rest[:-6]
    normed_ref, slope_ref, hid_ref, buf_ref, w_ref, sems = rest[-6:]
    rows, slab = normed_ref.shape
    at = pl.ds(pl.multiple_of(order_ref[0] * slab, slab), slab)
    w_copy = pltpu.make_async_copy(w_hbm.at[:, at], w_ref, sems.at[len(parts)])
    w_copy.start()
    copies = start_parts(parts, buf_ref, sems)
    w_copy.wait()
    chunks = slab // LANES
    ones = jnp.ones((LANES, LANES), F32)
    for g in range(2):
        for copy in copies[g * len(parts) // 2 : (g + 1) * len(parts) // 2]:
            copy.wait()
        start = g * rows // 2
        pre = jnp.dot(buf_ref[start : start + rows // 2, :], w_ref[...], preferred_element_type=F32)
        for h in range(chunks):
            at = pl.ds(order_ref[0] * chunks + h, 1)
            mean, inv, gain, bias = mean_ref[at, :], inv_ref[at, :], gain_ref[at, :], bias_ref[at, :]
            for b in range(rows // 2 // LANES):
                band = slice(start + b * LANES, start + (b + 1) * LANES)
                normed = (pre[b * LANES : (b + 1) * LANES, lane(h)] - mean) * inv
                hidden, back = jax.vjp(jax.nn.gelu, normed * gain + bias)
                normed_ref[band, lane(h)] = normed
                slope_ref[band, lane(h)] = back(ones)[0]
                hid_ref[band, lane(h)] = hidden.astype(BF)


def shift_kernel(
    order_ref, d_embed_ref, w2_ref, normed_ref, slope_ref, hid_ref, loss_ref, shift_ref, msg_ref, sum_ref
):
    n_blocks, own, _ = d_embed_ref.shape
    sum_ref[...] = jnp.zeros_like(sum_ref)
    gains = biases = second = None
    for k in range(0, n_blocks, 2):
        d_embed = jnp.concatenate([d_embed_ref[order_ref[k + 1]], d_embed_ref[order_ref[k + 2]]], axis=0)
        band = slice(k * own, (k + 2) * own)
        d_shift = tdot(d_embed, w2_ref[...], 1, 1) * slope_ref[band, :]
        shift_ref[band, :] = d_shift
        gain = jnp.sum(d_shift * normed_ref[band, :], axis=0, keepdims=True)
        bias = jnp.sum(d_shift, axis=0, keepdims=True)
        part = tdot(hid_ref[band, :], d_embed, 0, 0)
        gains = gain if gains is None else gains + gain
        biases = bias if biases is None else biases + bias
        second = part if second is None else second + part
    sum_ref[0:1, :] = gains
    sum_ref[1:2, :] = biases
    hits = jnp.sum(loss_ref[0:8, :], axis=0, keepdims=True)
    logs = jnp.sum(loss_ref[8:16, :], axis=0, keepdims=True)
    sum_ref[2:3, :] = jnp.concatenate([hits, logs], axis=1)
    n, height, slab = msg_ref.shape
    msg_ref[:, :8, :] = jnp.broadcast_to(sum_ref[...][None], (n, 8, slab))
    msg_ref[:, 8:, :] = second.reshape(n, height - 8, slab)


def first_kernel(total_rows, order_ref, recv_ref, shift_ref, normed_ref, inv_ref, gain_ref, *rest):
    parts = rest[:-6]
    out_ref, sums_ref, second_ref, d_pre_ref, buf_ref, sems = rest[-6:]
    copies = start_parts(parts, buf_ref, sems)
    got = jnp.sum(recv_ref[...], axis=0)
    sums_ref[...] = got[:8]
    second_ref[...] = got[8:]
    chunks = d_pre_ref.shape[1] // LANES
    for h in range(chunks):
        at = pl.ds(order_ref[0] * chunks + h, 1)
        factor = gain_ref[at, :] * inv_ref[at, :]
        gain_mean = got[0:1, lane(h)] / total_rows
        bias_mean = got[1:2, lane(h)] / total_rows
        for b in range(d_pre_ref.shape[0] // LANES):
            band = slice(b * LANES, (b + 1) * LANES)
            d_pre = factor * (shift_ref[band, lane(h)] - bias_mean - normed_ref[band, lane(h)] * gain_mean)
            d_pre_ref[band, lane(h)] = d_pre.astype(BF)
    for copy in copies:
        copy.wait()
    _, share, slab = out_ref.shape
    group = TILE // share
    for j in range(buf_ref.shape[1] // TILE):
        grad = tdot(buf_ref[:, j * TILE : (j + 1) * TILE], d_pre_ref[...], 0, 0)
        out_ref[j * group : (j + 1) * group] = grad.astype(BF).reshape(group, share, slab)


def tail_kernel(recv_ref, out_ref):
    n_batch, n_proto, _, slab = recv_ref.shape
    for p in range(n_proto):
        acc = recv_ref[0, p].astype(F32)
        for b in range(1, n_batch):
            acc += recv_ref[b, p].astype(F32)
        out_ref[:, p * slab : (p + 1) * slab] = acc


def sums_kernel(total_rows, order_ref, *rest):
    shown = rest[:-3]
    gain_ref, bias_ref, loss_ref = rest[-3:]
    n_proto = len(shown)
    hits = jnp.zeros((1, LANES), F32)
    for d, ref in enumerate(shown):
        at = pl.ds(lax.rem(order_ref[0] + n_proto - d, n_proto), 1)
        gain_ref[at, :] = ref[0:1, :]
        bias_ref[at, :] = ref[1:2, :]
        hits += ref[2:3, :LANES]
    loss = jnp.sum(shown[0][2:3, LANES:] - hits, axis=1, keepdims=True) / total_rows
    loss_ref[...] = jnp.broadcast_to(loss, loss_ref.shape)


def shape(dims, kind=F32):
    return jax.ShapeDtypeStruct(dims, kind)


def step_of_device(features, w_first, bn_gain, bn_bias, w_second, prototypes, pair):
    n_batch = lax.axis_size("batch")
    n_proto = lax.axis_size("proto")
    own, d_in = features.shape
    d_hid, width = w_second.shape
    cols = prototypes.shape[0]
    total_rows = own * n_batch * n_proto
    rows = own * n_proto
    part = lax.axis_index("proto")
    slab = d_hid // n_proto
    col_bands = cols // LANES
    row_bands = rows // LANES
    hid_bands = d_hid // LANES
    steps = rows // TILE
    gain = bn_gain.reshape(hid_bands, LANES)
    bias = bn_bias.reshape(hid_bands, LANES)

    def hop(x, moves):
        return lax.ppermute(x, "proto", moves)

    ring = n_proto // 2
    right = [(i * 2 + c, (i + 1) % ring * 2 + c) for i in range(ring) for c in range(2)]
    left = [(t, s) for s, t in right]
    swap = [(i, i ^ 1) for i in range(n_proto)]
    from_left = hop(features, right)
    from_right = hop(features, left)
    across = lax.shift_right_logical(part, 1)
    order = jnp.stack(
        [part]
        + [
            (lax.bitwise_and(across + d, ring - 1) * 2 + lax.bitwise_and(part, 1)) ^ o
            for o in range(2)
            for d in (0, 1, 3, 2)
        ]
    ).astype(jnp.int32)
    mate_row = (pair - lax.axis_index("batch") * rows).astype(F32).reshape(row_bands, LANES)

    raw_t = prototypes.T
    proto_bf, proto_t = pl.pallas_call(
        proto_kernel,
        grid=(cols // 512,),
        in_specs=[rows_of(512, width), cols_of(width, 512)],
        out_specs=[rows_of(512, width), cols_of(width, 512)],
        out_shape=[shape((cols, width), BF), shape((width, cols), BF)],
        name="proto_kernel",
    )(prototypes, raw_t)

    anywhere = pl.BlockSpec(memory_space=pl.ANY)
    pre, msg = pl.pallas_call(
        pre_kernel,
        in_specs=[pl.BlockSpec(features.shape, lambda: (0, 0)), anywhere],
        out_shape=[shape((own, d_hid)), shape((n_batch, 2 * hid_bands, LANES))],
        scratch_shapes=[
            pltpu.VMEM((2 * hid_bands, LANES), F32),
            pltpu.VMEM((d_hid // TILE, d_in, TILE), BF),
            pltpu.SemaphoreType.DMA((d_hid // TILE,)),
        ],
        name="pre_kernel",
    )(features, w_first)
    near_left, near_right, _ = lax.optimization_barrier((from_left, from_right, pre))
    far_top = hop(near_left[: own // 2], right)
    far_low = hop(near_right[own // 2 :], left)
    got = deal(msg, "batch")
    got, far_top, far_low, mate_row, order, proto_bf, proto_t, raw_t = lax.optimization_barrier(
        (got, far_top, far_low, mate_row, order, proto_bf, proto_t, raw_t)
    )
    mine = [features, from_right, from_left, far_top, far_low]
    parts = mine + [hop(piece, swap) for piece in mine]
    msg = pl.pallas_call(
        relay_kernel, out_shape=shape((n_proto, 2 * hid_bands, LANES)), compiler_params=PARAMS, name="relay_kernel"
    )(got)
    unit_embed, embed_scale, mean, inv, msg = pl.pallas_call(
        lambda *refs: embed_kernel(total_rows, *refs),
        in_specs=[anywhere, pl.BlockSpec((n_proto, 2 * hid_bands, LANES), lambda: (0, 0, 0))]
        + [pl.BlockSpec((hid_bands, LANES), lambda: (0, 0))] * 2
        + [anywhere],
        out_shape=[
            shape((own, width)),
            shape((own, LANES)),
            shape((hid_bands, LANES)),
            shape((hid_bands, LANES)),
            shape((n_proto, own, width), BF),
        ],
        scratch_shapes=[
            pltpu.VMEM((own, d_hid), BF),
            pltpu.VMEM((own, d_hid), F32),
            pltpu.VMEM((d_hid, width), BF),
            pltpu.SemaphoreType.DMA((2,)),
        ],
        name="embed_kernel",
    )(pre, deal(msg, "proto"), gain, bias, w_second)
    stat_spec = whole((hid_bands, LANES))
    normed, slope, hid = pl.pallas_call(
        slab_kernel,
        grid_spec=pltpu.PrefetchScalarGridSpec(
            num_scalar_prefetch=1,
            grid=(1,),
            in_specs=[stat_spec] * 4 + [anywhere] * (1 + len(parts)),
            out_specs=[whole((rows, slab))] * 3,
            scratch_shapes=[
                pltpu.VMEM((rows, d_in), BF),
                pltpu.VMEM((d_in, slab), BF),
                pltpu.SemaphoreType.DMA((len(parts) + 1,)),
            ],
        ),
        out_shape=[shape((rows, slab)), shape((rows, slab)), shape((rows, slab), BF)],
        name="slab_kernel",
    )(order, mean, inv, gain, bias, w_first, *parts)
    block_embed, normed, slope, hid = lax.optimization_barrier((deal(msg, "proto"), normed, slope, hid))
    block_embed = block_embed.reshape(rows, width)

    kern, col_msg, soft = pl.pallas_call(
        score_kernel,
        grid=(steps,),
        in_specs=[rows_of(TILE, width), anywhere],
        out_specs=[rows_of(TILE, cols), whole((n_batch, col_bands, LANES)), whole((row_bands, LANES))],
        out_shape=[shape((rows, cols), BF), shape((n_batch, col_bands, LANES)), shape((row_bands, LANES))],
        scratch_shapes=[
            pltpu.VMEM((col_bands * 8, LANES), F32),
            pltpu.VMEM((width, cols), BF),
            pltpu.SemaphoreType.DMA((cols // TILE,)),
        ],
        compiler_params=PARAMS,
        name="score_kernel",
    )(block_embed, proto_t)

    def row_pass(recv, extra):
        height = row_bands * (2 if extra else 1)
        return pl.pallas_call(
            row_kernel,
            grid=(steps,),
            in_specs=[whole((n_batch, col_bands, LANES)), rows_of(TILE, cols)]
            + [whole((row_bands, LANES)) for _ in extra],
            out_specs=whole((n_proto, height, LANES)),
            out_shape=shape((n_proto, height, LANES)),
            scratch_shapes=[pltpu.VMEM((col_bands, LANES), F32)],
            compiler_params=PARAMS,
        name="row_kernel",
        )(recv, kern, *extra)

    def col_pass(recv):
        return pl.pallas_call(
            col_kernel,
            grid=(steps,),
            in_specs=[whole(recv.shape), rows_of(TILE, cols)],
            out_specs=whole((n_batch, col_bands, LANES)),
            out_shape=shape((n_batch, col_bands, LANES)),
            scratch_shapes=[pltpu.VMEM((col_bands * 8, LANES), F32), pltpu.VMEM((row_bands, LANES), F32)],
            compiler_params=PARAMS,
        name="col_kernel",
        )(recv, kern)

    recv_soft = None
    for step in range(ITERS):
        recv_col = deal(col_msg, "batch")
        recv_row = deal(row_pass(recv_col, () if step else (soft,)), "proto")
        recv_soft = recv_row if recv_soft is None else recv_soft
        if step + 1 < ITERS:
            col_msg = col_pass(recv_row)

    d_unit, term, loss_tile = pl.pallas_call(
        final_kernel,
        grid=(steps,),
        in_specs=[
            whole((rows, width)),
            whole((row_bands, LANES)),
            whole((width, cols)),
            whole((cols, width)),
            whole((width, cols)),
            whole(recv_col.shape),
            whole(recv_row.shape),
            whole(recv_soft.shape),
        ],
        out_specs=[rows_of(TILE, width), whole((width, cols)), whole((16, LANES))],
        out_shape=[shape((rows, width), BF), shape((width, cols), BF), shape((16, LANES))],
        scratch_shapes=[
            pltpu.VMEM((rows, cols), BF),
            pltpu.VMEM((TILE, rows), BF),
            pltpu.VMEM((16, LANES), F32),
            pltpu.VMEM((col_bands, LANES), F32),
            pltpu.VMEM((row_bands, LANES), F32),
            pltpu.VMEM((row_bands, LANES), F32),
        ],
        compiler_params=PARAMS,
        name="final_kernel",
    )(block_embed, mate_row, proto_t, proto_bf, raw_t, recv_col, recv_row, recv_soft)

    side = 4
    b_of = [(b // side, b % side) for b in range(n_batch)]

    def shifted(axis, d):
        return [
            (b, (y + d) % side * side + z if axis == 0 else y * side + (z + d) % side) for b, (y, z) in enumerate(b_of)
        ]

    place = lax.axis_index("batch")
    spots = (lax.shift_right_logical(place, 2), lax.bitwise_and(place, side - 1))

    def scatter_sum(x, axis):
        pieces = x.reshape((side, -1) + x.shape[1:])
        kept = [lax.dynamic_index_in_dim(pieces, spots[axis], 0, keepdims=False)]
        for d in range(1, side):
            piece = lax.dynamic_index_in_dim(
                pieces, lax.bitwise_and(spots[axis] + d, side - 1), 0, keepdims=False
            )
            kept.append(lax.ppermute(piece, "batch", shifted(axis, d)))
        return kept

    def total(kept):
        acc = kept[0].astype(F32)
        for piece in kept[1:]:
            acc += piece.astype(F32)
        return acc

    first_stage = scatter_sum(term, 0)
    d_unit = deal(d_unit.reshape(n_proto, own, width), "proto")
    d_unit, *first_stage = lax.optimization_barrier((d_unit, *first_stage))
    d_embed = pl.pallas_call(
        d_embed_kernel, out_shape=shape((n_proto, own, width), BF), name="d_embed_kernel"
    )(d_unit, unit_embed, embed_scale)
    second_stage = scatter_sum(total(first_stage).astype(BF), 1)
    d_embed = deal(d_embed, "proto")
    d_embed, *second_stage = lax.optimization_barrier((d_embed, *second_stage))
    grad_proto = total(second_stage).T

    shift, msg = pl.pallas_call(
        shift_kernel,
        grid_spec=pltpu.PrefetchScalarGridSpec(
            num_scalar_prefetch=1,
            grid=(1,),
            in_specs=[
                whole((n_proto, own, width)),
                pl.BlockSpec((slab, width), lambda i, s: (s[0], 0)),
                whole((rows, slab)),
                whole((rows, slab)),
                whole((rows, slab)),
                whole((16, LANES)),
            ],
            out_specs=[whole((rows, slab)), whole((n_batch, 8 + slab // n_batch, width))],
            scratch_shapes=[pltpu.VMEM((8, slab), F32)],
        ),
        out_shape=[shape((rows, slab)), shape((n_batch, 8 + slab // n_batch, width))],
        name="shift_kernel",
    )(order, d_embed, w_second, normed, slope, hid, loss_tile)
    recv = deal(msg, "batch")

    share = d_in // (n_batch * n_proto)
    first, sums, second = pl.pallas_call(
        lambda *refs: first_kernel(total_rows, *refs),
        grid_spec=pltpu.PrefetchScalarGridSpec(
            num_scalar_prefetch=1,
            grid=(1,),
            in_specs=[whole(recv.shape), whole((rows, slab)), whole((rows, slab)), stat_spec, stat_spec]
            + [anywhere] * len(parts),
            out_specs=[
                whole((n_batch * n_proto, share, slab)),
                whole((8, slab)),
                whole((slab // n_batch, width)),
            ],
            scratch_shapes=[
                pltpu.VMEM((rows, slab), BF),
                pltpu.VMEM((rows, d_in), BF),
                pltpu.SemaphoreType.DMA((len(parts),)),
            ],
        ),
        out_shape=[
            shape((n_batch * n_proto, share, slab), BF),
            shape((8, slab)),
            shape((slab // n_batch, width)),
        ],
        compiler_params=PARAMS,
        name="first_kernel",
    )(order, recv, shift, normed, inv, gain, *parts)

    first = deal(first, ("batch", "proto")).reshape(n_batch, n_proto, share, slab)
    grad_first = pl.pallas_call(
        tail_kernel, out_shape=shape((share, d_hid)), compiler_params=PARAMS, name="tail_kernel"
    )(first)
    grad_second = lax.ppermute(
        second,
        ("batch", "proto"),
        [(b * n_proto + p, p * n_batch + b) for b in range(n_batch) for p in range(n_proto)],
    )
    shown = [sums] + [
        hop(sums, [(i, (i + d) % n_proto) for i in range(n_proto)]) for d in range(1, n_proto)
    ]
    grad_gain, grad_bias, loss = pl.pallas_call(
        lambda *refs: sums_kernel(total_rows, *refs),
        in_specs=[pl.BlockSpec(memory_space=pltpu.SMEM)] + [pl.BlockSpec((8, slab), lambda: (0, 0))] * n_proto,
        out_shape=[shape((n_proto, slab)), shape((n_proto, slab)), shape((1, LANES))],
        compiler_params=PARAMS,
        name="sums_kernel",
    )(order, *shown)
    grad_gain = grad_gain.reshape(-1)
    grad_bias = grad_bias.reshape(-1)
    loss = loss[0, 0]
    return (grad_first, grad_second, grad_gain, grad_bias, grad_proto, loss)


def solution(mesh):
    return jax.shard_map(
        step_of_device,
        mesh=mesh,
        in_specs=(P(("batch", "proto"), None), P(), P(), P(), P(), P("proto", None), P("batch")),
        out_specs=(
            P(("batch", "proto"), None),
            P(("batch", "proto"), None),
            P(),
            P(),
            P("proto", "batch"),
            P(),
        ),
        check_vma=False,
    )
```

time: 283 us -> 255 us (0.901)
  Pallas kernels: 94.6 us -> 53.7 us
  blocking collectives: 97.2 us -> 64.8 us
  starting transfers between devices: 42.1 us -> 73.1 us
  local copies, waits for them, and re-layouts: 10.7 us -> 19.5 us
  waiting for transfers between devices: 30.7 us -> 36.5 us
    all_to_all x8 -> x6, blocking collectives: 97.2 us -> 64.8 us  [deal(): return lax.all_to_all(x, axis, 0, 0, tiled=True)]
    pallas_call x12, Pallas kernels: 74.1 us -> 47.8 us  [the longest x1 9.61 us: step_of_device(): pl.pallas_call(final_kernel, grid=(steps,), in_specs=[whole((rows, width)...]
    all_to_all x7, waiting for transfers between devices: 29.5 us -> 11.3 us  [deal(): return lax.all_to_all(x, axis, 0, 0, tiled=True)]
    ppermute x1 -> x7, waiting for transfers between devices: 0.35 us -> 15.5 us  [the longest x6 15.5 us: scatter_sum(): kept.append(lax.ppermute(piece, 'batch', shifted(axis, d)))]
    ppermute x9 -> x16, starting transfers between devices: 5.67 us -> 18.5 us  [hop(): return lax.ppermute(x, 'proto', moves)]
    all_to_all x7, starting transfers between devices: 30.9 us -> 43.3 us  [deal(): return lax.all_to_all(x, axis, 0, 0, tiled=True)]
    ppermute x9 -> x16, waiting for transfers between devices: 0.88 us -> 9.66 us  [hop(): return lax.ppermute(x, 'proto', moves)]
    pallas_call x3, Pallas kernels: 12.3 us -> 3.57 us  [row_pass(): pl.pallas_call(row_kernel, grid=(steps,), in_specs=[whole((n_batch, col_b...]
  transfers between devices with their start and end apart: 17 -> 30, of which waited for: 8 -> 14; matrix products, arithmetic and copies ran while one was open for 3% -> 4% of each run, Pallas kernels for 17% -> 9%
where the time goes in v3:
time: 255 us; the launch traced here: 252 us
  starting transfers between devices  73.1 us (29%)
  blocking collectives  64.8 us (25%)
  Pallas kernels  53.7 us (21%)
  waiting for transfers between devices  36.5 us (14%)
  local copies, waits for them, and re-layouts  19.5 us (8%)
  other arithmetic  3.51 us (1%)
    all_to_all x6, blocking collectives, deal(): return lax.all_to_all(x, axis, 0, 0, tiled=True)  64.8 us
    all_to_all x7, starting transfers between devices, deal(): return lax.all_to_all(x, axis, 0, 0, tiled=True)  43.3 us
    ppermute x16, starting transfers between devices, hop(): return lax.ppermute(x, 'proto', moves)  18.5 us
    ppermute x6, waiting for transfers between devices, scatter_sum(): kept.append(lax.ppermute(piece, 'batch', shifted(axis, d)))  15.5 us
    unnamed x70, local copies, waits for them, and re-layouts  15 us
    all_to_all x7, waiting for transfers between devices, deal(): return lax.all_to_all(x, axis, 0, 0, tiled=True)  11.3 us
    ppermute x16, waiting for transfers between devices, hop(): return lax.ppermute(x, 'proto', moves)  9.66 us
    pallas_call x1, Pallas kernels, step_of_device(): pl.pallas_call(final_kernel, grid=(steps,), in_specs=[whole((rows, width)...  9.61 us
  transfers between devices with their start and end apart: 30, of which 14 were waited for; matrix products, arithmetic and copies ran while one was open for 4% of the time, Pallas kernels for 9%

profile of v3, /device:TPU:1, one launch (start us, length us, event | category | flops | bytes accessed | tf_op | source)
XLA Modules:
  0.0 252.2 jit_solution(6157936309642922906)
XLA Ops:
  0.7 2.1 collective-permute-start
  2.8 1.4 collective-permute-start.1
  4.1 6.9 %pre_kernel.1 = (f32[128,2048]{1,0:T(8,128)}, f32[16,32,128]{2,1,0:T(8,128)}) custom-call(bf16[128,2048]{1,0:T(8,128)(2,1)} %refs_6_.1, bf16[2048,2048]{1,0:T(8,128)(2,1)} %w_hbm.3), custom_call_target="tpu_custom_call" | custom-call | tf_op jit(solution)/shard_map/pre_kernel/pallas_call | solution.py:429
  11.0 4.5 %collective-permute-done.rest_2_.refs_8_ = bf16[128,2048]{1,0:T(8,128)(2,1)S(1)} collective-permute-done((bf16[128,2048]{1,0:T(8,128)(2,1)}, bf16[128,2048]{1,0:T(8,128)(2,1)S(1)}, u32[]{:S(2)}, u32[]{:S(2)}) %collective-permute-start) | collective-permute-done | bytes 524320 | tf_op jit(solution)/shard_map/ppermute | solution.py:399
  16.3 1.2 collective-permute-start.2
  18.2 1.5 collective-permute-start.3
  19.7 8.0 %all-to-all-start = ((f32[16,32,128]{2,1,0:T(8,128)}), f32[16,32,128]{2,1,0:T(8,128)S(1)}, u32[]{:S(2)}, u32[]{:S(2)}) async-start(f32[16,32,128]{2,1,0:T(8,128)} %get-tuple-element.56), calls=%async_computation | async-start | bytes 524288 | tf_op jit(solution)/shard_map/all_to_all | solution.py:19
  27.8 1.4 copy.13
  29.2 4.1 %proto_kernel.1 = (bf16[2048,256]{1,0:T(8,128)(2,1)}, bf16[256,2048]{1,0:T(8,128)(2,1)}) custom-call(bf16[2048,256]{1,0:T(8,128)(2,1)} %raw_ref.1, bf16[256,2048]{1,0:T(8,128)(2,1)} %bitcast.43), custom_call_target="tpu_custom_call" | custom-call | tf_op jit(solution)/shard_map/proto_kernel/pallas_call | solution.py:419
  35.9 6.7 %all-to-all-start.1 = ((f32[8,32,128]{2,1,0:T(8,128)}), f32[8,32,128]{2,1,0:T(8,128)S(1)}, u32[]{:S(2)}, u32[]{:S(2)}) async-start(f32[8,32,128]{2,1,0:T(8,128)} %relay_kernel.1), calls=%async_computation.1 | async-start | bytes 262144 | tf_op jit(solution)/shard_map/all_to_all | solution.py:19
  43.3 4.6 %all-to-all-done.1.refs_1_ = f32[8,32,128]{2,1,0:T(8,128)S(1)} async-done(((f32[8,32,128]{2,1,0:T(8,128)}), f32[8,32,128]{2,1,0:T(8,128)S(1)}, u32[]{:S(2)}, u32[]{:S(2)}) %all-to-all-start.1) | async-done | bytes 131104 | tf_op jit(solution)/shard_map/all_to_all | solution.py:19
  48.6 3.9 %embed_kernel.1 = (f32[128,256]{1,0:T(8,128)}, f32[128,128]{1,0:T(8,128)}, f32[16,128]{1,0:T(8,128)}, f32[16,128]{1,0:T(8,128)}, bf16[8,128,256]{2,1,0:T(8,128)(2,1)}) custom-call(f32[128,2048]{1,0:T(8,128)} %get-tuple-element.57.refs_0_, f32[8,32,128]{2,1,0:T(8,128)} %copy-done.31, f32[16,128]{1,0:T(8,128)} %bitcast.50, f32[16,128]{1,0:T(8,128)} %bitcast.56, ...), custom_call_target="tpu_custom_call" | custom-call | tf_op jit(solution)/shard_map/embed_kernel/pallas_call | solution.py:452
  52.5 4.3 %all-to-all-start.2 = ((bf16[8,128,256]{2,1,0:T(8,128)(2,1)}), bf16[8,128,256]{2,1,0:T(8,128)(2,1)S(1)}, u32[]{:S(2)}, u32[]{:S(2)}) async-start(bf16[8,128,256]{2,1,0:T(8,128)(2,1)} %get-tuple-element.64), calls=%async_computation.2 | async-start | bytes 1048576 | tf_op jit(solution)/shard_map/all_to_all | solution.py:19
  59.8 7.9 %slab_kernel.1 = (f32[1024,256]{1,0:T(8,128)}, f32[1024,256]{1,0:T(8,128)}, bf16[1024,256]{1,0:T(8,128)(2,1)}) custom-call(s32[9]{0:T(128)} %stack.39.order_ref.refs_0_, f32[16,128]{1,0:T(8,128)} %get-tuple-element.65.mean_ref, f32[16,128]{1,0:T(8,128)} %get-tuple-element.66.inv_ref.refs_4_, f32[16,128]{1,0:T(8,128)} %bitcast.51, f32[16,128]{1,0:T(8,128)} %bitcast.57, ...), custom_call_target="tpu_custom_call" | custom-call | tf_op jit(solution)/shard_map/slab_kernel/pallas_call | solution.py:473
  67.7 2.9 %score_kernel.1 = (bf16[1024,2048]{1,0:T(8,128)(2,1)S(1)}, f32[16,16,128]{2,1,0:T(8,128)S(1)}, f32[8,128]{1,0:T(8,128)S(1)}) custom-call(bf16[1024,256]{1,0:T(8,128)(2,1)S(1)} %bitcast.45, bf16[256,2048]{1,0:T(8,128)(2,1)S(1)} %copy-done.3), custom_call_target="tpu_custom_call" | custom-call | tf_op jit(solution)/shard_map/score_kernel/pallas_call | solution.py:492
  70.6 11.8 %all_to_all.65.recv_ref = f32[16,16,128]{2,1,0:T(8,128)S(1)} all-to-all(f32[16,16,128]{2,1,0:T(8,128)S(1)} %get-tuple-element.77), channel_id=1, replica_groups=mesh['batch'=16,'proto'=8] {'batch'}, dimensions={0} | all-to-all | bytes 262144 | tf_op jit(solution)/shard_map/all_to_all | solution.py:19
  83.6 10.9 %all_to_all.66.recv_ref.recv_soft_ref = f32[8,16,128]{2,1,0:T(8,128)S(1)} all-to-all(f32[8,16,128]{2,1,0:T(8,128)S(1)} %row_kernel.3), channel_id=1, replica_groups=mesh['batch'=16,'proto'=8] {'proto'}, dimensions={0} | all-to-all | bytes 131072 | tf_op jit(solution)/shard_map/all_to_all | solution.py:19
  96.4 9.8 %all_to_all.67.recv_ref = f32[16,16,128]{2,1,0:T(8,128)S(1)} all-to-all(f32[16,16,128]{2,1,0:T(8,128)S(1)} %col_kernel.2), channel_id=1, replica_groups=mesh['batch'=16,'proto'=8] {'batch'}, dimensions={0} | all-to-all | bytes 262144 | tf_op jit(solution)/shard_map/all_to_all | solution.py:19
  107.4 9.2 %all_to_all.68.recv_ref = f32[8,8,128]{2,1,0:T(8,128)S(1)} all-to-all(f32[8,8,128]{2,1,0:T(8,128)S(1)} %row_kernel.4), channel_id=1, replica_groups=mesh['batch'=16,'proto'=8] {'proto'}, dimensions={0} | all-to-all | bytes 65536 | tf_op jit(solution)/shard_map/all_to_all | solution.py:19
  117.8 9.9 %all_to_all.69.recv_ref.recv_col_ref = f32[16,16,128]{2,1,0:T(8,128)S(1)} all-to-all(f32[16,16,128]{2,1,0:T(8,128)S(1)} %col_kernel.3), channel_id=1, replica_groups=mesh['batch'=16,'proto'=8] {'batch'}, dimensions={0} | all-to-all | bytes 262144 | tf_op jit(solution)/shard_map/all_to_all | solution.py:19
  129.6 6.0 %all-to-all-start.8 = ((f32[8,8,128]{2,1,0:T(8,128)}), f32[8,8,128]{2,1,0:T(8,128)}, u32[]{:S(2)}, u32[]{:S(2)}) async-start(f32[8,8,128]{2,1,0:T(8,128)} %copy-done.24), calls=%async_computation.8 | async-start | bytes 65536 | tf_op jit(solution)/shard_map/all_to_all | solution.py:19
  135.6 4.8 %all-to-all-done.8.recv_row_ref = f32[8,8,128]{2,1,0:T(8,128)} async-done(((f32[8,8,128]{2,1,0:T(8,128)}), f32[8,8,128]{2,1,0:T(8,128)}, u32[]{:S(2)}, u32[]{:S(2)}) %all-to-all-start.8) | async-done | bytes 32800 | tf_op jit(solution)/shard_map/all_to_all | solution.py:19
  140.4 1.2 copy-done.9
  143.2 9.6 %final_kernel.1 = (bf16[1024,256]{1,0:T(8,128)(2,1)S(1)}, bf16[256,2048]{1,0:T(8,128)(2,1)S(1)}, f32[16,128]{1,0:T(8,128)S(1)}) custom-call(bf16[1024,256]{1,0:T(8,128)(2,1)S(1)} %bitcast.46, f32[8,128]{1,0:T(8,128)S(1)} %copy-done.27, bf16[256,2048]{1,0:T(8,128)(2,1)S(1)} %copy-done.3, bf16[2048,256]{1,0:T(8,128)(2,1)S(1)} %copy-done.9, ...), custom_call_target="tpu_custom_call" | custom-call | tf_op jit(solution)/shard_map/final_kernel/pallas_call | solution.py:541
  155.2 4.9 %all-to-all-start.9 = ((bf16[8,128,256]{2,1,0:T(8,128)(2,1)}), bf16[8,128,256]{2,1,0:T(8,128)(2,1)}, u32[]{:S(2)}, u32[]{:S(2)}) async-start(bf16[8,128,256]{2,1,0:T(8,128)(2,1)} %bitcast.49), calls=%async_computation.9 | async-start | bytes 1048576 | tf_op jit(solution)/shard_map/all_to_all | solution.py:19
  160.1 2.3 dynamic-slice_bitcast_fusion
  162.6 1.9 collective-permute-start.10
  165.4 6.8 %collective-permute-done.9 = bf16[64,2048]{1,0:T(8,128)(2,1)} collective-permute-done((bf16[64,2048]{1,0:T(8,128)(2,1)}, bf16[64,2048]{1,0:T(8,128)(2,1)}, u32[]{:S(2)}, u32[]{:S(2)}) %collective-permute-start.9) | collective-permute-done | bytes 262176 | tf_op jit(solution)/shard_map/ppermute | solution.py:586
  172.2 4.5 %collective-permute-done.10 = bf16[64,2048]{1,0:T(8,128)(2,1)} collective-permute-done((bf16[64,2048]{1,0:T(8,128)(2,1)}, bf16[64,2048]{1,0:T(8,128)(2,1)}, u32[]{:S(2)}, u32[]{:S(2)}) %collective-permute-start.10) | collective-permute-done | bytes 262176 | tf_op jit(solution)/shard_map/ppermute | solution.py:586
  177.6 2.1 d_embed_kernel.1
  179.7 5.7 %all-to-all-start.10 = ((bf16[8,128,256]{2,1,0:T(8,128)(2,1)}), bf16[8,128,256]{2,1,0:T(8,128)(2,1)}, u32[]{:S(2)}, u32[]{:S(2)}) async-start(bf16[8,128,256]{2,1,0:T(8,128)(2,1)} %d_embed_kernel.1), calls=%async_computation.10 | async-start | bytes 1048576 | tf_op jit(solution)/shard_map/all_to_all | solution.py:19
  185.5 1.3 add_convert_fusion
  187.1 2.0 collective-permute-start.13
  190.2 2.1 collective-permute-done.12
  193.5 1.4 all-to-all-done.10.d_embed_ref
  194.9 4.2 %shift_kernel.1 = (f32[1024,256]{1,0:T(8,128)}, f32[16,24,256]{2,1,0:T(8,128)}) custom-call(s32[9]{0:T(128)} %stack.39.order_ref.refs_0_, bf16[8,128,256]{2,1,0:T(8,128)(2,1)} %all-to-all-done.10.d_embed_ref, bf16[2048,256]{1,0:T(8,128)(2,1)} %w2_ref.1, f32[1024,256]{1,0:T(8,128)} %get-tuple-element.90.normed_ref.refs_3_, ...), custom_call_target="tpu_custom_call" | custom-call | tf_op jit(solution)/shard_map/shift_kernel/pallas_call | solution.py:606
  199.1 13.1 %all_to_all.70.refs_1_ = f32[16,24,256]{2,1,0:T(8,128)S(1)} all-to-all(f32[16,24,256]{2,1,0:T(8,128)} %get-tuple-element.94), channel_id=1, replica_groups=mesh['batch'=16,'proto'=8] {'batch'}, dimensions={0} | all-to-all | bytes 786432 | tf_op jit(solution)/shard_map/all_to_all | solution.py:19
  214.5 3.4 %first_kernel.1 = (bf16[128,16,256]{2,1,0:T(8,128)(2,1)S(1)}, f32[8,256]{1,0:T(8,128)S(1)}, f32[16,256]{1,0:T(8,128)S(1)}) custom-call(s32[9]{0:T(128)S(1)} %copy-done.28, f32[16,24,256]{2,1,0:T(8,128)S(1)} %all_to_all.70.refs_1_, f32[1024,256]{1,0:T(8,128)S(1)} %copy-done.12, f32[1024,256]{1,0:T(8,128)S(1)} %copy-done.4, f32[16,128]{1,0:T(8,128)S(1)} %copy-done.26, ...), custom_call_target="tpu_custom_call" | custom-call | tf_op jit(solution)/shard_map/first_kernel/pallas_call | solution.py:628
  218.9 7.7 %all-to-all-start.12 = ((bf16[128,16,256]{2,1,0:T(8,128)(2,1)}), bf16[128,16,256]{2,1,0:T(8,128)(2,1)S(1)}, u32[]{:S(2)}, u32[]{:S(2)}) async-start(bf16[128,16,256]{2,1,0:T(8,128)(2,1)} %copy-done.11), calls=%async_computation.12 | async-start | bytes 2097152 | tf_op jit(solution)/shard_map/all_to_all | solution.py:19
  226.6 1.6 collective-permute-start.16
  229.5 1.6 collective-permute-start.18
  231.6 2.4 collective-permute-start.20
  234.1 2.7 %collective-permute-done.16.refs_2_ = f32[8,256]{1,0:T(8,128)S(1)} collective-permute-done((f32[8,256]{1,0:T(8,128)S(1)}, f32[8,256]{1,0:T(8,128)S(1)}, u32[]{:S(2)}, u32[]{:S(2)}) %collective-permute-start.16) | collective-permute-done | bytes 8224 | tf_op jit(solution)/shard_map/ppermute | solution.py:399
  236.8 1.9 collective-permute-start.21
  238.7 1.4 collective-permute-done.17.refs_3_
  240.1 1.8 collective-permute-start.22
  241.9 4.9 %collective-permute-start.15 = (f32[16,256]{1,0:T(8,128)S(1)}, f32[16,256]{1,0:T(8,128)S(1)}, u32[]{:S(2)}, u32[]{:S(2)}) collective-permute-start(f32[16,256]{1,0:T(8,128)S(1)} %get-tuple-element.97), channel_id=1, source_target_pairs={{0,0},{1,16},{2,32},{3,48},{4,64},{5,80},{6,96},{7,112},{8,1},{9,1... | collective-permute-start | bytes 49160 | tf_op jit(solution)/shard_map/ppermute | solution.py:659
  246.8 1.6 add_bitcast_fusion
  (113 shorter events, 33.1 us)
Async XLA Ops:
  0.6 42.0 %copy-start.1 = (bf16[128,2048]{1,0:T(8,128)(2,1)S(1)}, bf16[128,2048]{1,0:T(8,128)(2,1)}, u32[]{:S(2)}) copy-start(bf16[128,2048]{1,0:T(8,128)(2,1)} %refs_6_.1) | copy-start | bytes 1572868
  0.6 27.1 %copy-start.30 = (bf16[2048,256]{1,0:T(8,128)(2,1)S(1)}, bf16[2048,256]{1,0:T(8,128)(2,1)}, u32[]{:S(2)}) copy-start(bf16[2048,256]{1,0:T(8,128)(2,1)} %raw_ref.1) | copy-start | bytes 3145732
  0.7 33.3 %copy-start.32 = (s32[1024]{0:T(1024)S(1)}, s32[1024]{0:T(1024)}, u32[]{:S(2)}) copy-start(s32[1024]{0:T(1024)} %param.13) | copy-start | bytes 12292
  0.7 14.8 %collective-permute-start = (bf16[128,2048]{1,0:T(8,128)(2,1)}, bf16[128,2048]{1,0:T(8,128)(2,1)S(1)}, u32[]{:S(2)}, u32[]{:S(2)}) collective-permute-start(bf16[128,2048]{1,0:T(8,128)(2,1)} %refs_6_.1), channel_id=1, source_target_pairs={{0,2},{1,3},{2,4},{3,5},{4,6},{5,7},{6,0},{7,1},{8,10},{9,11},{10,... | collective-permute-start | bytes 1572872 | tf_op jit(solution)/shard_map/ppermute | solution.py:399
  2.8 12.8 %collective-permute-start.1 = (bf16[128,2048]{1,0:T(8,128)(2,1)}, bf16[128,2048]{1,0:T(8,128)(2,1)S(1)}, u32[]{:S(2)}, u32[]{:S(2)}) collective-permute-start(bf16[128,2048]{1,0:T(8,128)(2,1)} %refs_6_.1), channel_id=1, source_target_pairs={{2,0},{3,1},{4,2},{5,3},{6,4},{7,5},{0,6},{1,7},{10,8},{11,9},{12,... | collective-permute-start | bytes 1572872 | tf_op jit(solution)/shard_map/ppermute | solution.py:399
  15.5 44.3 %copy-start.5 = (bf16[128,2048]{1,0:T(8,128)(2,1)}, bf16[128,2048]{1,0:T(8,128)(2,1)S(1)}, u32[]{:S(2)}) copy-start(bf16[128,2048]{1,0:T(8,128)(2,1)S(1)} %collective-permute-done.rest_2_.refs_8_) | copy-start | bytes 1572868
  15.5 44.3 %copy-start.7 = (bf16[128,2048]{1,0:T(8,128)(2,1)}, bf16[128,2048]{1,0:T(8,128)(2,1)S(1)}, u32[]{:S(2)}) copy-start(bf16[128,2048]{1,0:T(8,128)(2,1)S(1)} %collective-permute-done.1.rest_1_.refs_7_) | copy-start | bytes 1572868
  16.3 18.9 %collective-permute-start.2 = (bf16[64,2048]{1,0:T(8,128)(2,1)}, bf16[64,2048]{1,0:T(8,128)(2,1)S(1)}, u32[]{:S(2)}, u32[]{:S(2)}) collective-permute-start(bf16[64,2048]{1,0:T(8,128)(2,1)} %slice.9), channel_id=1, source_target_pairs={{0,2},{1,3},{2,4},{3,5},{4,6},{5,7},{6,0},{7,1},{8,10},{9,11},{10,... | collective-permute-start | bytes 786440 | tf_op jit(solution)/shard_map/ppermute | solution.py:399
  18.2 16.9 %collective-permute-start.3 = (bf16[64,2048]{1,0:T(8,128)(2,1)}, bf16[64,2048]{1,0:T(8,128)(2,1)S(1)}, u32[]{:S(2)}, u32[]{:S(2)}) collective-permute-start(bf16[64,2048]{1,0:T(8,128)(2,1)} %slice.10), channel_id=1, source_target_pairs={{2,0},{3,1},{4,2},{5,3},{6,4},{7,5},{0,6},{1,7},{10,8},{11,9},{12,... | collective-permute-start | bytes 786440 | tf_op jit(solution)/shard_map/ppermute | solution.py:399
  19.7 15.5 %all-to-all-start = ((f32[16,32,128]{2,1,0:T(8,128)}), f32[16,32,128]{2,1,0:T(8,128)S(1)}, u32[]{:S(2)}, u32[]{:S(2)}) async-start(f32[16,32,128]{2,1,0:T(8,128)} %get-tuple-element.56), calls=%async_computation | async-start | bytes 524288 | tf_op jit(solution)/shard_map/all_to_all | solution.py:19
  33.3 34.4 %copy-start.3 = (bf16[256,2048]{1,0:T(8,128)(2,1)S(1)}, bf16[256,2048]{1,0:T(8,128)(2,1)}, u32[]{:S(2)}) copy-start(bf16[256,2048]{1,0:T(8,128)(2,1)} %get-tuple-element.74.proto_t_hbm.proto_t_ref) | copy-start | bytes 3145732
  35.2 24.6 %copy-start.13 = (bf16[64,2048]{1,0:T(8,128)(2,1)}, bf16[64,2048]{1,0:T(8,128)(2,1)S(1)}, u32[]{:S(2)}) copy-start(bf16[64,2048]{1,0:T(8,128)(2,1)S(1)} %collective-permute-done.2.rest_3_.refs_9_) | copy-start | bytes 786436
  35.9 12.0 %all-to-all-start.1 = ((f32[8,32,128]{2,1,0:T(8,128)}), f32[8,32,128]{2,1,0:T(8,128)S(1)}, u32[]{:S(2)}, u32[]{:S(2)}) async-start(f32[8,32,128]{2,1,0:T(8,128)} %relay_kernel.1), calls=%async_computation.1 | async-start | bytes 262144 | tf_op jit(solution)/shard_map/all_to_all | solution.py:19
  42.6 14.7 %collective-permute-start.4 = (bf16[128,2048]{1,0:T(8,128)(2,1)S(1)}, bf16[128,2048]{1,0:T(8,128)(2,1)}, u32[]{:S(2)}, u32[]{:S(2)}) collective-permute-start(bf16[128,2048]{1,0:T(8,128)(2,1)S(1)} %copy-done.1), channel_id=1, source_target_pairs={{0,1},{1,0},{2,3},{3,2},{4,5},{5,4},{6,7},{7,6},{8,9},{9,8},{10,11... | collective-permute-start | bytes 1572872 | tf_op jit(solution)/shard_map/ppermute | solution.py:399
  42.8 14.5 %collective-permute-start.5 = (bf16[128,2048]{1,0:T(8,128)(2,1)S(1)}, bf16[128,2048]{1,0:T(8,128)(2,1)}, u32[]{:S(2)}, u32[]{:S(2)}) collective-permute-start(bf16[128,2048]{1,0:T(8,128)(2,1)S(1)} %collective-permute-done.1.rest_1_.refs_7_), channel_id=1, source_target_pairs={{0,1},{1,0},{2,3},{3,2},{4,5},{5,4},{6,7},{7,6},{8,9},{9,8},{10,11... | collective-permute-start | bytes 1572872 | tf_op jit(solution)/shard_map/ppermute | solution.py:399
  43.2 14.2 %collective-permute-start.6 = (bf16[128,2048]{1,0:T(8,128)(2,1)S(1)}, bf16[128,2048]{1,0:T(8,128)(2,1)}, u32[]{:S(2)}, u32[]{:S(2)}) collective-permute-start(bf16[128,2048]{1,0:T(8,128)(2,1)S(1)} %collective-permute-done.rest_2_.refs_8_), channel_id=1, source_target_pairs={{0,1},{1,0},{2,3},{3,2},{4,5},{5,4},{6,7},{7,6},{8,9},{9,8},{10,11... | collective-permute-start | bytes 1572872 | tf_op jit(solution)/shard_map/ppermute | solution.py:399
  52.5 15.2 %all-to-all-start.2 = ((bf16[8,128,256]{2,1,0:T(8,128)(2,1)}), bf16[8,128,256]{2,1,0:T(8,128)(2,1)S(1)}, u32[]{:S(2)}, u32[]{:S(2)}) async-start(bf16[8,128,256]{2,1,0:T(8,128)(2,1)} %get-tuple-element.64), calls=%async_computation.2 | async-start | bytes 1048576 | tf_op jit(solution)/shard_map/all_to_all | solution.py:19
  56.8 1.5 collective-permute-start.7
  57.0 2.1 collective-permute-start.8
  94.5 45.9 %copy-start = (bf16[2048,256]{0,1:T(8,128)(2,1)S(1)}, bf16[2048,256]{0,1:T(8,128)(2,1)}, u32[]{:S(2)}) copy-start(bf16[2048,256]{0,1:T(8,128)(2,1)} %copy.13) | copy-start | bytes 3145732
  127.7 84.5 %copy-start.14 = (bf16[64,2048]{1,0:T(8,128)(2,1)S(1)}, bf16[64,2048]{1,0:T(8,128)(2,1)}, u32[]{:S(2)}) copy-start(bf16[64,2048]{1,0:T(8,128)(2,1)} %copy-done.13) | copy-start | bytes 786436
  127.7 84.5 %copy-start.25 = (f32[2048]{0:T(1024)S(1)}, f32[2048]{0:T(1024)}, u32[]{:S(2)}) copy-start(f32[2048]{0:T(1024)} %param.9) | copy-start | bytes 24580
  127.7 84.5 %copy-start.26 = (f32[16,128]{1,0:T(8,128)S(1)}, f32[16,128]{1,0:T(8,128)}, u32[]{:S(2)}) copy-start(f32[16,128]{1,0:T(8,128)} %get-tuple-element.66.inv_ref.refs_4_) | copy-start | bytes 24580
  129.6 82.7 %copy-start.2 = (bf16[128,2048]{1,0:T(8,128)(2,1)S(1)}, bf16[128,2048]{1,0:T(8,128)(2,1)}, u32[]{:S(2)}) copy-start(bf16[128,2048]{1,0:T(8,128)(2,1)} %refs_6_.1) | copy-start | bytes 1572868
  129.6 10.9 %all-to-all-start.8 = ((f32[8,8,128]{2,1,0:T(8,128)}), f32[8,8,128]{2,1,0:T(8,128)}, u32[]{:S(2)}, u32[]{:S(2)}) async-start(f32[8,8,128]{2,1,0:T(8,128)} %copy-done.24), calls=%async_computation.8 | async-start | bytes 65536 | tf_op jit(solution)/shard_map/all_to_all | solution.py:19
  155.2 57.1 %copy-start.4 = (f32[1024,256]{1,0:T(8,128)S(1)}, f32[1024,256]{1,0:T(8,128)}, u32[]{:S(2)}) copy-start(f32[1024,256]{1,0:T(8,128)} %get-tuple-element.90.normed_ref.refs_3_) | copy-start | bytes 3145732
  155.2 57.1 %copy-start.6 = (bf16[128,2048]{1,0:T(8,128)(2,1)S(1)}, bf16[128,2048]{1,0:T(8,128)(2,1)}, u32[]{:S(2)}) copy-start(bf16[128,2048]{1,0:T(8,128)(2,1)} %copy-done.5) | copy-start | bytes 1572868
  155.2 57.1 %copy-start.8 = (bf16[128,2048]{1,0:T(8,128)(2,1)S(1)}, bf16[128,2048]{1,0:T(8,128)(2,1)}, u32[]{:S(2)}) copy-start(bf16[128,2048]{1,0:T(8,128)(2,1)} %copy-done.7) | copy-start | bytes 1572868
  155.2 57.1 %copy-start.16 = (bf16[64,2048]{1,0:T(8,128)(2,1)S(1)}, bf16[64,2048]{1,0:T(8,128)(2,1)}, u32[]{:S(2)}) copy-start(bf16[64,2048]{1,0:T(8,128)(2,1)} %copy-done.15) | copy-start | bytes 786436
  155.2 57.1 %copy-start.18 = (bf16[64,2048]{1,0:T(8,128)(2,1)S(1)}, bf16[64,2048]{1,0:T(8,128)(2,1)}, u32[]{:S(2)}) copy-start(bf16[64,2048]{1,0:T(8,128)(2,1)} %copy-done.17) | copy-start | bytes 786436
  155.2 57.1 %copy-start.28 = (s32[9]{0:T(128)S(1)}, s32[9]{0:T(128)}, u32[]{:S(2)}) copy-start(s32[9]{0:T(128)} %stack.39.order_ref.refs_0_) | copy-start | bytes 112
  155.2 22.4 %all-to-all-start.9 = ((bf16[8,128,256]{2,1,0:T(8,128)(2,1)}), bf16[8,128,256]{2,1,0:T(8,128)(2,1)}, u32[]{:S(2)}, u32[]{:S(2)}) async-start(bf16[8,128,256]{2,1,0:T(8,128)(2,1)} %bitcast.49), calls=%async_computation.9 | async-start | bytes 1048576 | tf_op jit(solution)/shard_map/all_to_all | solution.py:19
  162.4 9.8 %collective-permute-start.9 = (bf16[64,2048]{1,0:T(8,128)(2,1)}, bf16[64,2048]{1,0:T(8,128)(2,1)}, u32[]{:S(2)}, u32[]{:S(2)}) collective-permute-start(bf16[64,2048]{1,0:T(8,128)(2,1)} %get-tuple-element.108), channel_id=1, source_target_pairs={{0,32},{8,40},{16,48},{24,56},{32,64},{40,72},{48,80},{56,88},{64,... | collective-permute-start | bytes 786440 | tf_op jit(solution)/shard_map/ppermute | solution.py:586
  162.6 14.1 %collective-permute-start.10 = (bf16[64,2048]{1,0:T(8,128)(2,1)}, bf16[64,2048]{1,0:T(8,128)(2,1)}, u32[]{:S(2)}, u32[]{:S(2)}) collective-permute-start(bf16[64,2048]{1,0:T(8,128)(2,1)} %get-tuple-element.107), channel_id=1, source_target_pairs={{0,64},{8,72},{16,80},{24,88},{32,96},{40,104},{48,112},{56,120},{... | collective-permute-start | bytes 786440 | tf_op jit(solution)/shard_map/ppermute | solution.py:586
  164.5 13.1 %collective-permute-start.11 = (bf16[64,2048]{1,0:T(8,128)(2,1)}, bf16[64,2048]{1,0:T(8,128)(2,1)}, u32[]{:S(2)}, u32[]{:S(2)}) collective-permute-start(bf16[64,2048]{1,0:T(8,128)(2,1)} %get-tuple-element.106), channel_id=1, source_target_pairs={{0,96},{8,104},{16,112},{24,120},{32,0},{40,8},{48,16},{56,24},{64... | collective-permute-start | bytes 786440 | tf_op jit(solution)/shard_map/ppermute | solution.py:586
  179.7 15.2 %all-to-all-start.10 = ((bf16[8,128,256]{2,1,0:T(8,128)(2,1)}), bf16[8,128,256]{2,1,0:T(8,128)(2,1)}, u32[]{:S(2)}, u32[]{:S(2)}) async-start(bf16[8,128,256]{2,1,0:T(8,128)(2,1)} %d_embed_kernel.1), calls=%async_computation.10 | async-start | bytes 1048576 | tf_op jit(solution)/shard_map/all_to_all | solution.py:19
  186.8 5.4 %collective-permute-start.12 = (bf16[16,2048]{1,0:T(8,128)(2,1)S(1)}, bf16[16,2048]{1,0:T(8,128)(2,1)}, u32[]{:S(2)}, u32[]{:S(2)}) collective-permute-start(bf16[16,2048]{1,0:T(8,128)(2,1)S(1)} %get-tuple-element.112), channel_id=1, source_target_pairs={{0,8},{8,16},{16,24},{24,0},{32,40},{40,48},{48,56},{56,32},{64,72... | collective-permute-start | bytes 196616 | tf_op jit(solution)/shard_map/ppermute | solution.py:586
  187.1 5.7 %collective-permute-start.13 = (bf16[16,2048]{1,0:T(8,128)(2,1)S(1)}, bf16[16,2048]{1,0:T(8,128)(2,1)}, u32[]{:S(2)}, u32[]{:S(2)}) collective-permute-start(bf16[16,2048]{1,0:T(8,128)(2,1)S(1)} %get-tuple-element.111), channel_id=1, source_target_pairs={{0,16},{8,24},{16,0},{24,8},{32,48},{40,56},{48,32},{56,40},{64,80... | collective-permute-start | bytes 196616 | tf_op jit(solution)/shard_map/ppermute | solution.py:586
  189.1 4.5 %collective-permute-start.14 = (bf16[16,2048]{1,0:T(8,128)(2,1)S(1)}, bf16[16,2048]{1,0:T(8,128)(2,1)}, u32[]{:S(2)}, u32[]{:S(2)}) collective-permute-start(bf16[16,2048]{1,0:T(8,128)(2,1)S(1)} %get-tuple-element.110), channel_id=1, source_target_pairs={{0,24},{8,0},{16,8},{24,16},{32,56},{40,32},{48,40},{56,48},{64,88... | collective-permute-start | bytes 196616 | tf_op jit(solution)/shard_map/ppermute | solution.py:586
  218.9 31.8 %all-to-all-start.12 = ((bf16[128,16,256]{2,1,0:T(8,128)(2,1)}), bf16[128,16,256]{2,1,0:T(8,128)(2,1)S(1)}, u32[]{:S(2)}, u32[]{:S(2)}) async-start(bf16[128,16,256]{2,1,0:T(8,128)(2,1)} %copy-done.11), calls=%async_computation.12 | async-start | bytes 2097152 | tf_op jit(solution)/shard_map/all_to_all | solution.py:19
  226.6 10.1 %collective-permute-start.16 = (f32[8,256]{1,0:T(8,128)S(1)}, f32[8,256]{1,0:T(8,128)S(1)}, u32[]{:S(2)}, u32[]{:S(2)}) collective-permute-start(f32[8,256]{1,0:T(8,128)S(1)} %get-tuple-element.98.refs_1_), channel_id=1, source_target_pairs={{0,1},{1,2},{2,3},{3,4},{4,5},{5,6},{6,7},{7,0},{8,9},{9,10},{10,1... | collective-permute-start | bytes 24584 | tf_op jit(solution)/shard_map/ppermute | solution.py:399
  228.3 11.8 %collective-permute-start.17 = (f32[8,256]{1,0:T(8,128)S(1)}, f32[8,256]{1,0:T(8,128)S(1)}, u32[]{:S(2)}, u32[]{:S(2)}) collective-permute-start(f32[8,256]{1,0:T(8,128)S(1)} %get-tuple-element.98.refs_1_), channel_id=1, source_target_pairs={{0,2},{1,3},{2,4},{3,5},{4,6},{5,7},{6,0},{7,1},{8,10},{9,11},{10,... | collective-permute-start | bytes 24584 | tf_op jit(solution)/shard_map/ppermute | solution.py:399
  229.5 12.4 %collective-permute-start.18 = (f32[8,256]{1,0:T(8,128)S(1)}, f32[8,256]{1,0:T(8,128)S(1)}, u32[]{:S(2)}, u32[]{:S(2)}) collective-permute-start(f32[8,256]{1,0:T(8,128)S(1)} %get-tuple-element.98.refs_1_), channel_id=1, source_target_pairs={{0,3},{1,4},{2,5},{3,6},{4,7},{5,0},{6,1},{7,2},{8,11},{9,12},{10,... | collective-permute-start | bytes 24584 | tf_op jit(solution)/shard_map/ppermute | solution.py:399
  231.1 17.3 %collective-permute-start.19 = (f32[8,256]{1,0:T(8,128)S(1)}, f32[8,256]{1,0:T(8,128)S(1)}, u32[]{:S(2)}, u32[]{:S(2)}) collective-permute-start(f32[8,256]{1,0:T(8,128)S(1)} %get-tuple-element.98.refs_1_), channel_id=1, source_target_pairs={{0,4},{1,5},{2,6},{3,7},{4,0},{5,1},{6,2},{7,3},{8,12},{9,13},{10,... | collective-permute-start | bytes 24584 | tf_op jit(solution)/shard_map/ppermute | solution.py:399
  231.6 16.8 %collective-permute-start.20 = (f32[8,256]{1,0:T(8,128)S(1)}, f32[8,256]{1,0:T(8,128)S(1)}, u32[]{:S(2)}, u32[]{:S(2)}) collective-permute-start(f32[8,256]{1,0:T(8,128)S(1)} %get-tuple-element.98.refs_1_), channel_id=1, source_target_pairs={{0,5},{1,6},{2,7},{3,0},{4,1},{5,2},{6,3},{7,4},{8,13},{9,14},{10,... | collective-permute-start | bytes 24584 | tf_op jit(solution)/shard_map/ppermute | solution.py:399
  236.8 11.6 %collective-permute-start.21 = (f32[8,256]{1,0:T(8,128)S(1)}, f32[8,256]{1,0:T(8,128)S(1)}, u32[]{:S(2)}, u32[]{:S(2)}) collective-permute-start(f32[8,256]{1,0:T(8,128)S(1)} %get-tuple-element.98.refs_1_), channel_id=1, source_target_pairs={{0,6},{1,7},{2,0},{3,1},{4,2},{5,3},{6,4},{7,5},{8,14},{9,15},{10,... | collective-permute-start | bytes 24584 | tf_op jit(solution)/shard_map/ppermute | solution.py:399
  240.1 8.3 %collective-permute-start.22 = (f32[8,256]{1,0:T(8,128)S(1)}, f32[8,256]{1,0:T(8,128)S(1)}, u32[]{:S(2)}, u32[]{:S(2)}) collective-permute-start(f32[8,256]{1,0:T(8,128)S(1)} %get-tuple-element.98.refs_1_), channel_id=1, source_target_pairs={{0,7},{1,0},{2,1},{3,2},{4,3},{5,4},{6,5},{7,6},{8,15},{9,8},{10,9... | collective-permute-start | bytes 24584 | tf_op jit(solution)/shard_map/ppermute | solution.py:399
  241.9 8.9 %collective-permute-start.15 = (f32[16,256]{1,0:T(8,128)S(1)}, f32[16,256]{1,0:T(8,128)S(1)}, u32[]{:S(2)}, u32[]{:S(2)}) collective-permute-start(f32[16,256]{1,0:T(8,128)S(1)} %get-tuple-element.97), channel_id=1, source_target_pairs={{0,0},{1,16},{2,32},{3,48},{4,64},{5,80},{6,96},{7,112},{8,1},{9,1... | collective-permute-start | bytes 49160 | tf_op jit(solution)/shard_map/ppermute | solution.py:659
  (15 other events, 29.0 us)

commit v4 on v3

--- a/solution.py
+++ b/solution.py
@@ -41,10 +41,6 @@
 
 def rows_of(rows, width):
     return pl.BlockSpec((rows, width), lambda i, *_: (i, 0))
-
-
-def cols_of(rows, width):
-    return pl.BlockSpec((rows, width), lambda i, *_: (0, i))
 
 
 def pre_kernel(features_ref, w_hbm, pre_ref, msg_ref, stat_ref, w_buf, sems):
@@ -99,11 +95,15 @@
     msg_ref[...] = jnp.broadcast_to(unit.astype(BF)[None], msg_ref.shape)
 
 
-def proto_kernel(raw_ref, raw_t_ref, proto_ref, proto_t_ref):
-    raw = raw_ref[...].astype(F32)
-    proto_ref[...] = (raw * lax.rsqrt(jnp.sum(raw * raw, axis=1, keepdims=True) + 1e-06)).astype(BF)
-    raw_t = raw_t_ref[...].astype(F32)
-    proto_t_ref[...] = (raw_t * lax.rsqrt(jnp.sum(raw_t * raw_t, axis=0, keepdims=True) + 1e-06)).astype(BF)
+def proto_kernel(raw_ref, proto_ref, proto_t_ref, raw_t_ref):
+    for k in range(raw_ref.shape[0] // TILE):
+        span = slice(k * TILE, (k + 1) * TILE)
+        raw_t = raw_ref[span, :].T
+        raw_t_ref[:, span] = raw_t
+        wide = raw_t.astype(F32)
+        unit = (wide * lax.rsqrt(jnp.sum(wide * wide, axis=0, keepdims=True) + 1e-06)).astype(BF)
+        proto_t_ref[:, span] = unit
+        proto_ref[span, :] = unit.T
 
 
 def score_kernel(embed_ref, proto_t_hbm, kern_ref, msg_ref, soft_ref, acc_ref, proto_t_ref, sems):
@@ -191,9 +191,12 @@
 
 
 def final_kernel(
-    embed_ref, pair_ref, proto_t_ref, proto_ref, raw_t_ref, recv_col_ref, recv_row_ref, recv_soft_ref,
-    d_unit_ref, term_ref, loss_ref, grad_ref, mate_ref, loss_acc_ref, col_ref, row_ref, soft_ref,
+    order_ref, embed_hbm, pair_ref, proto_t_hbm, proto_hbm, raw_t_hbm, recv_col_ref, recv_row_ref, recv_soft_ref,
+    d_unit_ref, piece0_ref, piece1_ref, piece2_ref, piece3_ref, loss_ref,
+    grad_ref, mate_ref, loss_acc_ref, col_ref, row_ref, soft_ref, embed_ref, proto_t_ref, proto_ref, raw_t_ref, term_ref, sems,
 ):
+    pairs = ((embed_hbm, embed_ref), (proto_t_hbm, proto_t_ref), (proto_hbm, proto_ref), (raw_t_hbm, raw_t_ref))
+    copies = [pltpu.make_async_copy(src, dst, sems.at[k]) for k, (src, dst) in enumerate(pairs)]
     step = pl.program_id(0)
     rows = d_unit_ref.shape[0]
     cols = proto_t_ref.shape[1]
@@ -202,11 +205,15 @@
 
     @pl.when(step == 0)
     def _():
+        for copy in copies:
+            copy.start()
         loss_acc_ref[...] = jnp.zeros_like(loss_acc_ref)
         col_ref[...] = 10.0 / jnp.sum(recv_col_ref[...], axis=0)
         row_ref[...] = 1.0 / jnp.sum(recv_row_ref[:, :bands, :], axis=0)
         soft_ref[...] = jnp.sum(recv_soft_ref[:, bands:, :], axis=0)
         loss_acc_ref[8:16, :] = jnp.log(soft_ref[...])
+        copies[0].wait()
+        copies[1].wait()
 
     base = step * (rows // LANES)
     here = pl.ds(pl.multiple_of(step * rows, rows), rows)
@@ -235,11 +242,17 @@
             score = scores[:, lane(h)]
             loss_acc += fold_rows(target * score)
             grad_ref[here, lane(at)] = (jnp.exp2(score * (10.0 * LOG2_E)) * inv_soft - target).astype(BF)
+
+    @pl.when(step == 0)
+    def _():
+        copies[2].wait()
+
     d_unit_ref[...] = jnp.dot(grad_ref[here, :], proto_ref[...], preferred_element_type=F32).astype(BF)
     loss_acc_ref[0:8, :] += loss_acc
 
     @pl.when(step == pl.num_programs(0) - 1)
     def _():
+        copies[3].wait()
         embed_t = embed_ref[...].T
         for j in range(cols // TILE):
             span = slice(j * TILE, (j + 1) * TILE)
@@ -248,6 +261,11 @@
             unit = raw * scale
             acc = jnp.dot(embed_t, grad_ref[:, span], preferred_element_type=F32)
             term_ref[:, span] = ((acc - unit * jnp.sum(unit * acc, axis=0, keepdims=True)) * scale).astype(BF)
+        pieces = (piece0_ref, piece1_ref, piece2_ref, piece3_ref)
+        for d, piece in enumerate(pieces):
+            height = piece.shape[0]
+            at = pl.multiple_of(lax.rem(order_ref[9] + d, len(pieces)) * height, height)
+            piece[...] = term_ref[pl.ds(at, height), :]
         loss_ref[...] = loss_acc_ref[...]
 
 
@@ -293,8 +311,8 @@
                 band = slice(start + b * LANES, start + (b + 1) * LANES)
                 normed = (pre[b * LANES : (b + 1) * LANES, lane(h)] - mean) * inv
                 hidden, back = jax.vjp(jax.nn.gelu, normed * gain + bias)
-                normed_ref[band, lane(h)] = normed
-                slope_ref[band, lane(h)] = back(ones)[0]
+                normed_ref[band, lane(h)] = normed.astype(BF)
+                slope_ref[band, lane(h)] = back(ones)[0].astype(BF)
                 hid_ref[band, lane(h)] = hidden.astype(BF)
 
 
@@ -307,31 +325,42 @@
     for k in range(0, n_blocks, 2):
         d_embed = jnp.concatenate([d_embed_ref[order_ref[k + 1]], d_embed_ref[order_ref[k + 2]]], axis=0)
         band = slice(k * own, (k + 2) * own)
-        d_shift = tdot(d_embed, w2_ref[...], 1, 1) * slope_ref[band, :]
+        d_shift = tdot(d_embed, w2_ref[...], 1, 1) * slope_ref[band, :].astype(F32)
         shift_ref[band, :] = d_shift
-        gain = jnp.sum(d_shift * normed_ref[band, :], axis=0, keepdims=True)
+        gain = jnp.sum(d_shift * normed_ref[band, :].astype(F32), axis=0, keepdims=True)
         bias = jnp.sum(d_shift, axis=0, keepdims=True)
         part = tdot(hid_ref[band, :], d_embed, 0, 0)
         gains = gain if gains is None else gains + gain
         biases = bias if biases is None else biases + bias
         second = part if second is None else second + part
+    hits = jnp.sum(loss_ref[0:8, :], axis=0, keepdims=True)
+    logs = jnp.sum(loss_ref[8:16, :], axis=0, keepdims=True)
     sum_ref[0:1, :] = gains
     sum_ref[1:2, :] = biases
-    hits = jnp.sum(loss_ref[0:8, :], axis=0, keepdims=True)
-    logs = jnp.sum(loss_ref[8:16, :], axis=0, keepdims=True)
     sum_ref[2:3, :] = jnp.concatenate([hits, logs], axis=1)
-    n, height, slab = msg_ref.shape
-    msg_ref[:, :8, :] = jnp.broadcast_to(sum_ref[...][None], (n, 8, slab))
-    msg_ref[:, 8:, :] = second.reshape(n, height - 8, slab)
+    n, _, slab = msg_ref.shape
+    share = slab // n
+    sums = sum_ref[...]
+    high = sums.astype(BF)
+    rest = sums - high.astype(F32)
+    mid = rest.astype(BF)
+    low = (rest - mid.astype(F32)).astype(BF)
+    row = lax.broadcasted_iota(jnp.int32, sums.shape, 0)
+    lower = jnp.where(row < 4, mid.astype(F32), pltpu.roll(low.astype(F32), 4, 0))
+    packed = jnp.concatenate([high.astype(F32), lower], axis=0).astype(BF)
+    msg_ref[:, :share, :] = jnp.broadcast_to(packed[None], (n, share, slab))
+    msg_ref[:, share:, :] = second.astype(BF).reshape(n, share, slab)
 
 
 def first_kernel(total_rows, order_ref, recv_ref, shift_ref, normed_ref, inv_ref, gain_ref, *rest):
     parts = rest[:-6]
     out_ref, sums_ref, second_ref, d_pre_ref, buf_ref, sems = rest[-6:]
     copies = start_parts(parts, buf_ref, sems)
-    got = jnp.sum(recv_ref[...], axis=0)
-    sums_ref[...] = got[:8]
-    second_ref[...] = got[8:]
+    share = second_ref.shape[0]
+    second_ref[...] = jnp.sum(recv_ref[:, share:, :].astype(F32), axis=0)
+    got = jnp.sum(recv_ref[:, :share, :].astype(F32), axis=0)
+    got = got[0:8] + (got[8:16] + pltpu.roll(got[8:16], 4, 0))
+    sums_ref[...] = got
     chunks = d_pre_ref.shape[1] // LANES
     for h in range(chunks):
         at = pl.ds(order_ref[0] * chunks + h, 1)
@@ -340,7 +369,7 @@
         bias_mean = got[1:2, lane(h)] / total_rows
         for b in range(d_pre_ref.shape[0] // LANES):
             band = slice(b * LANES, (b + 1) * LANES)
-            d_pre = factor * (shift_ref[band, lane(h)] - bias_mean - normed_ref[band, lane(h)] * gain_mean)
+            d_pre = factor * (shift_ref[band, lane(h)] - bias_mean - normed_ref[band, lane(h)].astype(F32) * gain_mean)
             d_pre_ref[band, lane(h)] = d_pre.astype(BF)
     for copy in copies:
         copy.wait()
@@ -358,6 +387,16 @@
         for b in range(1, n_batch):
             acc += recv_ref[b, p].astype(F32)
         out_ref[:, p * slab : (p + 1) * slab] = acc
+
+
+def stage_kernel(order_ref, in0_ref, in1_ref, in2_ref, in3_ref, out0_ref, out1_ref, out2_ref, out3_ref, sum_ref):
+    near = in0_ref[...].astype(F32) + in1_ref[...].astype(F32)
+    sum_ref[...] = (near + (in2_ref[...].astype(F32) + in3_ref[...].astype(F32))).astype(BF)
+    outs = (out0_ref, out1_ref, out2_ref, out3_ref)
+    for d, out in enumerate(outs):
+        height = out.shape[0]
+        at = pl.multiple_of(lax.rem(order_ref[10] + d, len(outs)) * height, height)
+        out[...] = sum_ref[pl.ds(at, height), :]
 
 
 def sums_kernel(total_rows, order_ref, *rest):
@@ -405,6 +444,8 @@
     from_left = hop(features, right)
     from_right = hop(features, left)
     across = lax.shift_right_logical(part, 1)
+    place = lax.axis_index("batch")
+    side = 4
     order = jnp.stack(
         [part]
         + [
@@ -412,18 +453,9 @@
             for o in range(2)
             for d in (0, 1, 3, 2)
         ]
+        + [lax.shift_right_logical(place, 2), lax.bitwise_and(place, side - 1)]
     ).astype(jnp.int32)
-    mate_row = (pair - lax.axis_index("batch") * rows).astype(F32).reshape(row_bands, LANES)
-
-    raw_t = prototypes.T
-    proto_bf, proto_t = pl.pallas_call(
-        proto_kernel,
-        grid=(cols // 512,),
-        in_specs=[rows_of(512, width), cols_of(width, 512)],
-        out_specs=[rows_of(512, width), cols_of(width, 512)],
-        out_shape=[shape((cols, width), BF), shape((width, cols), BF)],
-        name="proto_kernel",
-    )(prototypes, raw_t)
+    mate_row = (pair - place * rows).astype(F32).reshape(row_bands, LANES)
 
     anywhere = pl.BlockSpec(memory_space=pl.ANY)
     pre, msg = pl.pallas_call(
@@ -441,14 +473,19 @@
     far_top = hop(near_left[: own // 2], right)
     far_low = hop(near_right[own // 2 :], left)
     got = deal(msg, "batch")
-    got, far_top, far_low, mate_row, order, proto_bf, proto_t, raw_t = lax.optimization_barrier(
-        (got, far_top, far_low, mate_row, order, proto_bf, proto_t, raw_t)
-    )
+    got, far_top, far_low, mate_row, order = lax.optimization_barrier((got, far_top, far_low, mate_row, order))
     mine = [features, from_right, from_left, far_top, far_low]
     parts = mine + [hop(piece, swap) for piece in mine]
     msg = pl.pallas_call(
         relay_kernel, out_shape=shape((n_proto, 2 * hid_bands, LANES)), compiler_params=PARAMS, name="relay_kernel"
     )(got)
+    raw, _ = lax.optimization_barrier((prototypes, msg))
+    proto_bf, proto_t, raw_t = pl.pallas_call(
+        proto_kernel,
+        out_shape=[shape((cols, width), BF), shape((width, cols), BF), shape((width, cols), BF)],
+        name="proto_kernel",
+    )(raw)
+    got, proto_bf, proto_t, raw_t = lax.optimization_barrier((deal(msg, "proto"), proto_bf, proto_t, raw_t))
     unit_embed, embed_scale, mean, inv, msg = pl.pallas_call(
         lambda *refs: embed_kernel(total_rows, *refs),
         in_specs=[anywhere, pl.BlockSpec((n_proto, 2 * hid_bands, LANES), lambda: (0, 0, 0))]
@@ -468,7 +505,7 @@
             pltpu.SemaphoreType.DMA((2,)),
         ],
         name="embed_kernel",
-    )(pre, deal(msg, "proto"), gain, bias, w_second)
+    )(pre, got, gain, bias, w_second)
     stat_spec = whole((hid_bands, LANES))
     normed, slope, hid = pl.pallas_call(
         slab_kernel,
@@ -483,7 +520,7 @@
                 pltpu.SemaphoreType.DMA((len(parts) + 1,)),
             ],
         ),
-        out_shape=[shape((rows, slab)), shape((rows, slab)), shape((rows, slab), BF)],
+        out_shape=[shape((rows, slab), BF)] * 3,
         name="slab_kernel",
     )(order, mean, inv, gain, bias, w_first, *parts)
     block_embed, normed, slope, hid = lax.optimization_barrier((deal(msg, "proto"), normed, slope, hid))
@@ -538,21 +575,22 @@
         if step + 1 < ITERS:
             col_msg = col_pass(recv_row)
 
-    d_unit, term, loss_tile = pl.pallas_call(
+    d_unit, *pieces, loss_tile = pl.pallas_call(
         final_kernel,
         grid=(steps,),
         in_specs=[
-            whole((rows, width)),
+            pl.BlockSpec(memory_space=pltpu.SMEM),
+            anywhere,
             whole((row_bands, LANES)),
-            whole((width, cols)),
-            whole((cols, width)),
-            whole((width, cols)),
+            anywhere,
+            anywhere,
+            anywhere,
             whole(recv_col.shape),
             whole(recv_row.shape),
             whole(recv_soft.shape),
         ],
-        out_specs=[rows_of(TILE, width), whole((width, cols)), whole((16, LANES))],
-        out_shape=[shape((rows, width), BF), shape((width, cols), BF), shape((16, LANES))],
+        out_specs=[rows_of(TILE, width)] + [whole((width // side, cols))] * side + [whole((16, LANES))],
+        out_shape=[shape((rows, width), BF)] + [shape((width // side, cols), BF)] * side + [shape((16, LANES))],
         scratch_shapes=[
             pltpu.VMEM((rows, cols), BF),
             pltpu.VMEM((TILE, rows), BF),
@@ -560,48 +598,30 @@
             pltpu.VMEM((col_bands, LANES), F32),
             pltpu.VMEM((row_bands, LANES), F32),
             pltpu.VMEM((row_bands, LANES), F32),
+            pltpu.VMEM((rows, width), BF),
+            pltpu.VMEM((width, cols), BF),
+            pltpu.VMEM((cols, width), BF),
+            pltpu.VMEM((width, cols), BF),
+            pltpu.VMEM((width, cols), BF),
+            pltpu.SemaphoreType.DMA((4,)),
         ],
-        compiler_params=PARAMS,
         name="final_kernel",
-    )(block_embed, mate_row, proto_t, proto_bf, raw_t, recv_col, recv_row, recv_soft)
-
-    side = 4
-    b_of = [(b // side, b % side) for b in range(n_batch)]
+    )(order, block_embed, mate_row, proto_t, proto_bf, raw_t, recv_col, recv_row, recv_soft)
+
 
     def shifted(axis, d):
-        return [
-            (b, (y + d) % side * side + z if axis == 0 else y * side + (z + d) % side) for b, (y, z) in enumerate(b_of)
-        ]
-
-    place = lax.axis_index("batch")
-    spots = (lax.shift_right_logical(place, 2), lax.bitwise_and(place, side - 1))
-
-    def scatter_sum(x, axis):
-        pieces = x.reshape((side, -1) + x.shape[1:])
-        kept = [lax.dynamic_index_in_dim(pieces, spots[axis], 0, keepdims=False)]
-        for d in range(1, side):
-            piece = lax.dynamic_index_in_dim(
-                pieces, lax.bitwise_and(spots[axis] + d, side - 1), 0, keepdims=False
-            )
-            kept.append(lax.ppermute(piece, "batch", shifted(axis, d)))
-        return kept
-
-    def total(kept):
-        acc = kept[0].astype(F32)
-        for piece in kept[1:]:
-            acc += piece.astype(F32)
-        return acc
-
-    first_stage = scatter_sum(term, 0)
+        moves = []
+        for b in range(n_batch):
+            y, z = divmod(b, side)
+            moves.append((b, (y + d) % side * side + z if axis == 0 else y * side + (z + d) % side))
+        return moves
+
+    pieces = [pieces[0]] + [lax.ppermute(pieces[d], "batch", shifted(0, d)) for d in range(1, side)]
     d_unit = deal(d_unit.reshape(n_proto, own, width), "proto")
-    d_unit, *first_stage = lax.optimization_barrier((d_unit, *first_stage))
     d_embed = pl.pallas_call(
-        d_embed_kernel, out_shape=shape((n_proto, own, width), BF), name="d_embed_kernel"
+        d_embed_kernel, out_shape=shape((n_proto, own, width), BF), compiler_params=PARAMS, name="d_embed_kernel"
     )(d_unit, unit_embed, embed_scale)
-    second_stage = scatter_sum(total(first_stage).astype(BF), 1)
     d_embed = deal(d_embed, "proto")
-    d_embed, *second_stage = lax.optimization_barrier((d_embed, *second_stage))
-    grad_proto = total(second_stage).T
 
     shift, msg = pl.pallas_call(
         shift_kernel,
@@ -616,10 +636,11 @@
                 whole((rows, slab)),
                 whole((16, LANES)),
             ],
-            out_specs=[whole((rows, slab)), whole((n_batch, 8 + slab // n_batch, width))],
+            out_specs=[whole((rows, slab)), whole((n_batch, 2 * slab // n_batch, width))],
             scratch_shapes=[pltpu.VMEM((8, slab), F32)],
         ),
-        out_shape=[shape((rows, slab)), shape((n_batch, 8 + slab // n_batch, width))],
+        out_shape=[shape((rows, slab)), shape((n_batch, 2 * slab // n_batch, width), BF)],
+        compiler_params=PARAMS,
         name="shift_kernel",
     )(order, d_embed, w_second, normed, slope, hid, loss_tile)
     recv = deal(msg, "batch")
@@ -648,10 +669,19 @@
             shape((8, slab)),
             shape((slab // n_batch, width)),
         ],
-        compiler_params=PARAMS,
         name="first_kernel",
     )(order, recv, shift, normed, inv, gain, *parts)
 
+    first, *pieces = lax.optimization_barrier((first, *pieces))
+    pieces = pl.pallas_call(
+        stage_kernel,
+        in_specs=[pl.BlockSpec(memory_space=pltpu.SMEM)] + [pl.BlockSpec((width // side, cols), lambda: (0, 0))] * side,
+        out_shape=[shape((width // n_batch, cols), BF)] * side,
+        scratch_shapes=[pltpu.VMEM((width // side, cols), BF)],
+        name="stage_kernel",
+    )(order, *pieces)
+    pieces = [pieces[0]] + [lax.ppermute(pieces[d], "batch", shifted(1, d)) for d in range(1, side)]
+    grad_proto = sum(piece.astype(F32) for piece in pieces).T
     first = deal(first, ("batch", "proto")).reshape(n_batch, n_proto, share, slab)
     grad_first = pl.pallas_call(
         tail_kernel, out_shape=shape((share, d_hid)), compiler_params=PARAMS, name="tail_kernel"

time: 255 us -> 246 us (0.965)
  the two profiles are of different devices: /device:TPU:1 before, /device:TPU:0 now
where the time goes in v4:
time: 246 us; the launch traced here: 245 us
  blocking collectives  86.1 us (35%)
  Pallas kernels  59.8 us (24%)
  starting transfers between devices  51.5 us (21%)
  waiting for transfers between devices  37.4 us (15%)
  local copies, waits for them, and re-layouts  6.66 us (3%)
    all_to_all x8, blocking collectives, deal(): return lax.all_to_all(x, axis, 0, 0, tiled=True)  86.1 us
    all_to_all x5, starting transfers between devices, deal(): return lax.all_to_all(x, axis, 0, 0, tiled=True)  23.2 us
    ppermute x16, waiting for transfers between devices, hop(): return lax.ppermute(x, 'proto', moves)  22.7 us
    ppermute x16, starting transfers between devices, hop(): return lax.ppermute(x, 'proto', moves)  17.5 us
    pallas_call x1, Pallas kernels, step_of_device(): pl.pallas_call(final_kernel, grid=(steps,), in_specs=[pl.BlockSpec(memory...  15 us
    all_to_all x5, waiting for transfers between devices, deal(): return lax.all_to_all(x, axis, 0, 0, tiled=True)  14.7 us
    pallas_call x1, Pallas kernels, step_of_device(): pl.pallas_call(slab_kernel, grid_spec=pltpu.PrefetchScalarGridSpec(num_sc...  7.64 us
    pallas_call x1, Pallas kernels, step_of_device(): pl.pallas_call(pre_kernel, in_specs=[pl.BlockSpec(features.shape, lambda:...  6.91 us
  transfers between devices with their start and end apart: 28, of which 13 were waited for; matrix products, arithmetic and copies ran while one was open for 2% of the time, Pallas kernels for 14%

profile of v4, /device:TPU:0, one launch (start us, length us, event | category | flops | bytes accessed | tf_op | source)
XLA Modules:
  0.0 244.6 jit_solution(7616625259639667000)
XLA Ops:
  0.7 2.9 %collective-permute-start.1 = (bf16[128,2048]{1,0:T(8,128)(2,1)}, bf16[128,2048]{1,0:T(8,128)(2,1)S(1)}, u32[]{:S(2)}, u32[]{:S(2)}) collective-permute-start(bf16[128,2048]{1,0:T(8,128)(2,1)} %refs_6_.1), channel_id=1, source_target_pairs={{2,0},{3,1},{4,2},{5,3},{6,4},{7,5},{0,6},{1,7},{10,8},{11,9},{12,... | collective-permute-start | bytes 1572872 | tf_op jit(solution)/shard_map/ppermute | solution.py:438
  3.6 6.9 %pre_kernel.1 = (f32[128,2048]{1,0:T(8,128)}, f32[16,32,128]{2,1,0:T(8,128)}) custom-call(bf16[128,2048]{1,0:T(8,128)(2,1)} %refs_6_.1, bf16[2048,2048]{1,0:T(8,128)(2,1)} %w_hbm.3), custom_call_target="tpu_custom_call" | custom-call | tf_op jit(solution)/shard_map/pre_kernel/pallas_call | solution.py:461
  10.5 4.6 %collective-permute-done.1.rest_1_.refs_7_ = bf16[128,2048]{1,0:T(8,128)(2,1)S(1)} collective-permute-done((bf16[128,2048]{1,0:T(8,128)(2,1)}, bf16[128,2048]{1,0:T(8,128)(2,1)S(1)}, u32[]{:S(2)}, u32[]{:S(2)}) %collective-permute-start.1) | collective-permute-done | bytes 524320 | tf_op jit(solution)/shard_map/ppermute | solution.py:438
  15.1 3.3 %collective-permute-done.rest_2_.refs_8_ = bf16[128,2048]{1,0:T(8,128)(2,1)S(1)} collective-permute-done((bf16[128,2048]{1,0:T(8,128)(2,1)}, bf16[128,2048]{1,0:T(8,128)(2,1)S(1)}, u32[]{:S(2)}, u32[]{:S(2)}) %collective-permute-start) | collective-permute-done | bytes 524320 | tf_op jit(solution)/shard_map/ppermute | solution.py:438
  18.8 1.7 collective-permute-start.2
  20.5 8.0 %all-to-all-start = ((f32[16,32,128]{2,1,0:T(8,128)}), f32[16,32,128]{2,1,0:T(8,128)S(1)}, u32[]{:S(2)}, u32[]{:S(2)}) async-start(f32[16,32,128]{2,1,0:T(8,128)} %get-tuple-element.61), calls=%async_computation | async-start | bytes 524288 | tf_op jit(solution)/shard_map/all_to_all | solution.py:19
  29.9 7.2 %all-to-all-done.recv_ref = f32[16,32,128]{2,1,0:T(8,128)S(1)} async-done(((f32[16,32,128]{2,1,0:T(8,128)}), f32[16,32,128]{2,1,0:T(8,128)S(1)}, u32[]{:S(2)}, u32[]{:S(2)}) %all-to-all-start) | async-done | bytes 262176 | tf_op jit(solution)/shard_map/all_to_all | solution.py:19
  37.8 3.4 %all-to-all-start.1 = ((f32[8,32,128]{2,1,0:T(8,128)}), f32[8,32,128]{2,1,0:T(8,128)S(1)}, u32[]{:S(2)}, u32[]{:S(2)}) async-start(f32[8,32,128]{2,1,0:T(8,128)} %relay_kernel.1), calls=%async_computation.1 | async-start | bytes 262144 | tf_op jit(solution)/shard_map/all_to_all | solution.py:19
  42.1 3.9 %proto_kernel.1 = (bf16[2048,256]{1,0:T(8,128)(2,1)}, bf16[256,2048]{1,0:T(8,128)(2,1)}, bf16[256,2048]{1,0:T(8,128)(2,1)}) custom-call(bf16[2048,256]{1,0:T(8,128)(2,1)} %raw_ref), custom_call_target="tpu_custom_call" | custom-call | tf_op jit(solution)/shard_map/proto_kernel/pallas_call | solution.py:483
  46.0 1.2 all-to-all-done.1.refs_1_
  47.9 4.0 %embed_kernel.1 = (f32[128,256]{1,0:T(8,128)}, f32[128,128]{1,0:T(8,128)}, f32[16,128]{1,0:T(8,128)}, f32[16,128]{1,0:T(8,128)}, bf16[8,128,256]{2,1,0:T(8,128)(2,1)}) custom-call(f32[128,2048]{1,0:T(8,128)} %get-tuple-element.62.refs_0_, f32[8,32,128]{2,1,0:T(8,128)} %copy-done.22, f32[16,128]{1,0:T(8,128)} %bitcast.32, f32[16,128]{1,0:T(8,128)} %bitcast.35, ...), custom_call_target="tpu_custom_call" | custom-call | tf_op jit(solution)/shard_map/embed_kernel/pallas_call | solution.py:489
  51.9 3.5 %all-to-all-start.2 = ((bf16[8,128,256]{2,1,0:T(8,128)(2,1)}), bf16[8,128,256]{2,1,0:T(8,128)(2,1)S(1)}, u32[]{:S(2)}, u32[]{:S(2)}) async-start(bf16[8,128,256]{2,1,0:T(8,128)(2,1)} %get-tuple-element.72), calls=%async_computation.2 | async-start | bytes 1048576 | tf_op jit(solution)/shard_map/all_to_all | solution.py:19
  56.0 1.2 collective-permute-done.7.rest_8_.refs_14_
  58.7 7.6 %slab_kernel.1 = (bf16[1024,256]{1,0:T(8,128)(2,1)}, bf16[1024,256]{1,0:T(8,128)(2,1)}, bf16[1024,256]{1,0:T(8,128)(2,1)}) custom-call(s32[11]{0:T(128)} %stack.47.order_ref.refs_0_, f32[16,128]{1,0:T(8,128)} %get-tuple-element.73.mean_ref, f32[16,128]{1,0:T(8,128)} %get-tuple-element.74.inv_ref.refs_4_, f32[16,128]{1,0:T(8,128)} %bitcast.33, ...), custom_call_target="tpu_custom_call" | custom-call | tf_op jit(solution)/shard_map/slab_kernel/pallas_call | solution.py:510
  66.3 2.9 %score_kernel.1 = (bf16[1024,2048]{1,0:T(8,128)(2,1)S(1)}, f32[16,16,128]{2,1,0:T(8,128)S(1)}, f32[8,128]{1,0:T(8,128)S(1)}) custom-call(bf16[1024,256]{1,0:T(8,128)(2,1)S(1)} %bitcast.26, bf16[256,2048]{1,0:T(8,128)(2,1)S(1)} %copy-done.1), custom_call_target="tpu_custom_call" | custom-call | tf_op jit(solution)/shard_map/score_kernel/pallas_call | solution.py:529
  69.3 11.3 %all_to_all.65.recv_ref = f32[16,16,128]{2,1,0:T(8,128)S(1)} all-to-all(f32[16,16,128]{2,1,0:T(8,128)S(1)} %get-tuple-element.85), channel_id=1, replica_groups=mesh['batch'=16,'proto'=8] {'batch'}, dimensions={0} | all-to-all | bytes 262144 | tf_op jit(solution)/shard_map/all_to_all | solution.py:19
  80.6 1.2 row_kernel.3
  81.8 10.1 %all_to_all.66.recv_ref.recv_soft_ref = f32[8,16,128]{2,1,0:T(8,128)S(1)} all-to-all(f32[8,16,128]{2,1,0:T(8,128)S(1)} %row_kernel.3), channel_id=1, replica_groups=mesh['batch'=16,'proto'=8] {'proto'}, dimensions={0} | all-to-all | bytes 131072 | tf_op jit(solution)/shard_map/all_to_all | solution.py:19
  91.8 1.2 col_kernel.2
  93.0 11.2 %all_to_all.67.recv_ref = f32[16,16,128]{2,1,0:T(8,128)S(1)} all-to-all(f32[16,16,128]{2,1,0:T(8,128)S(1)} %col_kernel.2), channel_id=1, replica_groups=mesh['batch'=16,'proto'=8] {'batch'}, dimensions={0} | all-to-all | bytes 262144 | tf_op jit(solution)/shard_map/all_to_all | solution.py:19
  104.3 1.2 row_kernel.4
  105.5 7.9 %all_to_all.68.recv_ref = f32[8,8,128]{2,1,0:T(8,128)S(1)} all-to-all(f32[8,8,128]{2,1,0:T(8,128)S(1)} %row_kernel.4), channel_id=1, replica_groups=mesh['batch'=16,'proto'=8] {'proto'}, dimensions={0} | all-to-all | bytes 65536 | tf_op jit(solution)/shard_map/all_to_all | solution.py:19
  113.5 1.2 col_kernel.3
  114.7 11.2 %all_to_all.69.recv_ref.recv_col_ref = f32[16,16,128]{2,1,0:T(8,128)S(1)} all-to-all(f32[16,16,128]{2,1,0:T(8,128)S(1)} %col_kernel.3), channel_id=1, replica_groups=mesh['batch'=16,'proto'=8] {'batch'}, dimensions={0} | all-to-all | bytes 262144 | tf_op jit(solution)/shard_map/all_to_all | solution.py:19
  125.9 1.2 row_kernel.5
  127.1 8.5 %all_to_all.70.recv_row_ref = f32[8,8,128]{2,1,0:T(8,128)} all-to-all(f32[8,8,128]{2,1,0:T(8,128)S(1)} %row_kernel.5), channel_id=1, replica_groups=mesh['batch'=16,'proto'=8] {'proto'}, dimensions={0} | all-to-all | bytes 65536 | tf_op jit(solution)/shard_map/all_to_all | solution.py:19
  135.6 15.0 %final_kernel.1 = (bf16[1024,256]{1,0:T(8,128)(2,1)}, bf16[64,2048]{1,0:T(8,128)(2,1)}, bf16[64,2048]{1,0:T(8,128)(2,1)}, bf16[64,2048]{1,0:T(8,128)(2,1)}, bf16[64,2048]{1,0:T(8,128)(2,1)}, /*index=5*/f32[16,128]{1,0:T(8,128)}) custom-call(s32[11]{0:T(128)} %stack.47.order_ref.refs_0_, bf16[1024,256]{1,0:T(8,128)(2,1)} %bitcast.27, ...), custom_call_target="tpu_custom_call" | custom-call | tf_op jit(solution)/shard_map/final_kernel/pallas_call | solution.py:578
  150.6 13.8 %all_to_all.71.recv_ref = bf16[8,128,256]{2,1,0:T(8,128)(2,1)S(1)} all-to-all(bf16[8,128,256]{2,1,0:T(8,128)(2,1)} %bitcast.31), channel_id=1, replica_groups=mesh['batch'=16,'proto'=8] {'proto'}, dimensions={0} | all-to-all | bytes 1048576 | tf_op jit(solution)/shard_map/all_to_all | solution.py:19
  165.4 3.5 %all-to-all-start.10 = ((bf16[8,128,256]{2,1,0:T(8,128)(2,1)}), bf16[8,128,256]{2,1,0:T(8,128)(2,1)S(1)}, u32[]{:S(2)}, u32[]{:S(2)}) async-start(bf16[8,128,256]{2,1,0:T(8,128)(2,1)} %d_embed_kernel.1), calls=%async_computation.10 | async-start | bytes 1048576 | tf_op jit(solution)/shard_map/all_to_all | solution.py:19
  169.4 2.2 collective-permute-start.10
  171.6 1.3 collective-permute-start.11
  172.8 6.3 %all-to-all-done.10.d_embed_ref = bf16[8,128,256]{2,1,0:T(8,128)(2,1)S(1)} async-done(((bf16[8,128,256]{2,1,0:T(8,128)(2,1)}), bf16[8,128,256]{2,1,0:T(8,128)(2,1)S(1)}, u32[]{:S(2)}, u32[]{:S(2)}) %all-to-all-start.10) | async-done | bytes 524320 | tf_op jit(solution)/shard_map/all_to_all | solution.py:19
  181.9 12.0 %all_to_all.72.refs_1_ = bf16[16,32,256]{2,1,0:T(8,128)(2,1)} all-to-all(bf16[16,32,256]{2,1,0:T(8,128)(2,1)S(1)} %get-tuple-element.95), channel_id=1, replica_groups=mesh['batch'=16,'proto'=8] {'batch'}, dimensions={0} | all-to-all | bytes 524288 | tf_op jit(solution)/shard_map/all_to_all | solution.py:19
  193.9 6.7 %first_kernel.1 = (bf16[128,16,256]{2,1,0:T(8,128)(2,1)}, f32[8,256]{1,0:T(8,128)}, f32[16,256]{1,0:T(8,128)}) custom-call(s32[11]{0:T(128)} %stack.47.order_ref.refs_0_, bf16[16,32,256]{2,1,0:T(8,128)(2,1)} %all_to_all.72.refs_1_, f32[1024,256]{1,0:T(8,128)} %copy-done.5, bf16[1024,256]{1,0:T(8,128)(2,1)} %get-tuple-element.91.normed_ref.refs_3_, ...), custom_call_target="tpu_custom_call" | custom-call | tf_op jit(solution)/shard_map/first_kernel/pallas_call | solution.py:649
  200.6 4.8 %all-to-all-start.12 = ((bf16[128,16,256]{2,1,0:T(8,128)(2,1)}), bf16[128,16,256]{2,1,0:T(8,128)(2,1)S(1)}, u32[]{:S(2)}, u32[]{:S(2)}) async-start(bf16[128,16,256]{2,1,0:T(8,128)(2,1)} %get-tuple-element.102), calls=%async_computation.12 | async-start | bytes 2097152 | tf_op jit(solution)/shard_map/all_to_all | solution.py:19
  205.4 2.1 stage_kernel.1
  208.6 3.2 %collective-permute-start.21 = (bf16[16,2048]{1,0:T(8,128)(2,1)}, bf16[16,2048]{1,0:T(8,128)(2,1)S(1)}, u32[]{:S(2)}, u32[]{:S(2)}) collective-permute-start(bf16[16,2048]{1,0:T(8,128)(2,1)} %get-tuple-element.113), channel_id=1, source_target_pairs={{0,16},{8,24},{16,0},{24,8},{32,48},{40,56},{48,32},{56,40},{64,80... | collective-permute-start | bytes 196616 | tf_op jit(solution)/shard_map/ppermute | solution.py:683
  211.8 1.2 collective-permute-start.22
  213.0 1.6 collective-permute-start.19
  216.2 4.3 %collective-permute-start.17 = (f32[8,256]{1,0:T(8,128)}, f32[8,256]{1,0:T(8,128)S(1)}, u32[]{:S(2)}, u32[]{:S(2)}) collective-permute-start(f32[8,256]{1,0:T(8,128)} %get-tuple-element.104.refs_1_), channel_id=1, source_target_pairs={{0,5},{1,6},{2,7},{3,0},{4,1},{5,2},{6,3},{7,4},{8,13},{9,14},{10,... | collective-permute-start | bytes 24584 | tf_op jit(solution)/shard_map/ppermute | solution.py:438
  222.1 1.8 collective-permute-start.15
  223.8 2.0 collective-permute-done.16.refs_5_
  225.9 1.3 collective-permute-done.15.refs_4_
  227.1 1.4 collective-permute-start.12
  228.5 2.4 collective-permute-done.14.refs_3_
  230.9 1.4 collective-permute-start.13
  232.3 6.3 %collective-permute-done.13.refs_2_ = f32[8,256]{1,0:T(8,128)S(1)} collective-permute-done((f32[8,256]{1,0:T(8,128)}, f32[8,256]{1,0:T(8,128)S(1)}, u32[]{:S(2)}, u32[]{:S(2)}) %collective-permute-start.13) | collective-permute-done | bytes 8224 | tf_op jit(solution)/shard_map/ppermute | solution.py:438
  241.6 1.5 add_bitcast_fusion
  (90 shorter events, 19.0 us)
Async XLA Ops:
  0.6 40.6 %copy-start.15 = (bf16[128,2048]{1,0:T(8,128)(2,1)S(1)}, bf16[128,2048]{1,0:T(8,128)(2,1)}, u32[]{:S(2)}) copy-start(bf16[128,2048]{1,0:T(8,128)(2,1)} %refs_6_.1) | copy-start | bytes 1572868
  0.6 28.6 %copy-start.23 = (s32[1024]{0:T(1024)S(1)}, s32[1024]{0:T(1024)}, u32[]{:S(2)}) copy-start(s32[1024]{0:T(1024)} %param.13) | copy-start | bytes 12292
  0.7 14.4 %collective-permute-start.1 = (bf16[128,2048]{1,0:T(8,128)(2,1)}, bf16[128,2048]{1,0:T(8,128)(2,1)S(1)}, u32[]{:S(2)}, u32[]{:S(2)}) collective-permute-start(bf16[128,2048]{1,0:T(8,128)(2,1)} %refs_6_.1), channel_id=1, source_target_pairs={{2,0},{3,1},{4,2},{5,3},{6,4},{7,5},{0,6},{1,7},{10,8},{11,9},{12,... | collective-permute-start | bytes 1572872 | tf_op jit(solution)/shard_map/ppermute | solution.py:438
  3.6 14.8 %collective-permute-start = (bf16[128,2048]{1,0:T(8,128)(2,1)}, bf16[128,2048]{1,0:T(8,128)(2,1)S(1)}, u32[]{:S(2)}, u32[]{:S(2)}) collective-permute-start(bf16[128,2048]{1,0:T(8,128)(2,1)} %refs_6_.1), channel_id=1, source_target_pairs={{0,2},{1,3},{2,4},{3,5},{4,6},{5,7},{6,0},{7,1},{8,10},{9,11},{10,... | collective-permute-start | bytes 1572872 | tf_op jit(solution)/shard_map/ppermute | solution.py:438
  15.1 43.6 %copy-start.16 = (bf16[128,2048]{1,0:T(8,128)(2,1)}, bf16[128,2048]{1,0:T(8,128)(2,1)S(1)}, u32[]{:S(2)}) copy-start(bf16[128,2048]{1,0:T(8,128)(2,1)S(1)} %collective-permute-done.1.rest_1_.refs_7_) | copy-start | bytes 1572868
  18.4 40.3 %copy-start.17 = (bf16[128,2048]{1,0:T(8,128)(2,1)}, bf16[128,2048]{1,0:T(8,128)(2,1)S(1)}, u32[]{:S(2)}) copy-start(bf16[128,2048]{1,0:T(8,128)(2,1)S(1)} %collective-permute-done.rest_2_.refs_8_) | copy-start | bytes 1572868
  18.4 18.6 %collective-permute-start.3 = (bf16[64,2048]{1,0:T(8,128)(2,1)S(1)}, bf16[64,2048]{1,0:T(8,128)(2,1)S(1)}, u32[]{:S(2)}, u32[]{:S(2)}) collective-permute-start(bf16[64,2048]{1,0:T(8,128)(2,1)S(1)} %slice.10), channel_id=1, source_target_pairs={{2,0},{3,1},{4,2},{5,3},{6,4},{7,5},{0,6},{1,7},{10,8},{11,9},{12,... | collective-permute-start | bytes 786440 | tf_op jit(solution)/shard_map/ppermute | solution.py:438
  18.8 18.3 %collective-permute-start.2 = (bf16[64,2048]{1,0:T(8,128)(2,1)S(1)}, bf16[64,2048]{1,0:T(8,128)(2,1)S(1)}, u32[]{:S(2)}, u32[]{:S(2)}) collective-permute-start(bf16[64,2048]{1,0:T(8,128)(2,1)S(1)} %slice.9), channel_id=1, source_target_pairs={{0,2},{1,3},{2,4},{3,5},{4,6},{5,7},{6,0},{7,1},{8,10},{9,11},{10,... | collective-permute-start | bytes 786440 | tf_op jit(solution)/shard_map/ppermute | solution.py:438
  20.5 16.5 %all-to-all-start = ((f32[16,32,128]{2,1,0:T(8,128)}), f32[16,32,128]{2,1,0:T(8,128)S(1)}, u32[]{:S(2)}, u32[]{:S(2)}) async-start(f32[16,32,128]{2,1,0:T(8,128)} %get-tuple-element.61), calls=%async_computation | async-start | bytes 524288 | tf_op jit(solution)/shard_map/all_to_all | solution.py:19
  37.1 21.6 %copy-start.18 = (bf16[64,2048]{1,0:T(8,128)(2,1)}, bf16[64,2048]{1,0:T(8,128)(2,1)S(1)}, u32[]{:S(2)}) copy-start(bf16[64,2048]{1,0:T(8,128)(2,1)S(1)} %collective-permute-done.3.rest_4_.refs_10_) | copy-start | bytes 786436
  37.1 14.8 %copy-start.19 = (bf16[64,2048]{1,0:T(8,128)(2,1)}, bf16[64,2048]{1,0:T(8,128)(2,1)S(1)}, u32[]{:S(2)}) copy-start(bf16[64,2048]{1,0:T(8,128)(2,1)S(1)} %collective-permute-done.2.rest_3_.refs_9_) | copy-start | bytes 786436
  37.8 9.4 %all-to-all-start.1 = ((f32[8,32,128]{2,1,0:T(8,128)}), f32[8,32,128]{2,1,0:T(8,128)S(1)}, u32[]{:S(2)}, u32[]{:S(2)}) async-start(f32[8,32,128]{2,1,0:T(8,128)} %relay_kernel.1), calls=%async_computation.1 | async-start | bytes 262144 | tf_op jit(solution)/shard_map/all_to_all | solution.py:19
  41.2 14.8 %collective-permute-start.4 = (bf16[128,2048]{1,0:T(8,128)(2,1)S(1)}, bf16[128,2048]{1,0:T(8,128)(2,1)}, u32[]{:S(2)}, u32[]{:S(2)}) collective-permute-start(bf16[128,2048]{1,0:T(8,128)(2,1)S(1)} %copy-done.15), channel_id=1, source_target_pairs={{0,1},{1,0},{2,3},{3,2},{4,5},{5,4},{6,7},{7,6},{8,9},{9,8},{10,11... | collective-permute-start | bytes 1572872 | tf_op jit(solution)/shard_map/ppermute | solution.py:438
  41.6 14.4 %collective-permute-start.5 = (bf16[128,2048]{1,0:T(8,128)(2,1)S(1)}, bf16[128,2048]{1,0:T(8,128)(2,1)}, u32[]{:S(2)}, u32[]{:S(2)}) collective-permute-start(bf16[128,2048]{1,0:T(8,128)(2,1)S(1)} %collective-permute-done.1.rest_1_.refs_7_), channel_id=1, source_target_pairs={{0,1},{1,0},{2,3},{3,2},{4,5},{5,4},{6,7},{7,6},{8,9},{9,8},{10,11... | collective-permute-start | bytes 1572872 | tf_op jit(solution)/shard_map/ppermute | solution.py:438
  41.8 14.2 %collective-permute-start.6 = (bf16[128,2048]{1,0:T(8,128)(2,1)S(1)}, bf16[128,2048]{1,0:T(8,128)(2,1)}, u32[]{:S(2)}, u32[]{:S(2)}) collective-permute-start(bf16[128,2048]{1,0:T(8,128)(2,1)S(1)} %collective-permute-done.rest_2_.refs_8_), channel_id=1, source_target_pairs={{0,1},{1,0},{2,3},{3,2},{4,5},{5,4},{6,7},{7,6},{8,9},{9,8},{10,11... | collective-permute-start | bytes 1572872 | tf_op jit(solution)/shard_map/ppermute | solution.py:438
  46.0 20.3 %copy-start.1 = (bf16[256,2048]{1,0:T(8,128)(2,1)S(1)}, bf16[256,2048]{1,0:T(8,128)(2,1)}, u32[]{:S(2)}) copy-start(bf16[256,2048]{1,0:T(8,128)(2,1)} %get-tuple-element.82.proto_t_hbm) | copy-start | bytes 3145732
  51.9 14.4 %all-to-all-start.2 = ((bf16[8,128,256]{2,1,0:T(8,128)(2,1)}), bf16[8,128,256]{2,1,0:T(8,128)(2,1)S(1)}, u32[]{:S(2)}, u32[]{:S(2)}) async-start(bf16[8,128,256]{2,1,0:T(8,128)(2,1)} %get-tuple-element.72), calls=%async_computation.2 | async-start | bytes 1048576 | tf_op jit(solution)/shard_map/all_to_all | solution.py:19
  55.4 1.8 collective-permute-start.7
  55.8 1.8 collective-permute-start.8
  57.3 0.7 copy-start.20
  66.3 48.3 %copy-start = (bf16[8,128,256]{2,1,0:T(8,128)(2,1)}, bf16[8,128,256]{2,1,0:T(8,128)(2,1)S(1)}, u32[]{:S(2)}) copy-start(bf16[8,128,256]{2,1,0:T(8,128)(2,1)S(1)} %all-to-all-done.2) | copy-start | bytes 1572868
  91.8 35.3 %copy-start.6 = (f32[8,16,128]{2,1,0:T(8,128)}, f32[8,16,128]{2,1,0:T(8,128)S(1)}, u32[]{:S(2)}) copy-start(f32[8,16,128]{2,1,0:T(8,128)S(1)} %all_to_all.66.recv_ref.recv_soft_ref) | copy-start | bytes 196612
  104.3 60.1 %copy-start.9 = (f32[128,256]{1,0:T(8,128)S(1)}, f32[128,256]{1,0:T(8,128)}, u32[]{:S(2)}) copy-start(f32[128,256]{1,0:T(8,128)} %get-tuple-element.89.unit_ref) | copy-start | bytes 393220
  104.3 60.1 %copy-start.10 = (f32[128,128]{1,0:T(8,128)S(1)}, f32[128,128]{1,0:T(8,128)}, u32[]{:S(2)}) copy-start(f32[128,128]{1,0:T(8,128)} %get-tuple-element.90.scale_ref) | copy-start | bytes 196612
  105.5 73.6 %copy-start.2 = (bf16[2048,256]{1,0:T(8,128)(2,1)S(1)}, bf16[2048,256]{1,0:T(8,128)(2,1)}, u32[]{:S(2)}) copy-start(bf16[2048,256]{1,0:T(8,128)(2,1)} %w2_ref.1) | copy-start | bytes 3145732
  105.5 73.6 %copy-start.3 = (bf16[1024,256]{1,0:T(8,128)(2,1)S(1)}, bf16[1024,256]{1,0:T(8,128)(2,1)}, u32[]{:S(2)}) copy-start(bf16[1024,256]{1,0:T(8,128)(2,1)} %get-tuple-element.91.normed_ref.refs_3_) | copy-start | bytes 1572868
  105.5 73.6 %copy-start.7 = (bf16[1024,256]{1,0:T(8,128)(2,1)S(1)}, bf16[1024,256]{1,0:T(8,128)(2,1)}, u32[]{:S(2)}) copy-start(bf16[1024,256]{1,0:T(8,128)(2,1)} %get-tuple-element.92.slope_ref) | copy-start | bytes 1572868
  105.5 73.6 %copy-start.8 = (bf16[1024,256]{1,0:T(8,128)(2,1)S(1)}, bf16[1024,256]{1,0:T(8,128)(2,1)}, u32[]{:S(2)}) copy-start(bf16[1024,256]{1,0:T(8,128)(2,1)} %get-tuple-element.93.hid_ref) | copy-start | bytes 1572868
  105.5 73.6 %copy-start.11 = (s32[11]{0:T(128)S(1)}, s32[11]{0:T(128)}, u32[]{:S(2)}) copy-start(s32[11]{0:T(128)} %stack.47.order_ref.refs_0_) | copy-start | bytes 136
  125.9 9.7 %copy-start.4 = (f32[16,16,128]{2,1,0:T(8,128)}, f32[16,16,128]{2,1,0:T(8,128)S(1)}, u32[]{:S(2)}) copy-start(f32[16,16,128]{2,1,0:T(8,128)S(1)} %all_to_all.69.recv_ref.recv_col_ref) | copy-start | bytes 393220
  150.6 88.0 %copy-start.12 = (s32[11]{0:T(128)S(1)}, s32[11]{0:T(128)}, u32[]{:S(2)}) copy-start(s32[11]{0:T(128)} %stack.47.order_ref.refs_0_) | copy-start | bytes 136
  165.4 13.7 %all-to-all-start.10 = ((bf16[8,128,256]{2,1,0:T(8,128)(2,1)}), bf16[8,128,256]{2,1,0:T(8,128)(2,1)S(1)}, u32[]{:S(2)}, u32[]{:S(2)}) async-start(bf16[8,128,256]{2,1,0:T(8,128)(2,1)} %d_embed_kernel.1), calls=%async_computation.10 | async-start | bytes 1048576 | tf_op jit(solution)/shard_map/all_to_all | solution.py:19
  168.9 31.7 %collective-permute-start.9 = (bf16[64,2048]{1,0:T(8,128)(2,1)}, bf16[64,2048]{1,0:T(8,128)(2,1)}, u32[]{:S(2)}, u32[]{:S(2)}) collective-permute-start(bf16[64,2048]{1,0:T(8,128)(2,1)} %get-tuple-element.99), channel_id=1, source_target_pairs={{0,32},{8,40},{16,48},{24,56},{32,64},{40,72},{48,80},{56,88},{64,... | collective-permute-start | bytes 786440 | tf_op jit(solution)/shard_map/ppermute | solution.py:619
  169.4 31.2 %collective-permute-start.10 = (bf16[64,2048]{1,0:T(8,128)(2,1)}, bf16[64,2048]{1,0:T(8,128)(2,1)}, u32[]{:S(2)}, u32[]{:S(2)}) collective-permute-start(bf16[64,2048]{1,0:T(8,128)(2,1)} %get-tuple-element.100), channel_id=1, source_target_pairs={{0,64},{8,72},{16,80},{24,88},{32,96},{40,104},{48,112},{56,120},{... | collective-permute-start | bytes 786440 | tf_op jit(solution)/shard_map/ppermute | solution.py:619
  171.6 29.0 %collective-permute-start.11 = (bf16[64,2048]{1,0:T(8,128)(2,1)}, bf16[64,2048]{1,0:T(8,128)(2,1)}, u32[]{:S(2)}, u32[]{:S(2)}) collective-permute-start(bf16[64,2048]{1,0:T(8,128)(2,1)} %get-tuple-element.101), channel_id=1, source_target_pairs={{0,96},{8,104},{16,112},{24,120},{32,0},{40,8},{48,16},{56,24},{64... | collective-permute-start | bytes 786440 | tf_op jit(solution)/shard_map/ppermute | solution.py:619
  180.9 1.0 copy-start.5
  200.6 42.5 %all-to-all-start.12 = ((bf16[128,16,256]{2,1,0:T(8,128)(2,1)}), bf16[128,16,256]{2,1,0:T(8,128)(2,1)S(1)}, u32[]{:S(2)}, u32[]{:S(2)}) async-start(bf16[128,16,256]{2,1,0:T(8,128)(2,1)} %get-tuple-element.102), calls=%async_computation.12 | async-start | bytes 2097152 | tf_op jit(solution)/shard_map/all_to_all | solution.py:19
  207.5 34.1 %collective-permute-start.20 = (bf16[16,2048]{1,0:T(8,128)(2,1)}, bf16[16,2048]{1,0:T(8,128)(2,1)S(1)}, u32[]{:S(2)}, u32[]{:S(2)}) collective-permute-start(bf16[16,2048]{1,0:T(8,128)(2,1)} %get-tuple-element.112), channel_id=1, source_target_pairs={{0,8},{8,16},{16,24},{24,0},{32,40},{40,48},{48,56},{56,32},{64,72... | collective-permute-start | bytes 196616 | tf_op jit(solution)/shard_map/ppermute | solution.py:683
  208.6 33.0 %collective-permute-start.21 = (bf16[16,2048]{1,0:T(8,128)(2,1)}, bf16[16,2048]{1,0:T(8,128)(2,1)S(1)}, u32[]{:S(2)}, u32[]{:S(2)}) collective-permute-start(bf16[16,2048]{1,0:T(8,128)(2,1)} %get-tuple-element.113), channel_id=1, source_target_pairs={{0,16},{8,24},{16,0},{24,8},{32,48},{40,56},{48,32},{56,40},{64,80... | collective-permute-start | bytes 196616 | tf_op jit(solution)/shard_map/ppermute | solution.py:683
  211.8 29.8 %collective-permute-start.22 = (bf16[16,2048]{1,0:T(8,128)(2,1)}, bf16[16,2048]{1,0:T(8,128)(2,1)S(1)}, u32[]{:S(2)}, u32[]{:S(2)}) collective-permute-start(bf16[16,2048]{1,0:T(8,128)(2,1)} %get-tuple-element.114), channel_id=1, source_target_pairs={{0,24},{8,0},{16,8},{24,16},{32,56},{40,32},{48,40},{56,48},{64,88... | collective-permute-start | bytes 196616 | tf_op jit(solution)/shard_map/ppermute | solution.py:683
  213.0 3.2 %collective-permute-start.19 = (f32[8,256]{1,0:T(8,128)}, f32[8,256]{1,0:T(8,128)S(1)}, u32[]{:S(2)}, u32[]{:S(2)}) collective-permute-start(f32[8,256]{1,0:T(8,128)} %get-tuple-element.104.refs_1_), channel_id=1, source_target_pairs={{0,7},{1,0},{2,1},{3,2},{4,3},{5,4},{6,5},{7,6},{8,15},{9,8},{10,9... | collective-permute-start | bytes 24584 | tf_op jit(solution)/shard_map/ppermute | solution.py:438
  214.6 5.8 %collective-permute-start.18 = (f32[8,256]{1,0:T(8,128)}, f32[8,256]{1,0:T(8,128)S(1)}, u32[]{:S(2)}, u32[]{:S(2)}) collective-permute-start(f32[8,256]{1,0:T(8,128)} %get-tuple-element.104.refs_1_), channel_id=1, source_target_pairs={{0,6},{1,7},{2,0},{3,1},{4,2},{5,3},{6,4},{7,5},{8,14},{9,15},{10,... | collective-permute-start | bytes 24584 | tf_op jit(solution)/shard_map/ppermute | solution.py:438
  216.2 5.8 %collective-permute-start.17 = (f32[8,256]{1,0:T(8,128)}, f32[8,256]{1,0:T(8,128)S(1)}, u32[]{:S(2)}, u32[]{:S(2)}) collective-permute-start(f32[8,256]{1,0:T(8,128)} %get-tuple-element.104.refs_1_), channel_id=1, source_target_pairs={{0,5},{1,6},{2,7},{3,0},{4,1},{5,2},{6,3},{7,4},{8,13},{9,14},{10,... | collective-permute-start | bytes 24584 | tf_op jit(solution)/shard_map/ppermute | solution.py:438
  220.5 5.4 %collective-permute-start.16 = (f32[8,256]{1,0:T(8,128)}, f32[8,256]{1,0:T(8,128)S(1)}, u32[]{:S(2)}, u32[]{:S(2)}) collective-permute-start(f32[8,256]{1,0:T(8,128)} %get-tuple-element.104.refs_1_), channel_id=1, source_target_pairs={{0,4},{1,5},{2,6},{3,7},{4,0},{5,1},{6,2},{7,3},{8,12},{9,13},{10,... | collective-permute-start | bytes 24584 | tf_op jit(solution)/shard_map/ppermute | solution.py:438
  222.1 5.1 %collective-permute-start.15 = (f32[8,256]{1,0:T(8,128)}, f32[8,256]{1,0:T(8,128)S(1)}, u32[]{:S(2)}, u32[]{:S(2)}) collective-permute-start(f32[8,256]{1,0:T(8,128)} %get-tuple-element.104.refs_1_), channel_id=1, source_target_pairs={{0,3},{1,4},{2,5},{3,6},{4,7},{5,0},{6,1},{7,2},{8,11},{9,12},{10,... | collective-permute-start | bytes 24584 | tf_op jit(solution)/shard_map/ppermute | solution.py:438
  225.8 5.1 %collective-permute-start.14 = (f32[8,256]{1,0:T(8,128)}, f32[8,256]{1,0:T(8,128)S(1)}, u32[]{:S(2)}, u32[]{:S(2)}) collective-permute-start(f32[8,256]{1,0:T(8,128)} %get-tuple-element.104.refs_1_), channel_id=1, source_target_pairs={{0,2},{1,3},{2,4},{3,5},{4,6},{5,7},{6,0},{7,1},{8,10},{9,11},{10,... | collective-permute-start | bytes 24584 | tf_op jit(solution)/shard_map/ppermute | solution.py:438
  227.1 14.5 %collective-permute-start.12 = (f32[16,256]{1,0:T(8,128)}, f32[16,256]{1,0:T(8,128)S(1)}, u32[]{:S(2)}, u32[]{:S(2)}) collective-permute-start(f32[16,256]{1,0:T(8,128)} %get-tuple-element.103), channel_id=1, source_target_pairs={{0,0},{1,16},{2,32},{3,48},{4,64},{5,80},{6,96},{7,112},{8,1},{9,1... | collective-permute-start | bytes 49160 | tf_op jit(solution)/shard_map/ppermute | solution.py:689
  230.9 7.6 %collective-permute-start.13 = (f32[8,256]{1,0:T(8,128)}, f32[8,256]{1,0:T(8,128)S(1)}, u32[]{:S(2)}, u32[]{:S(2)}) collective-permute-start(f32[8,256]{1,0:T(8,128)} %get-tuple-element.104.refs_1_), channel_id=1, source_target_pairs={{0,1},{1,2},{2,3},{3,4},{4,5},{5,6},{6,7},{7,0},{8,9},{9,10},{10,1... | collective-permute-start | bytes 24584 | tf_op jit(solution)/shard_map/ppermute | solution.py:438
  (4 other events, 2.7 us)

commit v5 on v4

--- a/solution.py
+++ b/solution.py
@@ -193,7 +193,7 @@
 def final_kernel(
     order_ref, embed_hbm, pair_ref, proto_t_hbm, proto_hbm, raw_t_hbm, recv_col_ref, recv_row_ref, recv_soft_ref,
     d_unit_ref, piece0_ref, piece1_ref, piece2_ref, piece3_ref, loss_ref,
-    grad_ref, mate_ref, loss_acc_ref, col_ref, row_ref, soft_ref, embed_ref, proto_t_ref, proto_ref, raw_t_ref, term_ref, sems,
+    grad_ref, mate_ref, loss_acc_ref, col_ref, row_ref, soft_ref, embed_ref, proto_t_ref, proto_ref, raw_t_ref, term_ref, both_ref, sems,
 ):
     pairs = ((embed_hbm, embed_ref), (proto_t_hbm, proto_t_ref), (proto_hbm, proto_ref), (raw_t_hbm, raw_t_ref))
     copies = [pltpu.make_async_copy(src, dst, sems.at[k]) for k, (src, dst) in enumerate(pairs)]
@@ -228,14 +228,15 @@
             mate_ref[b * LANES : (b + 1) * LANES, lane(q)] = jnp.where(hot, 1.0, 0.0).astype(BF)
         scales.append(jnp.broadcast_to(jnp.sum(found, axis=1, keepdims=True), (LANES, LANES)))
     mate_scale = jnp.concatenate(scales, axis=0)
-    mate = jnp.dot(mate_ref[...], embed_ref[...], preferred_element_type=F32).astype(BF)
+    both_ref[0:rows, :] = embed_ref[here, :]
+    both_ref[rows:, :] = jnp.dot(mate_ref[...], embed_ref[...], preferred_element_type=F32).astype(BF)
     soft = jnp.concatenate([as_column(soft_ref[pl.ds(base + b, 1), :]) for b in range(rows // LANES)], axis=0)
     inv_soft = 10.0 / soft
     loss_acc = jnp.zeros((8, LANES), F32)
     for j in range(cols // TILE):
         span = slice(j * TILE, (j + 1) * TILE)
-        scores = jnp.dot(embed_ref[here, :], proto_t_ref[:, span], preferred_element_type=F32)
-        mates = jnp.dot(mate, proto_t_ref[:, span], preferred_element_type=F32)
+        both = jnp.dot(both_ref[...], proto_t_ref[:, span], preferred_element_type=F32)
+        scores, mates = both[:rows], both[rows:]
         for h in range(chunks):
             at = j * chunks + h
             target = jnp.exp2(mates[:, lane(h)] * (20.0 * LOG2_E)) * mate_scale * col_ref[at : at + 1, :]
@@ -317,8 +318,10 @@
 
 
 def shift_kernel(
-    order_ref, d_embed_ref, w2_ref, normed_ref, slope_ref, hid_ref, loss_ref, shift_ref, msg_ref, sum_ref
+    order_ref, d_embed_ref, w2_ref, normed_ref, slope_ref, hid_ref, loss_hbm, shift_ref, msg_ref, sum_ref, loss_ref, sems
 ):
+    loss_copy = pltpu.make_async_copy(loss_hbm, loss_ref, sems.at[0])
+    loss_copy.start()
     n_blocks, own, _ = d_embed_ref.shape
     sum_ref[...] = jnp.zeros_like(sum_ref)
     gains = biases = second = None
@@ -333,6 +336,7 @@
         gains = gain if gains is None else gains + gain
         biases = bias if biases is None else biases + bias
         second = part if second is None else second + part
+    loss_copy.wait()
     hits = jnp.sum(loss_ref[0:8, :], axis=0, keepdims=True)
     logs = jnp.sum(loss_ref[8:16, :], axis=0, keepdims=True)
     sum_ref[0:1, :] = gains
@@ -352,16 +356,21 @@
     msg_ref[:, share:, :] = second.astype(BF).reshape(n, share, slab)
 
 
+def halves(v):
+    high = v.astype(BF)
+    return high, (v - high.astype(F32)).astype(BF)
+
+
 def first_kernel(total_rows, order_ref, recv_ref, shift_ref, normed_ref, inv_ref, gain_ref, *rest):
-    parts = rest[:-6]
-    out_ref, sums_ref, second_ref, d_pre_ref, buf_ref, sems = rest[-6:]
-    copies = start_parts(parts, buf_ref, sems)
+    parts = rest[:-5]
+    out_hbm, second_ref, d_pre_ref, out_ref, sems = rest[-5:]
+    n, _, _ = out_ref.shape
+    slab = d_pre_ref.shape[1]
     share = second_ref.shape[0]
     second_ref[...] = jnp.sum(recv_ref[:, share:, :].astype(F32), axis=0)
     got = jnp.sum(recv_ref[:, :share, :].astype(F32), axis=0)
     got = got[0:8] + (got[8:16] + pltpu.roll(got[8:16], 4, 0))
-    sums_ref[...] = got
-    chunks = d_pre_ref.shape[1] // LANES
+    chunks = slab // LANES
     for h in range(chunks):
         at = pl.ds(order_ref[0] * chunks + h, 1)
         factor = gain_ref[at, :] * inv_ref[at, :]
@@ -371,22 +380,54 @@
             band = slice(b * LANES, (b + 1) * LANES)
             d_pre = factor * (shift_ref[band, lane(h)] - bias_mean - normed_ref[band, lane(h)].astype(F32) * gain_mean)
             d_pre_ref[band, lane(h)] = d_pre.astype(BF)
+    high, low = halves(got[0:2])
+    sums = [piece[k : k + 1, lane(h)] for k in range(2) for piece in (high, low) for h in range(chunks)]
+    high, rest_of = got[2:3].astype(BF), got[2:3] - got[2:3].astype(BF).astype(F32)
+    losses = [piece[:, lane(h)] for piece in (high,) + halves(rest_of) for h in range(chunks)]
+    losses += [jnp.zeros((1, LANES), BF)] * (8 - len(losses))
+    odd = lax.rem(order_ref[10], 2) == 1
+    extra = jnp.where(
+        odd,
+        jnp.concatenate([v.astype(F32) for v in losses], axis=0),
+        jnp.concatenate([v.astype(F32) for v in sums], axis=0),
+    ).astype(BF)
+    out_ref[:, chunks * share :, :] = jnp.broadcast_to(extra[None], (n, 8, LANES))
+    group = TILE // share
+    copies = []
+    for j in range(n // group):
+        tile = jnp.concatenate([part[:, j * TILE : (j + 1) * TILE] for part in parts], axis=0)
+        grad = tdot(tile, d_pre_ref[...], 0, 0).astype(BF)
+        span = slice(j * group, (j + 1) * group)
+        for h in range(chunks):
+            out_ref[span, h * share : (h + 1) * share, :] = grad[:, lane(h)].reshape(group, share, LANES)
+        copies.append(pltpu.make_async_copy(out_ref.at[span], out_hbm.at[span], sems.at[j]))
+        copies[-1].start()
     for copy in copies:
         copy.wait()
-    _, share, slab = out_ref.shape
-    group = TILE // share
-    for j in range(buf_ref.shape[1] // TILE):
-        grad = tdot(buf_ref[:, j * TILE : (j + 1) * TILE], d_pre_ref[...], 0, 0)
-        out_ref[j * group : (j + 1) * group] = grad.astype(BF).reshape(group, share, slab)
-
-
-def tail_kernel(recv_ref, out_ref):
-    n_batch, n_proto, _, slab = recv_ref.shape
+
+
+def tail_kernel(total_rows, recv_ref, out_ref, gain_ref, bias_ref, loss_ref):
+    n_batch, n_proto, height, _ = recv_ref.shape
+    share = out_ref.shape[0]
+    chunks = height // share
+    lines = jnp.zeros((8, LANES), F32)
     for p in range(n_proto):
         acc = recv_ref[0, p].astype(F32)
         for b in range(1, n_batch):
             acc += recv_ref[b, p].astype(F32)
-        out_ref[:, p * slab : (p + 1) * slab] = acc
+        for h in range(chunks):
+            at = (p * chunks + h) * LANES
+            out_ref[:, at : at + LANES] = acc[h * share : (h + 1) * share, :]
+        sums = recv_ref[0, p, chunks * share :, :].astype(F32)
+        for h in range(chunks):
+            at = p * chunks + h
+            gain_ref[at : at + 1, :] = sums[h : h + 1] + sums[chunks + h : chunks + h + 1]
+            bias_ref[at : at + 1, :] = sums[2 * chunks + h : 2 * chunks + h + 1] + sums[3 * chunks + h : 3 * chunks + h + 1]
+        lines += recv_ref[1, p, chunks * share :, :].astype(F32)
+    hits = lines[0:1] + (lines[2:3] + lines[4:5])
+    logs = (lines[1:2] + (lines[3:4] + lines[5:6])) / n_proto
+    loss = jnp.sum(logs - hits, axis=1, keepdims=True) / total_rows
+    loss_ref[...] = jnp.broadcast_to(loss, loss_ref.shape)
 
 
 def stage_kernel(order_ref, in0_ref, in1_ref, in2_ref, in3_ref, out0_ref, out1_ref, out2_ref, out3_ref, sum_ref):
@@ -397,20 +438,6 @@
         height = out.shape[0]
         at = pl.multiple_of(lax.rem(order_ref[10] + d, len(outs)) * height, height)
         out[...] = sum_ref[pl.ds(at, height), :]
-
-
-def sums_kernel(total_rows, order_ref, *rest):
-    shown = rest[:-3]
-    gain_ref, bias_ref, loss_ref = rest[-3:]
-    n_proto = len(shown)
-    hits = jnp.zeros((1, LANES), F32)
-    for d, ref in enumerate(shown):
-        at = pl.ds(lax.rem(order_ref[0] + n_proto - d, n_proto), 1)
-        gain_ref[at, :] = ref[0:1, :]
-        bias_ref[at, :] = ref[1:2, :]
-        hits += ref[2:3, :LANES]
-    loss = jnp.sum(shown[0][2:3, LANES:] - hits, axis=1, keepdims=True) / total_rows
-    loss_ref[...] = jnp.broadcast_to(loss, loss_ref.shape)
 
 
 def shape(dims, kind=F32):
@@ -603,6 +630,7 @@
             pltpu.VMEM((cols, width), BF),
             pltpu.VMEM((width, cols), BF),
             pltpu.VMEM((width, cols), BF),
+            pltpu.VMEM((2 * TILE, width), BF),
             pltpu.SemaphoreType.DMA((4,)),
         ],
         name="final_kernel",
@@ -634,10 +662,10 @@
                 whole((rows, slab)),
                 whole((rows, slab)),
                 whole((rows, slab)),
-                whole((16, LANES)),
+                pl.BlockSpec(memory_space=pltpu.HBM),
             ],
             out_specs=[whole((rows, slab)), whole((n_batch, 2 * slab // n_batch, width))],
-            scratch_shapes=[pltpu.VMEM((8, slab), F32)],
+            scratch_shapes=[pltpu.VMEM((8, slab), F32), pltpu.VMEM((16, LANES), F32), pltpu.SemaphoreType.DMA((1,))],
         ),
         out_shape=[shape((rows, slab)), shape((n_batch, 2 * slab // n_batch, width), BF)],
         compiler_params=PARAMS,
@@ -646,29 +674,23 @@
     recv = deal(msg, "batch")
 
     share = d_in // (n_batch * n_proto)
-    first, sums, second = pl.pallas_call(
+    lines = slab // LANES * share + 8
+    first, second = pl.pallas_call(
         lambda *refs: first_kernel(total_rows, *refs),
         grid_spec=pltpu.PrefetchScalarGridSpec(
             num_scalar_prefetch=1,
             grid=(1,),
             in_specs=[whole(recv.shape), whole((rows, slab)), whole((rows, slab)), stat_spec, stat_spec]
-            + [anywhere] * len(parts),
-            out_specs=[
-                whole((n_batch * n_proto, share, slab)),
-                whole((8, slab)),
-                whole((slab // n_batch, width)),
-            ],
+            + [whole(piece.shape) for piece in parts],
+            out_specs=[pl.BlockSpec(memory_space=pltpu.HBM), whole((slab // n_batch, width))],
             scratch_shapes=[
                 pltpu.VMEM((rows, slab), BF),
-                pltpu.VMEM((rows, d_in), BF),
-                pltpu.SemaphoreType.DMA((len(parts),)),
+                pltpu.VMEM((n_batch * n_proto, lines, LANES), BF),
+                pltpu.SemaphoreType.DMA((d_in // TILE,)),
             ],
         ),
-        out_shape=[
-            shape((n_batch * n_proto, share, slab), BF),
-            shape((8, slab)),
-            shape((slab // n_batch, width)),
-        ],
+        out_shape=[shape((n_batch * n_proto, lines, LANES), BF), shape((slab // n_batch, width))],
+        compiler_params=PARAMS,
         name="first_kernel",
     )(order, recv, shift, normed, inv, gain, *parts)
 
@@ -682,25 +704,18 @@
     )(order, *pieces)
     pieces = [pieces[0]] + [lax.ppermute(pieces[d], "batch", shifted(1, d)) for d in range(1, side)]
     grad_proto = sum(piece.astype(F32) for piece in pieces).T
-    first = deal(first, ("batch", "proto")).reshape(n_batch, n_proto, share, slab)
-    grad_first = pl.pallas_call(
-        tail_kernel, out_shape=shape((share, d_hid)), compiler_params=PARAMS, name="tail_kernel"
+    first = deal(first, ("batch", "proto")).reshape(n_batch, n_proto, lines, LANES)
+    grad_first, grad_gain, grad_bias, loss = pl.pallas_call(
+        lambda *refs: tail_kernel(total_rows, *refs),
+        out_shape=[shape((share, d_hid)), shape((hid_bands, LANES)), shape((hid_bands, LANES)), shape((1, LANES))],
+        compiler_params=PARAMS,
+        name="tail_kernel",
     )(first)
     grad_second = lax.ppermute(
         second,
         ("batch", "proto"),
         [(b * n_proto + p, p * n_batch + b) for b in range(n_batch) for p in range(n_proto)],
     )
-    shown = [sums] + [
-        hop(sums, [(i, (i + d) % n_proto) for i in range(n_proto)]) for d in range(1, n_proto)
-    ]
-    grad_gain, grad_bias, loss = pl.pallas_call(
-        lambda *refs: sums_kernel(total_rows, *refs),
-        in_specs=[pl.BlockSpec(memory_space=pltpu.SMEM)] + [pl.BlockSpec((8, slab), lambda: (0, 0))] * n_proto,
-        out_shape=[shape((n_proto, slab)), shape((n_proto, slab)), shape((1, LANES))],
-        compiler_params=PARAMS,
-        name="sums_kernel",
-    )(order, *shown)
     grad_gain = grad_gain.reshape(-1)
     grad_bias = grad_bias.reshape(-1)
     loss = loss[0, 0]

time: 246 us -> 239 us (0.972)
  the two profiles are of different devices: /device:TPU:0 before, /device:TPU:1 now
where the time goes in v5:
time: 239 us; the launch traced here: 237 us
  blocking collectives  83.9 us (35%)
  Pallas kernels  56.4 us (24%)
  starting transfers between devices  48.1 us (20%)
  waiting for transfers between devices  33.2 us (14%)
  local copies, waits for them, and re-layouts  12.7 us (5%)
    all_to_all x8, blocking collectives, deal(): return lax.all_to_all(x, axis, 0, 0, tiled=True)  83.9 us
    all_to_all x5, starting transfers between devices, deal(): return lax.all_to_all(x, axis, 0, 0, tiled=True)  30.2 us
    pallas_call x1, Pallas kernels, step_of_device(): pl.pallas_call(final_kernel, grid=(steps,), in_specs=[pl.BlockSpec(memory...  15 us
    all_to_all x5, waiting for transfers between devices, deal(): return lax.all_to_all(x, axis, 0, 0, tiled=True)  13.2 us
    unnamed x71, local copies, waits for them, and re-layouts  12 us
    ppermute x1, waiting for transfers between devices, step_of_device(): lax.ppermute(second, ('batch', 'proto'), [(b * n_proto + p, p * n_batch +...  9.99 us
    ppermute x9, waiting for transfers between devices, hop(): return lax.ppermute(x, 'proto', moves)  8.64 us
    pallas_call x1, Pallas kernels, step_of_device(): pl.pallas_call(slab_kernel, grid_spec=pltpu.PrefetchScalarGridSpec(num_sc...  7.75 us
  transfers between devices with their start and end apart: 21, of which 9 were waited for; matrix products, arithmetic and copies ran while one was open for 1% of the time, Pallas kernels for 13%

profile of v5, /device:TPU:1, one launch (start us, length us, event | category | flops | bytes accessed | tf_op | source)
XLA Modules:
  0.0 237.5 jit_solution(2097840260885036296)
XLA Ops:
  0.7 3.4 %collective-permute-start.1 = (bf16[128,2048]{1,0:T(8,128)(2,1)}, bf16[128,2048]{1,0:T(8,128)(2,1)S(1)}, u32[]{:S(2)}, u32[]{:S(2)}) collective-permute-start(bf16[128,2048]{1,0:T(8,128)(2,1)} %refs_6_.1), channel_id=1, source_target_pairs={{2,0},{3,1},{4,2},{5,3},{6,4},{7,5},{0,6},{1,7},{10,8},{11,9},{12,... | collective-permute-start | bytes 1572872 | tf_op jit(solution)/shard_map/ppermute | solution.py:465
  4.0 6.9 %pre_kernel.1 = (f32[128,2048]{1,0:T(8,128)}, f32[16,32,128]{2,1,0:T(8,128)}) custom-call(bf16[128,2048]{1,0:T(8,128)(2,1)} %refs_6_.1, bf16[2048,2048]{1,0:T(8,128)(2,1)} %w_hbm.3), custom_call_target="tpu_custom_call" | custom-call | tf_op jit(solution)/shard_map/pre_kernel/pallas_call | solution.py:488
  10.9 4.0 %collective-permute-done.1.rest_1_.refs_7_ = bf16[128,2048]{1,0:T(8,128)(2,1)S(1)} collective-permute-done((bf16[128,2048]{1,0:T(8,128)(2,1)}, bf16[128,2048]{1,0:T(8,128)(2,1)S(1)}, u32[]{:S(2)}, u32[]{:S(2)}) %collective-permute-start.1) | collective-permute-done | bytes 524320 | tf_op jit(solution)/shard_map/ppermute | solution.py:465
  14.9 3.0 %collective-permute-done.rest_2_.refs_8_ = bf16[128,2048]{1,0:T(8,128)(2,1)S(1)} collective-permute-done((bf16[128,2048]{1,0:T(8,128)(2,1)}, bf16[128,2048]{1,0:T(8,128)(2,1)S(1)}, u32[]{:S(2)}, u32[]{:S(2)}) %collective-permute-start) | collective-permute-done | bytes 524320 | tf_op jit(solution)/shard_map/ppermute | solution.py:465
  18.4 1.2 collective-permute-start.2
  19.6 7.8 %all-to-all-start = ((f32[16,32,128]{2,1,0:T(8,128)}), f32[16,32,128]{2,1,0:T(8,128)S(1)}, u32[]{:S(2)}, u32[]{:S(2)}) async-start(f32[16,32,128]{2,1,0:T(8,128)} %get-tuple-element.61), calls=%async_computation | async-start | bytes 524288 | tf_op jit(solution)/shard_map/all_to_all | solution.py:19
  28.6 6.1 %all-to-all-done.recv_ref = f32[16,32,128]{2,1,0:T(8,128)S(1)} async-done(((f32[16,32,128]{2,1,0:T(8,128)}), f32[16,32,128]{2,1,0:T(8,128)S(1)}, u32[]{:S(2)}, u32[]{:S(2)}) %all-to-all-start) | async-done | bytes 262176 | tf_op jit(solution)/shard_map/all_to_all | solution.py:19
  35.4 7.1 %all-to-all-start.1 = ((f32[8,32,128]{2,1,0:T(8,128)}), f32[8,32,128]{2,1,0:T(8,128)S(1)}, u32[]{:S(2)}, u32[]{:S(2)}) async-start(f32[8,32,128]{2,1,0:T(8,128)} %relay_kernel.1), calls=%async_computation.1 | async-start | bytes 262144 | tf_op jit(solution)/shard_map/all_to_all | solution.py:19
  43.2 3.9 %proto_kernel.1 = (bf16[2048,256]{1,0:T(8,128)(2,1)}, bf16[256,2048]{1,0:T(8,128)(2,1)}, bf16[256,2048]{1,0:T(8,128)(2,1)}) custom-call(bf16[2048,256]{1,0:T(8,128)(2,1)} %raw_ref), custom_call_target="tpu_custom_call" | custom-call | tf_op jit(solution)/shard_map/proto_kernel/pallas_call | solution.py:510
  48.4 4.0 %embed_kernel.1 = (f32[128,256]{1,0:T(8,128)}, f32[128,128]{1,0:T(8,128)}, f32[16,128]{1,0:T(8,128)}, f32[16,128]{1,0:T(8,128)}, bf16[8,128,256]{2,1,0:T(8,128)(2,1)}) custom-call(f32[128,2048]{1,0:T(8,128)} %get-tuple-element.62.refs_0_, f32[8,32,128]{2,1,0:T(8,128)} %copy-done.33, f32[16,128]{1,0:T(8,128)} %bitcast.27, f32[16,128]{1,0:T(8,128)} %bitcast.31, ...), custom_call_target="tpu_custom_call" | custom-call | tf_op jit(solution)/shard_map/embed_kernel/pallas_call | solution.py:516
  52.4 4.3 %all-to-all-start.2 = ((bf16[8,128,256]{2,1,0:T(8,128)(2,1)}), bf16[8,128,256]{2,1,0:T(8,128)(2,1)S(1)}, u32[]{:S(2)}, u32[]{:S(2)}) async-start(bf16[8,128,256]{2,1,0:T(8,128)(2,1)} %get-tuple-element.72), calls=%async_computation.2 | async-start | bytes 1048576 | tf_op jit(solution)/shard_map/all_to_all | solution.py:19
  57.2 1.2 collective-permute-done.7.rest_8_.refs_14_
  59.5 7.7 %slab_kernel.1 = (bf16[1024,256]{1,0:T(8,128)(2,1)}, bf16[1024,256]{1,0:T(8,128)(2,1)}, bf16[1024,256]{1,0:T(8,128)(2,1)}) custom-call(s32[11]{0:T(128)} %stack.47.order_ref.refs_0_, f32[16,128]{1,0:T(8,128)} %get-tuple-element.73.mean_ref, f32[16,128]{1,0:T(8,128)} %get-tuple-element.74.inv_ref.refs_4_, f32[16,128]{1,0:T(8,128)} %bitcast.28, ...), custom_call_target="tpu_custom_call" | custom-call | tf_op jit(solution)/shard_map/slab_kernel/pallas_call | solution.py:537
  67.3 2.9 %score_kernel.1 = (bf16[1024,2048]{1,0:T(8,128)(2,1)S(1)}, f32[16,16,128]{2,1,0:T(8,128)S(1)}, f32[8,128]{1,0:T(8,128)S(1)}) custom-call(bf16[1024,256]{1,0:T(8,128)(2,1)S(1)} %bitcast.25, bf16[256,2048]{1,0:T(8,128)(2,1)S(1)} %copy-done.3), custom_call_target="tpu_custom_call" | custom-call | tf_op jit(solution)/shard_map/score_kernel/pallas_call | solution.py:556
  70.2 9.9 %all_to_all.65.recv_ref = f32[16,16,128]{2,1,0:T(8,128)S(1)} all-to-all(f32[16,16,128]{2,1,0:T(8,128)S(1)} %get-tuple-element.85), channel_id=1, replica_groups=mesh['batch'=16,'proto'=8] {'batch'}, dimensions={0} | all-to-all | bytes 262144 | tf_op jit(solution)/shard_map/all_to_all | solution.py:19
  80.2 1.2 row_kernel.3
  81.4 10.9 %all_to_all.66.recv_ref.recv_soft_ref = f32[8,16,128]{2,1,0:T(8,128)S(1)} all-to-all(f32[8,16,128]{2,1,0:T(8,128)S(1)} %row_kernel.3), channel_id=1, replica_groups=mesh['batch'=16,'proto'=8] {'proto'}, dimensions={0} | all-to-all | bytes 131072 | tf_op jit(solution)/shard_map/all_to_all | solution.py:19
  92.3 1.2 col_kernel.2
  93.4 9.9 %all_to_all.67.recv_ref = f32[16,16,128]{2,1,0:T(8,128)S(1)} all-to-all(f32[16,16,128]{2,1,0:T(8,128)S(1)} %col_kernel.2), channel_id=1, replica_groups=mesh['batch'=16,'proto'=8] {'batch'}, dimensions={0} | all-to-all | bytes 262144 | tf_op jit(solution)/shard_map/all_to_all | solution.py:19
  103.3 1.2 row_kernel.4
  104.5 9.2 %all_to_all.68.recv_ref = f32[8,8,128]{2,1,0:T(8,128)S(1)} all-to-all(f32[8,8,128]{2,1,0:T(8,128)S(1)} %row_kernel.4), channel_id=1, replica_groups=mesh['batch'=16,'proto'=8] {'proto'}, dimensions={0} | all-to-all | bytes 65536 | tf_op jit(solution)/shard_map/all_to_all | solution.py:19
  113.8 1.2 col_kernel.3
  114.9 9.9 %all_to_all.69.recv_ref.recv_col_ref = f32[16,16,128]{2,1,0:T(8,128)S(1)} all-to-all(f32[16,16,128]{2,1,0:T(8,128)S(1)} %col_kernel.3), channel_id=1, replica_groups=mesh['batch'=16,'proto'=8] {'batch'}, dimensions={0} | all-to-all | bytes 262144 | tf_op jit(solution)/shard_map/all_to_all | solution.py:19
  124.9 1.2 row_kernel.5
  126.1 10.0 %all_to_all.70.recv_row_ref = f32[8,8,128]{2,1,0:T(8,128)} all-to-all(f32[8,8,128]{2,1,0:T(8,128)S(1)} %row_kernel.5), channel_id=1, replica_groups=mesh['batch'=16,'proto'=8] {'proto'}, dimensions={0} | all-to-all | bytes 65536 | tf_op jit(solution)/shard_map/all_to_all | solution.py:19
  136.0 15.0 %final_kernel.1 = (bf16[1024,256]{1,0:T(8,128)(2,1)}, bf16[64,2048]{1,0:T(8,128)(2,1)}, bf16[64,2048]{1,0:T(8,128)(2,1)}, bf16[64,2048]{1,0:T(8,128)(2,1)}, bf16[64,2048]{1,0:T(8,128)(2,1)}, /*index=5*/f32[16,128]{1,0:T(8,128)}) custom-call(s32[11]{0:T(128)} %stack.47.order_ref.refs_0_, bf16[1024,256]{1,0:T(8,128)(2,1)} %bitcast.26, ...), custom_call_target="tpu_custom_call" | custom-call | tf_op jit(solution)/shard_map/final_kernel/pallas_call | solution.py:605
  151.1 13.6 %all_to_all.71.recv_ref = bf16[8,128,256]{2,1,0:T(8,128)(2,1)S(1)} all-to-all(bf16[8,128,256]{2,1,0:T(8,128)(2,1)} %bitcast.30), channel_id=1, replica_groups=mesh['batch'=16,'proto'=8] {'proto'}, dimensions={0} | all-to-all | bytes 1048576 | tf_op jit(solution)/shard_map/all_to_all | solution.py:19
  166.6 5.1 %all-to-all-start.10 = ((bf16[8,128,256]{2,1,0:T(8,128)(2,1)}), bf16[8,128,256]{2,1,0:T(8,128)(2,1)}, u32[]{:S(2)}, u32[]{:S(2)}) async-start(bf16[8,128,256]{2,1,0:T(8,128)(2,1)} %copy-done.14), calls=%async_computation.10 | async-start | bytes 1048576 | tf_op jit(solution)/shard_map/all_to_all | solution.py:19
  171.8 1.9 collective-permute-start.10
  173.7 1.0 collective-permute-start.11
  174.7 6.4 %all-to-all-done.10.d_embed_ref = bf16[8,128,256]{2,1,0:T(8,128)(2,1)} async-done(((bf16[8,128,256]{2,1,0:T(8,128)(2,1)}), bf16[8,128,256]{2,1,0:T(8,128)(2,1)}, u32[]{:S(2)}, u32[]{:S(2)}) %all-to-all-start.10) | async-done | bytes 524320 | tf_op jit(solution)/shard_map/all_to_all | solution.py:19
  181.1 1.0 copy-done.13
  182.2 1.0 copy-done.25
  183.2 1.0 copy-done.26
  185.6 2.1 shift_kernel.1
  187.7 10.6 %all_to_all.72.refs_1_ = bf16[16,32,256]{2,1,0:T(8,128)(2,1)S(1)} all-to-all(bf16[16,32,256]{2,1,0:T(8,128)(2,1)S(1)} %get-tuple-element.95), channel_id=1, replica_groups=mesh['batch'=16,'proto'=8] {'batch'}, dimensions={0} | all-to-all | bytes 524288 | tf_op jit(solution)/shard_map/all_to_all | solution.py:19
  198.3 1.0 copy-done.12
  199.4 0.9 copy-done.19
  200.3 0.9 copy-done.21
  202.2 4.0 %first_kernel.1 = (bf16[128,40,128]{2,1,0:T(8,128)(2,1)}, f32[16,256]{1,0:T(8,128)S(1)}) custom-call(s32[11]{0:T(128)S(1)} %copy-done.31, bf16[16,32,256]{2,1,0:T(8,128)(2,1)S(1)} %all_to_all.72.refs_1_, f32[1024,256]{1,0:T(8,128)S(1)} %get-tuple-element.96.refs_2_, bf16[1024,256]{1,0:T(8,128)(2,1)S(1)} %copy-done.13, f32[16,128]{1,0:T(8,128)S(1)} %copy-done.30, ...), custom_call_target="tpu_custom_call" | custom-call | tf_op jit(solution)/shard_map/first_kernel/pallas_call | solution.py:678
  206.3 6.0 %all-to-all-start.12 = ((bf16[128,40,128]{2,1,0:T(8,128)(2,1)}), bf16[128,40,128]{2,1,0:T(8,128)(2,1)S(1)}, u32[]{:S(2)}, u32[]{:S(2)}) async-start(bf16[128,40,128]{2,1,0:T(8,128)(2,1)} %get-tuple-element.102), calls=%async_computation.12 | async-start | bytes 2621440 | tf_op jit(solution)/shard_map/all_to_all | solution.py:19
  212.3 2.1 stage_kernel.1
  214.4 1.5 collective-permute-start.13
  215.9 2.9 %collective-permute-start.14 = (bf16[16,2048]{1,0:T(8,128)(2,1)}, bf16[16,2048]{1,0:T(8,128)(2,1)S(1)}, u32[]{:S(2)}, u32[]{:S(2)}) collective-permute-start(bf16[16,2048]{1,0:T(8,128)(2,1)} %get-tuple-element.113), channel_id=1, source_target_pairs={{0,16},{8,24},{16,0},{24,8},{32,48},{40,56},{48,32},{56,40},{64,80... | collective-permute-start | bytes 196616 | tf_op jit(solution)/shard_map/ppermute | solution.py:705
  219.7 3.4 %collective-permute-start.12 = (f32[16,256]{1,0:T(8,128)S(1)}, f32[16,256]{1,0:T(8,128)S(1)}, u32[]{:S(2)}, u32[]{:S(2)}) collective-permute-start(f32[16,256]{1,0:T(8,128)S(1)} %get-tuple-element.104), channel_id=1, source_target_pairs={{0,0},{1,16},{2,32},{3,48},{4,64},{5,80},{6,96},{7,112},{8,1},{9,1... | collective-permute-start | bytes 49160 | tf_op jit(solution)/shard_map/ppermute | solution.py:714
  223.2 10.0 %collective-permute-done.12 = f32[16,256]{1,0:T(8,128)S(1)} collective-permute-done((f32[16,256]{1,0:T(8,128)S(1)}, f32[16,256]{1,0:T(8,128)S(1)}, u32[]{:S(2)}, u32[]{:S(2)}) %collective-permute-start.12) | collective-permute-done | bytes 16416 | tf_op jit(solution)/shard_map/ppermute | solution.py:714
  233.1 1.4 collective-permute-done.14
  234.5 1.5 add_bitcast_fusion
  (95 shorter events, 12.8 us)
Async XLA Ops:
  0.6 41.9 %copy-start = (bf16[128,2048]{1,0:T(8,128)(2,1)S(1)}, bf16[128,2048]{1,0:T(8,128)(2,1)}, u32[]{:S(2)}) copy-start(bf16[128,2048]{1,0:T(8,128)(2,1)} %refs_6_.1) | copy-start | bytes 1572868
  0.6 27.3 %copy-start.34 = (s32[1024]{0:T(1024)S(1)}, s32[1024]{0:T(1024)}, u32[]{:S(2)}) copy-start(s32[1024]{0:T(1024)} %param.13) | copy-start | bytes 12292
  0.7 14.3 %collective-permute-start.1 = (bf16[128,2048]{1,0:T(8,128)(2,1)}, bf16[128,2048]{1,0:T(8,128)(2,1)S(1)}, u32[]{:S(2)}, u32[]{:S(2)}) collective-permute-start(bf16[128,2048]{1,0:T(8,128)(2,1)} %refs_6_.1), channel_id=1, source_target_pairs={{2,0},{3,1},{4,2},{5,3},{6,4},{7,5},{0,6},{1,7},{10,8},{11,9},{12,... | collective-permute-start | bytes 1572872 | tf_op jit(solution)/shard_map/ppermute | solution.py:465
  4.0 13.9 %collective-permute-start = (bf16[128,2048]{1,0:T(8,128)(2,1)}, bf16[128,2048]{1,0:T(8,128)(2,1)S(1)}, u32[]{:S(2)}, u32[]{:S(2)}) collective-permute-start(bf16[128,2048]{1,0:T(8,128)(2,1)} %refs_6_.1), channel_id=1, source_target_pairs={{0,2},{1,3},{2,4},{3,5},{4,6},{5,7},{6,0},{7,1},{8,10},{9,11},{10,... | collective-permute-start | bytes 1572872 | tf_op jit(solution)/shard_map/ppermute | solution.py:465
  14.9 44.6 %copy-start.5 = (bf16[128,2048]{1,0:T(8,128)(2,1)}, bf16[128,2048]{1,0:T(8,128)(2,1)S(1)}, u32[]{:S(2)}) copy-start(bf16[128,2048]{1,0:T(8,128)(2,1)S(1)} %collective-permute-done.1.rest_1_.refs_7_) | copy-start | bytes 1572868
  18.0 41.6 %copy-start.7 = (bf16[128,2048]{1,0:T(8,128)(2,1)}, bf16[128,2048]{1,0:T(8,128)(2,1)S(1)}, u32[]{:S(2)}) copy-start(bf16[128,2048]{1,0:T(8,128)(2,1)S(1)} %collective-permute-done.rest_2_.refs_8_) | copy-start | bytes 1572868
  18.0 16.6 %collective-permute-start.3 = (bf16[64,2048]{1,0:T(8,128)(2,1)S(1)}, bf16[64,2048]{1,0:T(8,128)(2,1)S(1)}, u32[]{:S(2)}, u32[]{:S(2)}) collective-permute-start(bf16[64,2048]{1,0:T(8,128)(2,1)S(1)} %slice.10), channel_id=1, source_target_pairs={{2,0},{3,1},{4,2},{5,3},{6,4},{7,5},{0,6},{1,7},{10,8},{11,9},{12,... | collective-permute-start | bytes 786440 | tf_op jit(solution)/shard_map/ppermute | solution.py:465
  18.4 16.3 %collective-permute-start.2 = (bf16[64,2048]{1,0:T(8,128)(2,1)S(1)}, bf16[64,2048]{1,0:T(8,128)(2,1)S(1)}, u32[]{:S(2)}, u32[]{:S(2)}) collective-permute-start(bf16[64,2048]{1,0:T(8,128)(2,1)S(1)} %slice.9), channel_id=1, source_target_pairs={{0,2},{1,3},{2,4},{3,5},{4,6},{5,7},{6,0},{7,1},{8,10},{9,11},{10,... | collective-permute-start | bytes 786440 | tf_op jit(solution)/shard_map/ppermute | solution.py:465
  19.6 15.1 %all-to-all-start = ((f32[16,32,128]{2,1,0:T(8,128)}), f32[16,32,128]{2,1,0:T(8,128)S(1)}, u32[]{:S(2)}, u32[]{:S(2)}) async-start(f32[16,32,128]{2,1,0:T(8,128)} %get-tuple-element.61), calls=%async_computation | async-start | bytes 524288 | tf_op jit(solution)/shard_map/all_to_all | solution.py:19
  34.7 24.9 %copy-start.16 = (bf16[64,2048]{1,0:T(8,128)(2,1)}, bf16[64,2048]{1,0:T(8,128)(2,1)S(1)}, u32[]{:S(2)}) copy-start(bf16[64,2048]{1,0:T(8,128)(2,1)S(1)} %collective-permute-done.3.rest_4_.refs_10_) | copy-start | bytes 786436
  34.7 17.8 %copy-start.18 = (bf16[64,2048]{1,0:T(8,128)(2,1)}, bf16[64,2048]{1,0:T(8,128)(2,1)S(1)}, u32[]{:S(2)}) copy-start(bf16[64,2048]{1,0:T(8,128)(2,1)S(1)} %collective-permute-done.2.rest_3_.refs_9_) | copy-start | bytes 786436
  35.4 12.3 %all-to-all-start.1 = ((f32[8,32,128]{2,1,0:T(8,128)}), f32[8,32,128]{2,1,0:T(8,128)S(1)}, u32[]{:S(2)}, u32[]{:S(2)}) async-start(f32[8,32,128]{2,1,0:T(8,128)} %relay_kernel.1), calls=%async_computation.1 | async-start | bytes 262144 | tf_op jit(solution)/shard_map/all_to_all | solution.py:19
  42.5 14.7 %collective-permute-start.4 = (bf16[128,2048]{1,0:T(8,128)(2,1)S(1)}, bf16[128,2048]{1,0:T(8,128)(2,1)S(1)}, u32[]{:S(2)}, u32[]{:S(2)}) collective-permute-start(bf16[128,2048]{1,0:T(8,128)(2,1)S(1)} %copy-done), channel_id=1, source_target_pairs={{0,1},{1,0},{2,3},{3,2},{4,5},{5,4},{6,7},{7,6},{8,9},{9,8},{10,11... | collective-permute-start | bytes 1572872 | tf_op jit(solution)/shard_map/ppermute | solution.py:465
  42.7 14.5 %collective-permute-start.5 = (bf16[128,2048]{1,0:T(8,128)(2,1)S(1)}, bf16[128,2048]{1,0:T(8,128)(2,1)S(1)}, u32[]{:S(2)}, u32[]{:S(2)}) collective-permute-start(bf16[128,2048]{1,0:T(8,128)(2,1)S(1)} %collective-permute-done.1.rest_1_.refs_7_), channel_id=1, source_target_pairs={{0,1},{1,0},{2,3},{3,2},{4,5},{5,4},{6,7},{7,6},{8,9},{9,8},{10,11... | collective-permute-start | bytes 1572872 | tf_op jit(solution)/shard_map/ppermute | solution.py:465
  43.0 14.2 %collective-permute-start.6 = (bf16[128,2048]{1,0:T(8,128)(2,1)S(1)}, bf16[128,2048]{1,0:T(8,128)(2,1)}, u32[]{:S(2)}, u32[]{:S(2)}) collective-permute-start(bf16[128,2048]{1,0:T(8,128)(2,1)S(1)} %collective-permute-done.rest_2_.refs_8_), channel_id=1, source_target_pairs={{0,1},{1,0},{2,3},{3,2},{4,5},{5,4},{6,7},{7,6},{8,9},{9,8},{10,11... | collective-permute-start | bytes 1572872 | tf_op jit(solution)/shard_map/ppermute | solution.py:465
  52.4 14.9 %all-to-all-start.2 = ((bf16[8,128,256]{2,1,0:T(8,128)(2,1)}), bf16[8,128,256]{2,1,0:T(8,128)(2,1)S(1)}, u32[]{:S(2)}, u32[]{:S(2)}) async-start(bf16[8,128,256]{2,1,0:T(8,128)(2,1)} %get-tuple-element.72), calls=%async_computation.2 | async-start | bytes 1048576 | tf_op jit(solution)/shard_map/all_to_all | solution.py:19
  56.7 1.7 collective-permute-start.7
  56.9 1.9 collective-permute-start.8
  57.2 1.6 copy-start.9
  57.2 1.6 copy-start.11
  59.5 7.8 %copy-start.3 = (bf16[256,2048]{1,0:T(8,128)(2,1)S(1)}, bf16[256,2048]{1,0:T(8,128)(2,1)}, u32[]{:S(2)}) copy-start(bf16[256,2048]{1,0:T(8,128)(2,1)} %get-tuple-element.82.proto_t_hbm) | copy-start | bytes 3145732
  67.3 26.1 %copy-start.2 = (bf16[8,128,256]{2,1,0:T(8,128)(2,1)}, bf16[8,128,256]{2,1,0:T(8,128)(2,1)S(1)}, u32[]{:S(2)}) copy-start(bf16[8,128,256]{2,1,0:T(8,128)(2,1)S(1)} %all-to-all-done.2) | copy-start | bytes 1572868
  92.2 12.3 %copy-start.24 = (f32[8,16,128]{2,1,0:T(8,128)}, f32[8,16,128]{2,1,0:T(8,128)S(1)}, u32[]{:S(2)}) copy-start(f32[8,16,128]{2,1,0:T(8,128)S(1)} %all_to_all.66.recv_ref.recv_soft_ref) | copy-start | bytes 196612
  124.9 11.2 %copy-start.15 = (f32[16,16,128]{2,1,0:T(8,128)}, f32[16,16,128]{2,1,0:T(8,128)S(1)}, u32[]{:S(2)}) copy-start(f32[16,16,128]{2,1,0:T(8,128)S(1)} %all_to_all.69.recv_ref.recv_col_ref) | copy-start | bytes 393220
  124.9 39.9 %copy-start.27 = (f32[128,256]{1,0:T(8,128)S(1)}, f32[128,256]{1,0:T(8,128)}, u32[]{:S(2)}) copy-start(f32[128,256]{1,0:T(8,128)} %get-tuple-element.89.unit_ref) | copy-start | bytes 393220
  126.1 55.1 %copy-start.4 = (bf16[2048,256]{1,0:T(8,128)(2,1)S(1)}, bf16[2048,256]{1,0:T(8,128)(2,1)}, u32[]{:S(2)}) copy-start(bf16[2048,256]{1,0:T(8,128)(2,1)} %w2_ref.1) | copy-start | bytes 3145732
  136.0 62.3 %copy-start.30 = (f32[16,128]{1,0:T(8,128)S(1)}, f32[16,128]{1,0:T(8,128)}, u32[]{:S(2)}) copy-start(f32[16,128]{1,0:T(8,128)} %get-tuple-element.74.inv_ref.refs_4_) | copy-start | bytes 24580
  151.1 47.2 %copy-start.1 = (bf16[128,2048]{1,0:T(8,128)(2,1)S(1)}, bf16[128,2048]{1,0:T(8,128)(2,1)}, u32[]{:S(2)}) copy-start(bf16[128,2048]{1,0:T(8,128)(2,1)} %refs_6_.1) | copy-start | bytes 1572868
  151.1 47.2 %copy-start.6 = (bf16[128,2048]{1,0:T(8,128)(2,1)S(1)}, bf16[128,2048]{1,0:T(8,128)(2,1)}, u32[]{:S(2)}) copy-start(bf16[128,2048]{1,0:T(8,128)(2,1)} %copy-done.5) | copy-start | bytes 1572868
  151.1 47.2 %copy-start.8 = (bf16[128,2048]{1,0:T(8,128)(2,1)S(1)}, bf16[128,2048]{1,0:T(8,128)(2,1)}, u32[]{:S(2)}) copy-start(bf16[128,2048]{1,0:T(8,128)(2,1)} %copy-done.7) | copy-start | bytes 1572868
  151.1 47.2 %copy-start.10 = (bf16[128,2048]{1,0:T(8,128)(2,1)S(1)}, bf16[128,2048]{1,0:T(8,128)(2,1)}, u32[]{:S(2)}) copy-start(bf16[128,2048]{1,0:T(8,128)(2,1)} %copy-done.9) | copy-start | bytes 1572868
  151.1 47.2 %copy-start.17 = (bf16[64,2048]{1,0:T(8,128)(2,1)S(1)}, bf16[64,2048]{1,0:T(8,128)(2,1)}, u32[]{:S(2)}) copy-start(bf16[64,2048]{1,0:T(8,128)(2,1)} %copy-done.16) | copy-start | bytes 786436
  151.1 47.2 %copy-start.28 = (f32[2048]{0:T(1024)S(1)}, f32[2048]{0:T(1024)}, u32[]{:S(2)}) copy-start(f32[2048]{0:T(1024)} %param.9) | copy-start | bytes 24580
  166.6 14.5 %all-to-all-start.10 = ((bf16[8,128,256]{2,1,0:T(8,128)(2,1)}), bf16[8,128,256]{2,1,0:T(8,128)(2,1)}, u32[]{:S(2)}, u32[]{:S(2)}) async-start(bf16[8,128,256]{2,1,0:T(8,128)(2,1)} %copy-done.14), calls=%async_computation.10 | async-start | bytes 1048576 | tf_op jit(solution)/shard_map/all_to_all | solution.py:19
  171.6 34.6 %collective-permute-start.9 = (bf16[64,2048]{1,0:T(8,128)(2,1)}, bf16[64,2048]{1,0:T(8,128)(2,1)}, u32[]{:S(2)}, u32[]{:S(2)}) collective-permute-start(bf16[64,2048]{1,0:T(8,128)(2,1)} %get-tuple-element.99), channel_id=1, source_target_pairs={{0,32},{8,40},{16,48},{24,56},{32,64},{40,72},{48,80},{56,88},{64,... | collective-permute-start | bytes 786440 | tf_op jit(solution)/shard_map/ppermute | solution.py:647
  171.8 34.4 %collective-permute-start.10 = (bf16[64,2048]{1,0:T(8,128)(2,1)}, bf16[64,2048]{1,0:T(8,128)(2,1)}, u32[]{:S(2)}, u32[]{:S(2)}) collective-permute-start(bf16[64,2048]{1,0:T(8,128)(2,1)} %get-tuple-element.100), channel_id=1, source_target_pairs={{0,64},{8,72},{16,80},{24,88},{32,96},{40,104},{48,112},{56,120},{... | collective-permute-start | bytes 786440 | tf_op jit(solution)/shard_map/ppermute | solution.py:647
  173.7 32.5 %collective-permute-start.11 = (bf16[64,2048]{1,0:T(8,128)(2,1)}, bf16[64,2048]{1,0:T(8,128)(2,1)}, u32[]{:S(2)}, u32[]{:S(2)}) collective-permute-start(bf16[64,2048]{1,0:T(8,128)(2,1)} %get-tuple-element.101), channel_id=1, source_target_pairs={{0,96},{8,104},{16,112},{24,120},{32,0},{40,8},{48,16},{56,24},{64... | collective-permute-start | bytes 786440 | tf_op jit(solution)/shard_map/ppermute | solution.py:647
  181.1 1.0 copy-start.13
  182.2 1.0 copy-start.25
  183.2 1.0 copy-start.26
  198.3 1.0 copy-start.12
  199.4 0.9 copy-start.19
  200.3 0.9 copy-start.21
  206.3 29.8 %all-to-all-start.12 = ((bf16[128,40,128]{2,1,0:T(8,128)(2,1)}), bf16[128,40,128]{2,1,0:T(8,128)(2,1)S(1)}, u32[]{:S(2)}, u32[]{:S(2)}) async-start(bf16[128,40,128]{2,1,0:T(8,128)(2,1)} %get-tuple-element.102), calls=%async_computation.12 | async-start | bytes 2621440 | tf_op jit(solution)/shard_map/all_to_all | solution.py:19
  214.4 18.7 %collective-permute-start.13 = (bf16[16,2048]{1,0:T(8,128)(2,1)}, bf16[16,2048]{1,0:T(8,128)(2,1)S(1)}, u32[]{:S(2)}, u32[]{:S(2)}) collective-permute-start(bf16[16,2048]{1,0:T(8,128)(2,1)} %get-tuple-element.112), channel_id=1, source_target_pairs={{0,8},{8,16},{16,24},{24,0},{32,40},{40,48},{48,56},{56,32},{64,72... | collective-permute-start | bytes 196616 | tf_op jit(solution)/shard_map/ppermute | solution.py:705
  215.9 18.6 %collective-permute-start.14 = (bf16[16,2048]{1,0:T(8,128)(2,1)}, bf16[16,2048]{1,0:T(8,128)(2,1)S(1)}, u32[]{:S(2)}, u32[]{:S(2)}) collective-permute-start(bf16[16,2048]{1,0:T(8,128)(2,1)} %get-tuple-element.113), channel_id=1, source_target_pairs={{0,16},{8,24},{16,0},{24,8},{32,48},{40,56},{48,32},{56,40},{64,80... | collective-permute-start | bytes 196616 | tf_op jit(solution)/shard_map/ppermute | solution.py:705
  218.8 15.7 %collective-permute-start.15 = (bf16[16,2048]{1,0:T(8,128)(2,1)}, bf16[16,2048]{1,0:T(8,128)(2,1)S(1)}, u32[]{:S(2)}, u32[]{:S(2)}) collective-permute-start(bf16[16,2048]{1,0:T(8,128)(2,1)} %get-tuple-element.114), channel_id=1, source_target_pairs={{0,24},{8,0},{16,8},{24,16},{32,56},{40,32},{48,40},{56,48},{64,88... | collective-permute-start | bytes 196616 | tf_op jit(solution)/shard_map/ppermute | solution.py:705
  219.7 13.4 %collective-permute-start.12 = (f32[16,256]{1,0:T(8,128)S(1)}, f32[16,256]{1,0:T(8,128)S(1)}, u32[]{:S(2)}, u32[]{:S(2)}) collective-permute-start(f32[16,256]{1,0:T(8,128)S(1)} %get-tuple-element.104), channel_id=1, source_target_pairs={{0,0},{1,16},{2,32},{3,48},{4,64},{5,80},{6,96},{7,112},{8,1},{9,1... | collective-permute-start | bytes 49160 | tf_op jit(solution)/shard_map/ppermute | solution.py:714
  (8 other events, 6.0 us)

commit v6 on v5

--- a/solution.py
+++ b/solution.py
@@ -69,39 +69,42 @@
 
 
 def embed_kernel(
-    total_rows, pre_hbm, recv_ref, gain_ref, bias_ref, w2_hbm, unit_ref, scale_ref, mean_ref, inv_ref, msg_ref, hid_ref,
-    pre_ref, w2_ref, sems,
+    total_rows, pre_ref, recv_ref, gain_ref, bias_ref, w2_ref, unit_hbm, scale_hbm, mean_hbm, inv_hbm, msg_hbm,
+    hid_ref, unit_ref, scale_ref, mean_ref, inv_ref, bf_ref, sems,
 ):
-    pre_copy = pltpu.make_async_copy(pre_hbm, pre_ref, sems.at[0])
-    w2_copy = pltpu.make_async_copy(w2_hbm, w2_ref, sems.at[1])
-    pre_copy.start()
-    w2_copy.start()
     stats = jnp.sum(recv_ref[...], axis=0)
     half = stats.shape[0] // 2
     mean = stats[:half] / total_rows
     inv = lax.rsqrt(stats[half:] / total_rows - mean * mean + 1e-05)
     mean_ref[...] = mean
     inv_ref[...] = inv
-    pre_copy.wait()
     for j in range(half):
         normed = (pre_ref[:, lane(j)] - mean[j : j + 1]) * inv[j : j + 1]
         hid_ref[:, lane(j)] = jax.nn.gelu(normed * gain_ref[j : j + 1, :] + bias_ref[j : j + 1, :]).astype(BF)
-    w2_copy.wait()
     embed = jnp.dot(hid_ref[...], w2_ref[...], preferred_element_type=F32)
     scale = lax.rsqrt(jnp.sum(embed * embed, axis=1, keepdims=True) + 1e-06)
     unit = embed * scale
+    bf_ref[...] = unit.astype(BF)
     unit_ref[...] = unit
     scale_ref[...] = jnp.broadcast_to(scale, scale_ref.shape)
-    msg_ref[...] = jnp.broadcast_to(unit.astype(BF)[None], msg_ref.shape)
-
-
-def proto_kernel(raw_ref, proto_ref, proto_t_ref, raw_t_ref):
+    moves = [(bf_ref, msg_hbm.at[k]) for k in range(msg_hbm.shape[0])]
+    moves += [(unit_ref, unit_hbm), (scale_ref, scale_hbm), (mean_ref, mean_hbm), (inv_ref, inv_hbm)]
+    copies = [pltpu.make_async_copy(src, dst, sems.at[k]) for k, (src, dst) in enumerate(moves)]
+    for copy in copies:
+        copy.start()
+    for copy in copies:
+        copy.wait()
+
+
+def proto_kernel(raw_ref, proto_ref, proto_t_ref, raw_t_ref, norm_ref):
     for k in range(raw_ref.shape[0] // TILE):
         span = slice(k * TILE, (k + 1) * TILE)
         raw_t = raw_ref[span, :].T
         raw_t_ref[:, span] = raw_t
         wide = raw_t.astype(F32)
-        unit = (wide * lax.rsqrt(jnp.sum(wide * wide, axis=0, keepdims=True) + 1e-06)).astype(BF)
+        scale = lax.rsqrt(jnp.sum(wide * wide, axis=0, keepdims=True) + 1e-06)
+        norm_ref[:, span] = jnp.broadcast_to(scale, (8, TILE))
+        unit = (wide * scale).astype(BF)
         proto_t_ref[:, span] = unit
         proto_ref[span, :] = unit.T
 
@@ -191,12 +194,10 @@
 
 
 def final_kernel(
-    order_ref, embed_hbm, pair_ref, proto_t_hbm, proto_hbm, raw_t_hbm, recv_col_ref, recv_row_ref, recv_soft_ref,
+    order_ref, embed_ref, pair_ref, proto_t_ref, proto_ref, raw_t_ref, norm_ref, recv_col_ref, recv_row_ref, recv_soft_ref,
     d_unit_ref, piece0_ref, piece1_ref, piece2_ref, piece3_ref, loss_ref,
-    grad_ref, mate_ref, loss_acc_ref, col_ref, row_ref, soft_ref, embed_ref, proto_t_ref, proto_ref, raw_t_ref, term_ref, both_ref, sems,
+    grad_ref, mate_ref, loss_acc_ref, col_ref, row_ref, soft_ref, term_ref, both_ref,
 ):
-    pairs = ((embed_hbm, embed_ref), (proto_t_hbm, proto_t_ref), (proto_hbm, proto_ref), (raw_t_hbm, raw_t_ref))
-    copies = [pltpu.make_async_copy(src, dst, sems.at[k]) for k, (src, dst) in enumerate(pairs)]
     step = pl.program_id(0)
     rows = d_unit_ref.shape[0]
     cols = proto_t_ref.shape[1]
@@ -205,15 +206,11 @@
 
     @pl.when(step == 0)
     def _():
-        for copy in copies:
-            copy.start()
         loss_acc_ref[...] = jnp.zeros_like(loss_acc_ref)
         col_ref[...] = 10.0 / jnp.sum(recv_col_ref[...], axis=0)
         row_ref[...] = 1.0 / jnp.sum(recv_row_ref[:, :bands, :], axis=0)
         soft_ref[...] = jnp.sum(recv_soft_ref[:, bands:, :], axis=0)
         loss_acc_ref[8:16, :] = jnp.log(soft_ref[...])
-        copies[0].wait()
-        copies[1].wait()
 
     base = step * (rows // LANES)
     here = pl.ds(pl.multiple_of(step * rows, rows), rows)
@@ -243,25 +240,19 @@
             score = scores[:, lane(h)]
             loss_acc += fold_rows(target * score)
             grad_ref[here, lane(at)] = (jnp.exp2(score * (10.0 * LOG2_E)) * inv_soft - target).astype(BF)
-
-    @pl.when(step == 0)
-    def _():
-        copies[2].wait()
-
     d_unit_ref[...] = jnp.dot(grad_ref[here, :], proto_ref[...], preferred_element_type=F32).astype(BF)
     loss_acc_ref[0:8, :] += loss_acc
 
     @pl.when(step == pl.num_programs(0) - 1)
     def _():
-        copies[3].wait()
         embed_t = embed_ref[...].T
         for j in range(cols // TILE):
             span = slice(j * TILE, (j + 1) * TILE)
             raw = raw_t_ref[:, span].astype(F32)
-            scale = lax.rsqrt(jnp.sum(raw * raw, axis=0, keepdims=True) + 1e-06)
-            unit = raw * scale
+            scale = norm_ref[0:1, span]
             acc = jnp.dot(embed_t, grad_ref[:, span], preferred_element_type=F32)
-            term_ref[:, span] = ((acc - unit * jnp.sum(unit * acc, axis=0, keepdims=True)) * scale).astype(BF)
+            along = scale * scale * jnp.sum(raw * acc, axis=0, keepdims=True)
+            term_ref[:, span] = ((acc - raw * along) * scale).astype(BF)
         pieces = (piece0_ref, piece1_ref, piece2_ref, piece3_ref)
         for d, piece in enumerate(pieces):
             height = piece.shape[0]
@@ -290,41 +281,60 @@
 
 
 def slab_kernel(order_ref, mean_ref, inv_ref, gain_ref, bias_ref, w_hbm, *rest):
-    parts = rest[:-6]
-    normed_ref, slope_ref, hid_ref, buf_ref, w_ref, sems = rest[-6:]
+    parts = rest[:-9]
+    outs, bufs = rest[-9:-6], rest[-6:-3]
+    buf_ref, w_ref, sems = rest[-3:]
+    normed_ref, slope_ref, hid_ref = bufs
     rows, slab = normed_ref.shape
     at = pl.ds(pl.multiple_of(order_ref[0] * slab, slab), slab)
     w_copy = pltpu.make_async_copy(w_hbm.at[:, at], w_ref, sems.at[len(parts)])
     w_copy.start()
     copies = start_parts(parts, buf_ref, sems)
+    stops = [sum(part.shape[0] for part in parts[: k + 1]) for k in range(len(parts))]
     w_copy.wait()
     chunks = slab // LANES
     ones = jnp.ones((LANES, LANES), F32)
-    for g in range(2):
-        for copy in copies[g * len(parts) // 2 : (g + 1) * len(parts) // 2]:
-            copy.wait()
-        start = g * rows // 2
-        pre = jnp.dot(buf_ref[start : start + rows // 2, :], w_ref[...], preferred_element_type=F32)
+    done = 0
+    sends = []
+    for g in range(rows // TILE):
+        start = g * TILE
+        while done < len(parts) and (stops[done - 1] if done else 0) < start + TILE:
+            copies[done].wait()
+            done += 1
+        pre = jnp.dot(buf_ref[start : start + TILE, :], w_ref[...], preferred_element_type=F32)
         for h in range(chunks):
             at = pl.ds(order_ref[0] * chunks + h, 1)
             mean, inv, gain, bias = mean_ref[at, :], inv_ref[at, :], gain_ref[at, :], bias_ref[at, :]
-            for b in range(rows // 2 // LANES):
+            for b in range(TILE // LANES):
                 band = slice(start + b * LANES, start + (b + 1) * LANES)
                 normed = (pre[b * LANES : (b + 1) * LANES, lane(h)] - mean) * inv
                 hidden, back = jax.vjp(jax.nn.gelu, normed * gain + bias)
                 normed_ref[band, lane(h)] = normed.astype(BF)
                 slope_ref[band, lane(h)] = back(ones)[0].astype(BF)
                 hid_ref[band, lane(h)] = hidden.astype(BF)
+        span = slice(start, start + TILE)
+        for k, (buf, out) in enumerate(zip(bufs, outs)):
+            sends.append(
+                pltpu.make_async_copy(buf.at[span], out.at[span], sems.at[len(parts) + 1 + g * len(outs) + k])
+            )
+            sends[-1].start()
+    for send in sends:
+        send.wait()
 
 
 def shift_kernel(
-    order_ref, d_embed_ref, w2_ref, normed_ref, slope_ref, hid_ref, loss_hbm, shift_ref, msg_ref, sum_ref, loss_ref, sems
+    order_ref, d_embed_ref, w2_ref, normed_hbm, slope_hbm, hid_hbm, loss_hbm, shift_ref, msg_ref, sum_ref, loss_ref,
+    normed_ref, slope_ref, hid_ref, sems,
 ):
-    loss_copy = pltpu.make_async_copy(loss_hbm, loss_ref, sems.at[0])
-    loss_copy.start()
+    moves = ((slope_hbm, slope_ref), (normed_hbm, normed_ref), (hid_hbm, hid_ref), (loss_hbm, loss_ref))
+    copies = [pltpu.make_async_copy(src, dst, sems.at[k]) for k, (src, dst) in enumerate(moves)]
+    for copy in copies:
+        copy.start()
     n_blocks, own, _ = d_embed_ref.shape
     sum_ref[...] = jnp.zeros_like(sum_ref)
     gains = biases = second = None
+    for copy in copies:
+        copy.wait()
     for k in range(0, n_blocks, 2):
         d_embed = jnp.concatenate([d_embed_ref[order_ref[k + 1]], d_embed_ref[order_ref[k + 2]]], axis=0)
         band = slice(k * own, (k + 2) * own)
@@ -336,7 +346,6 @@
         gains = gain if gains is None else gains + gain
         biases = bias if biases is None else biases + bias
         second = part if second is None else second + part
-    loss_copy.wait()
     hits = jnp.sum(loss_ref[0:8, :], axis=0, keepdims=True)
     logs = jnp.sum(loss_ref[8:16, :], axis=0, keepdims=True)
     sum_ref[0:1, :] = gains
@@ -444,6 +453,14 @@
     return jax.ShapeDtypeStruct(dims, kind)
 
 
+def far_shape(dims, kind=F32):
+    return pltpu.HBM(dims, kind)
+
+
+def far(x):
+    return pltpu.with_memory_space_constraint(x, pltpu.HBM)
+
+
 def step_of_device(features, w_first, bn_gain, bn_bias, w_second, prototypes, pair):
     n_batch = lax.axis_size("batch")
     n_proto = lax.axis_size("proto")
@@ -500,57 +517,43 @@
     far_top = hop(near_left[: own // 2], right)
     far_low = hop(near_right[own // 2 :], left)
     got = deal(msg, "batch")
-    got, far_top, far_low, mate_row, order = lax.optimization_barrier((got, far_top, far_low, mate_row, order))
-    mine = [features, from_right, from_left, far_top, far_low]
-    parts = mine + [hop(piece, swap) for piece in mine]
+    got, mate_row, order = lax.optimization_barrier((got, mate_row, order))
     msg = pl.pallas_call(
         relay_kernel, out_shape=shape((n_proto, 2 * hid_bands, LANES)), compiler_params=PARAMS, name="relay_kernel"
     )(got)
-    raw, _ = lax.optimization_barrier((prototypes, msg))
-    proto_bf, proto_t, raw_t = pl.pallas_call(
-        proto_kernel,
-        out_shape=[shape((cols, width), BF), shape((width, cols), BF), shape((width, cols), BF)],
-        name="proto_kernel",
-    )(raw)
-    got, proto_bf, proto_t, raw_t = lax.optimization_barrier((deal(msg, "proto"), proto_bf, proto_t, raw_t))
+    got = deal(msg, "proto")
     unit_embed, embed_scale, mean, inv, msg = pl.pallas_call(
         lambda *refs: embed_kernel(total_rows, *refs),
-        in_specs=[anywhere, pl.BlockSpec((n_proto, 2 * hid_bands, LANES), lambda: (0, 0, 0))]
-        + [pl.BlockSpec((hid_bands, LANES), lambda: (0, 0))] * 2
-        + [anywhere],
+        out_specs=[pl.BlockSpec(memory_space=pltpu.HBM)] * 5,
         out_shape=[
-            shape((own, width)),
-            shape((own, LANES)),
-            shape((hid_bands, LANES)),
-            shape((hid_bands, LANES)),
-            shape((n_proto, own, width), BF),
+            far_shape((own, width)),
+            far_shape((own, LANES)),
+            far_shape((hid_bands, LANES)),
+            far_shape((hid_bands, LANES)),
+            far_shape((n_proto, own, width), BF),
         ],
         scratch_shapes=[
             pltpu.VMEM((own, d_hid), BF),
-            pltpu.VMEM((own, d_hid), F32),
-            pltpu.VMEM((d_hid, width), BF),
-            pltpu.SemaphoreType.DMA((2,)),
+            pltpu.VMEM((own, width), F32),
+            pltpu.VMEM((own, LANES), F32),
+            pltpu.VMEM((hid_bands, LANES), F32),
+            pltpu.VMEM((hid_bands, LANES), F32),
+            pltpu.VMEM((own, width), BF),
+            pltpu.SemaphoreType.DMA((n_proto + 4,)),
         ],
+        compiler_params=PARAMS,
         name="embed_kernel",
     )(pre, got, gain, bias, w_second)
-    stat_spec = whole((hid_bands, LANES))
-    normed, slope, hid = pl.pallas_call(
-        slab_kernel,
-        grid_spec=pltpu.PrefetchScalarGridSpec(
-            num_scalar_prefetch=1,
-            grid=(1,),
-            in_specs=[stat_spec] * 4 + [anywhere] * (1 + len(parts)),
-            out_specs=[whole((rows, slab))] * 3,
-            scratch_shapes=[
-                pltpu.VMEM((rows, d_in), BF),
-                pltpu.VMEM((d_in, slab), BF),
-                pltpu.SemaphoreType.DMA((len(parts) + 1,)),
-            ],
-        ),
-        out_shape=[shape((rows, slab), BF)] * 3,
-        name="slab_kernel",
-    )(order, mean, inv, gain, bias, w_first, *parts)
-    block_embed, normed, slope, hid = lax.optimization_barrier((deal(msg, "proto"), normed, slope, hid))
+    raw, *mine, _ = lax.optimization_barrier((prototypes, features, from_right, from_left, far_top, far_low, msg))
+    parts = mine + [hop(piece, swap) for piece in mine]
+    proto_bf, proto_t, raw_t, norm = pl.pallas_call(
+        proto_kernel,
+        out_shape=[shape((cols, width), BF), shape((width, cols), BF), shape((width, cols), BF), shape((8, cols))],
+        name="proto_kernel",
+    )(raw)
+    block_embed, proto_bf, proto_t, raw_t, norm, *parts = lax.optimization_barrier(
+        (deal(msg, "proto"), proto_bf, proto_t, raw_t, norm, *parts)
+    )
     block_embed = block_embed.reshape(rows, width)
 
     kern, col_msg, soft = pl.pallas_call(
@@ -566,7 +569,7 @@
         ],
         compiler_params=PARAMS,
         name="score_kernel",
-    )(block_embed, proto_t)
+    )(block_embed, far(proto_t))
 
     def row_pass(recv, extra):
         height = row_bands * (2 if extra else 1)
@@ -607,17 +610,20 @@
         grid=(steps,),
         in_specs=[
             pl.BlockSpec(memory_space=pltpu.SMEM),
-            anywhere,
+            whole((rows, width)),
             whole((row_bands, LANES)),
-            anywhere,
-            anywhere,
-            anywhere,
+            whole((width, cols)),
+            whole((cols, width)),
+            whole((width, cols)),
+            whole((8, cols)),
             whole(recv_col.shape),
             whole(recv_row.shape),
             whole(recv_soft.shape),
         ],
         out_specs=[rows_of(TILE, width)] + [whole((width // side, cols))] * side + [whole((16, LANES))],
-        out_shape=[shape((rows, width), BF)] + [shape((width // side, cols), BF)] * side + [shape((16, LANES))],
+        out_shape=[far_shape((rows, width), BF)]
+        + [far_shape((width // side, cols), BF)] * side
+        + [far_shape((16, LANES))],
         scratch_shapes=[
             pltpu.VMEM((rows, cols), BF),
             pltpu.VMEM((TILE, rows), BF),
@@ -625,16 +631,12 @@
             pltpu.VMEM((col_bands, LANES), F32),
             pltpu.VMEM((row_bands, LANES), F32),
             pltpu.VMEM((row_bands, LANES), F32),
-            pltpu.VMEM((rows, width), BF),
-            pltpu.VMEM((width, cols), BF),
-            pltpu.VMEM((cols, width), BF),
-            pltpu.VMEM((width, cols), BF),
             pltpu.VMEM((width, cols), BF),
             pltpu.VMEM((2 * TILE, width), BF),
-            pltpu.SemaphoreType.DMA((4,)),
         ],
+        compiler_params=PARAMS,
         name="final_kernel",
-    )(order, block_embed, mate_row, proto_t, proto_bf, raw_t, recv_col, recv_row, recv_soft)
+    )(order, block_embed, mate_row, proto_t, proto_bf, raw_t, norm, recv_col, recv_row, recv_soft)
 
 
     def shifted(axis, d):
@@ -645,7 +647,27 @@
         return moves
 
     pieces = [pieces[0]] + [lax.ppermute(pieces[d], "batch", shifted(0, d)) for d in range(1, side)]
-    d_unit = deal(d_unit.reshape(n_proto, own, width), "proto")
+    d_unit_got = deal(d_unit.reshape(n_proto, own, width), "proto")
+    stat_spec = whole((hid_bands, LANES))
+    mean_late, inv, _ = lax.optimization_barrier((mean, inv, d_unit))
+    normed, slope, hid = pl.pallas_call(
+        slab_kernel,
+        grid_spec=pltpu.PrefetchScalarGridSpec(
+            num_scalar_prefetch=1,
+            grid=(1,),
+            in_specs=[stat_spec] * 4 + [anywhere] * (1 + len(parts)),
+            out_specs=[pl.BlockSpec(memory_space=pltpu.HBM)] * 3,
+            scratch_shapes=[pltpu.VMEM((rows, slab), BF)] * 3
+            + [
+                pltpu.VMEM((rows, d_in), BF),
+                pltpu.VMEM((d_in, slab), BF),
+                pltpu.SemaphoreType.DMA((len(parts) + 1 + 3 * (rows // TILE),)),
+            ],
+        ),
+        out_shape=[shape((rows, slab), BF)] * 3,
+        name="slab_kernel",
+    )(order, mean_late, inv, gain, bias, w_first, *parts)
+    d_unit, normed, slope, hid = lax.optimization_barrier((d_unit_got, normed, slope, hid))
     d_embed = pl.pallas_call(
         d_embed_kernel, out_shape=shape((n_proto, own, width), BF), compiler_params=PARAMS, name="d_embed_kernel"
     )(d_unit, unit_embed, embed_scale)
@@ -659,18 +681,20 @@
             in_specs=[
                 whole((n_proto, own, width)),
                 pl.BlockSpec((slab, width), lambda i, s: (s[0], 0)),
-                whole((rows, slab)),
-                whole((rows, slab)),
-                whole((rows, slab)),
-                pl.BlockSpec(memory_space=pltpu.HBM),
+                anywhere,
+                anywhere,
+                anywhere,
+                anywhere,
             ],
             out_specs=[whole((rows, slab)), whole((n_batch, 2 * slab // n_batch, width))],
-            scratch_shapes=[pltpu.VMEM((8, slab), F32), pltpu.VMEM((16, LANES), F32), pltpu.SemaphoreType.DMA((1,))],
+            scratch_shapes=[pltpu.VMEM((8, slab), F32), pltpu.VMEM((16, LANES), F32)]
+            + [pltpu.VMEM((rows, slab), BF)] * 3
+            + [pltpu.SemaphoreType.DMA((4,))],
         ),
         out_shape=[shape((rows, slab)), shape((n_batch, 2 * slab // n_batch, width), BF)],
         compiler_params=PARAMS,
         name="shift_kernel",
-    )(order, d_embed, w_second, normed, slope, hid, loss_tile)
+    )(order, d_embed, w_second, far(normed), far(slope), far(hid), far(loss_tile))
     recv = deal(msg, "batch")
 
     share = d_in // (n_batch * n_proto)
@@ -689,7 +713,7 @@
                 pltpu.SemaphoreType.DMA((d_in // TILE,)),
             ],
         ),
-        out_shape=[shape((n_batch * n_proto, lines, LANES), BF), shape((slab // n_batch, width))],
+        out_shape=[far_shape((n_batch * n_proto, lines, LANES), BF), shape((slab // n_batch, width))],
         compiler_params=PARAMS,
         name="first_kernel",
     )(order, recv, shift, normed, inv, gain, *parts)

time: 239 us -> 219 us (0.916)
  local copies, waits for them, and re-layouts: 12.7 us -> 6.75 us
  waiting for transfers between devices: 33.2 us -> 27.9 us
  blocking collectives: 83.9 us -> 80 us
  Pallas kernels: 56.4 us -> 53.6 us
    ppermute x9, waiting for transfers between devices: 8.64 us -> 0.02 us  [hop(): return lax.ppermute(x, 'proto', moves)]
    unnamed x71 -> x55, local copies, waits for them, and re-layouts: 12 us -> 5.15 us
    all_to_all x8, blocking collectives: 83.9 us -> 80 us  [deal(): return lax.all_to_all(x, axis, 0, 0, tiled=True)]
    pallas_call x1, Pallas kernels: 15 us -> 11.4 us  [step_of_device(): pl.pallas_call(final_kernel, grid=(steps,), in_specs=[pl.BlockSpec(memory...]
    all_to_all x5, waiting for transfers between devices: 13.2 us -> 16.4 us  [deal(): return lax.all_to_all(x, axis, 0, 0, tiled=True)]
    all_to_all x5, starting transfers between devices: 30.2 us -> 27.2 us  [deal(): return lax.all_to_all(x, axis, 0, 0, tiled=True)]
  transfers between devices with their start and end apart: 21 -> 21, of which waited for: 9 -> 6; matrix products, arithmetic and copies ran while one was open for 1% -> 1% of each run, Pallas kernels for 13% -> 14%
where the time goes in v6:
time: 219 us; the launch traced here: 218 us
  blocking collectives  80 us (37%)
  Pallas kernels  53.6 us (24%)
  starting transfers between devices  46.9 us (21%)
  waiting for transfers between devices  27.9 us (13%)
  local copies, waits for them, and re-layouts  6.75 us (3%)
    all_to_all x8, blocking collectives, deal(): return lax.all_to_all(x, axis, 0, 0, tiled=True)  80 us
    all_to_all x5, starting transfers between devices, deal(): return lax.all_to_all(x, axis, 0, 0, tiled=True)  27.2 us
    all_to_all x5, waiting for transfers between devices, deal(): return lax.all_to_all(x, axis, 0, 0, tiled=True)  16.4 us
    pallas_call x1, Pallas kernels, step_of_device(): pl.pallas_call(final_kernel, grid=(steps,), in_specs=[pl.BlockSpec(memory...  11.4 us
    ppermute x1, waiting for transfers between devices, step_of_device(): lax.ppermute(second, ('batch', 'proto'), [(b * n_proto + p, p * n_batch +...  10 us
    ppermute x9, starting transfers between devices, hop(): return lax.ppermute(x, 'proto', moves)  7.98 us
    pallas_call x1, Pallas kernels, step_of_device(): pl.pallas_call(slab_kernel, grid_spec=pltpu.PrefetchScalarGridSpec(num_sc...  7.5 us
    pallas_call x1, Pallas kernels, step_of_device(): pl.pallas_call(pre_kernel, in_specs=[pl.BlockSpec(features.shape, lambda:...  6.91 us
  transfers between devices with their start and end apart: 21, of which 6 were waited for; matrix products, arithmetic and copies ran while one was open for 1% of the time, Pallas kernels for 14%

profile of v6, /device:TPU:1, one launch (start us, length us, event | category | flops | bytes accessed | tf_op | source)
XLA Modules:
  0.0 217.7 jit_solution(3971154720982212832)
XLA Ops:
  0.7 3.4 %collective-permute-start = (bf16[128,2048]{1,0:T(8,128)(2,1)}, bf16[128,2048]{1,0:T(8,128)(2,1)S(1)}, u32[]{:S(2)}, u32[]{:S(2)}) collective-permute-start(bf16[128,2048]{1,0:T(8,128)(2,1)} %refs_6_), channel_id=1, source_target_pairs={{2,0},{3,1},{4,2},{5,3},{6,4},{7,5},{0,6},{1,7},{10,8},{11,9},{12,... | collective-permute-start | bytes 1572872 | tf_op jit(solution)/shard_map/ppermute | solution.py:482
  4.0 6.9 %pre_kernel.1 = (f32[128,2048]{1,0:T(8,128)}, f32[16,32,128]{2,1,0:T(8,128)}) custom-call(bf16[128,2048]{1,0:T(8,128)(2,1)} %refs_6_, bf16[2048,2048]{1,0:T(8,128)(2,1)} %w_hbm.3), custom_call_target="tpu_custom_call" | custom-call | tf_op jit(solution)/shard_map/pre_kernel/pallas_call | solution.py:505
  11.0 7.9 %all-to-all-start = ((f32[16,32,128]{2,1,0:T(8,128)}), f32[16,32,128]{2,1,0:T(8,128)S(1)}, u32[]{:S(2)}, u32[]{:S(2)}) async-start(f32[16,32,128]{2,1,0:T(8,128)} %get-tuple-element.78), calls=%async_computation | async-start | bytes 524288 | tf_op jit(solution)/shard_map/all_to_all | solution.py:19
  20.6 2.6 %collective-permute-start.3 = (bf16[64,2048]{1,0:T(8,128)(2,1)}, bf16[64,2048]{1,0:T(8,128)(2,1)S(1)}, u32[]{:S(2)}, u32[]{:S(2)}) collective-permute-start(bf16[64,2048]{1,0:T(8,128)(2,1)} %slice.10), channel_id=1, source_target_pairs={{2,0},{3,1},{4,2},{5,3},{6,4},{7,5},{0,6},{1,7},{10,8},{11,9},{12,... | collective-permute-start | bytes 786440 | tf_op jit(solution)/shard_map/ppermute | solution.py:482
  23.2 3.1 %all-to-all-done.recv_ref = f32[16,32,128]{2,1,0:T(8,128)S(1)} async-done(((f32[16,32,128]{2,1,0:T(8,128)}), f32[16,32,128]{2,1,0:T(8,128)S(1)}, u32[]{:S(2)}, u32[]{:S(2)}) %all-to-all-start) | async-done | bytes 262176 | tf_op jit(solution)/shard_map/all_to_all | solution.py:19
  26.4 11.8 %all_to_all.65.refs_1_ = f32[8,32,128]{2,1,0:T(8,128)S(1)} all-to-all(f32[8,32,128]{2,1,0:T(8,128)S(1)} %relay_kernel.1), channel_id=1, replica_groups=mesh['batch'=16,'proto'=8] {'proto'}, dimensions={0} | all-to-all | bytes 262144 | tf_op jit(solution)/shard_map/all_to_all | solution.py:19
  38.2 1.2 copy-done.16
  39.4 1.8 embed_kernel.1
  41.3 0.9 collective-permute-start.4
  42.7 3.5 %all-to-all-start.2 = ((bf16[8,128,256]{2,1,0:T(8,128)(2,1)}), bf16[8,128,256]{2,1,0:T(8,128)(2,1)S(1)}, u32[]{:S(2)}, u32[]{:S(2)}) async-start(bf16[8,128,256]{2,1,0:T(8,128)(2,1)} %get-tuple-element.82), calls=%async_computation.2 | async-start | bytes 1048576 | tf_op jit(solution)/shard_map/all_to_all | solution.py:19
  46.8 3.9 %proto_kernel.1 = (bf16[2048,256]{1,0:T(8,128)(2,1)}, bf16[256,2048]{1,0:T(8,128)(2,1)}, bf16[256,2048]{1,0:T(8,128)(2,1)}, f32[8,2048]{1,0:T(8,128)}) custom-call(bf16[2048,256]{1,0:T(8,128)(2,1)} %raw_ref), custom_call_target="tpu_custom_call" | custom-call | tf_op jit(solution)/shard_map/proto_kernel/pallas_call | solution.py:549
  50.7 5.0 %all-to-all-done.2 = bf16[8,128,256]{2,1,0:T(8,128)(2,1)S(1)} async-done(((bf16[8,128,256]{2,1,0:T(8,128)(2,1)}), bf16[8,128,256]{2,1,0:T(8,128)(2,1)S(1)}, u32[]{:S(2)}, u32[]{:S(2)}) %all-to-all-start.2) | async-done | bytes 524320 | tf_op jit(solution)/shard_map/all_to_all | solution.py:19
  55.7 4.0 %score_kernel.1 = (bf16[1024,2048]{1,0:T(8,128)(2,1)S(1)}, f32[16,16,128]{2,1,0:T(8,128)S(1)}, f32[8,128]{1,0:T(8,128)S(1)}) custom-call(bf16[1024,256]{1,0:T(8,128)(2,1)S(1)} %bitcast.25, bf16[256,2048]{1,0:T(8,128)(2,1)} %get-tuple-element.97.proto_t_hbm.proto_t_ref), custom_call_target="tpu_custom_call" | custom-call | tf_op jit(solution)/shard_map/score_kernel/pallas_call | solution.py:559
  59.8 9.8 %all_to_all.66.recv_ref = f32[16,16,128]{2,1,0:T(8,128)S(1)} all-to-all(f32[16,16,128]{2,1,0:T(8,128)S(1)} %get-tuple-element.101), channel_id=1, replica_groups=mesh['batch'=16,'proto'=8] {'batch'}, dimensions={0} | all-to-all | bytes 262144 | tf_op jit(solution)/shard_map/all_to_all | solution.py:19
  69.6 1.2 row_kernel.3
  70.8 9.6 %all_to_all.67.recv_ref.recv_soft_ref = f32[8,16,128]{2,1,0:T(8,128)S(1)} all-to-all(f32[8,16,128]{2,1,0:T(8,128)S(1)} %row_kernel.3), channel_id=1, replica_groups=mesh['batch'=16,'proto'=8] {'proto'}, dimensions={0} | all-to-all | bytes 131072 | tf_op jit(solution)/shard_map/all_to_all | solution.py:19
  80.4 1.2 col_kernel.2
  81.6 9.9 %all_to_all.68.recv_ref = f32[16,16,128]{2,1,0:T(8,128)S(1)} all-to-all(f32[16,16,128]{2,1,0:T(8,128)S(1)} %col_kernel.2), channel_id=1, replica_groups=mesh['batch'=16,'proto'=8] {'batch'}, dimensions={0} | all-to-all | bytes 262144 | tf_op jit(solution)/shard_map/all_to_all | solution.py:19
  91.5 1.2 row_kernel.4
  92.7 9.2 %all_to_all.69.recv_ref = f32[8,8,128]{2,1,0:T(8,128)S(1)} all-to-all(f32[8,8,128]{2,1,0:T(8,128)S(1)} %row_kernel.4), channel_id=1, replica_groups=mesh['batch'=16,'proto'=8] {'proto'}, dimensions={0} | all-to-all | bytes 65536 | tf_op jit(solution)/shard_map/all_to_all | solution.py:19
  101.9 1.2 col_kernel.3
  103.1 9.9 %all_to_all.70.recv_ref.recv_col_ref = f32[16,16,128]{2,1,0:T(8,128)S(1)} all-to-all(f32[16,16,128]{2,1,0:T(8,128)S(1)} %col_kernel.3), channel_id=1, replica_groups=mesh['batch'=16,'proto'=8] {'batch'}, dimensions={0} | all-to-all | bytes 262144 | tf_op jit(solution)/shard_map/all_to_all | solution.py:19
  113.0 1.2 row_kernel.5
  114.2 9.1 %all_to_all.71.recv_row_ref = f32[8,8,128]{2,1,0:T(8,128)S(1)} all-to-all(f32[8,8,128]{2,1,0:T(8,128)S(1)} %row_kernel.5), channel_id=1, replica_groups=mesh['batch'=16,'proto'=8] {'proto'}, dimensions={0} | all-to-all | bytes 65536 | tf_op jit(solution)/shard_map/all_to_all | solution.py:19
  123.4 11.4 %final_kernel.1 = (bf16[1024,256]{1,0:T(8,128)(2,1)}, bf16[64,2048]{1,0:T(8,128)(2,1)}, bf16[64,2048]{1,0:T(8,128)(2,1)}, bf16[64,2048]{1,0:T(8,128)(2,1)}, bf16[64,2048]{1,0:T(8,128)(2,1)}, /*index=5*/f32[16,128]{1,0:T(8,128)}) custom-call(s32[11]{0:T(128)S(1)} %stack.47.order_ref.refs_0_, bf16[1024,256]{1,0:T(8,128)(2,1)S(1)} %bitcast.26, ...), custom_call_target="tpu_custom_call" | custom-call | tf_op jit(solution)/shard_map/final_kernel/pallas_call | solution.py:608
  134.8 4.7 %all-to-all-start.9 = ((bf16[8,128,256]{2,1,0:T(8,128)(2,1)}), bf16[8,128,256]{2,1,0:T(8,128)(2,1)}, u32[]{:S(2)}, u32[]{:S(2)}) async-start(bf16[8,128,256]{2,1,0:T(8,128)(2,1)} %bitcast.32), calls=%async_computation.9 | async-start | bytes 1048576 | tf_op jit(solution)/shard_map/all_to_all | solution.py:19
  139.5 7.5 %slab_kernel.1 = (bf16[1024,256]{1,0:T(8,128)(2,1)}, bf16[1024,256]{1,0:T(8,128)(2,1)}, bf16[1024,256]{1,0:T(8,128)(2,1)}) custom-call(s32[11]{0:T(128)} %copy-done.24, f32[16,128]{1,0:T(8,128)} %get-tuple-element.107.mean_ref, f32[16,128]{1,0:T(8,128)} %get-tuple-element.108.inv_ref.refs_4_, f32[16,128]{1,0:T(8,128)} %bitcast.27, f32[16,128]{1,0:T(8,128)} %bitcast.30, ...), custom_call_target="tpu_custom_call" | custom-call | tf_op jit(solution)/shard_map/slab_kernel/pallas_call | solution.py:653
  147.1 1.9 all-to-all-done.9.recv_ref
  149.0 0.8 copy-done.21
  149.9 1.2 d_embed_kernel.1
  151.9 5.0 %all-to-all-start.10 = ((bf16[8,128,256]{2,1,0:T(8,128)(2,1)}), bf16[8,128,256]{2,1,0:T(8,128)(2,1)}, u32[]{:S(2)}, u32[]{:S(2)}) async-start(bf16[8,128,256]{2,1,0:T(8,128)(2,1)} %copy-done.9), calls=%async_computation.10 | async-start | bytes 1048576 | tf_op jit(solution)/shard_map/all_to_all | solution.py:19
  157.1 1.9 collective-permute-start.10
  159.0 1.0 collective-permute-start.11
  160.0 6.4 %all-to-all-done.10.d_embed_ref = bf16[8,128,256]{2,1,0:T(8,128)(2,1)} async-done(((bf16[8,128,256]{2,1,0:T(8,128)(2,1)}), bf16[8,128,256]{2,1,0:T(8,128)(2,1)}, u32[]{:S(2)}, u32[]{:S(2)}) %all-to-all-start.10) | async-done | bytes 524320 | tf_op jit(solution)/shard_map/all_to_all | solution.py:19
  167.0 3.5 %shift_kernel.1 = (f32[1024,256]{1,0:T(8,128)S(1)}, bf16[16,32,256]{2,1,0:T(8,128)(2,1)S(1)}) custom-call(s32[11]{0:T(128)S(1)} %copy-done.25, bf16[8,128,256]{2,1,0:T(8,128)(2,1)} %all-to-all-done.10.d_embed_ref, bf16[2048,256]{1,0:T(8,128)(2,1)S(1)} %copy-done.3, bf16[1024,256]{1,0:T(8,128)(2,1)} %get-tuple-element.125.normed_hbm.refs_3_, ...), custom_call_target="tpu_custom_call" | custom-call | tf_op jit(solution)/shard_map/shift_kernel/pallas_call | solution.py:676
  170.5 10.6 %all_to_all.72.refs_1_ = bf16[16,32,256]{2,1,0:T(8,128)(2,1)S(1)} all-to-all(bf16[16,32,256]{2,1,0:T(8,128)(2,1)S(1)} %get-tuple-element.129), channel_id=1, replica_groups=mesh['batch'=16,'proto'=8] {'batch'}, dimensions={0} | all-to-all | bytes 524288 | tf_op jit(solution)/shard_map/all_to_all | solution.py:19
  181.2 0.9 copy-done.15
  182.1 4.4 %first_kernel.1 = (bf16[128,40,128]{2,1,0:T(8,128)(2,1)}, f32[16,256]{1,0:T(8,128)S(1)}) custom-call(s32[11]{0:T(128)S(1)} %copy-done.25, bf16[16,32,256]{2,1,0:T(8,128)(2,1)S(1)} %all_to_all.72.refs_1_, f32[1024,256]{1,0:T(8,128)S(1)} %get-tuple-element.130.refs_2_, bf16[1024,256]{1,0:T(8,128)(2,1)S(1)} %copy-done.8, f32[16,128]{1,0:T(8,128)S(1)} %copy-done.23, ...), custom_call_target="tpu_custom_call" | custom-call | tf_op jit(solution)/shard_map/first_kernel/pallas_call | solution.py:702
  186.5 6.0 %all-to-all-start.12 = ((bf16[128,40,128]{2,1,0:T(8,128)(2,1)}), bf16[128,40,128]{2,1,0:T(8,128)(2,1)S(1)}, u32[]{:S(2)}, u32[]{:S(2)}) async-start(bf16[128,40,128]{2,1,0:T(8,128)(2,1)} %get-tuple-element.136), calls=%async_computation.12 | async-start | bytes 2621440 | tf_op jit(solution)/shard_map/all_to_all | solution.py:19
  192.6 2.1 stage_kernel.1
  194.7 1.5 collective-permute-start.13
  196.2 2.9 %collective-permute-start.14 = (bf16[16,2048]{1,0:T(8,128)(2,1)}, bf16[16,2048]{1,0:T(8,128)(2,1)S(1)}, u32[]{:S(2)}, u32[]{:S(2)}) collective-permute-start(bf16[16,2048]{1,0:T(8,128)(2,1)} %get-tuple-element.147), channel_id=1, source_target_pairs={{0,16},{8,24},{16,0},{24,8},{32,48},{40,56},{48,32},{56,40},{64,80... | collective-permute-start | bytes 196616 | tf_op jit(solution)/shard_map/ppermute | solution.py:729
  199.1 0.9 collective-permute-start.15
  200.0 3.4 %collective-permute-start.12 = (f32[16,256]{1,0:T(8,128)S(1)}, f32[16,256]{1,0:T(8,128)S(1)}, u32[]{:S(2)}, u32[]{:S(2)}) collective-permute-start(f32[16,256]{1,0:T(8,128)S(1)} %get-tuple-element.138), channel_id=1, source_target_pairs={{0,0},{1,16},{2,32},{3,48},{4,64},{5,80},{6,96},{7,112},{8,1},{9,1... | collective-permute-start | bytes 49160 | tf_op jit(solution)/shard_map/ppermute | solution.py:738
  203.4 10.0 %collective-permute-done.12 = f32[16,256]{1,0:T(8,128)S(1)} collective-permute-done((f32[16,256]{1,0:T(8,128)S(1)}, f32[16,256]{1,0:T(8,128)S(1)}, u32[]{:S(2)}, u32[]{:S(2)}) %collective-permute-start.12) | collective-permute-done | bytes 16416 | tf_op jit(solution)/shard_map/ppermute | solution.py:738
  213.4 1.4 collective-permute-done.14
  214.8 1.5 add_bitcast_fusion
  216.3 0.8 tail_kernel.1
  (79 shorter events, 5.0 us)
Async XLA Ops:
  0.6 22.6 %copy-start.26 = (s32[1024]{0:T(1024)S(1)}, s32[1024]{0:T(1024)}, u32[]{:S(2)}) copy-start(s32[1024]{0:T(1024)} %param.13) | copy-start | bytes 12292
  0.6 37.5 %copy-start.3 = (bf16[2048,256]{1,0:T(8,128)(2,1)S(1)}, bf16[2048,256]{1,0:T(8,128)(2,1)}, u32[]{:S(2)}) copy-start(bf16[2048,256]{1,0:T(8,128)(2,1)} %w2_ref.1) | copy-start | bytes 3145732
  0.7 37.5 %copy-start.22 = (f32[2048]{0:T(1024)S(1)}, f32[2048]{0:T(1024)}, u32[]{:S(2)}) copy-start(f32[2048]{0:T(1024)} %param.10) | copy-start | bytes 24580
  0.7 37.5 %copy-start.18 = (f32[2048]{0:T(1024)S(1)}, f32[2048]{0:T(1024)}, u32[]{:S(2)}) copy-start(f32[2048]{0:T(1024)} %param.9) | copy-start | bytes 24580
  0.7 18.3 %collective-permute-start = (bf16[128,2048]{1,0:T(8,128)(2,1)}, bf16[128,2048]{1,0:T(8,128)(2,1)S(1)}, u32[]{:S(2)}, u32[]{:S(2)}) collective-permute-start(bf16[128,2048]{1,0:T(8,128)(2,1)} %refs_6_), channel_id=1, source_target_pairs={{2,0},{3,1},{4,2},{5,3},{6,4},{7,5},{0,6},{1,7},{10,8},{11,9},{12,... | collective-permute-start | bytes 1572872 | tf_op jit(solution)/shard_map/ppermute | solution.py:482
  4.0 15.0 %collective-permute-start.1 = (bf16[128,2048]{1,0:T(8,128)(2,1)}, bf16[128,2048]{1,0:T(8,128)(2,1)S(1)}, u32[]{:S(2)}, u32[]{:S(2)}) collective-permute-start(bf16[128,2048]{1,0:T(8,128)(2,1)} %refs_6_), channel_id=1, source_target_pairs={{0,2},{1,3},{2,4},{3,5},{4,6},{5,7},{6,0},{7,1},{8,10},{9,11},{10,... | collective-permute-start | bytes 1572872 | tf_op jit(solution)/shard_map/ppermute | solution.py:482
  11.0 30.3 %copy-start = (bf16[128,2048]{1,0:T(8,128)(2,1)S(1)}, bf16[128,2048]{1,0:T(8,128)(2,1)}, u32[]{:S(2)}) copy-start(bf16[128,2048]{1,0:T(8,128)(2,1)} %refs_6_) | copy-start | bytes 1572868
  11.0 15.4 %all-to-all-start = ((f32[16,32,128]{2,1,0:T(8,128)}), f32[16,32,128]{2,1,0:T(8,128)S(1)}, u32[]{:S(2)}, u32[]{:S(2)}) async-start(f32[16,32,128]{2,1,0:T(8,128)} %get-tuple-element.78), calls=%async_computation | async-start | bytes 524288 | tf_op jit(solution)/shard_map/all_to_all | solution.py:19
  19.0 104.4 %copy-start.24 = (s32[11]{0:T(128)}, s32[11]{0:T(128)S(1)}, u32[]{:S(2)}) copy-start(s32[11]{0:T(128)S(1)} %stack.47.order_ref.refs_0_) | copy-start | bytes 136
  19.0 51.8 %copy-start.4 = (bf16[128,2048]{1,0:T(8,128)(2,1)}, bf16[128,2048]{1,0:T(8,128)(2,1)S(1)}, u32[]{:S(2)}) copy-start(bf16[128,2048]{1,0:T(8,128)(2,1)S(1)} %collective-permute-done.rest_1_.refs_7_) | copy-start | bytes 1572868
  19.0 51.8 %copy-start.6 = (bf16[128,2048]{1,0:T(8,128)(2,1)}, bf16[128,2048]{1,0:T(8,128)(2,1)S(1)}, u32[]{:S(2)}) copy-start(bf16[128,2048]{1,0:T(8,128)(2,1)S(1)} %collective-permute-done.1.rest_2_.refs_8_) | copy-start | bytes 1572868
  20.6 20.7 %collective-permute-start.3 = (bf16[64,2048]{1,0:T(8,128)(2,1)}, bf16[64,2048]{1,0:T(8,128)(2,1)S(1)}, u32[]{:S(2)}, u32[]{:S(2)}) collective-permute-start(bf16[64,2048]{1,0:T(8,128)(2,1)} %slice.10), channel_id=1, source_target_pairs={{2,0},{3,1},{4,2},{5,3},{6,4},{7,5},{0,6},{1,7},{10,8},{11,9},{12,... | collective-permute-start | bytes 786440 | tf_op jit(solution)/shard_map/ppermute | solution.py:482
  23.2 18.0 %collective-permute-start.2 = (bf16[64,2048]{1,0:T(8,128)(2,1)}, bf16[64,2048]{1,0:T(8,128)(2,1)S(1)}, u32[]{:S(2)}, u32[]{:S(2)}) collective-permute-start(bf16[64,2048]{1,0:T(8,128)(2,1)} %slice.9), channel_id=1, source_target_pairs={{0,2},{1,3},{2,4},{3,5},{4,6},{5,7},{6,0},{7,1},{8,10},{9,11},{10,... | collective-permute-start | bytes 786440 | tf_op jit(solution)/shard_map/ppermute | solution.py:482
  38.2 1.2 copy-start.16
  41.2 39.2 %copy-start.12 = (bf16[64,2048]{1,0:T(8,128)(2,1)}, bf16[64,2048]{1,0:T(8,128)(2,1)S(1)}, u32[]{:S(2)}) copy-start(bf16[64,2048]{1,0:T(8,128)(2,1)S(1)} %collective-permute-done.3.rest_4_.refs_10_) | copy-start | bytes 786436
  41.3 1.5 copy-start.14
  41.3 14.4 %collective-permute-start.4 = (bf16[128,2048]{1,0:T(8,128)(2,1)S(1)}, bf16[128,2048]{1,0:T(8,128)(2,1)}, u32[]{:S(2)}, u32[]{:S(2)}) collective-permute-start(bf16[128,2048]{1,0:T(8,128)(2,1)S(1)} %copy-done), channel_id=1, source_target_pairs={{0,1},{1,0},{2,3},{3,2},{4,5},{5,4},{6,7},{7,6},{8,9},{9,8},{10,11... | collective-permute-start | bytes 1572872 | tf_op jit(solution)/shard_map/ppermute | solution.py:482
  42.2 13.5 %collective-permute-start.5 = (bf16[128,2048]{1,0:T(8,128)(2,1)S(1)}, bf16[128,2048]{1,0:T(8,128)(2,1)}, u32[]{:S(2)}, u32[]{:S(2)}) collective-permute-start(bf16[128,2048]{1,0:T(8,128)(2,1)S(1)} %collective-permute-done.rest_1_.refs_7_), channel_id=1, source_target_pairs={{0,1},{1,0},{2,3},{3,2},{4,5},{5,4},{6,7},{7,6},{8,9},{9,8},{10,11... | collective-permute-start | bytes 1572872 | tf_op jit(solution)/shard_map/ppermute | solution.py:482
  42.3 13.4 %collective-permute-start.6 = (bf16[128,2048]{1,0:T(8,128)(2,1)S(1)}, bf16[128,2048]{1,0:T(8,128)(2,1)}, u32[]{:S(2)}, u32[]{:S(2)}) collective-permute-start(bf16[128,2048]{1,0:T(8,128)(2,1)S(1)} %collective-permute-done.1.rest_2_.refs_8_), channel_id=1, source_target_pairs={{0,1},{1,0},{2,3},{3,2},{4,5},{5,4},{6,7},{7,6},{8,9},{9,8},{10,11... | collective-permute-start | bytes 1572872 | tf_op jit(solution)/shard_map/ppermute | solution.py:482
  42.7 12.9 %all-to-all-start.2 = ((bf16[8,128,256]{2,1,0:T(8,128)(2,1)}), bf16[8,128,256]{2,1,0:T(8,128)(2,1)S(1)}, u32[]{:S(2)}, u32[]{:S(2)}) async-start(bf16[8,128,256]{2,1,0:T(8,128)(2,1)} %get-tuple-element.82), calls=%async_computation.2 | async-start | bytes 1048576 | tf_op jit(solution)/shard_map/all_to_all | solution.py:19
  46.3 9.4 %collective-permute-start.7 = (bf16[64,2048]{1,0:T(8,128)(2,1)}, bf16[64,2048]{1,0:T(8,128)(2,1)}, u32[]{:S(2)}, u32[]{:S(2)}) collective-permute-start(bf16[64,2048]{1,0:T(8,128)(2,1)} %copy-done.14), channel_id=1, source_target_pairs={{0,1},{1,0},{2,3},{3,2},{4,5},{5,4},{6,7},{7,6},{8,9},{9,8},{10,11... | collective-permute-start | bytes 786440 | tf_op jit(solution)/shard_map/ppermute | solution.py:482
  46.5 9.2 %collective-permute-start.8 = (bf16[64,2048]{1,0:T(8,128)(2,1)S(1)}, bf16[64,2048]{1,0:T(8,128)(2,1)}, u32[]{:S(2)}, u32[]{:S(2)}) collective-permute-start(bf16[64,2048]{1,0:T(8,128)(2,1)S(1)} %collective-permute-done.3.rest_4_.refs_10_), channel_id=1, source_target_pairs={{0,1},{1,0},{2,3},{3,2},{4,5},{5,4},{6,7},{7,6},{8,9},{9,8},{10,11... | collective-permute-start | bytes 786440 | tf_op jit(solution)/shard_map/ppermute | solution.py:482
  101.9 21.5 %copy-start.2 = (bf16[256,2048]{1,0:T(8,128)(2,1)S(1)}, bf16[256,2048]{1,0:T(8,128)(2,1)}, u32[]{:S(2)}) copy-start(bf16[256,2048]{1,0:T(8,128)(2,1)} %get-tuple-element.97.proto_t_hbm.proto_t_ref) | copy-start | bytes 3145732
  101.9 21.5 %copy-start.10 = (bf16[2048,256]{1,0:T(8,128)(2,1)S(1)}, bf16[2048,256]{1,0:T(8,128)(2,1)}, u32[]{:S(2)}) copy-start(bf16[2048,256]{1,0:T(8,128)(2,1)} %get-tuple-element.98.proto_ref) | copy-start | bytes 3145732
  101.9 21.5 %copy-start.11 = (bf16[256,2048]{1,0:T(8,128)(2,1)S(1)}, bf16[256,2048]{1,0:T(8,128)(2,1)}, u32[]{:S(2)}) copy-start(bf16[256,2048]{1,0:T(8,128)(2,1)} %get-tuple-element.99.raw_t_ref) | copy-start | bytes 3145732
  101.9 21.5 %copy-start.20 = (f32[8,2048]{1,0:T(8,128)S(1)}, f32[8,2048]{1,0:T(8,128)}, u32[]{:S(2)}) copy-start(f32[8,2048]{1,0:T(8,128)} %get-tuple-element.100.norm_ref) | copy-start | bytes 196612
  134.8 14.2 %all-to-all-start.9 = ((bf16[8,128,256]{2,1,0:T(8,128)(2,1)}), bf16[8,128,256]{2,1,0:T(8,128)(2,1)}, u32[]{:S(2)}, u32[]{:S(2)}) async-start(bf16[8,128,256]{2,1,0:T(8,128)(2,1)} %bitcast.32), calls=%async_computation.9 | async-start | bytes 1048576 | tf_op jit(solution)/shard_map/all_to_all | solution.py:19
  139.5 9.5 %copy-start.17 = (f32[128,256]{1,0:T(8,128)S(1)}, f32[128,256]{1,0:T(8,128)}, u32[]{:S(2)}) copy-start(f32[128,256]{1,0:T(8,128)} %get-tuple-element.123.unit_ref) | copy-start | bytes 393220
  139.5 41.6 %copy-start.23 = (f32[16,128]{1,0:T(8,128)S(1)}, f32[16,128]{1,0:T(8,128)}, u32[]{:S(2)}) copy-start(f32[16,128]{1,0:T(8,128)} %get-tuple-element.108.inv_ref.refs_4_) | copy-start | bytes 24580
  147.1 34.1 %copy-start.1 = (bf16[128,2048]{1,0:T(8,128)(2,1)S(1)}, bf16[128,2048]{1,0:T(8,128)(2,1)}, u32[]{:S(2)}) copy-start(bf16[128,2048]{1,0:T(8,128)(2,1)} %refs_6_) | copy-start | bytes 1572868
  147.1 34.1 %copy-start.5 = (bf16[128,2048]{1,0:T(8,128)(2,1)S(1)}, bf16[128,2048]{1,0:T(8,128)(2,1)}, u32[]{:S(2)}) copy-start(bf16[128,2048]{1,0:T(8,128)(2,1)} %copy-done.4) | copy-start | bytes 1572868
  147.1 34.0 %copy-start.7 = (bf16[128,2048]{1,0:T(8,128)(2,1)S(1)}, bf16[128,2048]{1,0:T(8,128)(2,1)}, u32[]{:S(2)}) copy-start(bf16[128,2048]{1,0:T(8,128)(2,1)} %copy-done.6) | copy-start | bytes 1572868
  147.1 34.0 %copy-start.8 = (bf16[1024,256]{1,0:T(8,128)(2,1)S(1)}, bf16[1024,256]{1,0:T(8,128)(2,1)}, u32[]{:S(2)}) copy-start(bf16[1024,256]{1,0:T(8,128)(2,1)} %get-tuple-element.125.normed_hbm.refs_3_) | copy-start | bytes 1572868
  147.1 34.0 %copy-start.13 = (bf16[64,2048]{1,0:T(8,128)(2,1)S(1)}, bf16[64,2048]{1,0:T(8,128)(2,1)}, u32[]{:S(2)}) copy-start(bf16[64,2048]{1,0:T(8,128)(2,1)} %copy-done.12) | copy-start | bytes 786436
  147.1 34.0 %copy-start.19 = (f32[2048]{0:T(1024)S(1)}, f32[2048]{0:T(1024)}, u32[]{:S(2)}) copy-start(f32[2048]{0:T(1024)} %param.9) | copy-start | bytes 24580
  149.0 0.8 copy-start.21
  151.1 0.8 copy-start.9
  151.9 14.5 %all-to-all-start.10 = ((bf16[8,128,256]{2,1,0:T(8,128)(2,1)}), bf16[8,128,256]{2,1,0:T(8,128)(2,1)}, u32[]{:S(2)}, u32[]{:S(2)}) async-start(bf16[8,128,256]{2,1,0:T(8,128)(2,1)} %copy-done.9), calls=%async_computation.10 | async-start | bytes 1048576 | tf_op jit(solution)/shard_map/all_to_all | solution.py:19
  156.9 29.6 %collective-permute-start.9 = (bf16[64,2048]{1,0:T(8,128)(2,1)}, bf16[64,2048]{1,0:T(8,128)(2,1)}, u32[]{:S(2)}, u32[]{:S(2)}) collective-permute-start(bf16[64,2048]{1,0:T(8,128)(2,1)} %get-tuple-element.133), channel_id=1, source_target_pairs={{0,32},{8,40},{16,48},{24,56},{32,64},{40,72},{48,80},{56,88},{64,... | collective-permute-start | bytes 786440 | tf_op jit(solution)/shard_map/ppermute | solution.py:649
  157.1 29.4 %collective-permute-start.10 = (bf16[64,2048]{1,0:T(8,128)(2,1)}, bf16[64,2048]{1,0:T(8,128)(2,1)}, u32[]{:S(2)}, u32[]{:S(2)}) collective-permute-start(bf16[64,2048]{1,0:T(8,128)(2,1)} %get-tuple-element.134), channel_id=1, source_target_pairs={{0,64},{8,72},{16,80},{24,88},{32,96},{40,104},{48,112},{56,120},{... | collective-permute-start | bytes 786440 | tf_op jit(solution)/shard_map/ppermute | solution.py:649
  159.0 27.6 %collective-permute-start.11 = (bf16[64,2048]{1,0:T(8,128)(2,1)}, bf16[64,2048]{1,0:T(8,128)(2,1)}, u32[]{:S(2)}, u32[]{:S(2)}) collective-permute-start(bf16[64,2048]{1,0:T(8,128)(2,1)} %get-tuple-element.135), channel_id=1, source_target_pairs={{0,96},{8,104},{16,112},{24,120},{32,0},{40,8},{48,16},{56,24},{64... | collective-permute-start | bytes 786440 | tf_op jit(solution)/shard_map/ppermute | solution.py:649
  166.4 0.7 copy-start.25
  181.2 1.0 copy-start.15
  186.5 29.8 %all-to-all-start.12 = ((bf16[128,40,128]{2,1,0:T(8,128)(2,1)}), bf16[128,40,128]{2,1,0:T(8,128)(2,1)S(1)}, u32[]{:S(2)}, u32[]{:S(2)}) async-start(bf16[128,40,128]{2,1,0:T(8,128)(2,1)} %get-tuple-element.136), calls=%async_computation.12 | async-start | bytes 2621440 | tf_op jit(solution)/shard_map/all_to_all | solution.py:19
  194.7 18.7 %collective-permute-start.13 = (bf16[16,2048]{1,0:T(8,128)(2,1)}, bf16[16,2048]{1,0:T(8,128)(2,1)S(1)}, u32[]{:S(2)}, u32[]{:S(2)}) collective-permute-start(bf16[16,2048]{1,0:T(8,128)(2,1)} %get-tuple-element.146), channel_id=1, source_target_pairs={{0,8},{8,16},{16,24},{24,0},{32,40},{40,48},{48,56},{56,32},{64,72... | collective-permute-start | bytes 196616 | tf_op jit(solution)/shard_map/ppermute | solution.py:729
  196.2 18.6 %collective-permute-start.14 = (bf16[16,2048]{1,0:T(8,128)(2,1)}, bf16[16,2048]{1,0:T(8,128)(2,1)S(1)}, u32[]{:S(2)}, u32[]{:S(2)}) collective-permute-start(bf16[16,2048]{1,0:T(8,128)(2,1)} %get-tuple-element.147), channel_id=1, source_target_pairs={{0,16},{8,24},{16,0},{24,8},{32,48},{40,56},{48,32},{56,40},{64,80... | collective-permute-start | bytes 196616 | tf_op jit(solution)/shard_map/ppermute | solution.py:729
  199.1 15.7 %collective-permute-start.15 = (bf16[16,2048]{1,0:T(8,128)(2,1)}, bf16[16,2048]{1,0:T(8,128)(2,1)S(1)}, u32[]{:S(2)}, u32[]{:S(2)}) collective-permute-start(bf16[16,2048]{1,0:T(8,128)(2,1)} %get-tuple-element.148), channel_id=1, source_target_pairs={{0,24},{8,0},{16,8},{24,16},{32,56},{40,32},{48,40},{56,48},{64,88... | collective-permute-start | bytes 196616 | tf_op jit(solution)/shard_map/ppermute | solution.py:729
  200.0 13.4 %collective-permute-start.12 = (f32[16,256]{1,0:T(8,128)S(1)}, f32[16,256]{1,0:T(8,128)S(1)}, u32[]{:S(2)}, u32[]{:S(2)}) collective-permute-start(f32[16,256]{1,0:T(8,128)S(1)} %get-tuple-element.138), channel_id=1, source_target_pairs={{0,0},{1,16},{2,32},{3,48},{4,64},{5,80},{6,96},{7,112},{8,1},{9,1... | collective-permute-start | bytes 49160 | tf_op jit(solution)/shard_map/ppermute | solution.py:738

commit v7 on v6

--- a/solution.py
+++ b/solution.py
@@ -44,23 +44,26 @@
 
 
 def pre_kernel(features_ref, w_hbm, pre_ref, msg_ref, stat_ref, w_buf, sems):
-    pieces = w_buf.shape[0]
+    pieces, depth, width = w_buf.shape
     copies = [
-        pltpu.make_async_copy(w_hbm.at[:, k * TILE : (k + 1) * TILE], w_buf.at[k], sems.at[k]) for k in range(pieces)
+        pltpu.make_async_copy(w_hbm.at[k * depth : (k + 1) * depth], w_buf.at[k], sems.at[k]) for k in range(pieces)
     ]
     for copy in copies:
         copy.start()
-    chunks = TILE // LANES
     half = stat_ref.shape[0] // 2
     for k in range(pieces):
         copies[k].wait()
-        pre = jnp.dot(features_ref[...], w_buf[k], preferred_element_type=F32)
-        pre_ref[:, k * TILE : (k + 1) * TILE] = pre
-        for h in range(chunks):
-            at = k * chunks + h
-            part = pre[:, lane(h)]
-            stat_ref[at : at + 1, :] = jnp.sum(part, axis=0, keepdims=True)
-            stat_ref[half + at : half + at + 1, :] = jnp.sum(part * part, axis=0, keepdims=True)
+        for j in range(width // TILE):
+            span = slice(j * TILE, (j + 1) * TILE)
+            part = jnp.dot(features_ref[:, k * depth : (k + 1) * depth], w_buf[k, :, span], preferred_element_type=F32)
+            pre = part if k == 0 else pre_ref[:, span] + part
+            pre_ref[:, span] = pre
+            if k == pieces - 1:
+                for h in range(TILE // LANES):
+                    at = j * (TILE // LANES) + h
+                    piece = pre[:, lane(h)]
+                    stat_ref[at : at + 1, :] = jnp.sum(piece, axis=0, keepdims=True)
+                    stat_ref[half + at : half + at + 1, :] = jnp.sum(piece * piece, axis=0, keepdims=True)
     msg_ref[...] = jnp.broadcast_to(stat_ref[...][None], msg_ref.shape)
 
 
@@ -69,8 +72,8 @@
 
 
 def embed_kernel(
-    total_rows, pre_ref, recv_ref, gain_ref, bias_ref, w2_ref, unit_hbm, scale_hbm, mean_hbm, inv_hbm, msg_hbm,
-    hid_ref, unit_ref, scale_ref, mean_ref, inv_ref, bf_ref, sems,
+    total_rows, pre_ref, recv_ref, gain_ref, bias_ref, w2_ref, unit_hbm, mean_hbm, inv_hbm, msg_hbm,
+    hid_ref, unit_ref, mean_ref, inv_ref, bf_ref, sems,
 ):
     stats = jnp.sum(recv_ref[...], axis=0)
     half = stats.shape[0] // 2
@@ -85,10 +88,11 @@
     scale = lax.rsqrt(jnp.sum(embed * embed, axis=1, keepdims=True) + 1e-06)
     unit = embed * scale
     bf_ref[...] = unit.astype(BF)
-    unit_ref[...] = unit
-    scale_ref[...] = jnp.broadcast_to(scale, scale_ref.shape)
+    width = unit.shape[1]
+    unit_ref[:, :width] = unit
+    unit_ref[:, width:] = jnp.broadcast_to(scale, (unit.shape[0], LANES))
     moves = [(bf_ref, msg_hbm.at[k]) for k in range(msg_hbm.shape[0])]
-    moves += [(unit_ref, unit_hbm), (scale_ref, scale_hbm), (mean_ref, mean_hbm), (inv_ref, inv_hbm)]
+    moves += [(unit_ref, unit_hbm), (mean_ref, mean_hbm), (inv_ref, inv_hbm)]
     copies = [pltpu.make_async_copy(src, dst, sems.at[k]) for k, (src, dst) in enumerate(moves)]
     for copy in copies:
         copy.start()
@@ -96,7 +100,12 @@
         copy.wait()
 
 
-def proto_kernel(raw_ref, proto_ref, proto_t_ref, raw_t_ref, norm_ref):
+def proto_kernel(order_ref, raw_ref, w_hbm, proto_ref, proto_t_ref, raw_t_ref, norm_ref, slab_hbm, slab_ref, sem):
+    slab = slab_ref.shape[1]
+    at = pl.ds(pl.multiple_of(order_ref[0] * slab, slab), slab)
+    fetch = pltpu.make_async_copy(w_hbm.at[:, at], slab_ref, sem)
+    store = pltpu.make_async_copy(slab_ref, slab_hbm, sem)
+    fetch.start()
     for k in range(raw_ref.shape[0] // TILE):
         span = slice(k * TILE, (k + 1) * TILE)
         raw_t = raw_ref[span, :].T
@@ -107,6 +116,10 @@
         unit = (wide * scale).astype(BF)
         proto_t_ref[:, span] = unit
         proto_ref[span, :] = unit.T
+        if k == 3:
+            fetch.wait()
+            store.start()
+    store.wait()
 
 
 def score_kernel(embed_ref, proto_t_hbm, kern_ref, msg_ref, soft_ref, acc_ref, proto_t_ref, sems):
@@ -123,12 +136,17 @@
         for j in range(cols // TILE):
             copy(j).start()
         acc_ref[...] = jnp.zeros_like(acc_ref)
-        for j in range(cols // TILE):
-            copy(j).wait()
 
     soft = [None] * (rows // LANES)
     for j in range(cols // TILE):
         span = slice(j * TILE, (j + 1) * TILE)
+        if j % 2 == 0:
+
+            @pl.when(step == 0)
+            def _():
+                copy(j).wait()
+                copy(j + 1).wait()
+
         scores = jnp.dot(embed_ref[...], proto_t_ref[:, span], preferred_element_type=F32)
         tempered = jnp.exp2(scores * (10.0 * LOG2_E))
         kern = tempered * tempered
@@ -261,10 +279,11 @@
         loss_ref[...] = loss_acc_ref[...]
 
 
-def d_embed_kernel(recv_ref, unit_ref, scale_ref, msg_ref):
+def d_embed_kernel(recv_ref, unit_ref, msg_ref):
     d_unit = jnp.sum(recv_ref[...].astype(F32), axis=0)
-    unit = unit_ref[...]
-    d_embed = (d_unit - unit * jnp.sum(unit * d_unit, axis=1, keepdims=True)) * scale_ref[:, :1]
+    width = d_unit.shape[1]
+    unit = unit_ref[:, :width]
+    d_embed = (d_unit - unit * jnp.sum(unit * d_unit, axis=1, keepdims=True)) * unit_ref[:, width : width + 1]
     msg_ref[...] = jnp.broadcast_to(d_embed.astype(BF)[None], msg_ref.shape)
 
 
@@ -286,8 +305,7 @@
     buf_ref, w_ref, sems = rest[-3:]
     normed_ref, slope_ref, hid_ref = bufs
     rows, slab = normed_ref.shape
-    at = pl.ds(pl.multiple_of(order_ref[0] * slab, slab), slab)
-    w_copy = pltpu.make_async_copy(w_hbm.at[:, at], w_ref, sems.at[len(parts)])
+    w_copy = pltpu.make_async_copy(w_hbm, w_ref, sems.at[len(parts)])
     w_copy.start()
     copies = start_parts(parts, buf_ref, sems)
     stops = [sum(part.shape[0] for part in parts[: k + 1]) for k in range(len(parts))]
@@ -508,8 +526,8 @@
         out_shape=[shape((own, d_hid)), shape((n_batch, 2 * hid_bands, LANES))],
         scratch_shapes=[
             pltpu.VMEM((2 * hid_bands, LANES), F32),
-            pltpu.VMEM((d_hid // TILE, d_in, TILE), BF),
-            pltpu.SemaphoreType.DMA((d_hid // TILE,)),
+            pltpu.VMEM((4, d_in // 4, d_hid), BF),
+            pltpu.SemaphoreType.DMA((4,)),
         ],
         name="pre_kernel",
     )(features, w_first)
@@ -522,37 +540,50 @@
         relay_kernel, out_shape=shape((n_proto, 2 * hid_bands, LANES)), compiler_params=PARAMS, name="relay_kernel"
     )(got)
     got = deal(msg, "proto")
-    unit_embed, embed_scale, mean, inv, msg = pl.pallas_call(
+    unit_embed, mean, inv, msg = pl.pallas_call(
         lambda *refs: embed_kernel(total_rows, *refs),
-        out_specs=[pl.BlockSpec(memory_space=pltpu.HBM)] * 5,
+        out_specs=[pl.BlockSpec(memory_space=pltpu.HBM)] * 4,
         out_shape=[
-            far_shape((own, width)),
-            far_shape((own, LANES)),
+            far_shape((own, width + LANES)),
             far_shape((hid_bands, LANES)),
             far_shape((hid_bands, LANES)),
             far_shape((n_proto, own, width), BF),
         ],
         scratch_shapes=[
             pltpu.VMEM((own, d_hid), BF),
-            pltpu.VMEM((own, width), F32),
-            pltpu.VMEM((own, LANES), F32),
+            pltpu.VMEM((own, width + LANES), F32),
             pltpu.VMEM((hid_bands, LANES), F32),
             pltpu.VMEM((hid_bands, LANES), F32),
             pltpu.VMEM((own, width), BF),
-            pltpu.SemaphoreType.DMA((n_proto + 4,)),
+            pltpu.SemaphoreType.DMA((n_proto + 3,)),
         ],
         compiler_params=PARAMS,
         name="embed_kernel",
     )(pre, got, gain, bias, w_second)
     raw, *mine, _ = lax.optimization_barrier((prototypes, features, from_right, from_left, far_top, far_low, msg))
     parts = mine + [hop(piece, swap) for piece in mine]
-    proto_bf, proto_t, raw_t, norm = pl.pallas_call(
+    proto_bf, proto_t, raw_t, norm, w_slab = pl.pallas_call(
         proto_kernel,
-        out_shape=[shape((cols, width), BF), shape((width, cols), BF), shape((width, cols), BF), shape((8, cols))],
+        in_specs=[pl.BlockSpec(memory_space=pltpu.SMEM), pl.BlockSpec((cols, width), lambda: (0, 0)), anywhere],
+        out_specs=[
+            pl.BlockSpec((cols, width), lambda: (0, 0)),
+            pl.BlockSpec((width, cols), lambda: (0, 0)),
+            pl.BlockSpec((width, cols), lambda: (0, 0)),
+            pl.BlockSpec((8, cols), lambda: (0, 0)),
+            anywhere,
+        ],
+        out_shape=[
+            shape((cols, width), BF),
+            shape((width, cols), BF),
+            shape((width, cols), BF),
+            shape((8, cols)),
+            far_shape((d_in, slab), BF),
+        ],
+        scratch_shapes=[pltpu.VMEM((d_in, slab), BF), pltpu.SemaphoreType.DMA],
         name="proto_kernel",
-    )(raw)
-    block_embed, proto_bf, proto_t, raw_t, norm, *parts = lax.optimization_barrier(
-        (deal(msg, "proto"), proto_bf, proto_t, raw_t, norm, *parts)
+    )(order, raw, w_first)
+    block_embed, proto_bf, proto_t, raw_t, norm, w_slab, *parts = lax.optimization_barrier(
+        (deal(msg, "proto"), proto_bf, proto_t, raw_t, norm, w_slab, *parts)
     )
     block_embed = block_embed.reshape(rows, width)
 
@@ -607,7 +638,7 @@
 
     d_unit, *pieces, loss_tile = pl.pallas_call(
         final_kernel,
-        grid=(steps,),
+        grid=(steps // 2,),
         in_specs=[
             pl.BlockSpec(memory_space=pltpu.SMEM),
             whole((rows, width)),
@@ -620,19 +651,19 @@
             whole(recv_row.shape),
             whole(recv_soft.shape),
         ],
-        out_specs=[rows_of(TILE, width)] + [whole((width // side, cols))] * side + [whole((16, LANES))],
+        out_specs=[rows_of(2 * TILE, width)] + [whole((width // side, cols))] * side + [whole((16, LANES))],
         out_shape=[far_shape((rows, width), BF)]
         + [far_shape((width // side, cols), BF)] * side
         + [far_shape((16, LANES))],
         scratch_shapes=[
             pltpu.VMEM((rows, cols), BF),
-            pltpu.VMEM((TILE, rows), BF),
+            pltpu.VMEM((2 * TILE, rows), BF),
             pltpu.VMEM((16, LANES), F32),
             pltpu.VMEM((col_bands, LANES), F32),
             pltpu.VMEM((row_bands, LANES), F32),
             pltpu.VMEM((row_bands, LANES), F32),
             pltpu.VMEM((width, cols), BF),
-            pltpu.VMEM((2 * TILE, width), BF),
+            pltpu.VMEM((4 * TILE, width), BF),
         ],
         compiler_params=PARAMS,
         name="final_kernel",
@@ -666,11 +697,11 @@
         ),
         out_shape=[shape((rows, slab), BF)] * 3,
         name="slab_kernel",
-    )(order, mean_late, inv, gain, bias, w_first, *parts)
+    )(order, mean_late, inv, gain, bias, w_slab, *parts)
     d_unit, normed, slope, hid = lax.optimization_barrier((d_unit_got, normed, slope, hid))
     d_embed = pl.pallas_call(
         d_embed_kernel, out_shape=shape((n_proto, own, width), BF), compiler_params=PARAMS, name="d_embed_kernel"
-    )(d_unit, unit_embed, embed_scale)
+    )(d_unit, unit_embed)
     d_embed = deal(d_embed, "proto")
 
     shift, msg = pl.pallas_call(

time: 219 us -> 218 us (level)
    unnamed x55 -> x49, local copies, waits for them, and re-layouts: 5.15 us -> 3.64 us
  transfers between devices with their start and end apart: 21 -> 21, of which waited for: 6 -> 6; matrix products, arithmetic and copies ran while one was open for 1% -> 2% of each run, Pallas kernels for 14% -> 14%
where the time goes in v7:
time: 218 us; the launch traced here: 217 us
  blocking collectives  80.6 us (37%)
  Pallas kernels  55 us (25%)
  starting transfers between devices  46.9 us (22%)
  waiting for transfers between devices  26 us (12%)
  local copies, waits for them, and re-layouts  5.85 us (3%)
    all_to_all x8, blocking collectives, deal(): return lax.all_to_all(x, axis, 0, 0, tiled=True)  80.6 us
    all_to_all x5, starting transfers between devices, deal(): return lax.all_to_all(x, axis, 0, 0, tiled=True)  27.1 us
    all_to_all x5, waiting for transfers between devices, deal(): return lax.all_to_all(x, axis, 0, 0, tiled=True)  14.6 us
    pallas_call x1, Pallas kernels, step_of_device(): pl.pallas_call(final_kernel, grid=(steps // 2,), in_specs=[pl.BlockSpec(m...  10.7 us
    ppermute x1, waiting for transfers between devices, step_of_device(): lax.ppermute(second, ('batch', 'proto'), [(b * n_proto + p, p * n_batch +...  10 us
    ppermute x9, starting transfers between devices, hop(): return lax.ppermute(x, 'proto', moves)  8.02 us
    pallas_call x1, Pallas kernels, step_of_device(): pl.pallas_call(slab_kernel, grid_spec=pltpu.PrefetchScalarGridSpec(num_sc...  7.45 us
    pallas_call x1, Pallas kernels, step_of_device(): pl.pallas_call(pre_kernel, in_specs=[pl.BlockSpec(features.shape, lambda:...  6.17 us
  transfers between devices with their start and end apart: 21, of which 6 were waited for; matrix products, arithmetic and copies ran while one was open for 2% of the time, Pallas kernels for 14%

profile of v7, /device:TPU:1, one launch (start us, length us, event | category | flops | bytes accessed | tf_op | source)
XLA Modules:
  0.0 217.0 jit_solution(14599023014758678614)
XLA Ops:
  0.7 3.4 %collective-permute-start = (bf16[128,2048]{1,0:T(8,128)(2,1)}, bf16[128,2048]{1,0:T(8,128)(2,1)S(1)}, u32[]{:S(2)}, u32[]{:S(2)}) collective-permute-start(bf16[128,2048]{1,0:T(8,128)(2,1)} %refs_6_), channel_id=1, source_target_pairs={{2,0},{3,1},{4,2},{5,3},{6,4},{7,5},{0,6},{1,7},{10,8},{11,9},{12,... | collective-permute-start | bytes 1572872 | tf_op jit(solution)/shard_map/ppermute | solution.py:500
  4.0 6.2 %pre_kernel.1 = (f32[128,2048]{1,0:T(8,128)}, f32[16,32,128]{2,1,0:T(8,128)}) custom-call(bf16[128,2048]{1,0:T(8,128)(2,1)} %refs_6_, bf16[2048,2048]{1,0:T(8,128)(2,1)} %w_hbm.3), custom_call_target="tpu_custom_call" | custom-call | tf_op jit(solution)/shard_map/pre_kernel/pallas_call | solution.py:523
  10.2 7.9 %all-to-all-start = ((f32[16,32,128]{2,1,0:T(8,128)}), f32[16,32,128]{2,1,0:T(8,128)S(1)}, u32[]{:S(2)}, u32[]{:S(2)}) async-start(f32[16,32,128]{2,1,0:T(8,128)} %get-tuple-element.79), calls=%async_computation | async-start | bytes 524288 | tf_op jit(solution)/shard_map/all_to_all | solution.py:19
  18.9 0.8 slice.9
  20.4 2.6 %collective-permute-start.3 = (bf16[64,2048]{1,0:T(8,128)(2,1)}, bf16[64,2048]{1,0:T(8,128)(2,1)S(1)}, u32[]{:S(2)}, u32[]{:S(2)}) collective-permute-start(bf16[64,2048]{1,0:T(8,128)(2,1)} %slice.10), channel_id=1, source_target_pairs={{2,0},{3,1},{4,2},{5,3},{6,4},{7,5},{0,6},{1,7},{10,8},{11,9},{12,... | collective-permute-start | bytes 786440 | tf_op jit(solution)/shard_map/ppermute | solution.py:500
  23.1 2.5 %all-to-all-done.recv_ref = f32[16,32,128]{2,1,0:T(8,128)S(1)} async-done(((f32[16,32,128]{2,1,0:T(8,128)}), f32[16,32,128]{2,1,0:T(8,128)S(1)}, u32[]{:S(2)}, u32[]{:S(2)}) %all-to-all-start) | async-done | bytes 262176 | tf_op jit(solution)/shard_map/all_to_all | solution.py:19
  25.6 11.8 %all_to_all.65.refs_1_ = f32[8,32,128]{2,1,0:T(8,128)S(1)} all-to-all(f32[8,32,128]{2,1,0:T(8,128)S(1)} %relay_kernel.1), channel_id=1, replica_groups=mesh['batch'=16,'proto'=8] {'proto'}, dimensions={0} | all-to-all | bytes 262144 | tf_op jit(solution)/shard_map/all_to_all | solution.py:19
  37.5 1.2 copy-done.14
  38.7 1.8 embed_kernel.1
  40.5 0.9 collective-permute-start.4
  42.0 3.5 %all-to-all-start.2 = ((bf16[8,128,256]{2,1,0:T(8,128)(2,1)}), bf16[8,128,256]{2,1,0:T(8,128)(2,1)S(1)}, u32[]{:S(2)}, u32[]{:S(2)}) async-start(bf16[8,128,256]{2,1,0:T(8,128)(2,1)} %get-tuple-element.83), calls=%async_computation.2 | async-start | bytes 1048576 | tf_op jit(solution)/shard_map/all_to_all | solution.py:19
  46.0 5.2 %proto_kernel.1 = (bf16[2048,256]{1,0:T(8,128)(2,1)}, bf16[256,2048]{1,0:T(8,128)(2,1)}, bf16[256,2048]{1,0:T(8,128)(2,1)}, f32[8,2048]{1,0:T(8,128)}, bf16[2048,256]{1,0:T(8,128)(2,1)}) custom-call(s32[11]{0:T(128)} %stack.47.order_ref.refs_0_, bf16[2048,256]{1,0:T(8,128)(2,1)} %raw_ref, bf16[2048,2048]{1,0:T(8,128)(2,1)} %w_hbm.3), custom_call_target="tpu_custom_call" | custom-call | tf_op jit(solution)/shard_map/proto_kernel/pallas_call | solution.py:565
  51.2 3.6 %all-to-all-done.2 = bf16[8,128,256]{2,1,0:T(8,128)(2,1)S(1)} async-done(((bf16[8,128,256]{2,1,0:T(8,128)(2,1)}), bf16[8,128,256]{2,1,0:T(8,128)(2,1)S(1)}, u32[]{:S(2)}, u32[]{:S(2)}) %all-to-all-start.2) | async-done | bytes 524320 | tf_op jit(solution)/shard_map/all_to_all | solution.py:19
  54.9 5.7 %score_kernel.1 = (bf16[1024,2048]{1,0:T(8,128)(2,1)S(1)}, f32[16,16,128]{2,1,0:T(8,128)S(1)}, f32[8,128]{1,0:T(8,128)S(1)}) custom-call(bf16[1024,256]{1,0:T(8,128)(2,1)S(1)} %bitcast.25, bf16[256,2048]{1,0:T(8,128)(2,1)} %get-tuple-element.99.proto_t_hbm.proto_t_ref), custom_call_target="tpu_custom_call" | custom-call | tf_op jit(solution)/shard_map/score_kernel/pallas_call | solution.py:590
  60.6 10.4 %all_to_all.66.recv_ref = f32[16,16,128]{2,1,0:T(8,128)S(1)} all-to-all(f32[16,16,128]{2,1,0:T(8,128)S(1)} %get-tuple-element.103), channel_id=1, replica_groups=mesh['batch'=16,'proto'=8] {'batch'}, dimensions={0} | all-to-all | bytes 262144 | tf_op jit(solution)/shard_map/all_to_all | solution.py:19
  71.0 1.2 row_kernel.3
  72.2 9.6 %all_to_all.67.recv_ref.recv_soft_ref = f32[8,16,128]{2,1,0:T(8,128)S(1)} all-to-all(f32[8,16,128]{2,1,0:T(8,128)S(1)} %row_kernel.3), channel_id=1, replica_groups=mesh['batch'=16,'proto'=8] {'proto'}, dimensions={0} | all-to-all | bytes 131072 | tf_op jit(solution)/shard_map/all_to_all | solution.py:19
  81.8 1.2 col_kernel.2
  83.0 9.9 %all_to_all.68.recv_ref = f32[16,16,128]{2,1,0:T(8,128)S(1)} all-to-all(f32[16,16,128]{2,1,0:T(8,128)S(1)} %col_kernel.2), channel_id=1, replica_groups=mesh['batch'=16,'proto'=8] {'batch'}, dimensions={0} | all-to-all | bytes 262144 | tf_op jit(solution)/shard_map/all_to_all | solution.py:19
  92.8 1.2 row_kernel.4
  94.0 9.2 %all_to_all.69.recv_ref = f32[8,8,128]{2,1,0:T(8,128)S(1)} all-to-all(f32[8,8,128]{2,1,0:T(8,128)S(1)} %row_kernel.4), channel_id=1, replica_groups=mesh['batch'=16,'proto'=8] {'proto'}, dimensions={0} | all-to-all | bytes 65536 | tf_op jit(solution)/shard_map/all_to_all | solution.py:19
  103.3 1.2 col_kernel.3
  104.5 9.9 %all_to_all.70.recv_ref.recv_col_ref = f32[16,16,128]{2,1,0:T(8,128)S(1)} all-to-all(f32[16,16,128]{2,1,0:T(8,128)S(1)} %col_kernel.3), channel_id=1, replica_groups=mesh['batch'=16,'proto'=8] {'batch'}, dimensions={0} | all-to-all | bytes 262144 | tf_op jit(solution)/shard_map/all_to_all | solution.py:19
  114.4 1.2 row_kernel.5
  115.6 9.1 %all_to_all.71.recv_row_ref = f32[8,8,128]{2,1,0:T(8,128)S(1)} all-to-all(f32[8,8,128]{2,1,0:T(8,128)S(1)} %row_kernel.5), channel_id=1, replica_groups=mesh['batch'=16,'proto'=8] {'proto'}, dimensions={0} | all-to-all | bytes 65536 | tf_op jit(solution)/shard_map/all_to_all | solution.py:19
  124.8 10.7 %final_kernel.1 = (bf16[1024,256]{1,0:T(8,128)(2,1)}, bf16[64,2048]{1,0:T(8,128)(2,1)}, bf16[64,2048]{1,0:T(8,128)(2,1)}, bf16[64,2048]{1,0:T(8,128)(2,1)}, bf16[64,2048]{1,0:T(8,128)(2,1)}, /*index=5*/f32[16,128]{1,0:T(8,128)}) custom-call(s32[11]{0:T(128)S(1)} %copy-done.21, bf16[1024,256]{1,0:T(8,128)(2,1)S(1)} %bitcast.26, ...), custom_call_target="tpu_custom_call" | custom-call | tf_op jit(solution)/shard_map/final_kernel/pallas_call | solution.py:639
  135.5 4.7 %all-to-all-start.9 = ((bf16[8,128,256]{2,1,0:T(8,128)(2,1)}), bf16[8,128,256]{2,1,0:T(8,128)(2,1)}, u32[]{:S(2)}, u32[]{:S(2)}) async-start(bf16[8,128,256]{2,1,0:T(8,128)(2,1)} %bitcast.32), calls=%async_computation.9 | async-start | bytes 1048576 | tf_op jit(solution)/shard_map/all_to_all | solution.py:19
  140.2 7.4 %slab_kernel.1 = (bf16[1024,256]{1,0:T(8,128)(2,1)}, bf16[1024,256]{1,0:T(8,128)(2,1)}, bf16[1024,256]{1,0:T(8,128)(2,1)}) custom-call(s32[11]{0:T(128)} %stack.47.order_ref.refs_0_, f32[16,128]{1,0:T(8,128)} %get-tuple-element.109.mean_ref, f32[16,128]{1,0:T(8,128)} %get-tuple-element.110.inv_ref.refs_4_, f32[16,128]{1,0:T(8,128)} %bitcast.27, ...), custom_call_target="tpu_custom_call" | custom-call | tf_op jit(solution)/shard_map/slab_kernel/pallas_call | solution.py:684
  147.7 2.0 all-to-all-done.9.recv_ref
  149.7 0.9 copy-done.15
  150.6 1.2 d_embed_kernel.1
  152.7 5.0 %all-to-all-start.10 = ((bf16[8,128,256]{2,1,0:T(8,128)(2,1)}), bf16[8,128,256]{2,1,0:T(8,128)(2,1)}, u32[]{:S(2)}, u32[]{:S(2)}) async-start(bf16[8,128,256]{2,1,0:T(8,128)(2,1)} %copy-done.9), calls=%async_computation.10 | async-start | bytes 1048576 | tf_op jit(solution)/shard_map/all_to_all | solution.py:19
  157.9 1.9 collective-permute-start.10
  159.7 1.0 collective-permute-start.11
  160.7 6.4 %all-to-all-done.10.d_embed_ref = bf16[8,128,256]{2,1,0:T(8,128)(2,1)} async-done(((bf16[8,128,256]{2,1,0:T(8,128)(2,1)}), bf16[8,128,256]{2,1,0:T(8,128)(2,1)}, u32[]{:S(2)}, u32[]{:S(2)}) %all-to-all-start.10) | async-done | bytes 524320 | tf_op jit(solution)/shard_map/all_to_all | solution.py:19
  167.2 3.5 %shift_kernel.1 = (f32[1024,256]{1,0:T(8,128)S(1)}, bf16[16,32,256]{2,1,0:T(8,128)(2,1)S(1)}) custom-call(s32[11]{0:T(128)S(1)} %copy-done.22, bf16[8,128,256]{2,1,0:T(8,128)(2,1)} %all-to-all-done.10.d_embed_ref, bf16[2048,256]{1,0:T(8,128)(2,1)S(1)} %copy-done.3, bf16[1024,256]{1,0:T(8,128)(2,1)} %get-tuple-element.127.normed_hbm.refs_3_, ...), custom_call_target="tpu_custom_call" | custom-call | tf_op jit(solution)/shard_map/shift_kernel/pallas_call | solution.py:707
  170.6 10.6 %all_to_all.72.refs_1_ = bf16[16,32,256]{2,1,0:T(8,128)(2,1)S(1)} all-to-all(bf16[16,32,256]{2,1,0:T(8,128)(2,1)S(1)} %get-tuple-element.131), channel_id=1, replica_groups=mesh['batch'=16,'proto'=8] {'batch'}, dimensions={0} | all-to-all | bytes 524288 | tf_op jit(solution)/shard_map/all_to_all | solution.py:19
  181.3 4.5 %first_kernel.1 = (bf16[128,40,128]{2,1,0:T(8,128)(2,1)}, f32[16,256]{1,0:T(8,128)S(1)}) custom-call(s32[11]{0:T(128)S(1)} %copy-done.22, bf16[16,32,256]{2,1,0:T(8,128)(2,1)S(1)} %all_to_all.72.refs_1_, f32[1024,256]{1,0:T(8,128)S(1)} %get-tuple-element.132.refs_2_, bf16[1024,256]{1,0:T(8,128)(2,1)S(1)} %copy-done.8, f32[16,128]{1,0:T(8,128)S(1)} %copy-done.20, ...), custom_call_target="tpu_custom_call" | custom-call | tf_op jit(solution)/shard_map/first_kernel/pallas_call | solution.py:733
  185.8 6.0 %all-to-all-start.12 = ((bf16[128,40,128]{2,1,0:T(8,128)(2,1)}), bf16[128,40,128]{2,1,0:T(8,128)(2,1)S(1)}, u32[]{:S(2)}, u32[]{:S(2)}) async-start(bf16[128,40,128]{2,1,0:T(8,128)(2,1)} %get-tuple-element.138), calls=%async_computation.12 | async-start | bytes 2621440 | tf_op jit(solution)/shard_map/all_to_all | solution.py:19
  191.8 2.1 stage_kernel.1
  193.9 1.5 collective-permute-start.13
  195.4 2.9 %collective-permute-start.14 = (bf16[16,2048]{1,0:T(8,128)(2,1)}, bf16[16,2048]{1,0:T(8,128)(2,1)S(1)}, u32[]{:S(2)}, u32[]{:S(2)}) collective-permute-start(bf16[16,2048]{1,0:T(8,128)(2,1)} %get-tuple-element.149), channel_id=1, source_target_pairs={{0,16},{8,24},{16,0},{24,8},{32,48},{40,56},{48,32},{56,40},{64,80... | collective-permute-start | bytes 196616 | tf_op jit(solution)/shard_map/ppermute | solution.py:760
  198.3 0.9 collective-permute-start.15
  199.2 3.4 %collective-permute-start.12 = (f32[16,256]{1,0:T(8,128)S(1)}, f32[16,256]{1,0:T(8,128)S(1)}, u32[]{:S(2)}, u32[]{:S(2)}) collective-permute-start(f32[16,256]{1,0:T(8,128)S(1)} %get-tuple-element.140), channel_id=1, source_target_pairs={{0,0},{1,16},{2,32},{3,48},{4,64},{5,80},{6,96},{7,112},{8,1},{9,1... | collective-permute-start | bytes 49160 | tf_op jit(solution)/shard_map/ppermute | solution.py:769
  202.7 10.0 %collective-permute-done.12 = f32[16,256]{1,0:T(8,128)S(1)} collective-permute-done((f32[16,256]{1,0:T(8,128)S(1)}, f32[16,256]{1,0:T(8,128)S(1)}, u32[]{:S(2)}, u32[]{:S(2)}) %collective-permute-start.12) | collective-permute-done | bytes 16416 | tf_op jit(solution)/shard_map/ppermute | solution.py:769
  212.7 1.4 collective-permute-done.14
  214.1 1.5 add_bitcast_fusion
  215.6 0.8 tail_kernel.1
  (73 shorter events, 4.2 us)
Async XLA Ops:
  0.6 22.4 %copy-start.23 = (s32[1024]{0:T(1024)S(1)}, s32[1024]{0:T(1024)}, u32[]{:S(2)}) copy-start(s32[1024]{0:T(1024)} %param.13) | copy-start | bytes 12292
  0.6 36.8 %copy-start.3 = (bf16[2048,256]{1,0:T(8,128)(2,1)S(1)}, bf16[2048,256]{1,0:T(8,128)(2,1)}, u32[]{:S(2)}) copy-start(bf16[2048,256]{1,0:T(8,128)(2,1)} %w2_ref.1) | copy-start | bytes 3145732
  0.7 36.8 %copy-start.19 = (f32[2048]{0:T(1024)S(1)}, f32[2048]{0:T(1024)}, u32[]{:S(2)}) copy-start(f32[2048]{0:T(1024)} %param.10) | copy-start | bytes 24580
  0.7 36.8 %copy-start.16 = (f32[2048]{0:T(1024)S(1)}, f32[2048]{0:T(1024)}, u32[]{:S(2)}) copy-start(f32[2048]{0:T(1024)} %param.9) | copy-start | bytes 24580
  0.7 18.2 %collective-permute-start = (bf16[128,2048]{1,0:T(8,128)(2,1)}, bf16[128,2048]{1,0:T(8,128)(2,1)S(1)}, u32[]{:S(2)}, u32[]{:S(2)}) collective-permute-start(bf16[128,2048]{1,0:T(8,128)(2,1)} %refs_6_), channel_id=1, source_target_pairs={{2,0},{3,1},{4,2},{5,3},{6,4},{7,5},{0,6},{1,7},{10,8},{11,9},{12,... | collective-permute-start | bytes 1572872 | tf_op jit(solution)/shard_map/ppermute | solution.py:500
  4.0 14.8 %collective-permute-start.1 = (bf16[128,2048]{1,0:T(8,128)(2,1)}, bf16[128,2048]{1,0:T(8,128)(2,1)S(1)}, u32[]{:S(2)}, u32[]{:S(2)}) collective-permute-start(bf16[128,2048]{1,0:T(8,128)(2,1)} %refs_6_), channel_id=1, source_target_pairs={{0,2},{1,3},{2,4},{3,5},{4,6},{5,7},{6,0},{7,1},{8,10},{9,11},{10,... | collective-permute-start | bytes 1572872 | tf_op jit(solution)/shard_map/ppermute | solution.py:500
  10.2 30.3 %copy-start = (bf16[128,2048]{1,0:T(8,128)(2,1)S(1)}, bf16[128,2048]{1,0:T(8,128)(2,1)}, u32[]{:S(2)}) copy-start(bf16[128,2048]{1,0:T(8,128)(2,1)} %refs_6_) | copy-start | bytes 1572868
  10.2 15.4 %all-to-all-start = ((f32[16,32,128]{2,1,0:T(8,128)}), f32[16,32,128]{2,1,0:T(8,128)S(1)}, u32[]{:S(2)}, u32[]{:S(2)}) async-start(f32[16,32,128]{2,1,0:T(8,128)} %get-tuple-element.79), calls=%async_computation | async-start | bytes 524288 | tf_op jit(solution)/shard_map/all_to_all | solution.py:19
  18.9 32.4 %copy-start.4 = (bf16[128,2048]{1,0:T(8,128)(2,1)}, bf16[128,2048]{1,0:T(8,128)(2,1)S(1)}, u32[]{:S(2)}) copy-start(bf16[128,2048]{1,0:T(8,128)(2,1)S(1)} %collective-permute-done.rest_1_.refs_7_) | copy-start | bytes 1572868
  18.9 32.4 %copy-start.6 = (bf16[128,2048]{1,0:T(8,128)(2,1)}, bf16[128,2048]{1,0:T(8,128)(2,1)S(1)}, u32[]{:S(2)}) copy-start(bf16[128,2048]{1,0:T(8,128)(2,1)S(1)} %collective-permute-done.1.rest_2_.refs_8_) | copy-start | bytes 1572868
  20.4 20.1 %collective-permute-start.3 = (bf16[64,2048]{1,0:T(8,128)(2,1)}, bf16[64,2048]{1,0:T(8,128)(2,1)S(1)}, u32[]{:S(2)}, u32[]{:S(2)}) collective-permute-start(bf16[64,2048]{1,0:T(8,128)(2,1)} %slice.10), channel_id=1, source_target_pairs={{2,0},{3,1},{4,2},{5,3},{6,4},{7,5},{0,6},{1,7},{10,8},{11,9},{12,... | collective-permute-start | bytes 786440 | tf_op jit(solution)/shard_map/ppermute | solution.py:500
  23.1 17.5 %collective-permute-start.2 = (bf16[64,2048]{1,0:T(8,128)(2,1)}, bf16[64,2048]{1,0:T(8,128)(2,1)}, u32[]{:S(2)}, u32[]{:S(2)}) collective-permute-start(bf16[64,2048]{1,0:T(8,128)(2,1)} %slice.9), channel_id=1, source_target_pairs={{0,2},{1,3},{2,4},{3,5},{4,6},{5,7},{6,0},{7,1},{8,10},{9,11},{10,... | collective-permute-start | bytes 786440 | tf_op jit(solution)/shard_map/ppermute | solution.py:500
  37.5 1.2 copy-start.14
  40.5 10.7 %copy-start.12 = (bf16[64,2048]{1,0:T(8,128)(2,1)}, bf16[64,2048]{1,0:T(8,128)(2,1)S(1)}, u32[]{:S(2)}) copy-start(bf16[64,2048]{1,0:T(8,128)(2,1)S(1)} %collective-permute-done.3.rest_4_.refs_10_) | copy-start | bytes 786436
  40.5 14.3 %collective-permute-start.4 = (bf16[128,2048]{1,0:T(8,128)(2,1)S(1)}, bf16[128,2048]{1,0:T(8,128)(2,1)}, u32[]{:S(2)}, u32[]{:S(2)}) collective-permute-start(bf16[128,2048]{1,0:T(8,128)(2,1)S(1)} %copy-done), channel_id=1, source_target_pairs={{0,1},{1,0},{2,3},{3,2},{4,5},{5,4},{6,7},{7,6},{8,9},{9,8},{10,11... | collective-permute-start | bytes 1572872 | tf_op jit(solution)/shard_map/ppermute | solution.py:500
  41.5 13.4 %collective-permute-start.5 = (bf16[128,2048]{1,0:T(8,128)(2,1)S(1)}, bf16[128,2048]{1,0:T(8,128)(2,1)}, u32[]{:S(2)}, u32[]{:S(2)}) collective-permute-start(bf16[128,2048]{1,0:T(8,128)(2,1)S(1)} %collective-permute-done.rest_1_.refs_7_), channel_id=1, source_target_pairs={{0,1},{1,0},{2,3},{3,2},{4,5},{5,4},{6,7},{7,6},{8,9},{9,8},{10,11... | collective-permute-start | bytes 1572872 | tf_op jit(solution)/shard_map/ppermute | solution.py:500
  41.6 13.3 %collective-permute-start.6 = (bf16[128,2048]{1,0:T(8,128)(2,1)S(1)}, bf16[128,2048]{1,0:T(8,128)(2,1)}, u32[]{:S(2)}, u32[]{:S(2)}) collective-permute-start(bf16[128,2048]{1,0:T(8,128)(2,1)S(1)} %collective-permute-done.1.rest_2_.refs_8_), channel_id=1, source_target_pairs={{0,1},{1,0},{2,3},{3,2},{4,5},{5,4},{6,7},{7,6},{8,9},{9,8},{10,11... | collective-permute-start | bytes 1572872 | tf_op jit(solution)/shard_map/ppermute | solution.py:500
  42.0 12.9 %all-to-all-start.2 = ((bf16[8,128,256]{2,1,0:T(8,128)(2,1)}), bf16[8,128,256]{2,1,0:T(8,128)(2,1)S(1)}, u32[]{:S(2)}, u32[]{:S(2)}) async-start(bf16[8,128,256]{2,1,0:T(8,128)(2,1)} %get-tuple-element.83), calls=%async_computation.2 | async-start | bytes 1048576 | tf_op jit(solution)/shard_map/all_to_all | solution.py:19
  45.5 9.4 %collective-permute-start.7 = (bf16[64,2048]{1,0:T(8,128)(2,1)}, bf16[64,2048]{1,0:T(8,128)(2,1)}, u32[]{:S(2)}, u32[]{:S(2)}) collective-permute-start(bf16[64,2048]{1,0:T(8,128)(2,1)} %collective-permute-done.2.rest_3_.refs_9_), channel_id=1, source_target_pairs={{0,1},{1,0},{2,3},{3,2},{4,5},{5,4},{6,7},{7,6},{8,9},{9,8},{10,11... | collective-permute-start | bytes 786440 | tf_op jit(solution)/shard_map/ppermute | solution.py:500
  45.7 9.2 %collective-permute-start.8 = (bf16[64,2048]{1,0:T(8,128)(2,1)S(1)}, bf16[64,2048]{1,0:T(8,128)(2,1)}, u32[]{:S(2)}, u32[]{:S(2)}) collective-permute-start(bf16[64,2048]{1,0:T(8,128)(2,1)S(1)} %collective-permute-done.3.rest_4_.refs_10_), channel_id=1, source_target_pairs={{0,1},{1,0},{2,3},{3,2},{4,5},{5,4},{6,7},{7,6},{8,9},{9,8},{10,11... | collective-permute-start | bytes 786440 | tf_op jit(solution)/shard_map/ppermute | solution.py:500
  103.3 21.5 %copy-start.2 = (bf16[256,2048]{1,0:T(8,128)(2,1)S(1)}, bf16[256,2048]{1,0:T(8,128)(2,1)}, u32[]{:S(2)}) copy-start(bf16[256,2048]{1,0:T(8,128)(2,1)} %get-tuple-element.99.proto_t_hbm.proto_t_ref) | copy-start | bytes 3145732
  103.3 21.5 %copy-start.10 = (bf16[2048,256]{1,0:T(8,128)(2,1)S(1)}, bf16[2048,256]{1,0:T(8,128)(2,1)}, u32[]{:S(2)}) copy-start(bf16[2048,256]{1,0:T(8,128)(2,1)} %get-tuple-element.100.proto_ref) | copy-start | bytes 3145732
  103.3 21.5 %copy-start.11 = (bf16[256,2048]{1,0:T(8,128)(2,1)S(1)}, bf16[256,2048]{1,0:T(8,128)(2,1)}, u32[]{:S(2)}) copy-start(bf16[256,2048]{1,0:T(8,128)(2,1)} %get-tuple-element.101.raw_t_ref) | copy-start | bytes 3145732
  103.3 21.5 %copy-start.18 = (f32[8,2048]{1,0:T(8,128)S(1)}, f32[8,2048]{1,0:T(8,128)}, u32[]{:S(2)}) copy-start(f32[8,2048]{1,0:T(8,128)} %get-tuple-element.102.norm_ref) | copy-start | bytes 196612
  103.3 21.5 %copy-start.21 = (s32[11]{0:T(128)S(1)}, s32[11]{0:T(128)}, u32[]{:S(2)}) copy-start(s32[11]{0:T(128)} %stack.47.order_ref.refs_0_) | copy-start | bytes 136
  135.5 31.7 %copy-start.22 = (s32[11]{0:T(128)S(1)}, s32[11]{0:T(128)}, u32[]{:S(2)}) copy-start(s32[11]{0:T(128)} %stack.47.order_ref.refs_0_) | copy-start | bytes 136
  135.5 14.2 %all-to-all-start.9 = ((bf16[8,128,256]{2,1,0:T(8,128)(2,1)}), bf16[8,128,256]{2,1,0:T(8,128)(2,1)}, u32[]{:S(2)}, u32[]{:S(2)}) async-start(bf16[8,128,256]{2,1,0:T(8,128)(2,1)} %bitcast.32), calls=%async_computation.9 | async-start | bytes 1048576 | tf_op jit(solution)/shard_map/all_to_all | solution.py:19
  140.2 41.0 %copy-start.17 = (f32[2048]{0:T(1024)S(1)}, f32[2048]{0:T(1024)}, u32[]{:S(2)}) copy-start(f32[2048]{0:T(1024)} %param.9) | copy-start | bytes 24580
  140.2 41.0 %copy-start.20 = (f32[16,128]{1,0:T(8,128)S(1)}, f32[16,128]{1,0:T(8,128)}, u32[]{:S(2)}) copy-start(f32[16,128]{1,0:T(8,128)} %get-tuple-element.110.inv_ref.refs_4_) | copy-start | bytes 24580
  147.7 33.6 %copy-start.1 = (bf16[128,2048]{1,0:T(8,128)(2,1)S(1)}, bf16[128,2048]{1,0:T(8,128)(2,1)}, u32[]{:S(2)}) copy-start(bf16[128,2048]{1,0:T(8,128)(2,1)} %refs_6_) | copy-start | bytes 1572868
  147.7 33.6 %copy-start.5 = (bf16[128,2048]{1,0:T(8,128)(2,1)S(1)}, bf16[128,2048]{1,0:T(8,128)(2,1)}, u32[]{:S(2)}) copy-start(bf16[128,2048]{1,0:T(8,128)(2,1)} %copy-done.4) | copy-start | bytes 1572868
  147.7 33.6 %copy-start.7 = (bf16[128,2048]{1,0:T(8,128)(2,1)S(1)}, bf16[128,2048]{1,0:T(8,128)(2,1)}, u32[]{:S(2)}) copy-start(bf16[128,2048]{1,0:T(8,128)(2,1)} %copy-done.6) | copy-start | bytes 1572868
  147.7 33.6 %copy-start.8 = (bf16[1024,256]{1,0:T(8,128)(2,1)S(1)}, bf16[1024,256]{1,0:T(8,128)(2,1)}, u32[]{:S(2)}) copy-start(bf16[1024,256]{1,0:T(8,128)(2,1)} %get-tuple-element.127.normed_hbm.refs_3_) | copy-start | bytes 1572868
  147.7 33.6 %copy-start.13 = (bf16[64,2048]{1,0:T(8,128)(2,1)S(1)}, bf16[64,2048]{1,0:T(8,128)(2,1)}, u32[]{:S(2)}) copy-start(bf16[64,2048]{1,0:T(8,128)(2,1)} %copy-done.12) | copy-start | bytes 786436
  149.7 0.9 copy-start.15
  151.9 0.8 copy-start.9
  152.7 14.5 %all-to-all-start.10 = ((bf16[8,128,256]{2,1,0:T(8,128)(2,1)}), bf16[8,128,256]{2,1,0:T(8,128)(2,1)}, u32[]{:S(2)}, u32[]{:S(2)}) async-start(bf16[8,128,256]{2,1,0:T(8,128)(2,1)} %copy-done.9), calls=%async_computation.10 | async-start | bytes 1048576 | tf_op jit(solution)/shard_map/all_to_all | solution.py:19
  157.7 28.1 %collective-permute-start.9 = (bf16[64,2048]{1,0:T(8,128)(2,1)}, bf16[64,2048]{1,0:T(8,128)(2,1)}, u32[]{:S(2)}, u32[]{:S(2)}) collective-permute-start(bf16[64,2048]{1,0:T(8,128)(2,1)} %get-tuple-element.135), channel_id=1, source_target_pairs={{0,32},{8,40},{16,48},{24,56},{32,64},{40,72},{48,80},{56,88},{64,... | collective-permute-start | bytes 786440 | tf_op jit(solution)/shard_map/ppermute | solution.py:680
  157.9 27.9 %collective-permute-start.10 = (bf16[64,2048]{1,0:T(8,128)(2,1)}, bf16[64,2048]{1,0:T(8,128)(2,1)}, u32[]{:S(2)}, u32[]{:S(2)}) collective-permute-start(bf16[64,2048]{1,0:T(8,128)(2,1)} %get-tuple-element.136), channel_id=1, source_target_pairs={{0,64},{8,72},{16,80},{24,88},{32,96},{40,104},{48,112},{56,120},{... | collective-permute-start | bytes 786440 | tf_op jit(solution)/shard_map/ppermute | solution.py:680
  159.7 26.0 %collective-permute-start.11 = (bf16[64,2048]{1,0:T(8,128)(2,1)}, bf16[64,2048]{1,0:T(8,128)(2,1)}, u32[]{:S(2)}, u32[]{:S(2)}) collective-permute-start(bf16[64,2048]{1,0:T(8,128)(2,1)} %get-tuple-element.137), channel_id=1, source_target_pairs={{0,96},{8,104},{16,112},{24,120},{32,0},{40,8},{48,16},{56,24},{64... | collective-permute-start | bytes 786440 | tf_op jit(solution)/shard_map/ppermute | solution.py:680
  185.8 29.8 %all-to-all-start.12 = ((bf16[128,40,128]{2,1,0:T(8,128)(2,1)}), bf16[128,40,128]{2,1,0:T(8,128)(2,1)S(1)}, u32[]{:S(2)}, u32[]{:S(2)}) async-start(bf16[128,40,128]{2,1,0:T(8,128)(2,1)} %get-tuple-element.138), calls=%async_computation.12 | async-start | bytes 2621440 | tf_op jit(solution)/shard_map/all_to_all | solution.py:19
  193.9 18.8 %collective-permute-start.13 = (bf16[16,2048]{1,0:T(8,128)(2,1)}, bf16[16,2048]{1,0:T(8,128)(2,1)S(1)}, u32[]{:S(2)}, u32[]{:S(2)}) collective-permute-start(bf16[16,2048]{1,0:T(8,128)(2,1)} %get-tuple-element.148), channel_id=1, source_target_pairs={{0,8},{8,16},{16,24},{24,0},{32,40},{40,48},{48,56},{56,32},{64,72... | collective-permute-start | bytes 196616 | tf_op jit(solution)/shard_map/ppermute | solution.py:760
  195.4 18.7 %collective-permute-start.14 = (bf16[16,2048]{1,0:T(8,128)(2,1)}, bf16[16,2048]{1,0:T(8,128)(2,1)S(1)}, u32[]{:S(2)}, u32[]{:S(2)}) collective-permute-start(bf16[16,2048]{1,0:T(8,128)(2,1)} %get-tuple-element.149), channel_id=1, source_target_pairs={{0,16},{8,24},{16,0},{24,8},{32,48},{40,56},{48,32},{56,40},{64,80... | collective-permute-start | bytes 196616 | tf_op jit(solution)/shard_map/ppermute | solution.py:760
  198.3 15.7 %collective-permute-start.15 = (bf16[16,2048]{1,0:T(8,128)(2,1)}, bf16[16,2048]{1,0:T(8,128)(2,1)S(1)}, u32[]{:S(2)}, u32[]{:S(2)}) collective-permute-start(bf16[16,2048]{1,0:T(8,128)(2,1)} %get-tuple-element.150), channel_id=1, source_target_pairs={{0,24},{8,0},{16,8},{24,16},{32,56},{40,32},{48,40},{56,48},{64,88... | collective-permute-start | bytes 196616 | tf_op jit(solution)/shard_map/ppermute | solution.py:760
  199.2 13.4 %collective-permute-start.12 = (f32[16,256]{1,0:T(8,128)S(1)}, f32[16,256]{1,0:T(8,128)S(1)}, u32[]{:S(2)}, u32[]{:S(2)}) collective-permute-start(f32[16,256]{1,0:T(8,128)S(1)} %get-tuple-element.140), channel_id=1, source_target_pairs={{0,0},{1,16},{2,32},{3,48},{4,64},{5,80},{6,96},{7,112},{8,1},{9,1... | collective-permute-start | bytes 49160 | tf_op jit(solution)/shard_map/ppermute | solution.py:769

commit v8 on v7

--- a/solution.py
+++ b/solution.py
@@ -123,48 +123,36 @@
 
 
 def score_kernel(embed_ref, proto_t_hbm, kern_ref, msg_ref, soft_ref, acc_ref, proto_t_ref, sems):
-    step = pl.program_id(0)
-    rows = embed_ref.shape[0]
-    cols = proto_t_ref.shape[1]
-
-    def copy(j):
-        span = slice(j * TILE, (j + 1) * TILE)
-        return pltpu.make_async_copy(proto_t_hbm.at[:, span], proto_t_ref.at[:, span], sems.at[j])
-
-    @pl.when(step == 0)
-    def _():
-        for j in range(cols // TILE):
-            copy(j).start()
-        acc_ref[...] = jnp.zeros_like(acc_ref)
-
-    soft = [None] * (rows // LANES)
+    total, cols = kern_ref.shape
+    copies = []
     for j in range(cols // TILE):
         span = slice(j * TILE, (j + 1) * TILE)
-        if j % 2 == 0:
-
-            @pl.when(step == 0)
-            def _():
-                copy(j).wait()
-                copy(j + 1).wait()
-
-        scores = jnp.dot(embed_ref[...], proto_t_ref[:, span], preferred_element_type=F32)
-        tempered = jnp.exp2(scores * (10.0 * LOG2_E))
-        kern = tempered * tempered
-        kern_ref[:, span] = kern.astype(BF)
-        for h in range(TILE // LANES):
-            at = (j * (TILE // LANES) + h) * 8
-            acc_ref[at : at + 8, :] += fold_rows(kern[:, lane(h)])
-        for b in range(rows // LANES):
-            part = tempered[b * LANES : (b + 1) * LANES]
-            part = part[:, :LANES] + part[:, LANES:]
-            soft[b] = part if soft[b] is None else soft[b] + part
-    for b in range(rows // LANES):
-        soft_ref[pl.ds(step * (rows // LANES) + b, 1), :] = jnp.sum(soft[b].T, axis=0, keepdims=True)
-
-    @pl.when(step == pl.num_programs(0) - 1)
-    def _():
-        total = jnp.sum(acc_ref[...].reshape(cols // LANES, 8, LANES), axis=1)
-        msg_ref[...] = jnp.broadcast_to(total[None], msg_ref.shape)
+        copies.append(pltpu.make_async_copy(proto_t_hbm.at[:, span], proto_t_ref.at[:, span], sems.at[j]))
+        copies[-1].start()
+    acc_ref[...] = jnp.zeros_like(acc_ref)
+    for step in range(total // TILE):
+        band = slice(step * TILE, (step + 1) * TILE)
+        soft = [None] * (TILE // LANES)
+        for j in range(cols // TILE):
+            span = slice(j * TILE, (j + 1) * TILE)
+            if step == 0:
+                copies[j].wait()
+            scores = jnp.dot(embed_ref[band, :], proto_t_ref[:, span], preferred_element_type=F32)
+            tempered = jnp.exp2(scores * (10.0 * LOG2_E))
+            kern = tempered * tempered
+            kern_ref[band, span] = kern.astype(BF)
+            for h in range(TILE // LANES):
+                at = (j * (TILE // LANES) + h) * 8
+                acc_ref[at : at + 8, :] += fold_rows(kern[:, lane(h)])
+            for b in range(TILE // LANES):
+                part = tempered[b * LANES : (b + 1) * LANES]
+                part = part[:, :LANES] + part[:, LANES:]
+                soft[b] = part if soft[b] is None else soft[b] + part
+        for b in range(TILE // LANES):
+            at = step * (TILE // LANES) + b
+            soft_ref[at : at + 1, :] = jnp.sum(soft[b].T, axis=0, keepdims=True)
+    sums = jnp.sum(acc_ref[...].reshape(cols // LANES, 8, LANES), axis=1)
+    msg_ref[...] = jnp.broadcast_to(sums[None], msg_ref.shape)
 
 
 def row_kernel(recv_ref, kern_ref, *rest):
@@ -279,7 +267,12 @@
         loss_ref[...] = loss_acc_ref[...]
 
 
-def d_embed_kernel(recv_ref, unit_ref, msg_ref):
+def d_embed_kernel(recv_hbm, unit_hbm, msg_ref, recv_ref, unit_ref, sems):
+    copies = [pltpu.make_async_copy(recv_hbm, recv_ref, sems.at[0]), pltpu.make_async_copy(unit_hbm, unit_ref, sems.at[1])]
+    for copy in copies:
+        copy.start()
+    for copy in copies:
+        copy.wait()
     d_unit = jnp.sum(recv_ref[...].astype(F32), axis=0)
     width = d_unit.shape[1]
     unit = unit_ref[:, :width]
@@ -299,17 +292,24 @@
     return copies
 
 
-def slab_kernel(order_ref, mean_ref, inv_ref, gain_ref, bias_ref, w_hbm, *rest):
-    parts = rest[:-9]
-    outs, bufs = rest[-9:-6], rest[-6:-3]
-    buf_ref, w_ref, sems = rest[-3:]
+def slab_kernel(order_ref, mean_hbm, inv_hbm, gain_hbm, bias_hbm, w_hbm, *rest):
+    parts = rest[:-13]
+    outs, bufs = rest[-13:-10], rest[-10:-7]
+    mean_ref, inv_ref, gain_ref, bias_ref, buf_ref, w_ref, sems = rest[-7:]
     normed_ref, slope_ref, hid_ref = bufs
     rows, slab = normed_ref.shape
     w_copy = pltpu.make_async_copy(w_hbm, w_ref, sems.at[len(parts)])
     w_copy.start()
     copies = start_parts(parts, buf_ref, sems)
     stops = [sum(part.shape[0] for part in parts[: k + 1]) for k in range(len(parts))]
+    moves = ((mean_hbm, mean_ref), (inv_hbm, inv_ref), (gain_hbm, gain_ref), (bias_hbm, bias_ref))
+    base = sems.shape[0] - len(moves)
+    stats = [pltpu.make_async_copy(src, dst, sems.at[base + k]) for k, (src, dst) in enumerate(moves)]
+    for copy in stats:
+        copy.start()
     w_copy.wait()
+    for copy in stats:
+        copy.wait()
     chunks = slab // LANES
     ones = jnp.ones((LANES, LANES), F32)
     done = 0
@@ -341,10 +341,13 @@
 
 
 def shift_kernel(
-    order_ref, d_embed_ref, w2_ref, normed_hbm, slope_hbm, hid_hbm, loss_hbm, shift_ref, msg_ref, sum_ref, loss_ref,
-    normed_ref, slope_ref, hid_ref, sems,
+    order_ref, d_embed_hbm, w2_hbm, normed_hbm, slope_hbm, hid_hbm, loss_hbm, shift_ref, msg_ref, sum_ref, loss_ref,
+    normed_ref, slope_ref, hid_ref, d_embed_ref, w2_ref, sems,
 ):
-    moves = ((slope_hbm, slope_ref), (normed_hbm, normed_ref), (hid_hbm, hid_ref), (loss_hbm, loss_ref))
+    slab = w2_ref.shape[0]
+    at = pl.ds(pl.multiple_of(order_ref[0] * slab, slab), slab)
+    moves = ((d_embed_hbm, d_embed_ref), (w2_hbm.at[at], w2_ref))
+    moves += ((slope_hbm, slope_ref), (normed_hbm, normed_ref), (hid_hbm, hid_ref), (loss_hbm, loss_ref))
     copies = [pltpu.make_async_copy(src, dst, sems.at[k]) for k, (src, dst) in enumerate(moves)]
     for copy in copies:
         copy.start()
@@ -589,9 +592,7 @@
 
     kern, col_msg, soft = pl.pallas_call(
         score_kernel,
-        grid=(steps,),
-        in_specs=[rows_of(TILE, width), anywhere],
-        out_specs=[rows_of(TILE, cols), whole((n_batch, col_bands, LANES)), whole((row_bands, LANES))],
+        in_specs=[pl.BlockSpec((rows, width), lambda: (0, 0)), anywhere],
         out_shape=[shape((rows, cols), BF), shape((n_batch, col_bands, LANES)), shape((row_bands, LANES))],
         scratch_shapes=[
             pltpu.VMEM((col_bands * 8, LANES), F32),
@@ -686,13 +687,14 @@
         grid_spec=pltpu.PrefetchScalarGridSpec(
             num_scalar_prefetch=1,
             grid=(1,),
-            in_specs=[stat_spec] * 4 + [anywhere] * (1 + len(parts)),
+            in_specs=[anywhere] * (5 + len(parts)),
             out_specs=[pl.BlockSpec(memory_space=pltpu.HBM)] * 3,
             scratch_shapes=[pltpu.VMEM((rows, slab), BF)] * 3
+            + [pltpu.VMEM((hid_bands, LANES), F32)] * 4
             + [
                 pltpu.VMEM((rows, d_in), BF),
                 pltpu.VMEM((d_in, slab), BF),
-                pltpu.SemaphoreType.DMA((len(parts) + 1 + 3 * (rows // TILE),)),
+                pltpu.SemaphoreType.DMA((len(parts) + 5 + 3 * (rows // TILE),)),
             ],
         ),
         out_shape=[shape((rows, slab), BF)] * 3,
@@ -700,8 +702,25 @@
     )(order, mean_late, inv, gain, bias, w_slab, *parts)
     d_unit, normed, slope, hid = lax.optimization_barrier((d_unit_got, normed, slope, hid))
     d_embed = pl.pallas_call(
-        d_embed_kernel, out_shape=shape((n_proto, own, width), BF), compiler_params=PARAMS, name="d_embed_kernel"
-    )(d_unit, unit_embed)
+        d_embed_kernel,
+        in_specs=[anywhere] * 2,
+        out_shape=far_shape((n_proto, own, width), BF),
+        scratch_shapes=[
+            pltpu.VMEM((n_proto, own, width), BF),
+            pltpu.VMEM((own, width + LANES), F32),
+            pltpu.SemaphoreType.DMA((2,)),
+        ],
+        name="d_embed_kernel",
+    )(far(d_unit), far(unit_embed))
+    pieces[0], _ = lax.optimization_barrier((pieces[0], d_embed))
+    pieces = pl.pallas_call(
+        stage_kernel,
+        in_specs=[pl.BlockSpec(memory_space=pltpu.SMEM)] + [pl.BlockSpec((width // side, cols), lambda: (0, 0))] * side,
+        out_shape=[shape((width // n_batch, cols), BF)] * side,
+        scratch_shapes=[pltpu.VMEM((width // side, cols), BF)],
+        name="stage_kernel",
+    )(order, *pieces)
+    pieces = [pieces[0]] + [lax.ppermute(pieces[d], "batch", shifted(1, d)) for d in range(1, side)]
     d_embed = deal(d_embed, "proto")
 
     shift, msg = pl.pallas_call(
@@ -710,8 +729,8 @@
             num_scalar_prefetch=1,
             grid=(1,),
             in_specs=[
-                whole((n_proto, own, width)),
-                pl.BlockSpec((slab, width), lambda i, s: (s[0], 0)),
+                anywhere,
+                anywhere,
                 anywhere,
                 anywhere,
                 anywhere,
@@ -720,12 +739,12 @@
             out_specs=[whole((rows, slab)), whole((n_batch, 2 * slab // n_batch, width))],
             scratch_shapes=[pltpu.VMEM((8, slab), F32), pltpu.VMEM((16, LANES), F32)]
             + [pltpu.VMEM((rows, slab), BF)] * 3
-            + [pltpu.SemaphoreType.DMA((4,))],
+            + [pltpu.VMEM((n_proto, own, width), BF), pltpu.VMEM((slab, width), BF), pltpu.SemaphoreType.DMA((6,))],
         ),
         out_shape=[shape((rows, slab)), shape((n_batch, 2 * slab // n_batch, width), BF)],
         compiler_params=PARAMS,
         name="shift_kernel",
-    )(order, d_embed, w_second, far(normed), far(slope), far(hid), far(loss_tile))
+    )(order, far(d_embed), far(w_second), far(normed), far(slope), far(hid), far(loss_tile))
     recv = deal(msg, "batch")
 
     share = d_in // (n_batch * n_proto)
@@ -750,14 +769,6 @@
     )(order, recv, shift, normed, inv, gain, *parts)
 
     first, *pieces = lax.optimization_barrier((first, *pieces))
-    pieces = pl.pallas_call(
-        stage_kernel,
-        in_specs=[pl.BlockSpec(memory_space=pltpu.SMEM)] + [pl.BlockSpec((width // side, cols), lambda: (0, 0))] * side,
-        out_shape=[shape((width // n_batch, cols), BF)] * side,
-        scratch_shapes=[pltpu.VMEM((width // side, cols), BF)],
-        name="stage_kernel",
-    )(order, *pieces)
-    pieces = [pieces[0]] + [lax.ppermute(pieces[d], "batch", shifted(1, d)) for d in range(1, side)]
     grad_proto = sum(piece.astype(F32) for piece in pieces).T
     first = deal(first, ("batch", "proto")).reshape(n_batch, n_proto, lines, LANES)
     grad_first, grad_gain, grad_bias, loss = pl.pallas_call(

time: 218 us -> 218 us (level)
  blocking collectives: 80.6 us -> 70 us
  starting transfers between devices: 46.9 us -> 52.6 us
  waiting for transfers between devices: 26 us -> 30.2 us
    all_to_all x5 -> x6, waiting for transfers between devices: 14.6 us -> 30.2 us  [deal(): return lax.all_to_all(x, axis, 0, 0, tiled=True)]
    all_to_all x8 -> x7, blocking collectives: 80.6 us -> 70 us  [deal(): return lax.all_to_all(x, axis, 0, 0, tiled=True)]
    ppermute x1, waiting for transfers between devices: 10 us -> 0.01 us  [step_of_device(): lax.ppermute(second, ('batch', 'proto'), [(b * n_proto + p, p * n_batch +...]
    all_to_all x5 -> x6, starting transfers between devices: 27.1 us -> 31.4 us  [deal(): return lax.all_to_all(x, axis, 0, 0, tiled=True)]
    unnamed x49 -> x63, local copies, waits for them, and re-layouts: 3.64 us -> 4.9 us
  transfers between devices with their start and end apart: 21 -> 22, of which waited for: 6 -> 6; matrix products, arithmetic and copies ran while one was open for 2% -> 2% of each run, Pallas kernels for 14% -> 14%
where the time goes in v8:
time: 218 us; the launch traced here: 216 us
  blocking collectives  70 us (32%)
  Pallas kernels  53.6 us (25%)
  starting transfers between devices  52.6 us (24%)
  waiting for transfers between devices  30.2 us (14%)
  local copies, waits for them, and re-layouts  7.08 us (3%)
    all_to_all x7, blocking collectives, deal(): return lax.all_to_all(x, axis, 0, 0, tiled=True)  70 us
    all_to_all x6, starting transfers between devices, deal(): return lax.all_to_all(x, axis, 0, 0, tiled=True)  31.4 us
    all_to_all x6, waiting for transfers between devices, deal(): return lax.all_to_all(x, axis, 0, 0, tiled=True)  30.2 us
    pallas_call x1, Pallas kernels, step_of_device(): pl.pallas_call(final_kernel, grid=(steps // 2,), in_specs=[pl.BlockSpec(m...  10.7 us
    ppermute x9, starting transfers between devices, hop(): return lax.ppermute(x, 'proto', moves)  8.03 us
    pallas_call x1, Pallas kernels, step_of_device(): pl.pallas_call(slab_kernel, grid_spec=pltpu.PrefetchScalarGridSpec(num_sc...  7.36 us
    pallas_call x1, Pallas kernels, step_of_device(): pl.pallas_call(pre_kernel, in_specs=[pl.BlockSpec(features.shape, lambda:...  6.16 us
    ppermute x1, starting transfers between devices, step_of_device(): lax.ppermute(second, ('batch', 'proto'), [(b * n_proto + p, p * n_batch +...  5.44 us
  transfers between devices with their start and end apart: 22, of which 6 were waited for; matrix products, arithmetic and copies ran while one was open for 2% of the time, Pallas kernels for 14%

profile of v8, /device:TPU:1, one launch (start us, length us, event | category | flops | bytes accessed | tf_op | source)
XLA Modules:
  0.0 216.3 jit_solution(1752585115922482812)
XLA Ops:
  0.7 3.4 %collective-permute-start = (bf16[128,2048]{1,0:T(8,128)(2,1)}, bf16[128,2048]{1,0:T(8,128)(2,1)S(1)}, u32[]{:S(2)}, u32[]{:S(2)}) collective-permute-start(bf16[128,2048]{1,0:T(8,128)(2,1)} %refs_6_), channel_id=1, source_target_pairs={{2,0},{3,1},{4,2},{5,3},{6,4},{7,5},{0,6},{1,7},{10,8},{11,9},{12,... | collective-permute-start | bytes 1572872 | tf_op jit(solution)/shard_map/ppermute | solution.py:503
  4.0 6.2 %pre_kernel.1 = (f32[128,2048]{1,0:T(8,128)}, f32[16,32,128]{2,1,0:T(8,128)}) custom-call(bf16[128,2048]{1,0:T(8,128)(2,1)} %refs_6_, bf16[2048,2048]{1,0:T(8,128)(2,1)} %w_hbm.3), custom_call_target="tpu_custom_call" | custom-call | tf_op jit(solution)/shard_map/pre_kernel/pallas_call | solution.py:526
  10.2 7.9 %all-to-all-start = ((f32[16,32,128]{2,1,0:T(8,128)}), f32[16,32,128]{2,1,0:T(8,128)S(1)}, u32[]{:S(2)}, u32[]{:S(2)}) async-start(f32[16,32,128]{2,1,0:T(8,128)} %get-tuple-element.80), calls=%async_computation | async-start | bytes 524288 | tf_op jit(solution)/shard_map/all_to_all | solution.py:19
  18.8 0.8 slice.9
  20.4 2.6 %collective-permute-start.3 = (bf16[64,2048]{1,0:T(8,128)(2,1)}, bf16[64,2048]{1,0:T(8,128)(2,1)S(1)}, u32[]{:S(2)}, u32[]{:S(2)}) collective-permute-start(bf16[64,2048]{1,0:T(8,128)(2,1)} %slice.10), channel_id=1, source_target_pairs={{2,0},{3,1},{4,2},{5,3},{6,4},{7,5},{0,6},{1,7},{10,8},{11,9},{12,... | collective-permute-start | bytes 786440 | tf_op jit(solution)/shard_map/ppermute | solution.py:503
  23.0 2.6 %all-to-all-done.recv_ref = f32[16,32,128]{2,1,0:T(8,128)S(1)} async-done(((f32[16,32,128]{2,1,0:T(8,128)}), f32[16,32,128]{2,1,0:T(8,128)S(1)}, u32[]{:S(2)}, u32[]{:S(2)}) %all-to-all-start) | async-done | bytes 262176 | tf_op jit(solution)/shard_map/all_to_all | solution.py:19
  25.6 11.8 %all_to_all.65.refs_1_ = f32[8,32,128]{2,1,0:T(8,128)S(1)} all-to-all(f32[8,32,128]{2,1,0:T(8,128)S(1)} %relay_kernel.1), channel_id=1, replica_groups=mesh['batch'=16,'proto'=8] {'proto'}, dimensions={0} | all-to-all | bytes 262144 | tf_op jit(solution)/shard_map/all_to_all | solution.py:19
  37.5 1.2 copy-done.17
  38.7 1.8 embed_kernel.1
  40.6 0.9 collective-permute-start.4
  42.0 3.5 %all-to-all-start.2 = ((bf16[8,128,256]{2,1,0:T(8,128)(2,1)}), bf16[8,128,256]{2,1,0:T(8,128)(2,1)S(1)}, u32[]{:S(2)}, u32[]{:S(2)}) async-start(bf16[8,128,256]{2,1,0:T(8,128)(2,1)} %get-tuple-element.84), calls=%async_computation.2 | async-start | bytes 1048576 | tf_op jit(solution)/shard_map/all_to_all | solution.py:19
  46.1 5.2 %proto_kernel.1 = (bf16[2048,256]{1,0:T(8,128)(2,1)}, bf16[256,2048]{1,0:T(8,128)(2,1)}, bf16[256,2048]{1,0:T(8,128)(2,1)}, f32[8,2048]{1,0:T(8,128)}, bf16[2048,256]{1,0:T(8,128)(2,1)}) custom-call(s32[11]{0:T(128)} %stack.47.order_ref.refs_0_, bf16[2048,256]{1,0:T(8,128)(2,1)} %raw_ref, bf16[2048,2048]{1,0:T(8,128)(2,1)} %w_hbm.3), custom_call_target="tpu_custom_call" | custom-call | tf_op jit(solution)/shard_map/proto_kernel/pallas_call | solution.py:568
  51.3 3.6 %all-to-all-done.2 = bf16[8,128,256]{2,1,0:T(8,128)(2,1)S(1)} async-done(((bf16[8,128,256]{2,1,0:T(8,128)(2,1)}), bf16[8,128,256]{2,1,0:T(8,128)(2,1)S(1)}, u32[]{:S(2)}, u32[]{:S(2)}) %all-to-all-start.2) | async-done | bytes 524320 | tf_op jit(solution)/shard_map/all_to_all | solution.py:19
  54.9 4.5 %score_kernel.1 = (bf16[1024,2048]{1,0:T(8,128)(2,1)S(1)}, f32[16,16,128]{2,1,0:T(8,128)S(1)}, f32[8,128]{1,0:T(8,128)S(1)}) custom-call(bf16[1024,256]{1,0:T(8,128)(2,1)S(1)} %bitcast.25, bf16[256,2048]{1,0:T(8,128)(2,1)} %get-tuple-element.100.proto_t_hbm.proto_t_ref), custom_call_target="tpu_custom_call" | custom-call | tf_op jit(solution)/shard_map/score_kernel/pallas_call | solution.py:593
  59.4 10.4 %all_to_all.66.recv_ref = f32[16,16,128]{2,1,0:T(8,128)S(1)} all-to-all(f32[16,16,128]{2,1,0:T(8,128)S(1)} %get-tuple-element.104), channel_id=1, replica_groups=mesh['batch'=16,'proto'=8] {'batch'}, dimensions={0} | all-to-all | bytes 262144 | tf_op jit(solution)/shard_map/all_to_all | solution.py:19
  69.8 1.2 row_kernel.3
  71.0 9.6 %all_to_all.67.recv_ref.recv_soft_ref = f32[8,16,128]{2,1,0:T(8,128)S(1)} all-to-all(f32[8,16,128]{2,1,0:T(8,128)S(1)} %row_kernel.3), channel_id=1, replica_groups=mesh['batch'=16,'proto'=8] {'proto'}, dimensions={0} | all-to-all | bytes 131072 | tf_op jit(solution)/shard_map/all_to_all | solution.py:19
  80.6 1.2 col_kernel.2
  81.8 9.9 %all_to_all.68.recv_ref = f32[16,16,128]{2,1,0:T(8,128)S(1)} all-to-all(f32[16,16,128]{2,1,0:T(8,128)S(1)} %col_kernel.2), channel_id=1, replica_groups=mesh['batch'=16,'proto'=8] {'batch'}, dimensions={0} | all-to-all | bytes 262144 | tf_op jit(solution)/shard_map/all_to_all | solution.py:19
  91.7 1.2 row_kernel.4
  92.9 9.2 %all_to_all.69.recv_ref = f32[8,8,128]{2,1,0:T(8,128)S(1)} all-to-all(f32[8,8,128]{2,1,0:T(8,128)S(1)} %row_kernel.4), channel_id=1, replica_groups=mesh['batch'=16,'proto'=8] {'proto'}, dimensions={0} | all-to-all | bytes 65536 | tf_op jit(solution)/shard_map/all_to_all | solution.py:19
  102.1 1.2 col_kernel.3
  103.3 9.9 %all_to_all.70.recv_ref.recv_col_ref = f32[16,16,128]{2,1,0:T(8,128)S(1)} all-to-all(f32[16,16,128]{2,1,0:T(8,128)S(1)} %col_kernel.3), channel_id=1, replica_groups=mesh['batch'=16,'proto'=8] {'batch'}, dimensions={0} | all-to-all | bytes 262144 | tf_op jit(solution)/shard_map/all_to_all | solution.py:19
  113.2 1.2 row_kernel.5
  114.4 9.1 %all_to_all.71.recv_row_ref = f32[8,8,128]{2,1,0:T(8,128)S(1)} all-to-all(f32[8,8,128]{2,1,0:T(8,128)S(1)} %row_kernel.5), channel_id=1, replica_groups=mesh['batch'=16,'proto'=8] {'proto'}, dimensions={0} | all-to-all | bytes 65536 | tf_op jit(solution)/shard_map/all_to_all | solution.py:19
  123.6 10.7 %final_kernel.1 = (bf16[1024,256]{1,0:T(8,128)(2,1)}, bf16[64,2048]{1,0:T(8,128)(2,1)}, bf16[64,2048]{1,0:T(8,128)(2,1)}, bf16[64,2048]{1,0:T(8,128)(2,1)}, bf16[64,2048]{1,0:T(8,128)(2,1)}, /*index=5*/f32[16,128]{1,0:T(8,128)}) custom-call(s32[11]{0:T(128)S(1)} %copy-done.26, bf16[1024,256]{1,0:T(8,128)(2,1)S(1)} %bitcast.26, ...), custom_call_target="tpu_custom_call" | custom-call | tf_op jit(solution)/shard_map/final_kernel/pallas_call | solution.py:640
  134.3 4.8 %all-to-all-start.9 = ((bf16[8,128,256]{2,1,0:T(8,128)(2,1)}), bf16[8,128,256]{2,1,0:T(8,128)(2,1)}, u32[]{:S(2)}, u32[]{:S(2)}) async-start(bf16[8,128,256]{2,1,0:T(8,128)(2,1)} %bitcast.32), calls=%async_computation.9 | async-start | bytes 1048576 | tf_op jit(solution)/shard_map/all_to_all | solution.py:19
  139.1 7.4 %slab_kernel.1 = (bf16[1024,256]{1,0:T(8,128)(2,1)}, bf16[1024,256]{1,0:T(8,128)(2,1)}, bf16[1024,256]{1,0:T(8,128)(2,1)}) custom-call(s32[11]{0:T(128)} %stack.47.order_ref.refs_0_, f32[16,128]{1,0:T(8,128)} %get-tuple-element.110.mean_hbm, f32[16,128]{1,0:T(8,128)} %get-tuple-element.111.inv_hbm.refs_4_, f32[16,128]{1,0:T(8,128)} %bitcast.27, ...), custom_call_target="tpu_custom_call" | custom-call | tf_op jit(solution)/shard_map/slab_kernel/pallas_call | solution.py:685
  146.6 2.0 all-to-all-done.9.recv_hbm
  148.6 2.1 d_embed_kernel.1
  150.7 5.0 %all-to-all-start.10 = ((bf16[8,128,256]{2,1,0:T(8,128)(2,1)}), bf16[8,128,256]{2,1,0:T(8,128)(2,1)}, u32[]{:S(2)}, u32[]{:S(2)}) async-start(bf16[8,128,256]{2,1,0:T(8,128)(2,1)} %d_embed_kernel.1), calls=%async_computation.10 | async-start | bytes 1048576 | tf_op jit(solution)/shard_map/all_to_all | solution.py:19
  155.9 1.9 collective-permute-start.10
  157.8 1.0 collective-permute-start.11
  158.8 6.4 %all-to-all-done.10.d_embed_hbm = bf16[8,128,256]{2,1,0:T(8,128)(2,1)} async-done(((bf16[8,128,256]{2,1,0:T(8,128)(2,1)}), bf16[8,128,256]{2,1,0:T(8,128)(2,1)}, u32[]{:S(2)}, u32[]{:S(2)}) %all-to-all-start.10) | async-done | bytes 524320 | tf_op jit(solution)/shard_map/all_to_all | solution.py:19
  165.2 2.7 %shift_kernel.1 = (f32[1024,256]{1,0:T(8,128)S(1)}, bf16[16,32,256]{2,1,0:T(8,128)(2,1)S(1)}) custom-call(s32[11]{0:T(128)S(1)} %copy-done.27, bf16[8,128,256]{2,1,0:T(8,128)(2,1)} %all-to-all-done.10.d_embed_hbm, bf16[2048,256]{1,0:T(8,128)(2,1)} %w2_hbm.1, bf16[1024,256]{1,0:T(8,128)(2,1)} %get-tuple-element.128.normed_hbm.refs_3_, ...), custom_call_target="tpu_custom_call" | custom-call | tf_op jit(solution)/shard_map/shift_kernel/pallas_call | solution.py:726
  167.9 1.0 copy-done.18
  169.6 4.2 %all-to-all-start.11 = ((bf16[16,32,256]{2,1,0:T(8,128)(2,1)}), bf16[16,32,256]{2,1,0:T(8,128)(2,1)}, u32[]{:S(2)}, u32[]{:S(2)}) async-start(bf16[16,32,256]{2,1,0:T(8,128)(2,1)} %copy-done.20), calls=%async_computation.11 | async-start | bytes 524288 | tf_op jit(solution)/shard_map/all_to_all | solution.py:19
  173.8 2.1 stage_kernel.1
  175.9 1.2 collective-permute-start.12
  177.1 2.4 %collective-permute-start.13 = (bf16[16,2048]{1,0:T(8,128)(2,1)}, bf16[16,2048]{1,0:T(8,128)(2,1)}, u32[]{:S(2)}, u32[]{:S(2)}) collective-permute-start(bf16[16,2048]{1,0:T(8,128)(2,1)} %get-tuple-element.142), channel_id=1, source_target_pairs={{0,16},{8,24},{16,0},{24,8},{32,48},{40,56},{48,32},{56,40},{64,80... | collective-permute-start | bytes 196616 | tf_op jit(solution)/shard_map/ppermute | solution.py:723
  179.5 1.2 collective-permute-start.14
  181.4 1.2 copy-done.19
  182.6 4.2 %first_kernel.1 = (bf16[128,40,128]{2,1,0:T(8,128)(2,1)}, f32[16,256]{1,0:T(8,128)S(1)}) custom-call(s32[11]{0:T(128)S(1)} %copy-done.28, bf16[16,32,256]{2,1,0:T(8,128)(2,1)} %all-to-all-done.11.refs_1_, f32[1024,256]{1,0:T(8,128)S(1)} %copy-done.19, bf16[1024,256]{1,0:T(8,128)(2,1)S(1)} %copy-done.8, f32[16,128]{1,0:T(8,128)S(1)} %copy-done.25, ...), custom_call_target="tpu_custom_call" | custom-call | tf_op jit(solution)/shard_map/first_kernel/pallas_call | solution.py:752
  186.9 6.0 %all-to-all-start.12 = ((bf16[128,40,128]{2,1,0:T(8,128)(2,1)}), bf16[128,40,128]{2,1,0:T(8,128)(2,1)S(1)}, u32[]{:S(2)}, u32[]{:S(2)}) async-start(bf16[128,40,128]{2,1,0:T(8,128)(2,1)} %get-tuple-element.144), calls=%async_computation.12 | async-start | bytes 2621440 | tf_op jit(solution)/shard_map/all_to_all | solution.py:19
  192.9 5.4 %collective-permute-start.15 = (f32[16,256]{1,0:T(8,128)S(1)}, f32[16,256]{1,0:T(8,128)S(1)}, u32[]{:S(2)}, u32[]{:S(2)}) collective-permute-start(f32[16,256]{1,0:T(8,128)S(1)} %get-tuple-element.146), channel_id=1, source_target_pairs={{0,0},{1,16},{2,32},{3,48},{4,64},{5,80},{6,96},{7,112},{8,1},{9,1... | collective-permute-start | bytes 49160 | tf_op jit(solution)/shard_map/ppermute | solution.py:780
  198.3 1.6 add_bitcast_fusion
  199.9 15.0 %all-to-all-done.12 = bf16[128,40,128]{2,1,0:T(8,128)(2,1)S(1)} async-done(((bf16[128,40,128]{2,1,0:T(8,128)(2,1)}), bf16[128,40,128]{2,1,0:T(8,128)(2,1)S(1)}, u32[]{:S(2)}, u32[]{:S(2)}) %all-to-all-start.12) | async-done | bytes 1310752 | tf_op jit(solution)/shard_map/all_to_all | solution.py:19
  214.9 0.8 tail_kernel.1
  (88 shorter events, 4.7 us)
Async XLA Ops:
  0.6 22.4 %copy-start.30 = (s32[1024]{0:T(1024)S(1)}, s32[1024]{0:T(1024)}, u32[]{:S(2)}) copy-start(s32[1024]{0:T(1024)} %param.13) | copy-start | bytes 12292
  0.6 36.8 %copy-start.3 = (bf16[2048,256]{1,0:T(8,128)(2,1)S(1)}, bf16[2048,256]{1,0:T(8,128)(2,1)}, u32[]{:S(2)}) copy-start(bf16[2048,256]{1,0:T(8,128)(2,1)} %w2_hbm.1) | copy-start | bytes 3145732
  0.7 36.8 %copy-start.24 = (f32[2048]{0:T(1024)S(1)}, f32[2048]{0:T(1024)}, u32[]{:S(2)}) copy-start(f32[2048]{0:T(1024)} %param.10) | copy-start | bytes 24580
  0.7 36.8 %copy-start.21 = (f32[2048]{0:T(1024)S(1)}, f32[2048]{0:T(1024)}, u32[]{:S(2)}) copy-start(f32[2048]{0:T(1024)} %param.9) | copy-start | bytes 24580
  0.7 18.1 %collective-permute-start = (bf16[128,2048]{1,0:T(8,128)(2,1)}, bf16[128,2048]{1,0:T(8,128)(2,1)S(1)}, u32[]{:S(2)}, u32[]{:S(2)}) collective-permute-start(bf16[128,2048]{1,0:T(8,128)(2,1)} %refs_6_), channel_id=1, source_target_pairs={{2,0},{3,1},{4,2},{5,3},{6,4},{7,5},{0,6},{1,7},{10,8},{11,9},{12,... | collective-permute-start | bytes 1572872 | tf_op jit(solution)/shard_map/ppermute | solution.py:503
  4.0 14.8 %collective-permute-start.1 = (bf16[128,2048]{1,0:T(8,128)(2,1)}, bf16[128,2048]{1,0:T(8,128)(2,1)S(1)}, u32[]{:S(2)}, u32[]{:S(2)}) collective-permute-start(bf16[128,2048]{1,0:T(8,128)(2,1)} %refs_6_), channel_id=1, source_target_pairs={{0,2},{1,3},{2,4},{3,5},{4,6},{5,7},{6,0},{7,1},{8,10},{9,11},{10,... | collective-permute-start | bytes 1572872 | tf_op jit(solution)/shard_map/ppermute | solution.py:503
  10.2 30.3 %copy-start = (bf16[128,2048]{1,0:T(8,128)(2,1)S(1)}, bf16[128,2048]{1,0:T(8,128)(2,1)}, u32[]{:S(2)}) copy-start(bf16[128,2048]{1,0:T(8,128)(2,1)} %refs_6_) | copy-start | bytes 1572868
  10.2 15.4 %all-to-all-start = ((f32[16,32,128]{2,1,0:T(8,128)}), f32[16,32,128]{2,1,0:T(8,128)S(1)}, u32[]{:S(2)}, u32[]{:S(2)}) async-start(f32[16,32,128]{2,1,0:T(8,128)} %get-tuple-element.80), calls=%async_computation | async-start | bytes 524288 | tf_op jit(solution)/shard_map/all_to_all | solution.py:19
  18.8 32.4 %copy-start.4 = (bf16[128,2048]{1,0:T(8,128)(2,1)}, bf16[128,2048]{1,0:T(8,128)(2,1)S(1)}, u32[]{:S(2)}) copy-start(bf16[128,2048]{1,0:T(8,128)(2,1)S(1)} %collective-permute-done.rest_1_.refs_7_) | copy-start | bytes 1572868
  18.8 32.4 %copy-start.6 = (bf16[128,2048]{1,0:T(8,128)(2,1)}, bf16[128,2048]{1,0:T(8,128)(2,1)S(1)}, u32[]{:S(2)}) copy-start(bf16[128,2048]{1,0:T(8,128)(2,1)S(1)} %collective-permute-done.1.rest_2_.refs_8_) | copy-start | bytes 1572868
  20.4 20.2 %collective-permute-start.3 = (bf16[64,2048]{1,0:T(8,128)(2,1)}, bf16[64,2048]{1,0:T(8,128)(2,1)S(1)}, u32[]{:S(2)}, u32[]{:S(2)}) collective-permute-start(bf16[64,2048]{1,0:T(8,128)(2,1)} %slice.10), channel_id=1, source_target_pairs={{2,0},{3,1},{4,2},{5,3},{6,4},{7,5},{0,6},{1,7},{10,8},{11,9},{12,... | collective-permute-start | bytes 786440 | tf_op jit(solution)/shard_map/ppermute | solution.py:503
  23.0 17.5 %collective-permute-start.2 = (bf16[64,2048]{1,0:T(8,128)(2,1)}, bf16[64,2048]{1,0:T(8,128)(2,1)}, u32[]{:S(2)}, u32[]{:S(2)}) collective-permute-start(bf16[64,2048]{1,0:T(8,128)(2,1)} %slice.9), channel_id=1, source_target_pairs={{0,2},{1,3},{2,4},{3,5},{4,6},{5,7},{6,0},{7,1},{8,10},{9,11},{10,... | collective-permute-start | bytes 786440 | tf_op jit(solution)/shard_map/ppermute | solution.py:503
  40.6 14.3 %collective-permute-start.4 = (bf16[128,2048]{1,0:T(8,128)(2,1)S(1)}, bf16[128,2048]{1,0:T(8,128)(2,1)S(1)}, u32[]{:S(2)}, u32[]{:S(2)}) collective-permute-start(bf16[128,2048]{1,0:T(8,128)(2,1)S(1)} %copy-done), channel_id=1, source_target_pairs={{0,1},{1,0},{2,3},{3,2},{4,5},{5,4},{6,7},{7,6},{8,9},{9,8},{10,11... | collective-permute-start | bytes 1572872 | tf_op jit(solution)/shard_map/ppermute | solution.py:503
  41.5 13.4 %collective-permute-start.5 = (bf16[128,2048]{1,0:T(8,128)(2,1)S(1)}, bf16[128,2048]{1,0:T(8,128)(2,1)S(1)}, u32[]{:S(2)}, u32[]{:S(2)}) collective-permute-start(bf16[128,2048]{1,0:T(8,128)(2,1)S(1)} %collective-permute-done.rest_1_.refs_7_), channel_id=1, source_target_pairs={{0,1},{1,0},{2,3},{3,2},{4,5},{5,4},{6,7},{7,6},{8,9},{9,8},{10,11... | collective-permute-start | bytes 1572872 | tf_op jit(solution)/shard_map/ppermute | solution.py:503
  41.6 13.3 %collective-permute-start.6 = (bf16[128,2048]{1,0:T(8,128)(2,1)S(1)}, bf16[128,2048]{1,0:T(8,128)(2,1)}, u32[]{:S(2)}, u32[]{:S(2)}) collective-permute-start(bf16[128,2048]{1,0:T(8,128)(2,1)S(1)} %collective-permute-done.1.rest_2_.refs_8_), channel_id=1, source_target_pairs={{0,1},{1,0},{2,3},{3,2},{4,5},{5,4},{6,7},{7,6},{8,9},{9,8},{10,11... | collective-permute-start | bytes 1572872 | tf_op jit(solution)/shard_map/ppermute | solution.py:503
  42.0 12.9 %all-to-all-start.2 = ((bf16[8,128,256]{2,1,0:T(8,128)(2,1)}), bf16[8,128,256]{2,1,0:T(8,128)(2,1)S(1)}, u32[]{:S(2)}, u32[]{:S(2)}) async-start(bf16[8,128,256]{2,1,0:T(8,128)(2,1)} %get-tuple-element.84), calls=%async_computation.2 | async-start | bytes 1048576 | tf_op jit(solution)/shard_map/all_to_all | solution.py:19
  45.5 9.4 %collective-permute-start.7 = (bf16[64,2048]{1,0:T(8,128)(2,1)}, bf16[64,2048]{1,0:T(8,128)(2,1)}, u32[]{:S(2)}, u32[]{:S(2)}) collective-permute-start(bf16[64,2048]{1,0:T(8,128)(2,1)} %collective-permute-done.2.rest_3_.refs_9_), channel_id=1, source_target_pairs={{0,1},{1,0},{2,3},{3,2},{4,5},{5,4},{6,7},{7,6},{8,9},{9,8},{10,11... | collective-permute-start | bytes 786440 | tf_op jit(solution)/shard_map/ppermute | solution.py:503
  45.7 9.2 %collective-permute-start.8 = (bf16[64,2048]{1,0:T(8,128)(2,1)S(1)}, bf16[64,2048]{1,0:T(8,128)(2,1)}, u32[]{:S(2)}, u32[]{:S(2)}) collective-permute-start(bf16[64,2048]{1,0:T(8,128)(2,1)S(1)} %collective-permute-done.3.rest_4_.refs_10_), channel_id=1, source_target_pairs={{0,1},{1,0},{2,3},{3,2},{4,5},{5,4},{6,7},{7,6},{8,9},{9,8},{10,11... | collective-permute-start | bytes 786440 | tf_op jit(solution)/shard_map/ppermute | solution.py:503
  54.9 26.9 %copy-start.9 = (bf16[128,2048]{1,0:T(8,128)(2,1)}, bf16[128,2048]{1,0:T(8,128)(2,1)S(1)}, u32[]{:S(2)}) copy-start(bf16[128,2048]{1,0:T(8,128)(2,1)S(1)} %collective-permute-done.4.rest_5_.refs_11_) | copy-start | bytes 1572868
  54.9 26.9 %copy-start.11 = (bf16[128,2048]{1,0:T(8,128)(2,1)}, bf16[128,2048]{1,0:T(8,128)(2,1)S(1)}, u32[]{:S(2)}) copy-start(bf16[128,2048]{1,0:T(8,128)(2,1)S(1)} %collective-permute-done.5.rest_6_.refs_12_) | copy-start | bytes 1572868
  102.1 21.5 %copy-start.2 = (bf16[256,2048]{1,0:T(8,128)(2,1)S(1)}, bf16[256,2048]{1,0:T(8,128)(2,1)}, u32[]{:S(2)}) copy-start(bf16[256,2048]{1,0:T(8,128)(2,1)} %get-tuple-element.100.proto_t_hbm.proto_t_ref) | copy-start | bytes 3145732
  102.1 21.5 %copy-start.13 = (bf16[2048,256]{1,0:T(8,128)(2,1)S(1)}, bf16[2048,256]{1,0:T(8,128)(2,1)}, u32[]{:S(2)}) copy-start(bf16[2048,256]{1,0:T(8,128)(2,1)} %get-tuple-element.101.proto_ref) | copy-start | bytes 3145732
  102.1 21.5 %copy-start.14 = (bf16[256,2048]{1,0:T(8,128)(2,1)S(1)}, bf16[256,2048]{1,0:T(8,128)(2,1)}, u32[]{:S(2)}) copy-start(bf16[256,2048]{1,0:T(8,128)(2,1)} %get-tuple-element.102.raw_t_ref) | copy-start | bytes 3145732
  102.1 21.5 %copy-start.23 = (f32[8,2048]{1,0:T(8,128)S(1)}, f32[8,2048]{1,0:T(8,128)}, u32[]{:S(2)}) copy-start(f32[8,2048]{1,0:T(8,128)} %get-tuple-element.103.norm_ref) | copy-start | bytes 196612
  102.1 21.5 %copy-start.26 = (s32[11]{0:T(128)S(1)}, s32[11]{0:T(128)}, u32[]{:S(2)}) copy-start(s32[11]{0:T(128)} %stack.47.order_ref.refs_0_) | copy-start | bytes 136
  134.3 30.9 %copy-start.27 = (s32[11]{0:T(128)S(1)}, s32[11]{0:T(128)}, u32[]{:S(2)}) copy-start(s32[11]{0:T(128)} %stack.47.order_ref.refs_0_) | copy-start | bytes 136
  134.3 14.3 %all-to-all-start.9 = ((bf16[8,128,256]{2,1,0:T(8,128)(2,1)}), bf16[8,128,256]{2,1,0:T(8,128)(2,1)}, u32[]{:S(2)}, u32[]{:S(2)}) async-start(bf16[8,128,256]{2,1,0:T(8,128)(2,1)} %bitcast.32), calls=%async_computation.9 | async-start | bytes 1048576 | tf_op jit(solution)/shard_map/all_to_all | solution.py:19
  146.5 34.8 %copy-start.1 = (bf16[128,2048]{1,0:T(8,128)(2,1)S(1)}, bf16[128,2048]{1,0:T(8,128)(2,1)}, u32[]{:S(2)}) copy-start(bf16[128,2048]{1,0:T(8,128)(2,1)} %refs_6_) | copy-start | bytes 1572868
  146.5 34.8 %copy-start.5 = (bf16[128,2048]{1,0:T(8,128)(2,1)S(1)}, bf16[128,2048]{1,0:T(8,128)(2,1)}, u32[]{:S(2)}) copy-start(bf16[128,2048]{1,0:T(8,128)(2,1)} %copy-done.4) | copy-start | bytes 1572868
  146.5 34.8 %copy-start.7 = (bf16[128,2048]{1,0:T(8,128)(2,1)S(1)}, bf16[128,2048]{1,0:T(8,128)(2,1)}, u32[]{:S(2)}) copy-start(bf16[128,2048]{1,0:T(8,128)(2,1)} %copy-done.6) | copy-start | bytes 1572868
  146.5 34.8 %copy-start.8 = (bf16[1024,256]{1,0:T(8,128)(2,1)S(1)}, bf16[1024,256]{1,0:T(8,128)(2,1)}, u32[]{:S(2)}) copy-start(bf16[1024,256]{1,0:T(8,128)(2,1)} %get-tuple-element.128.normed_hbm.refs_3_) | copy-start | bytes 1572868
  146.5 34.8 %copy-start.10 = (bf16[128,2048]{1,0:T(8,128)(2,1)S(1)}, bf16[128,2048]{1,0:T(8,128)(2,1)}, u32[]{:S(2)}) copy-start(bf16[128,2048]{1,0:T(8,128)(2,1)} %copy-done.9) | copy-start | bytes 1572868
  146.5 34.8 %copy-start.12 = (bf16[128,2048]{1,0:T(8,128)(2,1)S(1)}, bf16[128,2048]{1,0:T(8,128)(2,1)}, u32[]{:S(2)}) copy-start(bf16[128,2048]{1,0:T(8,128)(2,1)} %copy-done.11) | copy-start | bytes 1572868
  146.5 34.8 %copy-start.16 = (bf16[64,2048]{1,0:T(8,128)(2,1)S(1)}, bf16[64,2048]{1,0:T(8,128)(2,1)}, u32[]{:S(2)}) copy-start(bf16[64,2048]{1,0:T(8,128)(2,1)} %copy-done.15) | copy-start | bytes 786436
  146.6 34.8 %copy-start.22 = (f32[2048]{0:T(1024)S(1)}, f32[2048]{0:T(1024)}, u32[]{:S(2)}) copy-start(f32[2048]{0:T(1024)} %param.9) | copy-start | bytes 24580
  146.6 34.8 %copy-start.25 = (f32[16,128]{1,0:T(8,128)S(1)}, f32[16,128]{1,0:T(8,128)}, u32[]{:S(2)}) copy-start(f32[16,128]{1,0:T(8,128)} %get-tuple-element.111.inv_hbm.refs_4_) | copy-start | bytes 24580
  146.6 34.8 %copy-start.28 = (s32[11]{0:T(128)S(1)}, s32[11]{0:T(128)}, u32[]{:S(2)}) copy-start(s32[11]{0:T(128)} %stack.47.order_ref.refs_0_) | copy-start | bytes 136
  150.7 14.5 %all-to-all-start.10 = ((bf16[8,128,256]{2,1,0:T(8,128)(2,1)}), bf16[8,128,256]{2,1,0:T(8,128)(2,1)}, u32[]{:S(2)}, u32[]{:S(2)}) async-start(bf16[8,128,256]{2,1,0:T(8,128)(2,1)} %d_embed_kernel.1), calls=%async_computation.10 | async-start | bytes 1048576 | tf_op jit(solution)/shard_map/all_to_all | solution.py:19
  155.7 18.1 %collective-permute-start.9 = (bf16[64,2048]{1,0:T(8,128)(2,1)}, bf16[64,2048]{1,0:T(8,128)(2,1)}, u32[]{:S(2)}, u32[]{:S(2)}) collective-permute-start(bf16[64,2048]{1,0:T(8,128)(2,1)} %get-tuple-element.137), channel_id=1, source_target_pairs={{0,32},{8,40},{16,48},{24,56},{32,64},{40,72},{48,80},{56,88},{64,... | collective-permute-start | bytes 786440 | tf_op jit(solution)/shard_map/ppermute | solution.py:681
  155.9 17.9 %collective-permute-start.10 = (bf16[64,2048]{1,0:T(8,128)(2,1)}, bf16[64,2048]{1,0:T(8,128)(2,1)}, u32[]{:S(2)}, u32[]{:S(2)}) collective-permute-start(bf16[64,2048]{1,0:T(8,128)(2,1)} %get-tuple-element.138), channel_id=1, source_target_pairs={{0,64},{8,72},{16,80},{24,88},{32,96},{40,104},{48,112},{56,120},{... | collective-permute-start | bytes 786440 | tf_op jit(solution)/shard_map/ppermute | solution.py:681
  157.8 16.1 %collective-permute-start.11 = (bf16[64,2048]{1,0:T(8,128)(2,1)}, bf16[64,2048]{1,0:T(8,128)(2,1)}, u32[]{:S(2)}, u32[]{:S(2)}) collective-permute-start(bf16[64,2048]{1,0:T(8,128)(2,1)} %get-tuple-element.139), channel_id=1, source_target_pairs={{0,96},{8,104},{16,112},{24,120},{32,0},{40,8},{48,16},{56,24},{64... | collective-permute-start | bytes 786440 | tf_op jit(solution)/shard_map/ppermute | solution.py:681
  169.6 11.7 %all-to-all-start.11 = ((bf16[16,32,256]{2,1,0:T(8,128)(2,1)}), bf16[16,32,256]{2,1,0:T(8,128)(2,1)}, u32[]{:S(2)}, u32[]{:S(2)}) async-start(bf16[16,32,256]{2,1,0:T(8,128)(2,1)} %copy-done.20), calls=%async_computation.11 | async-start | bytes 524288 | tf_op jit(solution)/shard_map/all_to_all | solution.py:19
  175.9 10.9 %collective-permute-start.12 = (bf16[16,2048]{1,0:T(8,128)(2,1)}, bf16[16,2048]{1,0:T(8,128)(2,1)}, u32[]{:S(2)}, u32[]{:S(2)}) collective-permute-start(bf16[16,2048]{1,0:T(8,128)(2,1)} %get-tuple-element.141), channel_id=1, source_target_pairs={{0,8},{8,16},{16,24},{24,0},{32,40},{40,48},{48,56},{56,32},{64,72... | collective-permute-start | bytes 196616 | tf_op jit(solution)/shard_map/ppermute | solution.py:723
  177.1 9.7 %collective-permute-start.13 = (bf16[16,2048]{1,0:T(8,128)(2,1)}, bf16[16,2048]{1,0:T(8,128)(2,1)}, u32[]{:S(2)}, u32[]{:S(2)}) collective-permute-start(bf16[16,2048]{1,0:T(8,128)(2,1)} %get-tuple-element.142), channel_id=1, source_target_pairs={{0,16},{8,24},{16,0},{24,8},{32,48},{40,56},{48,32},{56,40},{64,80... | collective-permute-start | bytes 196616 | tf_op jit(solution)/shard_map/ppermute | solution.py:723
  179.5 7.3 %collective-permute-start.14 = (bf16[16,2048]{1,0:T(8,128)(2,1)}, bf16[16,2048]{1,0:T(8,128)(2,1)}, u32[]{:S(2)}, u32[]{:S(2)}) collective-permute-start(bf16[16,2048]{1,0:T(8,128)(2,1)} %get-tuple-element.143), channel_id=1, source_target_pairs={{0,24},{8,0},{16,8},{24,16},{32,56},{40,32},{48,40},{56,48},{64,88... | collective-permute-start | bytes 196616 | tf_op jit(solution)/shard_map/ppermute | solution.py:723
  182.6 15.7 %copy-start.29 = (bf16[16,2048]{1,0:T(8,128)(2,1)S(1)}, bf16[16,2048]{1,0:T(8,128)(2,1)}, u32[]{:S(2)}) copy-start(bf16[16,2048]{1,0:T(8,128)(2,1)} %get-tuple-element.149) | copy-start | bytes 196612
  186.9 28.0 %all-to-all-start.12 = ((bf16[128,40,128]{2,1,0:T(8,128)(2,1)}), bf16[128,40,128]{2,1,0:T(8,128)(2,1)S(1)}, u32[]{:S(2)}, u32[]{:S(2)}) async-start(bf16[128,40,128]{2,1,0:T(8,128)(2,1)} %get-tuple-element.144), calls=%async_computation.12 | async-start | bytes 2621440 | tf_op jit(solution)/shard_map/all_to_all | solution.py:19
  192.9 7.1 %collective-permute-start.15 = (f32[16,256]{1,0:T(8,128)S(1)}, f32[16,256]{1,0:T(8,128)S(1)}, u32[]{:S(2)}, u32[]{:S(2)}) collective-permute-start(f32[16,256]{1,0:T(8,128)S(1)} %get-tuple-element.146), channel_id=1, source_target_pairs={{0,0},{1,16},{2,32},{3,48},{4,64},{5,80},{6,96},{7,112},{8,1},{9,1... | collective-permute-start | bytes 49160 | tf_op jit(solution)/shard_map/ppermute | solution.py:780
  (5 other events, 14.9 us)

commit v9 on v8

--- a/solution.py
+++ b/solution.py
@@ -123,36 +123,43 @@
 
 
 def score_kernel(embed_ref, proto_t_hbm, kern_ref, msg_ref, soft_ref, acc_ref, proto_t_ref, sems):
-    total, cols = kern_ref.shape
-    copies = []
+    step = pl.program_id(0)
+    rows = embed_ref.shape[0]
+    cols = proto_t_ref.shape[1]
+
+    def copy(j):
+        span = slice(j * TILE, (j + 1) * TILE)
+        return pltpu.make_async_copy(proto_t_hbm.at[:, span], proto_t_ref.at[:, span], sems.at[j])
+
+    @pl.when(step == 0)
+    def _():
+        for j in range(cols // TILE):
+            copy(j).start()
+        acc_ref[...] = jnp.zeros_like(acc_ref)
+        for j in range(cols // TILE):
+            copy(j).wait()
+
+    soft = [None] * (rows // LANES)
     for j in range(cols // TILE):
         span = slice(j * TILE, (j + 1) * TILE)
-        copies.append(pltpu.make_async_copy(proto_t_hbm.at[:, span], proto_t_ref.at[:, span], sems.at[j]))
-        copies[-1].start()
-    acc_ref[...] = jnp.zeros_like(acc_ref)
-    for step in range(total // TILE):
-        band = slice(step * TILE, (step + 1) * TILE)
-        soft = [None] * (TILE // LANES)
-        for j in range(cols // TILE):
-            span = slice(j * TILE, (j + 1) * TILE)
-            if step == 0:
-                copies[j].wait()
-            scores = jnp.dot(embed_ref[band, :], proto_t_ref[:, span], preferred_element_type=F32)
-            tempered = jnp.exp2(scores * (10.0 * LOG2_E))
-            kern = tempered * tempered
-            kern_ref[band, span] = kern.astype(BF)
-            for h in range(TILE // LANES):
-                at = (j * (TILE // LANES) + h) * 8
-                acc_ref[at : at + 8, :] += fold_rows(kern[:, lane(h)])
-            for b in range(TILE // LANES):
-                part = tempered[b * LANES : (b + 1) * LANES]
-                part = part[:, :LANES] + part[:, LANES:]
-                soft[b] = part if soft[b] is None else soft[b] + part
-        for b in range(TILE // LANES):
-            at = step * (TILE // LANES) + b
-            soft_ref[at : at + 1, :] = jnp.sum(soft[b].T, axis=0, keepdims=True)
-    sums = jnp.sum(acc_ref[...].reshape(cols // LANES, 8, LANES), axis=1)
-    msg_ref[...] = jnp.broadcast_to(sums[None], msg_ref.shape)
+        scores = jnp.dot(embed_ref[...], proto_t_ref[:, span], preferred_element_type=F32)
+        tempered = jnp.exp2(scores * (10.0 * LOG2_E))
+        kern = tempered * tempered
+        kern_ref[:, span] = kern.astype(BF)
+        for h in range(TILE // LANES):
+            at = (j * (TILE // LANES) + h) * 8
+            acc_ref[at : at + 8, :] += fold_rows(kern[:, lane(h)])
+        for b in range(rows // LANES):
+            part = tempered[b * LANES : (b + 1) * LANES]
+            part = part[:, :LANES] + part[:, LANES:]
+            soft[b] = part if soft[b] is None else soft[b] + part
+    for b in range(rows // LANES):
+        soft_ref[pl.ds(step * (rows // LANES) + b, 1), :] = jnp.sum(soft[b].T, axis=0, keepdims=True)
+
+    @pl.when(step == pl.num_programs(0) - 1)
+    def _():
+        total = jnp.sum(acc_ref[...].reshape(cols // LANES, 8, LANES), axis=1)
+        msg_ref[...] = jnp.broadcast_to(total[None], msg_ref.shape)
 
 
 def row_kernel(recv_ref, kern_ref, *rest):
@@ -436,7 +443,8 @@
         copy.wait()
 
 
-def tail_kernel(total_rows, recv_ref, out_ref, gain_ref, bias_ref, loss_ref):
+def tail_kernel(total_rows, recv_ref, second_ref, out_ref, gain_ref, bias_ref, loss_ref, second_out_ref):
+    second_out_ref[...] = second_ref[...]
     n_batch, n_proto, height, _ = recv_ref.shape
     share = out_ref.shape[0]
     chunks = height // share
@@ -592,7 +600,9 @@
 
     kern, col_msg, soft = pl.pallas_call(
         score_kernel,
-        in_specs=[pl.BlockSpec((rows, width), lambda: (0, 0)), anywhere],
+        grid=(steps,),
+        in_specs=[rows_of(TILE, width), anywhere],
+        out_specs=[rows_of(TILE, cols), whole((n_batch, col_bands, LANES)), whole((row_bands, LANES))],
         out_shape=[shape((rows, cols), BF), shape((n_batch, col_bands, LANES)), shape((row_bands, LANES))],
         scratch_shapes=[
             pltpu.VMEM((col_bands * 8, LANES), F32),
@@ -771,17 +781,17 @@
     first, *pieces = lax.optimization_barrier((first, *pieces))
     grad_proto = sum(piece.astype(F32) for piece in pieces).T
     first = deal(first, ("batch", "proto")).reshape(n_batch, n_proto, lines, LANES)
-    grad_first, grad_gain, grad_bias, loss = pl.pallas_call(
-        lambda *refs: tail_kernel(total_rows, *refs),
-        out_shape=[shape((share, d_hid)), shape((hid_bands, LANES)), shape((hid_bands, LANES)), shape((1, LANES))],
-        compiler_params=PARAMS,
-        name="tail_kernel",
-    )(first)
-    grad_second = lax.ppermute(
+    second = lax.ppermute(
         second,
         ("batch", "proto"),
         [(b * n_proto + p, p * n_batch + b) for b in range(n_batch) for p in range(n_proto)],
     )
+    grad_first, grad_gain, grad_bias, loss, grad_second = pl.pallas_call(
+        lambda *refs: tail_kernel(total_rows, *refs),
+        out_shape=[shape((share, d_hid)), shape((hid_bands, LANES)), shape((hid_bands, LANES)), shape((1, LANES)), shape(second.shape)],
+        compiler_params=PARAMS,
+        name="tail_kernel",
+    )(first, second)
     grad_gain = grad_gain.reshape(-1)
     grad_bias = grad_bias.reshape(-1)
     loss = loss[0, 0]

time: 218 us -> 217 us (level)
    unnamed x63 -> x62, local copies, waits for them, and re-layouts: 4.9 us -> 4.29 us
where the time goes in v9:
time: 217 us; the launch traced here: 216 us
  blocking collectives  70 us (32%)
  Pallas kernels  53.5 us (25%)
  starting transfers between devices  52.6 us (24%)
  waiting for transfers between devices  30.2 us (14%)
  local copies, waits for them, and re-layouts  6.48 us (3%)
    all_to_all x7, blocking collectives, deal(): return lax.all_to_all(x, axis, 0, 0, tiled=True)  70 us
    all_to_all x6, starting transfers between devices, deal(): return lax.all_to_all(x, axis, 0, 0, tiled=True)  31.4 us
    all_to_all x6, waiting for transfers between devices, deal(): return lax.all_to_all(x, axis, 0, 0, tiled=True)  30.2 us
    pallas_call x1, Pallas kernels, step_of_device(): pl.pallas_call(final_kernel, grid=(steps // 2,), in_specs=[pl.BlockSpec(m...  10.7 us
    ppermute x9, starting transfers between devices, hop(): return lax.ppermute(x, 'proto', moves)  8.03 us
    pallas_call x1, Pallas kernels, step_of_device(): pl.pallas_call(slab_kernel, grid_spec=pltpu.PrefetchScalarGridSpec(num_sc...  7.36 us
    pallas_call x1, Pallas kernels, step_of_device(): pl.pallas_call(pre_kernel, in_specs=[pl.BlockSpec(features.shape, lambda:...  6.16 us
    ppermute x1, starting transfers between devices, step_of_device(): lax.ppermute(second, ('batch', 'proto'), [(b * n_proto + p, p * n_batch +...  5.44 us
  transfers between devices with their start and end apart: 22, of which 6 were waited for; matrix products, arithmetic and copies ran while one was open for 2% of the time, Pallas kernels for 14%

profile of v9, /device:TPU:1, one launch (start us, length us, event | category | flops | bytes accessed | tf_op | source)
XLA Modules:
  0.0 215.7 jit_solution(11036447137876451539)
XLA Ops:
  0.7 3.4 %collective-permute-start = (bf16[128,2048]{1,0:T(8,128)(2,1)}, bf16[128,2048]{1,0:T(8,128)(2,1)S(1)}, u32[]{:S(2)}, u32[]{:S(2)}) collective-permute-start(bf16[128,2048]{1,0:T(8,128)(2,1)} %refs_6_), channel_id=1, source_target_pairs={{2,0},{3,1},{4,2},{5,3},{6,4},{7,5},{0,6},{1,7},{10,8},{11,9},{12,... | collective-permute-start | bytes 1572872 | tf_op jit(solution)/shard_map/ppermute | solution.py:511
  4.0 6.2 %pre_kernel.1 = (f32[128,2048]{1,0:T(8,128)}, f32[16,32,128]{2,1,0:T(8,128)}) custom-call(bf16[128,2048]{1,0:T(8,128)(2,1)} %refs_6_, bf16[2048,2048]{1,0:T(8,128)(2,1)} %w_hbm.3), custom_call_target="tpu_custom_call" | custom-call | tf_op jit(solution)/shard_map/pre_kernel/pallas_call | solution.py:534
  10.2 7.9 %all-to-all-start = ((f32[16,32,128]{2,1,0:T(8,128)}), f32[16,32,128]{2,1,0:T(8,128)S(1)}, u32[]{:S(2)}, u32[]{:S(2)}) async-start(f32[16,32,128]{2,1,0:T(8,128)} %get-tuple-element.81), calls=%async_computation | async-start | bytes 524288 | tf_op jit(solution)/shard_map/all_to_all | solution.py:19
  18.8 0.8 slice.9
  20.4 2.6 %collective-permute-start.3 = (bf16[64,2048]{1,0:T(8,128)(2,1)}, bf16[64,2048]{1,0:T(8,128)(2,1)S(1)}, u32[]{:S(2)}, u32[]{:S(2)}) collective-permute-start(bf16[64,2048]{1,0:T(8,128)(2,1)} %slice.10), channel_id=1, source_target_pairs={{2,0},{3,1},{4,2},{5,3},{6,4},{7,5},{0,6},{1,7},{10,8},{11,9},{12,... | collective-permute-start | bytes 786440 | tf_op jit(solution)/shard_map/ppermute | solution.py:511
  23.0 2.6 %all-to-all-done.recv_ref = f32[16,32,128]{2,1,0:T(8,128)S(1)} async-done(((f32[16,32,128]{2,1,0:T(8,128)}), f32[16,32,128]{2,1,0:T(8,128)S(1)}, u32[]{:S(2)}, u32[]{:S(2)}) %all-to-all-start) | async-done | bytes 262176 | tf_op jit(solution)/shard_map/all_to_all | solution.py:19
  25.6 11.8 %all_to_all.65.refs_1_ = f32[8,32,128]{2,1,0:T(8,128)S(1)} all-to-all(f32[8,32,128]{2,1,0:T(8,128)S(1)} %relay_kernel.1), channel_id=1, replica_groups=mesh['batch'=16,'proto'=8] {'proto'}, dimensions={0} | all-to-all | bytes 262144 | tf_op jit(solution)/shard_map/all_to_all | solution.py:19
  37.5 1.2 copy-done.17
  38.7 1.8 embed_kernel.1
  40.6 0.9 collective-permute-start.4
  42.0 3.5 %all-to-all-start.2 = ((bf16[8,128,256]{2,1,0:T(8,128)(2,1)}), bf16[8,128,256]{2,1,0:T(8,128)(2,1)S(1)}, u32[]{:S(2)}, u32[]{:S(2)}) async-start(bf16[8,128,256]{2,1,0:T(8,128)(2,1)} %get-tuple-element.85), calls=%async_computation.2 | async-start | bytes 1048576 | tf_op jit(solution)/shard_map/all_to_all | solution.py:19
  46.1 5.2 %proto_kernel.1 = (bf16[2048,256]{1,0:T(8,128)(2,1)}, bf16[256,2048]{1,0:T(8,128)(2,1)}, bf16[256,2048]{1,0:T(8,128)(2,1)}, f32[8,2048]{1,0:T(8,128)}, bf16[2048,256]{1,0:T(8,128)(2,1)}) custom-call(s32[11]{0:T(128)} %stack.47.order_ref.refs_0_, bf16[2048,256]{1,0:T(8,128)(2,1)} %raw_ref, bf16[2048,2048]{1,0:T(8,128)(2,1)} %w_hbm.3), custom_call_target="tpu_custom_call" | custom-call | tf_op jit(solution)/shard_map/proto_kernel/pallas_call | solution.py:576
  51.3 3.6 %all-to-all-done.2 = bf16[8,128,256]{2,1,0:T(8,128)(2,1)S(1)} async-done(((bf16[8,128,256]{2,1,0:T(8,128)(2,1)}), bf16[8,128,256]{2,1,0:T(8,128)(2,1)S(1)}, u32[]{:S(2)}, u32[]{:S(2)}) %all-to-all-start.2) | async-done | bytes 524320 | tf_op jit(solution)/shard_map/all_to_all | solution.py:19
  54.9 4.4 %score_kernel.1 = (bf16[1024,2048]{1,0:T(8,128)(2,1)S(1)}, f32[16,16,128]{2,1,0:T(8,128)S(1)}, f32[8,128]{1,0:T(8,128)S(1)}) custom-call(bf16[1024,256]{1,0:T(8,128)(2,1)S(1)} %bitcast.25, bf16[256,2048]{1,0:T(8,128)(2,1)} %get-tuple-element.101.proto_t_hbm.proto_t_ref), custom_call_target="tpu_custom_call" | custom-call | tf_op jit(solution)/shard_map/score_kernel/pallas_call | solution.py:601
  59.3 10.4 %all_to_all.66.recv_ref = f32[16,16,128]{2,1,0:T(8,128)S(1)} all-to-all(f32[16,16,128]{2,1,0:T(8,128)S(1)} %get-tuple-element.105), channel_id=1, replica_groups=mesh['batch'=16,'proto'=8] {'batch'}, dimensions={0} | all-to-all | bytes 262144 | tf_op jit(solution)/shard_map/all_to_all | solution.py:19
  69.7 1.2 row_kernel.3
  70.9 9.6 %all_to_all.67.recv_ref.recv_soft_ref = f32[8,16,128]{2,1,0:T(8,128)S(1)} all-to-all(f32[8,16,128]{2,1,0:T(8,128)S(1)} %row_kernel.3), channel_id=1, replica_groups=mesh['batch'=16,'proto'=8] {'proto'}, dimensions={0} | all-to-all | bytes 131072 | tf_op jit(solution)/shard_map/all_to_all | solution.py:19
  80.5 1.2 col_kernel.2
  81.7 9.9 %all_to_all.68.recv_ref = f32[16,16,128]{2,1,0:T(8,128)S(1)} all-to-all(f32[16,16,128]{2,1,0:T(8,128)S(1)} %col_kernel.2), channel_id=1, replica_groups=mesh['batch'=16,'proto'=8] {'batch'}, dimensions={0} | all-to-all | bytes 262144 | tf_op jit(solution)/shard_map/all_to_all | solution.py:19
  91.6 1.2 row_kernel.4
  92.8 9.2 %all_to_all.69.recv_ref = f32[8,8,128]{2,1,0:T(8,128)S(1)} all-to-all(f32[8,8,128]{2,1,0:T(8,128)S(1)} %row_kernel.4), channel_id=1, replica_groups=mesh['batch'=16,'proto'=8] {'proto'}, dimensions={0} | all-to-all | bytes 65536 | tf_op jit(solution)/shard_map/all_to_all | solution.py:19
  102.0 1.2 col_kernel.3
  103.2 9.9 %all_to_all.70.recv_ref.recv_col_ref = f32[16,16,128]{2,1,0:T(8,128)S(1)} all-to-all(f32[16,16,128]{2,1,0:T(8,128)S(1)} %col_kernel.3), channel_id=1, replica_groups=mesh['batch'=16,'proto'=8] {'batch'}, dimensions={0} | all-to-all | bytes 262144 | tf_op jit(solution)/shard_map/all_to_all | solution.py:19
  113.1 1.2 row_kernel.5
  114.3 9.1 %all_to_all.71.recv_row_ref = f32[8,8,128]{2,1,0:T(8,128)S(1)} all-to-all(f32[8,8,128]{2,1,0:T(8,128)S(1)} %row_kernel.5), channel_id=1, replica_groups=mesh['batch'=16,'proto'=8] {'proto'}, dimensions={0} | all-to-all | bytes 65536 | tf_op jit(solution)/shard_map/all_to_all | solution.py:19
  123.5 10.7 %final_kernel.1 = (bf16[1024,256]{1,0:T(8,128)(2,1)}, bf16[64,2048]{1,0:T(8,128)(2,1)}, bf16[64,2048]{1,0:T(8,128)(2,1)}, bf16[64,2048]{1,0:T(8,128)(2,1)}, bf16[64,2048]{1,0:T(8,128)(2,1)}, /*index=5*/f32[16,128]{1,0:T(8,128)}) custom-call(s32[11]{0:T(128)S(1)} %copy-done.26, bf16[1024,256]{1,0:T(8,128)(2,1)S(1)} %bitcast.26, ...), custom_call_target="tpu_custom_call" | custom-call | tf_op jit(solution)/shard_map/final_kernel/pallas_call | solution.py:650
  134.2 4.8 %all-to-all-start.9 = ((bf16[8,128,256]{2,1,0:T(8,128)(2,1)}), bf16[8,128,256]{2,1,0:T(8,128)(2,1)}, u32[]{:S(2)}, u32[]{:S(2)}) async-start(bf16[8,128,256]{2,1,0:T(8,128)(2,1)} %bitcast.32), calls=%async_computation.9 | async-start | bytes 1048576 | tf_op jit(solution)/shard_map/all_to_all | solution.py:19
  139.0 7.4 %slab_kernel.1 = (bf16[1024,256]{1,0:T(8,128)(2,1)}, bf16[1024,256]{1,0:T(8,128)(2,1)}, bf16[1024,256]{1,0:T(8,128)(2,1)}) custom-call(s32[11]{0:T(128)} %stack.47.order_ref.refs_0_, f32[16,128]{1,0:T(8,128)} %get-tuple-element.111.mean_hbm, f32[16,128]{1,0:T(8,128)} %get-tuple-element.112.inv_hbm.refs_4_, f32[16,128]{1,0:T(8,128)} %bitcast.27, ...), custom_call_target="tpu_custom_call" | custom-call | tf_op jit(solution)/shard_map/slab_kernel/pallas_call | solution.py:695
  146.5 2.0 all-to-all-done.9.recv_hbm
  148.5 2.1 d_embed_kernel.1
  150.6 5.0 %all-to-all-start.10 = ((bf16[8,128,256]{2,1,0:T(8,128)(2,1)}), bf16[8,128,256]{2,1,0:T(8,128)(2,1)}, u32[]{:S(2)}, u32[]{:S(2)}) async-start(bf16[8,128,256]{2,1,0:T(8,128)(2,1)} %d_embed_kernel.1), calls=%async_computation.10 | async-start | bytes 1048576 | tf_op jit(solution)/shard_map/all_to_all | solution.py:19
  155.8 1.9 collective-permute-start.10
  157.7 1.0 collective-permute-start.11
  158.7 6.4 %all-to-all-done.10.d_embed_hbm = bf16[8,128,256]{2,1,0:T(8,128)(2,1)} async-done(((bf16[8,128,256]{2,1,0:T(8,128)(2,1)}), bf16[8,128,256]{2,1,0:T(8,128)(2,1)}, u32[]{:S(2)}, u32[]{:S(2)}) %all-to-all-start.10) | async-done | bytes 524320 | tf_op jit(solution)/shard_map/all_to_all | solution.py:19
  165.1 2.7 %shift_kernel.1 = (f32[1024,256]{1,0:T(8,128)S(1)}, bf16[16,32,256]{2,1,0:T(8,128)(2,1)S(1)}) custom-call(s32[11]{0:T(128)S(1)} %copy-done.27, bf16[8,128,256]{2,1,0:T(8,128)(2,1)} %all-to-all-done.10.d_embed_hbm, bf16[2048,256]{1,0:T(8,128)(2,1)} %w2_hbm.1, bf16[1024,256]{1,0:T(8,128)(2,1)} %get-tuple-element.129.normed_hbm.refs_3_, ...), custom_call_target="tpu_custom_call" | custom-call | tf_op jit(solution)/shard_map/shift_kernel/pallas_call | solution.py:736
  167.8 1.0 copy-done.18
  169.5 4.2 %all-to-all-start.11 = ((bf16[16,32,256]{2,1,0:T(8,128)(2,1)}), bf16[16,32,256]{2,1,0:T(8,128)(2,1)}, u32[]{:S(2)}, u32[]{:S(2)}) async-start(bf16[16,32,256]{2,1,0:T(8,128)(2,1)} %copy-done.20), calls=%async_computation.11 | async-start | bytes 524288 | tf_op jit(solution)/shard_map/all_to_all | solution.py:19
  173.7 2.1 stage_kernel.1
  175.8 1.2 collective-permute-start.12
  177.0 2.4 %collective-permute-start.13 = (bf16[16,2048]{1,0:T(8,128)(2,1)}, bf16[16,2048]{1,0:T(8,128)(2,1)}, u32[]{:S(2)}, u32[]{:S(2)}) collective-permute-start(bf16[16,2048]{1,0:T(8,128)(2,1)} %get-tuple-element.143), channel_id=1, source_target_pairs={{0,16},{8,24},{16,0},{24,8},{32,48},{40,56},{48,32},{56,40},{64,80... | collective-permute-start | bytes 196616 | tf_op jit(solution)/shard_map/ppermute | solution.py:733
  179.4 1.2 collective-permute-start.14
  181.3 1.2 copy-done.19
  182.5 4.2 %first_kernel.1 = (bf16[128,40,128]{2,1,0:T(8,128)(2,1)}, f32[16,256]{1,0:T(8,128)S(1)}) custom-call(s32[11]{0:T(128)S(1)} %copy-done.28, bf16[16,32,256]{2,1,0:T(8,128)(2,1)} %all-to-all-done.11.refs_1_, f32[1024,256]{1,0:T(8,128)S(1)} %copy-done.19, bf16[1024,256]{1,0:T(8,128)(2,1)S(1)} %copy-done.8, f32[16,128]{1,0:T(8,128)S(1)} %copy-done.25, ...), custom_call_target="tpu_custom_call" | custom-call | tf_op jit(solution)/shard_map/first_kernel/pallas_call | solution.py:762
  186.8 6.0 %all-to-all-start.12 = ((bf16[128,40,128]{2,1,0:T(8,128)(2,1)}), bf16[128,40,128]{2,1,0:T(8,128)(2,1)S(1)}, u32[]{:S(2)}, u32[]{:S(2)}) async-start(bf16[128,40,128]{2,1,0:T(8,128)(2,1)} %get-tuple-element.145), calls=%async_computation.12 | async-start | bytes 2621440 | tf_op jit(solution)/shard_map/all_to_all | solution.py:19
  192.8 5.4 %collective-permute-start.15 = (f32[16,256]{1,0:T(8,128)S(1)}, f32[16,256]{1,0:T(8,128)S(1)}, u32[]{:S(2)}, u32[]{:S(2)}) collective-permute-start(f32[16,256]{1,0:T(8,128)S(1)} %get-tuple-element.146), channel_id=1, source_target_pairs={{0,0},{1,16},{2,32},{3,48},{4,64},{5,80},{6,96},{7,112},{8,1},{9,1... | collective-permute-start | bytes 49160 | tf_op jit(solution)/shard_map/ppermute | solution.py:784
  198.2 1.6 add_bitcast_fusion
  199.8 15.0 %all-to-all-done.12 = bf16[128,40,128]{2,1,0:T(8,128)(2,1)S(1)} async-done(((bf16[128,40,128]{2,1,0:T(8,128)(2,1)}), bf16[128,40,128]{2,1,0:T(8,128)(2,1)S(1)}, u32[]{:S(2)}, u32[]{:S(2)}) %all-to-all-start.12) | async-done | bytes 1310752 | tf_op jit(solution)/shard_map/all_to_all | solution.py:19
  214.8 0.8 tail_kernel.1
  (87 shorter events, 4.2 us)
Async XLA Ops:
  0.6 22.4 %copy-start.30 = (s32[1024]{0:T(1024)S(1)}, s32[1024]{0:T(1024)}, u32[]{:S(2)}) copy-start(s32[1024]{0:T(1024)} %param.13) | copy-start | bytes 12292
  0.6 36.8 %copy-start.3 = (bf16[2048,256]{1,0:T(8,128)(2,1)S(1)}, bf16[2048,256]{1,0:T(8,128)(2,1)}, u32[]{:S(2)}) copy-start(bf16[2048,256]{1,0:T(8,128)(2,1)} %w2_hbm.1) | copy-start | bytes 3145732
  0.7 36.8 %copy-start.24 = (f32[2048]{0:T(1024)S(1)}, f32[2048]{0:T(1024)}, u32[]{:S(2)}) copy-start(f32[2048]{0:T(1024)} %param.10) | copy-start | bytes 24580
  0.7 36.8 %copy-start.21 = (f32[2048]{0:T(1024)S(1)}, f32[2048]{0:T(1024)}, u32[]{:S(2)}) copy-start(f32[2048]{0:T(1024)} %param.9) | copy-start | bytes 24580
  0.7 18.1 %collective-permute-start = (bf16[128,2048]{1,0:T(8,128)(2,1)}, bf16[128,2048]{1,0:T(8,128)(2,1)S(1)}, u32[]{:S(2)}, u32[]{:S(2)}) collective-permute-start(bf16[128,2048]{1,0:T(8,128)(2,1)} %refs_6_), channel_id=1, source_target_pairs={{2,0},{3,1},{4,2},{5,3},{6,4},{7,5},{0,6},{1,7},{10,8},{11,9},{12,... | collective-permute-start | bytes 1572872 | tf_op jit(solution)/shard_map/ppermute | solution.py:511
  4.0 14.8 %collective-permute-start.1 = (bf16[128,2048]{1,0:T(8,128)(2,1)}, bf16[128,2048]{1,0:T(8,128)(2,1)S(1)}, u32[]{:S(2)}, u32[]{:S(2)}) collective-permute-start(bf16[128,2048]{1,0:T(8,128)(2,1)} %refs_6_), channel_id=1, source_target_pairs={{0,2},{1,3},{2,4},{3,5},{4,6},{5,7},{6,0},{7,1},{8,10},{9,11},{10,... | collective-permute-start | bytes 1572872 | tf_op jit(solution)/shard_map/ppermute | solution.py:511
  10.2 30.3 %copy-start = (bf16[128,2048]{1,0:T(8,128)(2,1)S(1)}, bf16[128,2048]{1,0:T(8,128)(2,1)}, u32[]{:S(2)}) copy-start(bf16[128,2048]{1,0:T(8,128)(2,1)} %refs_6_) | copy-start | bytes 1572868
  10.2 15.4 %all-to-all-start = ((f32[16,32,128]{2,1,0:T(8,128)}), f32[16,32,128]{2,1,0:T(8,128)S(1)}, u32[]{:S(2)}, u32[]{:S(2)}) async-start(f32[16,32,128]{2,1,0:T(8,128)} %get-tuple-element.81), calls=%async_computation | async-start | bytes 524288 | tf_op jit(solution)/shard_map/all_to_all | solution.py:19
  18.8 32.4 %copy-start.4 = (bf16[128,2048]{1,0:T(8,128)(2,1)}, bf16[128,2048]{1,0:T(8,128)(2,1)S(1)}, u32[]{:S(2)}) copy-start(bf16[128,2048]{1,0:T(8,128)(2,1)S(1)} %collective-permute-done.rest_1_.refs_7_) | copy-start | bytes 1572868
  18.8 32.4 %copy-start.6 = (bf16[128,2048]{1,0:T(8,128)(2,1)}, bf16[128,2048]{1,0:T(8,128)(2,1)S(1)}, u32[]{:S(2)}) copy-start(bf16[128,2048]{1,0:T(8,128)(2,1)S(1)} %collective-permute-done.1.rest_2_.refs_8_) | copy-start | bytes 1572868
  20.4 20.2 %collective-permute-start.3 = (bf16[64,2048]{1,0:T(8,128)(2,1)}, bf16[64,2048]{1,0:T(8,128)(2,1)S(1)}, u32[]{:S(2)}, u32[]{:S(2)}) collective-permute-start(bf16[64,2048]{1,0:T(8,128)(2,1)} %slice.10), channel_id=1, source_target_pairs={{2,0},{3,1},{4,2},{5,3},{6,4},{7,5},{0,6},{1,7},{10,8},{11,9},{12,... | collective-permute-start | bytes 786440 | tf_op jit(solution)/shard_map/ppermute | solution.py:511
  23.0 17.5 %collective-permute-start.2 = (bf16[64,2048]{1,0:T(8,128)(2,1)}, bf16[64,2048]{1,0:T(8,128)(2,1)}, u32[]{:S(2)}, u32[]{:S(2)}) collective-permute-start(bf16[64,2048]{1,0:T(8,128)(2,1)} %slice.9), channel_id=1, source_target_pairs={{0,2},{1,3},{2,4},{3,5},{4,6},{5,7},{6,0},{7,1},{8,10},{9,11},{10,... | collective-permute-start | bytes 786440 | tf_op jit(solution)/shard_map/ppermute | solution.py:511
  40.6 14.3 %collective-permute-start.4 = (bf16[128,2048]{1,0:T(8,128)(2,1)S(1)}, bf16[128,2048]{1,0:T(8,128)(2,1)S(1)}, u32[]{:S(2)}, u32[]{:S(2)}) collective-permute-start(bf16[128,2048]{1,0:T(8,128)(2,1)S(1)} %copy-done), channel_id=1, source_target_pairs={{0,1},{1,0},{2,3},{3,2},{4,5},{5,4},{6,7},{7,6},{8,9},{9,8},{10,11... | collective-permute-start | bytes 1572872 | tf_op jit(solution)/shard_map/ppermute | solution.py:511
  41.5 13.4 %collective-permute-start.5 = (bf16[128,2048]{1,0:T(8,128)(2,1)S(1)}, bf16[128,2048]{1,0:T(8,128)(2,1)S(1)}, u32[]{:S(2)}, u32[]{:S(2)}) collective-permute-start(bf16[128,2048]{1,0:T(8,128)(2,1)S(1)} %collective-permute-done.rest_1_.refs_7_), channel_id=1, source_target_pairs={{0,1},{1,0},{2,3},{3,2},{4,5},{5,4},{6,7},{7,6},{8,9},{9,8},{10,11... | collective-permute-start | bytes 1572872 | tf_op jit(solution)/shard_map/ppermute | solution.py:511
  41.6 13.3 %collective-permute-start.6 = (bf16[128,2048]{1,0:T(8,128)(2,1)S(1)}, bf16[128,2048]{1,0:T(8,128)(2,1)}, u32[]{:S(2)}, u32[]{:S(2)}) collective-permute-start(bf16[128,2048]{1,0:T(8,128)(2,1)S(1)} %collective-permute-done.1.rest_2_.refs_8_), channel_id=1, source_target_pairs={{0,1},{1,0},{2,3},{3,2},{4,5},{5,4},{6,7},{7,6},{8,9},{9,8},{10,11... | collective-permute-start | bytes 1572872 | tf_op jit(solution)/shard_map/ppermute | solution.py:511
  42.0 12.9 %all-to-all-start.2 = ((bf16[8,128,256]{2,1,0:T(8,128)(2,1)}), bf16[8,128,256]{2,1,0:T(8,128)(2,1)S(1)}, u32[]{:S(2)}, u32[]{:S(2)}) async-start(bf16[8,128,256]{2,1,0:T(8,128)(2,1)} %get-tuple-element.85), calls=%async_computation.2 | async-start | bytes 1048576 | tf_op jit(solution)/shard_map/all_to_all | solution.py:19
  45.5 9.4 %collective-permute-start.7 = (bf16[64,2048]{1,0:T(8,128)(2,1)}, bf16[64,2048]{1,0:T(8,128)(2,1)}, u32[]{:S(2)}, u32[]{:S(2)}) collective-permute-start(bf16[64,2048]{1,0:T(8,128)(2,1)} %collective-permute-done.2.rest_3_.refs_9_), channel_id=1, source_target_pairs={{0,1},{1,0},{2,3},{3,2},{4,5},{5,4},{6,7},{7,6},{8,9},{9,8},{10,11... | collective-permute-start | bytes 786440 | tf_op jit(solution)/shard_map/ppermute | solution.py:511
  45.7 9.2 %collective-permute-start.8 = (bf16[64,2048]{1,0:T(8,128)(2,1)S(1)}, bf16[64,2048]{1,0:T(8,128)(2,1)}, u32[]{:S(2)}, u32[]{:S(2)}) collective-permute-start(bf16[64,2048]{1,0:T(8,128)(2,1)S(1)} %collective-permute-done.3.rest_4_.refs_10_), channel_id=1, source_target_pairs={{0,1},{1,0},{2,3},{3,2},{4,5},{5,4},{6,7},{7,6},{8,9},{9,8},{10,11... | collective-permute-start | bytes 786440 | tf_op jit(solution)/shard_map/ppermute | solution.py:511
  54.9 26.8 %copy-start.9 = (bf16[128,2048]{1,0:T(8,128)(2,1)}, bf16[128,2048]{1,0:T(8,128)(2,1)S(1)}, u32[]{:S(2)}) copy-start(bf16[128,2048]{1,0:T(8,128)(2,1)S(1)} %collective-permute-done.4.rest_5_.refs_11_) | copy-start | bytes 1572868
  54.9 26.8 %copy-start.11 = (bf16[128,2048]{1,0:T(8,128)(2,1)}, bf16[128,2048]{1,0:T(8,128)(2,1)S(1)}, u32[]{:S(2)}) copy-start(bf16[128,2048]{1,0:T(8,128)(2,1)S(1)} %collective-permute-done.5.rest_6_.refs_12_) | copy-start | bytes 1572868
  102.0 21.5 %copy-start.2 = (bf16[256,2048]{1,0:T(8,128)(2,1)S(1)}, bf16[256,2048]{1,0:T(8,128)(2,1)}, u32[]{:S(2)}) copy-start(bf16[256,2048]{1,0:T(8,128)(2,1)} %get-tuple-element.101.proto_t_hbm.proto_t_ref) | copy-start | bytes 3145732
  102.0 21.5 %copy-start.13 = (bf16[2048,256]{1,0:T(8,128)(2,1)S(1)}, bf16[2048,256]{1,0:T(8,128)(2,1)}, u32[]{:S(2)}) copy-start(bf16[2048,256]{1,0:T(8,128)(2,1)} %get-tuple-element.102.proto_ref) | copy-start | bytes 3145732
  102.0 21.5 %copy-start.14 = (bf16[256,2048]{1,0:T(8,128)(2,1)S(1)}, bf16[256,2048]{1,0:T(8,128)(2,1)}, u32[]{:S(2)}) copy-start(bf16[256,2048]{1,0:T(8,128)(2,1)} %get-tuple-element.103.raw_t_ref) | copy-start | bytes 3145732
  102.0 21.5 %copy-start.23 = (f32[8,2048]{1,0:T(8,128)S(1)}, f32[8,2048]{1,0:T(8,128)}, u32[]{:S(2)}) copy-start(f32[8,2048]{1,0:T(8,128)} %get-tuple-element.104.norm_ref) | copy-start | bytes 196612
  102.0 21.5 %copy-start.26 = (s32[11]{0:T(128)S(1)}, s32[11]{0:T(128)}, u32[]{:S(2)}) copy-start(s32[11]{0:T(128)} %stack.47.order_ref.refs_0_) | copy-start | bytes 136
  134.2 30.9 %copy-start.27 = (s32[11]{0:T(128)S(1)}, s32[11]{0:T(128)}, u32[]{:S(2)}) copy-start(s32[11]{0:T(128)} %stack.47.order_ref.refs_0_) | copy-start | bytes 136
  134.2 14.3 %all-to-all-start.9 = ((bf16[8,128,256]{2,1,0:T(8,128)(2,1)}), bf16[8,128,256]{2,1,0:T(8,128)(2,1)}, u32[]{:S(2)}, u32[]{:S(2)}) async-start(bf16[8,128,256]{2,1,0:T(8,128)(2,1)} %bitcast.32), calls=%async_computation.9 | async-start | bytes 1048576 | tf_op jit(solution)/shard_map/all_to_all | solution.py:19
  146.4 34.8 %copy-start.1 = (bf16[128,2048]{1,0:T(8,128)(2,1)S(1)}, bf16[128,2048]{1,0:T(8,128)(2,1)}, u32[]{:S(2)}) copy-start(bf16[128,2048]{1,0:T(8,128)(2,1)} %refs_6_) | copy-start | bytes 1572868
  146.4 34.8 %copy-start.5 = (bf16[128,2048]{1,0:T(8,128)(2,1)S(1)}, bf16[128,2048]{1,0:T(8,128)(2,1)}, u32[]{:S(2)}) copy-start(bf16[128,2048]{1,0:T(8,128)(2,1)} %copy-done.4) | copy-start | bytes 1572868
  146.4 34.8 %copy-start.7 = (bf16[128,2048]{1,0:T(8,128)(2,1)S(1)}, bf16[128,2048]{1,0:T(8,128)(2,1)}, u32[]{:S(2)}) copy-start(bf16[128,2048]{1,0:T(8,128)(2,1)} %copy-done.6) | copy-start | bytes 1572868
  146.4 34.8 %copy-start.8 = (bf16[1024,256]{1,0:T(8,128)(2,1)S(1)}, bf16[1024,256]{1,0:T(8,128)(2,1)}, u32[]{:S(2)}) copy-start(bf16[1024,256]{1,0:T(8,128)(2,1)} %get-tuple-element.129.normed_hbm.refs_3_) | copy-start | bytes 1572868
  146.4 34.8 %copy-start.10 = (bf16[128,2048]{1,0:T(8,128)(2,1)S(1)}, bf16[128,2048]{1,0:T(8,128)(2,1)}, u32[]{:S(2)}) copy-start(bf16[128,2048]{1,0:T(8,128)(2,1)} %copy-done.9) | copy-start | bytes 1572868
  146.4 34.8 %copy-start.12 = (bf16[128,2048]{1,0:T(8,128)(2,1)S(1)}, bf16[128,2048]{1,0:T(8,128)(2,1)}, u32[]{:S(2)}) copy-start(bf16[128,2048]{1,0:T(8,128)(2,1)} %copy-done.11) | copy-start | bytes 1572868
  146.4 34.8 %copy-start.16 = (bf16[64,2048]{1,0:T(8,128)(2,1)S(1)}, bf16[64,2048]{1,0:T(8,128)(2,1)}, u32[]{:S(2)}) copy-start(bf16[64,2048]{1,0:T(8,128)(2,1)} %copy-done.15) | copy-start | bytes 786436
  146.5 34.8 %copy-start.22 = (f32[2048]{0:T(1024)S(1)}, f32[2048]{0:T(1024)}, u32[]{:S(2)}) copy-start(f32[2048]{0:T(1024)} %param.9) | copy-start | bytes 24580
  146.5 34.8 %copy-start.25 = (f32[16,128]{1,0:T(8,128)S(1)}, f32[16,128]{1,0:T(8,128)}, u32[]{:S(2)}) copy-start(f32[16,128]{1,0:T(8,128)} %get-tuple-element.112.inv_hbm.refs_4_) | copy-start | bytes 24580
  146.5 34.8 %copy-start.28 = (s32[11]{0:T(128)S(1)}, s32[11]{0:T(128)}, u32[]{:S(2)}) copy-start(s32[11]{0:T(128)} %stack.47.order_ref.refs_0_) | copy-start | bytes 136
  150.6 14.5 %all-to-all-start.10 = ((bf16[8,128,256]{2,1,0:T(8,128)(2,1)}), bf16[8,128,256]{2,1,0:T(8,128)(2,1)}, u32[]{:S(2)}, u32[]{:S(2)}) async-start(bf16[8,128,256]{2,1,0:T(8,128)(2,1)} %d_embed_kernel.1), calls=%async_computation.10 | async-start | bytes 1048576 | tf_op jit(solution)/shard_map/all_to_all | solution.py:19
  155.6 18.1 %collective-permute-start.9 = (bf16[64,2048]{1,0:T(8,128)(2,1)}, bf16[64,2048]{1,0:T(8,128)(2,1)}, u32[]{:S(2)}, u32[]{:S(2)}) collective-permute-start(bf16[64,2048]{1,0:T(8,128)(2,1)} %get-tuple-element.138), channel_id=1, source_target_pairs={{0,32},{8,40},{16,48},{24,56},{32,64},{40,72},{48,80},{56,88},{64,... | collective-permute-start | bytes 786440 | tf_op jit(solution)/shard_map/ppermute | solution.py:691
  155.8 17.9 %collective-permute-start.10 = (bf16[64,2048]{1,0:T(8,128)(2,1)}, bf16[64,2048]{1,0:T(8,128)(2,1)}, u32[]{:S(2)}, u32[]{:S(2)}) collective-permute-start(bf16[64,2048]{1,0:T(8,128)(2,1)} %get-tuple-element.139), channel_id=1, source_target_pairs={{0,64},{8,72},{16,80},{24,88},{32,96},{40,104},{48,112},{56,120},{... | collective-permute-start | bytes 786440 | tf_op jit(solution)/shard_map/ppermute | solution.py:691
  157.7 16.0 %collective-permute-start.11 = (bf16[64,2048]{1,0:T(8,128)(2,1)}, bf16[64,2048]{1,0:T(8,128)(2,1)}, u32[]{:S(2)}, u32[]{:S(2)}) collective-permute-start(bf16[64,2048]{1,0:T(8,128)(2,1)} %get-tuple-element.140), channel_id=1, source_target_pairs={{0,96},{8,104},{16,112},{24,120},{32,0},{40,8},{48,16},{56,24},{64... | collective-permute-start | bytes 786440 | tf_op jit(solution)/shard_map/ppermute | solution.py:691
  169.5 11.7 %all-to-all-start.11 = ((bf16[16,32,256]{2,1,0:T(8,128)(2,1)}), bf16[16,32,256]{2,1,0:T(8,128)(2,1)}, u32[]{:S(2)}, u32[]{:S(2)}) async-start(bf16[16,32,256]{2,1,0:T(8,128)(2,1)} %copy-done.20), calls=%async_computation.11 | async-start | bytes 524288 | tf_op jit(solution)/shard_map/all_to_all | solution.py:19
  175.8 10.9 %collective-permute-start.12 = (bf16[16,2048]{1,0:T(8,128)(2,1)}, bf16[16,2048]{1,0:T(8,128)(2,1)}, u32[]{:S(2)}, u32[]{:S(2)}) collective-permute-start(bf16[16,2048]{1,0:T(8,128)(2,1)} %get-tuple-element.142), channel_id=1, source_target_pairs={{0,8},{8,16},{16,24},{24,0},{32,40},{40,48},{48,56},{56,32},{64,72... | collective-permute-start | bytes 196616 | tf_op jit(solution)/shard_map/ppermute | solution.py:733
  177.0 9.7 %collective-permute-start.13 = (bf16[16,2048]{1,0:T(8,128)(2,1)}, bf16[16,2048]{1,0:T(8,128)(2,1)}, u32[]{:S(2)}, u32[]{:S(2)}) collective-permute-start(bf16[16,2048]{1,0:T(8,128)(2,1)} %get-tuple-element.143), channel_id=1, source_target_pairs={{0,16},{8,24},{16,0},{24,8},{32,48},{40,56},{48,32},{56,40},{64,80... | collective-permute-start | bytes 196616 | tf_op jit(solution)/shard_map/ppermute | solution.py:733
  179.4 7.3 %collective-permute-start.14 = (bf16[16,2048]{1,0:T(8,128)(2,1)}, bf16[16,2048]{1,0:T(8,128)(2,1)}, u32[]{:S(2)}, u32[]{:S(2)}) collective-permute-start(bf16[16,2048]{1,0:T(8,128)(2,1)} %get-tuple-element.144), channel_id=1, source_target_pairs={{0,24},{8,0},{16,8},{24,16},{32,56},{40,32},{48,40},{56,48},{64,88... | collective-permute-start | bytes 196616 | tf_op jit(solution)/shard_map/ppermute | solution.py:733
  182.5 15.7 %copy-start.29 = (bf16[16,2048]{1,0:T(8,128)(2,1)S(1)}, bf16[16,2048]{1,0:T(8,128)(2,1)}, u32[]{:S(2)}) copy-start(bf16[16,2048]{1,0:T(8,128)(2,1)} %get-tuple-element.151) | copy-start | bytes 196612
  186.8 28.0 %all-to-all-start.12 = ((bf16[128,40,128]{2,1,0:T(8,128)(2,1)}), bf16[128,40,128]{2,1,0:T(8,128)(2,1)S(1)}, u32[]{:S(2)}, u32[]{:S(2)}) async-start(bf16[128,40,128]{2,1,0:T(8,128)(2,1)} %get-tuple-element.145), calls=%async_computation.12 | async-start | bytes 2621440 | tf_op jit(solution)/shard_map/all_to_all | solution.py:19
  192.8 7.1 %collective-permute-start.15 = (f32[16,256]{1,0:T(8,128)S(1)}, f32[16,256]{1,0:T(8,128)S(1)}, u32[]{:S(2)}, u32[]{:S(2)}) collective-permute-start(f32[16,256]{1,0:T(8,128)S(1)} %get-tuple-element.146), channel_id=1, source_target_pairs={{0,0},{1,16},{2,32},{3,48},{4,64},{5,80},{6,96},{7,112},{8,1},{9,1... | collective-permute-start | bytes 49160 | tf_op jit(solution)/shard_map/ppermute | solution.py:784
  (5 other events, 14.9 us)

commit v10 on v9

--- a/solution.py
+++ b/solution.py
@@ -72,9 +72,19 @@
 
 
 def embed_kernel(
-    total_rows, pre_ref, recv_ref, gain_ref, bias_ref, w2_ref, unit_hbm, mean_hbm, inv_hbm, msg_hbm,
-    hid_ref, unit_ref, mean_ref, inv_ref, bf_ref, sems,
+    total_rows, pre_hbm, recv_ref, gain_ref, bias_ref, w2_ref, unit_hbm, mean_hbm, inv_hbm, msg_hbm,
+    hid_ref, unit_ref, mean_ref, inv_ref, bf_ref, pre_ref, sems, pre_sems,
 ):
+    stretch = 4
+    span = pre_ref.shape[1] // stretch
+    fetches = [
+        pltpu.make_async_copy(
+            pre_hbm.at[:, k * span : (k + 1) * span], pre_ref.at[:, k * span : (k + 1) * span], pre_sems.at[k]
+        )
+        for k in range(stretch)
+    ]
+    for fetch in fetches:
+        fetch.start()
     stats = jnp.sum(recv_ref[...], axis=0)
     half = stats.shape[0] // 2
     mean = stats[:half] / total_rows
@@ -82,6 +92,8 @@
     mean_ref[...] = mean
     inv_ref[...] = inv
     for j in range(half):
+        if j * LANES % span == 0:
+            fetches[j * LANES // span].wait()
         normed = (pre_ref[:, lane(j)] - mean[j : j + 1]) * inv[j : j + 1]
         hid_ref[:, lane(j)] = jax.nn.gelu(normed * gain_ref[j : j + 1, :] + bias_ref[j : j + 1, :]).astype(BF)
     embed = jnp.dot(hid_ref[...], w2_ref[...], preferred_element_type=F32)
@@ -553,6 +565,13 @@
     got = deal(msg, "proto")
     unit_embed, mean, inv, msg = pl.pallas_call(
         lambda *refs: embed_kernel(total_rows, *refs),
+        in_specs=[
+            anywhere,
+            pl.BlockSpec((n_proto, 2 * hid_bands, LANES), lambda: (0, 0, 0)),
+            pl.BlockSpec((hid_bands, LANES), lambda: (0, 0)),
+            pl.BlockSpec((hid_bands, LANES), lambda: (0, 0)),
+            pl.BlockSpec((d_hid, width), lambda: (0, 0)),
+        ],
         out_specs=[pl.BlockSpec(memory_space=pltpu.HBM)] * 4,
         out_shape=[
             far_shape((own, width + LANES)),
@@ -566,11 +585,13 @@
             pltpu.VMEM((hid_bands, LANES), F32),
             pltpu.VMEM((hid_bands, LANES), F32),
             pltpu.VMEM((own, width), BF),
+            pltpu.VMEM((own, d_hid), F32),
             pltpu.SemaphoreType.DMA((n_proto + 3,)),
+            pltpu.SemaphoreType.DMA((4,)),
         ],
         compiler_params=PARAMS,
         name="embed_kernel",
-    )(pre, got, gain, bias, w_second)
+    )(far(pre), got, gain, bias, w_second)
     raw, *mine, _ = lax.optimization_barrier((prototypes, features, from_right, from_left, far_top, far_low, msg))
     parts = mine + [hop(piece, swap) for piece in mine]
     proto_bf, proto_t, raw_t, norm, w_slab = pl.pallas_call(

time: 217 us -> 217 us (level)
  no operation moved by 1% of the time
where the time goes in v10:
time: 217 us; the launch traced here: 215 us
  blocking collectives  70 us (32%)
  Pallas kernels  54.6 us (25%)
  starting transfers between devices  52.6 us (24%)
  waiting for transfers between devices  30.3 us (14%)
  local copies, waits for them, and re-layouts  5.24 us (2%)
    all_to_all x7, blocking collectives, deal(): return lax.all_to_all(x, axis, 0, 0, tiled=True)  70 us
    all_to_all x6, starting transfers between devices, deal(): return lax.all_to_all(x, axis, 0, 0, tiled=True)  31.3 us
    all_to_all x6, waiting for transfers between devices, deal(): return lax.all_to_all(x, axis, 0, 0, tiled=True)  30.2 us
    pallas_call x1, Pallas kernels, step_of_device(): pl.pallas_call(final_kernel, grid=(steps // 2,), in_specs=[pl.BlockSpec(m...  10.7 us
    ppermute x9, starting transfers between devices, hop(): return lax.ppermute(x, 'proto', moves)  8.03 us
    pallas_call x1, Pallas kernels, step_of_device(): pl.pallas_call(slab_kernel, grid_spec=pltpu.PrefetchScalarGridSpec(num_sc...  7.36 us
    pallas_call x1, Pallas kernels, step_of_device(): pl.pallas_call(pre_kernel, in_specs=[pl.BlockSpec(features.shape, lambda:...  6.16 us
    ppermute x1, starting transfers between devices, step_of_device(): lax.ppermute(second, ('batch', 'proto'), [(b * n_proto + p, p * n_batch +...  5.44 us
  transfers between devices with their start and end apart: 22, of which 6 were waited for; matrix products, arithmetic and copies ran while one was open for 2% of the time, Pallas kernels for 14%

profile of v10, /device:TPU:1, one launch (start us, length us, event | category | flops | bytes accessed | tf_op | source)
XLA Modules:
  0.0 215.4 jit_solution(8621313921866771361)
XLA Ops:
  0.7 3.4 %collective-permute-start = (bf16[128,2048]{1,0:T(8,128)(2,1)}, bf16[128,2048]{1,0:T(8,128)(2,1)S(1)}, u32[]{:S(2)}, u32[]{:S(2)}) collective-permute-start(bf16[128,2048]{1,0:T(8,128)(2,1)} %refs_6_), channel_id=1, source_target_pairs={{2,0},{3,1},{4,2},{5,3},{6,4},{7,5},{0,6},{1,7},{10,8},{11,9},{12,... | collective-permute-start | bytes 1572872 | tf_op jit(solution)/shard_map/ppermute | solution.py:523
  4.0 6.2 %pre_kernel.1 = (f32[128,2048]{1,0:T(8,128)}, f32[16,32,128]{2,1,0:T(8,128)}) custom-call(bf16[128,2048]{1,0:T(8,128)(2,1)} %refs_6_, bf16[2048,2048]{1,0:T(8,128)(2,1)} %w_hbm.3), custom_call_target="tpu_custom_call" | custom-call | tf_op jit(solution)/shard_map/pre_kernel/pallas_call | solution.py:546
  10.2 7.9 %all-to-all-start = ((f32[16,32,128]{2,1,0:T(8,128)}), f32[16,32,128]{2,1,0:T(8,128)S(1)}, u32[]{:S(2)}, u32[]{:S(2)}) async-start(f32[16,32,128]{2,1,0:T(8,128)} %get-tuple-element.81), calls=%async_computation | async-start | bytes 524288 | tf_op jit(solution)/shard_map/all_to_all | solution.py:19
  18.9 0.8 slice.9
  20.4 2.6 %collective-permute-start.3 = (bf16[64,2048]{1,0:T(8,128)(2,1)}, bf16[64,2048]{1,0:T(8,128)(2,1)S(1)}, u32[]{:S(2)}, u32[]{:S(2)}) collective-permute-start(bf16[64,2048]{1,0:T(8,128)(2,1)} %slice.10), channel_id=1, source_target_pairs={{2,0},{3,1},{4,2},{5,3},{6,4},{7,5},{0,6},{1,7},{10,8},{11,9},{12,... | collective-permute-start | bytes 786440 | tf_op jit(solution)/shard_map/ppermute | solution.py:523
  23.0 2.6 %all-to-all-done.recv_ref = f32[16,32,128]{2,1,0:T(8,128)S(1)} async-done(((f32[16,32,128]{2,1,0:T(8,128)}), f32[16,32,128]{2,1,0:T(8,128)S(1)}, u32[]{:S(2)}, u32[]{:S(2)}) %all-to-all-start) | async-done | bytes 262176 | tf_op jit(solution)/shard_map/all_to_all | solution.py:19
  25.6 11.8 %all_to_all.65.refs_1_ = f32[8,32,128]{2,1,0:T(8,128)S(1)} all-to-all(f32[8,32,128]{2,1,0:T(8,128)S(1)} %relay_kernel.1), channel_id=1, replica_groups=mesh['batch'=16,'proto'=8] {'proto'}, dimensions={0} | all-to-all | bytes 262144 | tf_op jit(solution)/shard_map/all_to_all | solution.py:19
  37.4 2.8 %embed_kernel.1 = (f32[128,384]{1,0:T(8,128)}, f32[16,128]{1,0:T(8,128)}, f32[16,128]{1,0:T(8,128)}, bf16[8,128,256]{2,1,0:T(8,128)(2,1)}) custom-call(f32[128,2048]{1,0:T(8,128)} %get-tuple-element.83.refs_0_, f32[8,32,128]{2,1,0:T(8,128)S(1)} %all_to_all.65.refs_1_, f32[16,128]{1,0:T(8,128)S(1)} %bitcast.28, f32[16,128]{1,0:T(8,128)S(1)} %bitcast.31, ...), custom_call_target="tpu_custom_call" | custom-call | tf_op jit(solution)/shard_map/embed_kernel/pallas_call | solution.py:566
  40.3 0.9 collective-permute-start.4
  41.8 3.5 %all-to-all-start.2 = ((bf16[8,128,256]{2,1,0:T(8,128)(2,1)}), bf16[8,128,256]{2,1,0:T(8,128)(2,1)S(1)}, u32[]{:S(2)}, u32[]{:S(2)}) async-start(bf16[8,128,256]{2,1,0:T(8,128)(2,1)} %get-tuple-element.85), calls=%async_computation.2 | async-start | bytes 1048576 | tf_op jit(solution)/shard_map/all_to_all | solution.py:19
  45.8 5.2 %proto_kernel.1 = (bf16[2048,256]{1,0:T(8,128)(2,1)}, bf16[256,2048]{1,0:T(8,128)(2,1)}, bf16[256,2048]{1,0:T(8,128)(2,1)}, f32[8,2048]{1,0:T(8,128)}, bf16[2048,256]{1,0:T(8,128)(2,1)}) custom-call(s32[11]{0:T(128)} %stack.47.order_ref.refs_0_, bf16[2048,256]{1,0:T(8,128)(2,1)} %raw_ref, bf16[2048,2048]{1,0:T(8,128)(2,1)} %w_hbm.3), custom_call_target="tpu_custom_call" | custom-call | tf_op jit(solution)/shard_map/proto_kernel/pallas_call | solution.py:597
  51.0 3.6 %all-to-all-done.2 = bf16[8,128,256]{2,1,0:T(8,128)(2,1)S(1)} async-done(((bf16[8,128,256]{2,1,0:T(8,128)(2,1)}), bf16[8,128,256]{2,1,0:T(8,128)(2,1)S(1)}, u32[]{:S(2)}, u32[]{:S(2)}) %all-to-all-start.2) | async-done | bytes 524320 | tf_op jit(solution)/shard_map/all_to_all | solution.py:19
  54.7 4.4 %score_kernel.1 = (bf16[1024,2048]{1,0:T(8,128)(2,1)S(1)}, f32[16,16,128]{2,1,0:T(8,128)S(1)}, f32[8,128]{1,0:T(8,128)S(1)}) custom-call(bf16[1024,256]{1,0:T(8,128)(2,1)S(1)} %bitcast.25, bf16[256,2048]{1,0:T(8,128)(2,1)} %get-tuple-element.101.proto_t_hbm.proto_t_ref), custom_call_target="tpu_custom_call" | custom-call | tf_op jit(solution)/shard_map/score_kernel/pallas_call | solution.py:622
  59.1 10.4 %all_to_all.66.recv_ref = f32[16,16,128]{2,1,0:T(8,128)S(1)} all-to-all(f32[16,16,128]{2,1,0:T(8,128)S(1)} %get-tuple-element.105), channel_id=1, replica_groups=mesh['batch'=16,'proto'=8] {'batch'}, dimensions={0} | all-to-all | bytes 262144 | tf_op jit(solution)/shard_map/all_to_all | solution.py:19
  69.5 1.2 row_kernel.3
  70.7 9.6 %all_to_all.67.recv_ref.recv_soft_ref = f32[8,16,128]{2,1,0:T(8,128)S(1)} all-to-all(f32[8,16,128]{2,1,0:T(8,128)S(1)} %row_kernel.3), channel_id=1, replica_groups=mesh['batch'=16,'proto'=8] {'proto'}, dimensions={0} | all-to-all | bytes 131072 | tf_op jit(solution)/shard_map/all_to_all | solution.py:19
  80.3 1.2 col_kernel.2
  81.5 9.9 %all_to_all.68.recv_ref = f32[16,16,128]{2,1,0:T(8,128)S(1)} all-to-all(f32[16,16,128]{2,1,0:T(8,128)S(1)} %col_kernel.2), channel_id=1, replica_groups=mesh['batch'=16,'proto'=8] {'batch'}, dimensions={0} | all-to-all | bytes 262144 | tf_op jit(solution)/shard_map/all_to_all | solution.py:19
  91.4 1.2 row_kernel.4
  92.6 9.2 %all_to_all.69.recv_ref = f32[8,8,128]{2,1,0:T(8,128)S(1)} all-to-all(f32[8,8,128]{2,1,0:T(8,128)S(1)} %row_kernel.4), channel_id=1, replica_groups=mesh['batch'=16,'proto'=8] {'proto'}, dimensions={0} | all-to-all | bytes 65536 | tf_op jit(solution)/shard_map/all_to_all | solution.py:19
  101.8 1.2 col_kernel.3
  103.0 9.9 %all_to_all.70.recv_ref.recv_col_ref = f32[16,16,128]{2,1,0:T(8,128)S(1)} all-to-all(f32[16,16,128]{2,1,0:T(8,128)S(1)} %col_kernel.3), channel_id=1, replica_groups=mesh['batch'=16,'proto'=8] {'batch'}, dimensions={0} | all-to-all | bytes 262144 | tf_op jit(solution)/shard_map/all_to_all | solution.py:19
  112.9 1.2 row_kernel.5
  114.1 9.1 %all_to_all.71.recv_row_ref = f32[8,8,128]{2,1,0:T(8,128)S(1)} all-to-all(f32[8,8,128]{2,1,0:T(8,128)S(1)} %row_kernel.5), channel_id=1, replica_groups=mesh['batch'=16,'proto'=8] {'proto'}, dimensions={0} | all-to-all | bytes 65536 | tf_op jit(solution)/shard_map/all_to_all | solution.py:19
  123.3 10.7 %final_kernel.1 = (bf16[1024,256]{1,0:T(8,128)(2,1)}, bf16[64,2048]{1,0:T(8,128)(2,1)}, bf16[64,2048]{1,0:T(8,128)(2,1)}, bf16[64,2048]{1,0:T(8,128)(2,1)}, bf16[64,2048]{1,0:T(8,128)(2,1)}, /*index=5*/f32[16,128]{1,0:T(8,128)}) custom-call(s32[11]{0:T(128)S(1)} %copy-done.25, bf16[1024,256]{1,0:T(8,128)(2,1)S(1)} %bitcast.26, ...), custom_call_target="tpu_custom_call" | custom-call | tf_op jit(solution)/shard_map/final_kernel/pallas_call | solution.py:671
  134.1 4.8 %all-to-all-start.9 = ((bf16[8,128,256]{2,1,0:T(8,128)(2,1)}), bf16[8,128,256]{2,1,0:T(8,128)(2,1)}, u32[]{:S(2)}, u32[]{:S(2)}) async-start(bf16[8,128,256]{2,1,0:T(8,128)(2,1)} %bitcast.32), calls=%async_computation.9 | async-start | bytes 1048576 | tf_op jit(solution)/shard_map/all_to_all | solution.py:19
  138.8 7.4 %slab_kernel.1 = (bf16[1024,256]{1,0:T(8,128)(2,1)}, bf16[1024,256]{1,0:T(8,128)(2,1)}, bf16[1024,256]{1,0:T(8,128)(2,1)}) custom-call(s32[11]{0:T(128)} %stack.47.order_ref.refs_0_, f32[16,128]{1,0:T(8,128)} %get-tuple-element.111.mean_hbm, f32[16,128]{1,0:T(8,128)} %get-tuple-element.112.inv_hbm.refs_4_, f32[16,128]{1,0:T(8,128)} %bitcast.27, ...), custom_call_target="tpu_custom_call" | custom-call | tf_op jit(solution)/shard_map/slab_kernel/pallas_call | solution.py:716
  146.3 2.0 all-to-all-done.9.recv_hbm
  148.3 2.1 d_embed_kernel.1
  150.4 5.0 %all-to-all-start.10 = ((bf16[8,128,256]{2,1,0:T(8,128)(2,1)}), bf16[8,128,256]{2,1,0:T(8,128)(2,1)}, u32[]{:S(2)}, u32[]{:S(2)}) async-start(bf16[8,128,256]{2,1,0:T(8,128)(2,1)} %d_embed_kernel.1), calls=%async_computation.10 | async-start | bytes 1048576 | tf_op jit(solution)/shard_map/all_to_all | solution.py:19
  155.6 1.9 collective-permute-start.10
  157.5 1.0 collective-permute-start.11
  158.5 6.4 %all-to-all-done.10.d_embed_hbm = bf16[8,128,256]{2,1,0:T(8,128)(2,1)} async-done(((bf16[8,128,256]{2,1,0:T(8,128)(2,1)}), bf16[8,128,256]{2,1,0:T(8,128)(2,1)}, u32[]{:S(2)}, u32[]{:S(2)}) %all-to-all-start.10) | async-done | bytes 524320 | tf_op jit(solution)/shard_map/all_to_all | solution.py:19
  164.9 2.7 %shift_kernel.1 = (f32[1024,256]{1,0:T(8,128)S(1)}, bf16[16,32,256]{2,1,0:T(8,128)(2,1)S(1)}) custom-call(s32[11]{0:T(128)S(1)} %copy-done.26, bf16[8,128,256]{2,1,0:T(8,128)(2,1)} %all-to-all-done.10.d_embed_hbm, bf16[2048,256]{1,0:T(8,128)(2,1)} %w2_hbm.1, bf16[1024,256]{1,0:T(8,128)(2,1)} %get-tuple-element.129.normed_hbm.refs_3_, ...), custom_call_target="tpu_custom_call" | custom-call | tf_op jit(solution)/shard_map/shift_kernel/pallas_call | solution.py:757
  167.6 1.0 copy-done.17
  168.6 0.7 copy-done.19
  169.3 4.2 %all-to-all-start.11 = ((bf16[16,32,256]{2,1,0:T(8,128)(2,1)}), bf16[16,32,256]{2,1,0:T(8,128)(2,1)}, u32[]{:S(2)}, u32[]{:S(2)}) async-start(bf16[16,32,256]{2,1,0:T(8,128)(2,1)} %copy-done.19), calls=%async_computation.11 | async-start | bytes 524288 | tf_op jit(solution)/shard_map/all_to_all | solution.py:19
  173.5 2.1 stage_kernel.1
  175.6 1.2 collective-permute-start.12
  176.8 2.4 %collective-permute-start.13 = (bf16[16,2048]{1,0:T(8,128)(2,1)}, bf16[16,2048]{1,0:T(8,128)(2,1)}, u32[]{:S(2)}, u32[]{:S(2)}) collective-permute-start(bf16[16,2048]{1,0:T(8,128)(2,1)} %get-tuple-element.143), channel_id=1, source_target_pairs={{0,16},{8,24},{16,0},{24,8},{32,48},{40,56},{48,32},{56,40},{64,80... | collective-permute-start | bytes 196616 | tf_op jit(solution)/shard_map/ppermute | solution.py:754
  179.2 1.2 collective-permute-start.14
  181.1 1.2 copy-done.18
  182.3 4.2 %first_kernel.1 = (bf16[128,40,128]{2,1,0:T(8,128)(2,1)}, f32[16,256]{1,0:T(8,128)S(1)}) custom-call(s32[11]{0:T(128)S(1)} %copy-done.27, bf16[16,32,256]{2,1,0:T(8,128)(2,1)} %all-to-all-done.11.refs_1_, f32[1024,256]{1,0:T(8,128)S(1)} %copy-done.18, bf16[1024,256]{1,0:T(8,128)(2,1)S(1)} %copy-done.8, f32[16,128]{1,0:T(8,128)S(1)} %copy-done.24, ...), custom_call_target="tpu_custom_call" | custom-call | tf_op jit(solution)/shard_map/first_kernel/pallas_call | solution.py:783
  186.6 6.0 %all-to-all-start.12 = ((bf16[128,40,128]{2,1,0:T(8,128)(2,1)}), bf16[128,40,128]{2,1,0:T(8,128)(2,1)S(1)}, u32[]{:S(2)}, u32[]{:S(2)}) async-start(bf16[128,40,128]{2,1,0:T(8,128)(2,1)} %get-tuple-element.145), calls=%async_computation.12 | async-start | bytes 2621440 | tf_op jit(solution)/shard_map/all_to_all | solution.py:19
  192.6 5.4 %collective-permute-start.15 = (f32[16,256]{1,0:T(8,128)S(1)}, f32[16,256]{1,0:T(8,128)S(1)}, u32[]{:S(2)}, u32[]{:S(2)}) collective-permute-start(f32[16,256]{1,0:T(8,128)S(1)} %get-tuple-element.146), channel_id=1, source_target_pairs={{0,0},{1,16},{2,32},{3,48},{4,64},{5,80},{6,96},{7,112},{8,1},{9,1... | collective-permute-start | bytes 49160 | tf_op jit(solution)/shard_map/ppermute | solution.py:805
  198.0 1.6 add_bitcast_fusion
  199.6 15.0 %all-to-all-done.12 = bf16[128,40,128]{2,1,0:T(8,128)(2,1)S(1)} async-done(((bf16[128,40,128]{2,1,0:T(8,128)(2,1)}), bf16[128,40,128]{2,1,0:T(8,128)(2,1)S(1)}, u32[]{:S(2)}, u32[]{:S(2)}) %all-to-all-start.12) | async-done | bytes 1310752 | tf_op jit(solution)/shard_map/all_to_all | solution.py:19
  214.6 0.8 tail_kernel.1
  (85 shorter events, 3.5 us)
Async XLA Ops:
  0.6 22.4 %copy-start.29 = (s32[1024]{0:T(1024)S(1)}, s32[1024]{0:T(1024)}, u32[]{:S(2)}) copy-start(s32[1024]{0:T(1024)} %param.13) | copy-start | bytes 12292
  0.6 36.8 %copy-start.3 = (bf16[2048,256]{1,0:T(8,128)(2,1)S(1)}, bf16[2048,256]{1,0:T(8,128)(2,1)}, u32[]{:S(2)}) copy-start(bf16[2048,256]{1,0:T(8,128)(2,1)} %w2_hbm.1) | copy-start | bytes 3145732
  0.7 36.8 %copy-start.23 = (f32[2048]{0:T(1024)S(1)}, f32[2048]{0:T(1024)}, u32[]{:S(2)}) copy-start(f32[2048]{0:T(1024)} %param.10) | copy-start | bytes 24580
  0.7 36.8 %copy-start.20 = (f32[2048]{0:T(1024)S(1)}, f32[2048]{0:T(1024)}, u32[]{:S(2)}) copy-start(f32[2048]{0:T(1024)} %param.9) | copy-start | bytes 24580
  0.7 18.2 %collective-permute-start = (bf16[128,2048]{1,0:T(8,128)(2,1)}, bf16[128,2048]{1,0:T(8,128)(2,1)S(1)}, u32[]{:S(2)}, u32[]{:S(2)}) collective-permute-start(bf16[128,2048]{1,0:T(8,128)(2,1)} %refs_6_), channel_id=1, source_target_pairs={{2,0},{3,1},{4,2},{5,3},{6,4},{7,5},{0,6},{1,7},{10,8},{11,9},{12,... | collective-permute-start | bytes 1572872 | tf_op jit(solution)/shard_map/ppermute | solution.py:523
  4.0 14.8 %collective-permute-start.1 = (bf16[128,2048]{1,0:T(8,128)(2,1)}, bf16[128,2048]{1,0:T(8,128)(2,1)S(1)}, u32[]{:S(2)}, u32[]{:S(2)}) collective-permute-start(bf16[128,2048]{1,0:T(8,128)(2,1)} %refs_6_), channel_id=1, source_target_pairs={{0,2},{1,3},{2,4},{3,5},{4,6},{5,7},{6,0},{7,1},{8,10},{9,11},{10,... | collective-permute-start | bytes 1572872 | tf_op jit(solution)/shard_map/ppermute | solution.py:523
  10.2 30.1 %copy-start = (bf16[128,2048]{1,0:T(8,128)(2,1)S(1)}, bf16[128,2048]{1,0:T(8,128)(2,1)}, u32[]{:S(2)}) copy-start(bf16[128,2048]{1,0:T(8,128)(2,1)} %refs_6_) | copy-start | bytes 1572868
  10.2 15.4 %all-to-all-start = ((f32[16,32,128]{2,1,0:T(8,128)}), f32[16,32,128]{2,1,0:T(8,128)S(1)}, u32[]{:S(2)}, u32[]{:S(2)}) async-start(f32[16,32,128]{2,1,0:T(8,128)} %get-tuple-element.81), calls=%async_computation | async-start | bytes 524288 | tf_op jit(solution)/shard_map/all_to_all | solution.py:19
  18.9 32.2 %copy-start.4 = (bf16[128,2048]{1,0:T(8,128)(2,1)}, bf16[128,2048]{1,0:T(8,128)(2,1)S(1)}, u32[]{:S(2)}) copy-start(bf16[128,2048]{1,0:T(8,128)(2,1)S(1)} %collective-permute-done.rest_1_.refs_7_) | copy-start | bytes 1572868
  18.9 32.2 %copy-start.6 = (bf16[128,2048]{1,0:T(8,128)(2,1)}, bf16[128,2048]{1,0:T(8,128)(2,1)S(1)}, u32[]{:S(2)}) copy-start(bf16[128,2048]{1,0:T(8,128)(2,1)S(1)} %collective-permute-done.1.rest_2_.refs_8_) | copy-start | bytes 1572868
  20.4 19.9 %collective-permute-start.3 = (bf16[64,2048]{1,0:T(8,128)(2,1)}, bf16[64,2048]{1,0:T(8,128)(2,1)S(1)}, u32[]{:S(2)}, u32[]{:S(2)}) collective-permute-start(bf16[64,2048]{1,0:T(8,128)(2,1)} %slice.10), channel_id=1, source_target_pairs={{2,0},{3,1},{4,2},{5,3},{6,4},{7,5},{0,6},{1,7},{10,8},{11,9},{12,... | collective-permute-start | bytes 786440 | tf_op jit(solution)/shard_map/ppermute | solution.py:523
  23.0 17.3 %collective-permute-start.2 = (bf16[64,2048]{1,0:T(8,128)(2,1)}, bf16[64,2048]{1,0:T(8,128)(2,1)}, u32[]{:S(2)}, u32[]{:S(2)}) collective-permute-start(bf16[64,2048]{1,0:T(8,128)(2,1)} %slice.9), channel_id=1, source_target_pairs={{0,2},{1,3},{2,4},{3,5},{4,6},{5,7},{6,0},{7,1},{8,10},{9,11},{10,... | collective-permute-start | bytes 786440 | tf_op jit(solution)/shard_map/ppermute | solution.py:523
  40.3 14.3 %collective-permute-start.4 = (bf16[128,2048]{1,0:T(8,128)(2,1)S(1)}, bf16[128,2048]{1,0:T(8,128)(2,1)S(1)}, u32[]{:S(2)}, u32[]{:S(2)}) collective-permute-start(bf16[128,2048]{1,0:T(8,128)(2,1)S(1)} %copy-done), channel_id=1, source_target_pairs={{0,1},{1,0},{2,3},{3,2},{4,5},{5,4},{6,7},{7,6},{8,9},{9,8},{10,11... | collective-permute-start | bytes 1572872 | tf_op jit(solution)/shard_map/ppermute | solution.py:523
  41.3 13.4 %collective-permute-start.5 = (bf16[128,2048]{1,0:T(8,128)(2,1)S(1)}, bf16[128,2048]{1,0:T(8,128)(2,1)S(1)}, u32[]{:S(2)}, u32[]{:S(2)}) collective-permute-start(bf16[128,2048]{1,0:T(8,128)(2,1)S(1)} %collective-permute-done.rest_1_.refs_7_), channel_id=1, source_target_pairs={{0,1},{1,0},{2,3},{3,2},{4,5},{5,4},{6,7},{7,6},{8,9},{9,8},{10,11... | collective-permute-start | bytes 1572872 | tf_op jit(solution)/shard_map/ppermute | solution.py:523
  41.4 13.3 %collective-permute-start.6 = (bf16[128,2048]{1,0:T(8,128)(2,1)S(1)}, bf16[128,2048]{1,0:T(8,128)(2,1)}, u32[]{:S(2)}, u32[]{:S(2)}) collective-permute-start(bf16[128,2048]{1,0:T(8,128)(2,1)S(1)} %collective-permute-done.1.rest_2_.refs_8_), channel_id=1, source_target_pairs={{0,1},{1,0},{2,3},{3,2},{4,5},{5,4},{6,7},{7,6},{8,9},{9,8},{10,11... | collective-permute-start | bytes 1572872 | tf_op jit(solution)/shard_map/ppermute | solution.py:523
  41.8 12.9 %all-to-all-start.2 = ((bf16[8,128,256]{2,1,0:T(8,128)(2,1)}), bf16[8,128,256]{2,1,0:T(8,128)(2,1)S(1)}, u32[]{:S(2)}, u32[]{:S(2)}) async-start(bf16[8,128,256]{2,1,0:T(8,128)(2,1)} %get-tuple-element.85), calls=%async_computation.2 | async-start | bytes 1048576 | tf_op jit(solution)/shard_map/all_to_all | solution.py:19
  45.3 9.4 %collective-permute-start.7 = (bf16[64,2048]{1,0:T(8,128)(2,1)}, bf16[64,2048]{1,0:T(8,128)(2,1)}, u32[]{:S(2)}, u32[]{:S(2)}) collective-permute-start(bf16[64,2048]{1,0:T(8,128)(2,1)} %collective-permute-done.2.rest_3_.refs_9_), channel_id=1, source_target_pairs={{0,1},{1,0},{2,3},{3,2},{4,5},{5,4},{6,7},{7,6},{8,9},{9,8},{10,11... | collective-permute-start | bytes 786440 | tf_op jit(solution)/shard_map/ppermute | solution.py:523
  45.5 9.2 %collective-permute-start.8 = (bf16[64,2048]{1,0:T(8,128)(2,1)S(1)}, bf16[64,2048]{1,0:T(8,128)(2,1)}, u32[]{:S(2)}, u32[]{:S(2)}) collective-permute-start(bf16[64,2048]{1,0:T(8,128)(2,1)S(1)} %collective-permute-done.3.rest_4_.refs_10_), channel_id=1, source_target_pairs={{0,1},{1,0},{2,3},{3,2},{4,5},{5,4},{6,7},{7,6},{8,9},{9,8},{10,11... | collective-permute-start | bytes 786440 | tf_op jit(solution)/shard_map/ppermute | solution.py:523
  54.7 26.8 %copy-start.9 = (bf16[128,2048]{1,0:T(8,128)(2,1)}, bf16[128,2048]{1,0:T(8,128)(2,1)S(1)}, u32[]{:S(2)}) copy-start(bf16[128,2048]{1,0:T(8,128)(2,1)S(1)} %collective-permute-done.4.rest_5_.refs_11_) | copy-start | bytes 1572868
  54.7 26.8 %copy-start.11 = (bf16[128,2048]{1,0:T(8,128)(2,1)}, bf16[128,2048]{1,0:T(8,128)(2,1)S(1)}, u32[]{:S(2)}) copy-start(bf16[128,2048]{1,0:T(8,128)(2,1)S(1)} %collective-permute-done.5.rest_6_.refs_12_) | copy-start | bytes 1572868
  101.8 21.5 %copy-start.2 = (bf16[256,2048]{1,0:T(8,128)(2,1)S(1)}, bf16[256,2048]{1,0:T(8,128)(2,1)}, u32[]{:S(2)}) copy-start(bf16[256,2048]{1,0:T(8,128)(2,1)} %get-tuple-element.101.proto_t_hbm.proto_t_ref) | copy-start | bytes 3145732
  101.8 21.5 %copy-start.13 = (bf16[2048,256]{1,0:T(8,128)(2,1)S(1)}, bf16[2048,256]{1,0:T(8,128)(2,1)}, u32[]{:S(2)}) copy-start(bf16[2048,256]{1,0:T(8,128)(2,1)} %get-tuple-element.102.proto_ref) | copy-start | bytes 3145732
  101.8 21.5 %copy-start.14 = (bf16[256,2048]{1,0:T(8,128)(2,1)S(1)}, bf16[256,2048]{1,0:T(8,128)(2,1)}, u32[]{:S(2)}) copy-start(bf16[256,2048]{1,0:T(8,128)(2,1)} %get-tuple-element.103.raw_t_ref) | copy-start | bytes 3145732
  101.8 21.5 %copy-start.22 = (f32[8,2048]{1,0:T(8,128)S(1)}, f32[8,2048]{1,0:T(8,128)}, u32[]{:S(2)}) copy-start(f32[8,2048]{1,0:T(8,128)} %get-tuple-element.104.norm_ref) | copy-start | bytes 196612
  101.8 21.5 %copy-start.25 = (s32[11]{0:T(128)S(1)}, s32[11]{0:T(128)}, u32[]{:S(2)}) copy-start(s32[11]{0:T(128)} %stack.47.order_ref.refs_0_) | copy-start | bytes 136
  134.0 30.8 %copy-start.26 = (s32[11]{0:T(128)S(1)}, s32[11]{0:T(128)}, u32[]{:S(2)}) copy-start(s32[11]{0:T(128)} %stack.47.order_ref.refs_0_) | copy-start | bytes 136
  134.1 14.2 %all-to-all-start.9 = ((bf16[8,128,256]{2,1,0:T(8,128)(2,1)}), bf16[8,128,256]{2,1,0:T(8,128)(2,1)}, u32[]{:S(2)}, u32[]{:S(2)}) async-start(bf16[8,128,256]{2,1,0:T(8,128)(2,1)} %bitcast.32), calls=%async_computation.9 | async-start | bytes 1048576 | tf_op jit(solution)/shard_map/all_to_all | solution.py:19
  146.2 34.8 %copy-start.1 = (bf16[128,2048]{1,0:T(8,128)(2,1)S(1)}, bf16[128,2048]{1,0:T(8,128)(2,1)}, u32[]{:S(2)}) copy-start(bf16[128,2048]{1,0:T(8,128)(2,1)} %refs_6_) | copy-start | bytes 1572868
  146.2 34.8 %copy-start.5 = (bf16[128,2048]{1,0:T(8,128)(2,1)S(1)}, bf16[128,2048]{1,0:T(8,128)(2,1)}, u32[]{:S(2)}) copy-start(bf16[128,2048]{1,0:T(8,128)(2,1)} %copy-done.4) | copy-start | bytes 1572868
  146.2 34.8 %copy-start.7 = (bf16[128,2048]{1,0:T(8,128)(2,1)S(1)}, bf16[128,2048]{1,0:T(8,128)(2,1)}, u32[]{:S(2)}) copy-start(bf16[128,2048]{1,0:T(8,128)(2,1)} %copy-done.6) | copy-start | bytes 1572868
  146.2 34.8 %copy-start.8 = (bf16[1024,256]{1,0:T(8,128)(2,1)S(1)}, bf16[1024,256]{1,0:T(8,128)(2,1)}, u32[]{:S(2)}) copy-start(bf16[1024,256]{1,0:T(8,128)(2,1)} %get-tuple-element.129.normed_hbm.refs_3_) | copy-start | bytes 1572868
  146.2 34.8 %copy-start.10 = (bf16[128,2048]{1,0:T(8,128)(2,1)S(1)}, bf16[128,2048]{1,0:T(8,128)(2,1)}, u32[]{:S(2)}) copy-start(bf16[128,2048]{1,0:T(8,128)(2,1)} %copy-done.9) | copy-start | bytes 1572868
  146.2 34.8 %copy-start.12 = (bf16[128,2048]{1,0:T(8,128)(2,1)S(1)}, bf16[128,2048]{1,0:T(8,128)(2,1)}, u32[]{:S(2)}) copy-start(bf16[128,2048]{1,0:T(8,128)(2,1)} %copy-done.11) | copy-start | bytes 1572868
  146.2 34.8 %copy-start.16 = (bf16[64,2048]{1,0:T(8,128)(2,1)S(1)}, bf16[64,2048]{1,0:T(8,128)(2,1)}, u32[]{:S(2)}) copy-start(bf16[64,2048]{1,0:T(8,128)(2,1)} %copy-done.15) | copy-start | bytes 786436
  146.3 34.8 %copy-start.21 = (f32[2048]{0:T(1024)S(1)}, f32[2048]{0:T(1024)}, u32[]{:S(2)}) copy-start(f32[2048]{0:T(1024)} %param.9) | copy-start | bytes 24580
  146.3 34.8 %copy-start.24 = (f32[16,128]{1,0:T(8,128)S(1)}, f32[16,128]{1,0:T(8,128)}, u32[]{:S(2)}) copy-start(f32[16,128]{1,0:T(8,128)} %get-tuple-element.112.inv_hbm.refs_4_) | copy-start | bytes 24580
  146.3 34.8 %copy-start.27 = (s32[11]{0:T(128)S(1)}, s32[11]{0:T(128)}, u32[]{:S(2)}) copy-start(s32[11]{0:T(128)} %stack.47.order_ref.refs_0_) | copy-start | bytes 136
  150.4 14.5 %all-to-all-start.10 = ((bf16[8,128,256]{2,1,0:T(8,128)(2,1)}), bf16[8,128,256]{2,1,0:T(8,128)(2,1)}, u32[]{:S(2)}, u32[]{:S(2)}) async-start(bf16[8,128,256]{2,1,0:T(8,128)(2,1)} %d_embed_kernel.1), calls=%async_computation.10 | async-start | bytes 1048576 | tf_op jit(solution)/shard_map/all_to_all | solution.py:19
  155.4 18.1 %collective-permute-start.9 = (bf16[64,2048]{1,0:T(8,128)(2,1)}, bf16[64,2048]{1,0:T(8,128)(2,1)}, u32[]{:S(2)}, u32[]{:S(2)}) collective-permute-start(bf16[64,2048]{1,0:T(8,128)(2,1)} %get-tuple-element.138), channel_id=1, source_target_pairs={{0,32},{8,40},{16,48},{24,56},{32,64},{40,72},{48,80},{56,88},{64,... | collective-permute-start | bytes 786440 | tf_op jit(solution)/shard_map/ppermute | solution.py:712
  155.6 17.9 %collective-permute-start.10 = (bf16[64,2048]{1,0:T(8,128)(2,1)}, bf16[64,2048]{1,0:T(8,128)(2,1)}, u32[]{:S(2)}, u32[]{:S(2)}) collective-permute-start(bf16[64,2048]{1,0:T(8,128)(2,1)} %get-tuple-element.139), channel_id=1, source_target_pairs={{0,64},{8,72},{16,80},{24,88},{32,96},{40,104},{48,112},{56,120},{... | collective-permute-start | bytes 786440 | tf_op jit(solution)/shard_map/ppermute | solution.py:712
  157.5 16.0 %collective-permute-start.11 = (bf16[64,2048]{1,0:T(8,128)(2,1)}, bf16[64,2048]{1,0:T(8,128)(2,1)}, u32[]{:S(2)}, u32[]{:S(2)}) collective-permute-start(bf16[64,2048]{1,0:T(8,128)(2,1)} %get-tuple-element.140), channel_id=1, source_target_pairs={{0,96},{8,104},{16,112},{24,120},{32,0},{40,8},{48,16},{56,24},{64... | collective-permute-start | bytes 786440 | tf_op jit(solution)/shard_map/ppermute | solution.py:712
  169.3 11.7 %all-to-all-start.11 = ((bf16[16,32,256]{2,1,0:T(8,128)(2,1)}), bf16[16,32,256]{2,1,0:T(8,128)(2,1)}, u32[]{:S(2)}, u32[]{:S(2)}) async-start(bf16[16,32,256]{2,1,0:T(8,128)(2,1)} %copy-done.19), calls=%async_computation.11 | async-start | bytes 524288 | tf_op jit(solution)/shard_map/all_to_all | solution.py:19
  175.6 10.9 %collective-permute-start.12 = (bf16[16,2048]{1,0:T(8,128)(2,1)}, bf16[16,2048]{1,0:T(8,128)(2,1)}, u32[]{:S(2)}, u32[]{:S(2)}) collective-permute-start(bf16[16,2048]{1,0:T(8,128)(2,1)} %get-tuple-element.142), channel_id=1, source_target_pairs={{0,8},{8,16},{16,24},{24,0},{32,40},{40,48},{48,56},{56,32},{64,72... | collective-permute-start | bytes 196616 | tf_op jit(solution)/shard_map/ppermute | solution.py:754
  176.8 9.8 %collective-permute-start.13 = (bf16[16,2048]{1,0:T(8,128)(2,1)}, bf16[16,2048]{1,0:T(8,128)(2,1)}, u32[]{:S(2)}, u32[]{:S(2)}) collective-permute-start(bf16[16,2048]{1,0:T(8,128)(2,1)} %get-tuple-element.143), channel_id=1, source_target_pairs={{0,16},{8,24},{16,0},{24,8},{32,48},{40,56},{48,32},{56,40},{64,80... | collective-permute-start | bytes 196616 | tf_op jit(solution)/shard_map/ppermute | solution.py:754
  179.2 7.4 %collective-permute-start.14 = (bf16[16,2048]{1,0:T(8,128)(2,1)}, bf16[16,2048]{1,0:T(8,128)(2,1)}, u32[]{:S(2)}, u32[]{:S(2)}) collective-permute-start(bf16[16,2048]{1,0:T(8,128)(2,1)} %get-tuple-element.144), channel_id=1, source_target_pairs={{0,24},{8,0},{16,8},{24,16},{32,56},{40,32},{48,40},{56,48},{64,88... | collective-permute-start | bytes 196616 | tf_op jit(solution)/shard_map/ppermute | solution.py:754
  182.3 15.7 %copy-start.28 = (bf16[16,2048]{1,0:T(8,128)(2,1)S(1)}, bf16[16,2048]{1,0:T(8,128)(2,1)}, u32[]{:S(2)}) copy-start(bf16[16,2048]{1,0:T(8,128)(2,1)} %get-tuple-element.151) | copy-start | bytes 196612
  186.6 28.0 %all-to-all-start.12 = ((bf16[128,40,128]{2,1,0:T(8,128)(2,1)}), bf16[128,40,128]{2,1,0:T(8,128)(2,1)S(1)}, u32[]{:S(2)}, u32[]{:S(2)}) async-start(bf16[128,40,128]{2,1,0:T(8,128)(2,1)} %get-tuple-element.145), calls=%async_computation.12 | async-start | bytes 2621440 | tf_op jit(solution)/shard_map/all_to_all | solution.py:19
  192.6 7.1 %collective-permute-start.15 = (f32[16,256]{1,0:T(8,128)S(1)}, f32[16,256]{1,0:T(8,128)S(1)}, u32[]{:S(2)}, u32[]{:S(2)}) collective-permute-start(f32[16,256]{1,0:T(8,128)S(1)} %get-tuple-element.146), channel_id=1, source_target_pairs={{0,0},{1,16},{2,32},{3,48},{4,64},{5,80},{6,96},{7,112},{8,1},{9,1... | collective-permute-start | bytes 49160 | tf_op jit(solution)/shard_map/ppermute | solution.py:805
  (4 other events, 13.7 us)
